TPU v7x, 32 devices: a whole 2x2x4 slice. The times are simulated.
32 devices in a mesh: wide: 8 (over z, x), narrow: 4 (over y, core).
Axes of the slice: x: 2, y: 2, z: 4, core: 2. Of those that a mesh axis runs over, the one named last changes fastest.
Arguments:
- layer_input: bfloat16 [32, 1024, 768], P(('wide', 'narrow')), may hold values from -6 to 6
- cotangent: bfloat16 [32, 1024, 768], P(('wide', 'narrow')), may hold values from -6 to 6
- block_size: int32 [32], P(('wide', 'narrow')), may hold values from 4 to 16, as said below
- gain_attn: bfloat16 [768], P('narrow'), may hold values from 0.5 to 1.5
- w_qkv: bfloat16 [768, 2304], P('narrow'), may hold values from -0.21875 to 0.21875
- w_out: bfloat16 [768, 768], P('narrow'), may hold values from -0.875 to 0.875
- gain_mlp: bfloat16 [768], P('narrow'), may hold values from 0.5 to 1.5
- w_up: bfloat16 [768, 3072], P('narrow'), may hold values from -0.21875 to 0.21875
- b_up: bfloat16 [3072], P('narrow'), may hold values from -3 to 3
- w_down: bfloat16 [3072, 768], P('narrow'), may hold values from -0.109375 to 0.109375
- b_down: bfloat16 [768], P('narrow'), may hold values from -3 to 3
Outputs:
- layer_output: bfloat16 [32, 1024, 768], P(('wide', 'narrow'))
- d_x: bfloat16 [32, 1024, 768], P(('wide', 'narrow'))
- grad_gain_attn: float32 [768], P('narrow')
- grad_qkv: float32 [768, 2304], P('narrow')
- grad_out: float32 [768, 768], P('narrow')
- grad_gain_mlp: float32 [768], P('narrow')
- grad_up: float32 [768, 3072], P('narrow')
- grad_b_up: float32 [3072], P('narrow')
- grad_down: float32 [3072, 768], P('narrow')
- grad_b_down: float32 [768], P('narrow')
Inputs may be any that keep to these rules, and one draw needn't show every extreme that they name: `block_size`: each example's block size is 4, 8 or 16; every draw has examples with 4 and with 16.
All inputs are finite; a program needn't handle non-finite values.
Results may differ from a plain program's by a relative error of at most 0.015.
Values may be sent and summed in bfloat16 or wider, within the bound.
No kernel may reach another device: no remote copies, remote signals or barrier semaphores. Data moves between devices by JAX's collectives and lax.ppermute only.
A program may use at most 256 MiB of HBM per device.

v0:
```python
import jax
import jax.numpy as jnp
from jax import lax
from jax.sharding import PartitionSpec as P

HEAD = 64


def norm_fwd(values, gain):
    centre = values - jnp.mean(values, axis=-1, keepdims=True)
    spread = jnp.mean(centre * centre, axis=-1, keepdims=True)
    inverse = lax.rsqrt(spread + 1e-05)
    scaled = centre * inverse
    return (scaled * gain, scaled, inverse)


def norm_back(d_norm, scaled, inverse, gain):
    d_gain = jnp.sum(d_norm * scaled, axis=0)
    d_scaled = d_norm * gain
    d_in = inverse * (
        d_scaled
        - jnp.mean(d_scaled, axis=-1, keepdims=True)
        - scaled * jnp.mean(d_scaled * scaled, axis=-1, keepdims=True)
    )
    return (d_in, d_gain)


def rotate(tensor, cosine, sine):
    half = tensor.shape[-1] // 2
    first = tensor[..., :half]
    second = tensor[..., half:]
    return jnp.concatenate(
        [first * cosine - second * sine, second * cosine + first * sine], axis=-1
    )


def rotate_back(tensor, cosine, sine):
    half = tensor.shape[-1] // 2
    first = tensor[..., :half]
    second = tensor[..., half:]
    return jnp.concatenate(
        [first * cosine + second * sine, second * cosine - first * sine], axis=-1
    )


def probs_of(q_part, k_part, allowed):
    scores = jnp.einsum("qhd,khd->hqk", q_part, k_part, preferred_element_type=jnp.float32) * 0.125
    scores = jnp.where(allowed[None], scores, -1e30)
    expo = jnp.exp(scores - jnp.max(scores, axis=-1, keepdims=True))
    return expo / jnp.sum(expo, axis=-1, keepdims=True)


def part_back(q_part, k_part, v_part, allowed, d_out):
    probs = probs_of(q_part, k_part, allowed)
    probs_low = probs.astype(jnp.bfloat16)
    d_vals = jnp.einsum("hqk,qhd->khd", probs_low, d_out, preferred_element_type=jnp.float32)
    d_probs = jnp.einsum("qhd,khd->hqk", d_out, v_part, preferred_element_type=jnp.float32)
    d_scores = probs * (d_probs - jnp.sum(d_probs * probs, axis=-1, keepdims=True))
    d_low = d_scores.astype(jnp.bfloat16)
    d_query = jnp.einsum("hqk,khd->qhd", d_low, k_part, preferred_element_type=jnp.float32) * 0.125
    d_keys = jnp.einsum("hqk,qhd->khd", d_low, q_part, preferred_element_type=jnp.float32) * 0.125
    return (d_query, d_keys, d_vals)


def outer_sum(left, right):
    return lax.dot_general(
        left, right, (((0,), (0,)), ((), ())), preferred_element_type=jnp.float32
    )


def inner_prod(left, right):
    return lax.dot_general(
        left, right, (((1,), (1,)), ((), ())), preferred_element_type=jnp.float32
    )


def shards(
    layer_input,
    cotangent,
    block_size,
    gain_attn,
    w_qkv,
    w_out,
    gain_mlp,
    w_up,
    b_up,
    w_down,
    b_down,
):
    full = (
        lax.all_gather(gain_attn, "narrow", axis=0, tiled=True),
        lax.all_gather(w_qkv, "narrow", axis=0, tiled=True),
        lax.all_gather(w_out, "narrow", axis=0, tiled=True),
        lax.all_gather(gain_mlp, "narrow", axis=0, tiled=True),
        lax.all_gather(w_up, "narrow", axis=0, tiled=True),
        lax.all_gather(b_up, "narrow", axis=0, tiled=True),
        lax.all_gather(w_down, "narrow", axis=0, tiled=True),
        lax.all_gather(b_down, "narrow", axis=0, tiled=True),
    )
    g_attn, wqkv, wout, g_mlp, wup, bup, wdown, bdown = full
    xval = layer_input[0].astype(jnp.float32)
    rows = xval.shape[0]
    seq = rows // 2
    width = xval.shape[1]
    heads = width // HEAD
    half = HEAD // 2
    posit = jnp.concatenate([jnp.arange(seq), jnp.arange(seq)])
    freq = 10000.0 ** (-jnp.arange(half).astype(jnp.float32) / half)
    angles = posit.astype(jnp.float32)[:, None] * freq[None, :]
    cosine = jnp.cos(angles)[:, None, :]
    sine = jnp.sin(angles)[:, None, :]
    block = jnp.arange(seq, dtype=jnp.int32) // block_size[0]
    same_block = block[None, :] == block[:, None]
    earlier = block[None, :] < block[:, None]
    noisy_mask = jnp.concatenate([same_block, earlier], axis=1)
    clean_mask = block[None, :] <= block[:, None]
    normed, scaled1, inverse1 = norm_fwd(xval, g_attn.astype(jnp.float32))
    a1 = normed.astype(jnp.bfloat16)
    qkv = jnp.dot(a1, wqkv, preferred_element_type=jnp.float32)
    query = rotate(qkv[:, :width].reshape(rows, heads, HEAD), cosine, sine).astype(jnp.bfloat16)
    keys = rotate(qkv[:, width : 2 * width].reshape(rows, heads, HEAD), cosine, sine).astype(
        jnp.bfloat16
    )
    vals = qkv[:, 2 * width :].reshape(rows, heads, HEAD).astype(jnp.bfloat16)
    probs_noisy = probs_of(query[:seq], keys, noisy_mask).astype(jnp.bfloat16)
    probs_clean = probs_of(query[seq:], keys[seq:], clean_mask).astype(jnp.bfloat16)
    out_noisy = jnp.einsum("hqk,khd->qhd", probs_noisy, vals, preferred_element_type=jnp.float32)
    out_clean = jnp.einsum(
        "hqk,khd->qhd", probs_clean, vals[seq:], preferred_element_type=jnp.float32
    )
    attended = (
        jnp.concatenate([out_noisy, out_clean], axis=0).reshape(rows, width).astype(jnp.bfloat16)
    )
    x_mid = xval + jnp.dot(attended, wout, preferred_element_type=jnp.float32)
    normed2, scaled2, inverse2 = norm_fwd(x_mid, g_mlp.astype(jnp.float32))
    a2 = normed2.astype(jnp.bfloat16)
    upper = jnp.dot(a2, wup, preferred_element_type=jnp.float32) + bup.astype(jnp.float32)
    active, gelu_pull = jax.vjp(lambda value: jax.nn.gelu(value, approximate=True), upper)
    hidden = active.astype(jnp.bfloat16)
    output = (
        x_mid
        + jnp.dot(hidden, wdown, preferred_element_type=jnp.float32)
        + bdown.astype(jnp.float32)
    )
    again = (
        lax.all_gather(gain_attn, "narrow", axis=0, tiled=True),
        lax.all_gather(w_qkv, "narrow", axis=0, tiled=True),
        lax.all_gather(w_out, "narrow", axis=0, tiled=True),
        lax.all_gather(gain_mlp, "narrow", axis=0, tiled=True),
        lax.all_gather(w_up, "narrow", axis=0, tiled=True),
        lax.all_gather(b_up, "narrow", axis=0, tiled=True),
        lax.all_gather(w_down, "narrow", axis=0, tiled=True),
        lax.all_gather(b_down, "narrow", axis=0, tiled=True),
    )
    g_attn, wqkv, wout, g_mlp, wup, bup, wdown, bdown = again
    d_out_low = cotangent[0]
    d_out = d_out_low.astype(jnp.float32)
    grad_b_down = jnp.sum(d_out, axis=0)
    grad_down = outer_sum(hidden, d_out_low)
    d_hidden = inner_prod(d_out_low, wdown)
    d_upper = gelu_pull(d_hidden)[0]
    d_upper_low = d_upper.astype(jnp.bfloat16)
    grad_b_up = jnp.sum(d_upper, axis=0)
    grad_up = outer_sum(a2, d_upper_low)
    d_a2 = inner_prod(d_upper_low, wup)
    d_mid_norm, grad_gain_mlp = norm_back(d_a2, scaled2, inverse2, g_mlp.astype(jnp.float32))
    d_mid = d_out + d_mid_norm
    d_mid_low = d_mid.astype(jnp.bfloat16)
    grad_out = outer_sum(attended, d_mid_low)
    d_att = inner_prod(d_mid_low, wout).astype(jnp.bfloat16).reshape(rows, heads, HEAD)
    dq_noisy, dk_noisy, dv_noisy = part_back(query[:seq], keys, vals, noisy_mask, d_att[:seq])
    dq_clean, dk_clean, dv_clean = part_back(
        query[seq:], keys[seq:], vals[seq:], clean_mask, d_att[seq:]
    )
    d_query = jnp.concatenate([dq_noisy, dq_clean], axis=0)
    d_keys = dk_noisy.at[seq:].add(dk_clean)
    d_vals = dv_noisy.at[seq:].add(dv_clean)
    d_qkv = jnp.concatenate(
        [
            rotate_back(d_query, cosine, sine).reshape(rows, width),
            rotate_back(d_keys, cosine, sine).reshape(rows, width),
            d_vals.reshape(rows, width),
        ],
        axis=1,
    ).astype(jnp.bfloat16)
    grad_qkv = outer_sum(a1, d_qkv)
    d_a1 = inner_prod(d_qkv, wqkv)
    d_in_norm, grad_gain_attn = norm_back(d_a1, scaled1, inverse1, g_attn.astype(jnp.float32))
    d_input = (d_mid + d_in_norm).astype(jnp.bfloat16)
    shares = (
        lax.psum_scatter(
            grad_gain_attn.astype(jnp.bfloat16), "narrow", scatter_dimension=0, tiled=True
        ).astype(jnp.float32),
        lax.psum_scatter(
            grad_qkv.astype(jnp.bfloat16), "narrow", scatter_dimension=0, tiled=True
        ).astype(jnp.float32),
        lax.psum_scatter(
            grad_out.astype(jnp.bfloat16), "narrow", scatter_dimension=0, tiled=True
        ).astype(jnp.float32),
        lax.psum_scatter(
            grad_gain_mlp.astype(jnp.bfloat16), "narrow", scatter_dimension=0, tiled=True
        ).astype(jnp.float32),
        lax.psum_scatter(
            grad_up.astype(jnp.bfloat16), "narrow", scatter_dimension=0, tiled=True
        ).astype(jnp.float32),
        lax.psum_scatter(
            grad_b_up.astype(jnp.bfloat16), "narrow", scatter_dimension=0, tiled=True
        ).astype(jnp.float32),
        lax.psum_scatter(
            grad_down.astype(jnp.bfloat16), "narrow", scatter_dimension=0, tiled=True
        ).astype(jnp.float32),
        lax.psum_scatter(
            grad_b_down.astype(jnp.bfloat16), "narrow", scatter_dimension=0, tiled=True
        ).astype(jnp.float32),
    )
    totals = lax.psum(
        (shares[0], shares[1], shares[2], shares[3], shares[4], shares[5], shares[6], shares[7]),
        "wide",
    )
    return (
        output.astype(jnp.bfloat16)[None],
        d_input[None],
        totals[0],
        totals[1],
        totals[2],
        totals[3],
        totals[4],
        totals[5],
        totals[6],
        totals[7],
    )


def solution(mesh):
    return jax.shard_map(
        shards,
        mesh=mesh,
        in_specs=(
            P(("wide", "narrow"), None, None),
            P(("wide", "narrow"), None, None),
            P(("wide", "narrow")),
            P("narrow"),
            P("narrow", None),
            P("narrow", None),
            P("narrow"),
            P("narrow", None),
            P("narrow"),
            P("narrow", None),
            P("narrow"),
        ),
        out_specs=(
            P(("wide", "narrow"), None, None),
            P(("wide", "narrow"), None, None),
            P("narrow"),
            P("narrow", None),
            P("narrow", None),
            P("narrow"),
            P("narrow", None),
            P("narrow"),
            P("narrow", None),
            P("narrow"),
        ),
        check_vma=False,
    )
```

profile of v0, /device:TPU:0, one launch (start us, length us, event | category | flops | bytes accessed | tf_op | source)
XLA Modules:
  0.0 715.2 jit_solution(14938052615353714872)
XLA Ops:
  12.5 8.3 %all-reduce.9 = (bf16[768]{0:T(1024)(128)(2,1)S(1)}, bf16[768]{0:T(1024)(128)(2,1)S(1)}) all-reduce(bf16[768]{0:T(1024)(128)(2,1)S(1)} %dynamic-update-slice.6, bf16[768]{0:T(1024)(128)(2,1)S(1)} %dynamic-update-slice.7), channel_id=1, replica_groups=mesh['wide'=8,'narrow'=4] {'narrow'}, use_global_device_ids=true, to_apply=%add | all-reduce | flops 1536 | bytes 6144
  20.9 5.2 all-gather
  28.6 1.8 copy.53
  31.2 1.6 copy.61
  33.4 2.0 pad_add_fusion
  35.4 7.8 %all-gather.6.cloned.1.call-done = bf16[768,2304]{1,0:T(8,128)(2,1)} async-done(((bf16[192,2304]{1,0:T(8,128)(2,1)}), bf16[768,2304]{1,0:T(8,128)(2,1)}) %all-gather.6.cloned.1.call-update) | async-done | bytes 3538960 | tf_op jit(solution)/shard_map/all_gather | solution.py:92
  43.2 6.1 fusion.90
  51.5 3.1 fusion.87
  54.6 2.4 copy.56
  57.0 2.6 copy.54
  59.6 2.3 copy.57
  61.9 3.6 copy.55
  65.4 2.9 subtract_convert_fusion.2
  70.0 10.8 %fusion.68 = f32[12,512,1024]{2,1,0:T(8,128)} fusion(bf16[1024,12,32]{0,2,1:T(8,128)(2,1)S(1)} %get-tuple-element.92, bf16[1024,12,32]{0,2,1:T(8,128)(2,1)S(1)} %get-tuple-element.91, bf16[1024,12,32]{0,2,1:T(8,128)(2,1)S(1)} %get-tuple-element.100, bf16[1024,12,32]{0,2,1:T(8,128)(2,1)S(1)} %get-tuple-element.99), kind=kOutput, calls=%fused_computation.110 | convolution fusion | flops 810024960 | bytes 28311552 | tf_op jit(solution)/shard_map/qhd,khd->hqk/dot_general | solution.py:47
  80.8 10.6 %fusion.91 = (f32[12,512]{1,0:T(8,128)S(1)}, f32[12,512,512]{1,2,0:T(8,128)}) fusion(pred[512,512]{0,1:T(8,128)(4,1)S(1)} %copy-done.39, bf16[1024,12,32]{0,2,1:T(8,128)(2,1)} %copy-done.11, bf16[1024,12,32]{0,2,1:T(8,128)(2,1)} %copy-done.13, bf16[1024,12,32]{0,2,1:T(8,128)(2,1)} %copy-done.9, bf16[1024,12,32]{0,2,1:T(8,128)(2,1)} %copy-done.7), kind=kOutput, calls=%fused_computation.153 | convolution fusion | flops 418382336 | bytes 16015360 | tf_op jit(solution)/shard_map/sub | solution.py:49
  91.4 33.6 %fusion.92 = (f32[12,512]{1,0:T(8,128)S(1)}, f32[12,512,1024]{2,1,0:T(8,128)}) fusion(f32[12,512,1024]{2,1,0:T(8,128)} %fusion.68, pred[512,1024]{1,0:T(8,128)(4,1)S(1)} %copy-done.32), kind=kOutput, calls=%fused_computation.154 | output fusion | flops 37749760 | bytes 50880512 | tf_op jit(solution)/shard_map/sub | solution.py:49
  124.9 6.0 fusion.65
  130.9 10.8 %fusion.62 = bf16[512,12,64]{0,2,1:T(8,128)(2,1)S(1)} fusion(bf16[1024,12,64]{0,2,1:T(8,128)(2,1)S(1)} %bitcast.117, f32[12,512,1024]{2,1,0:T(8,128)} %get-tuple-element.113, f32[12,512]{1,0:T(8,128)S(1)} %get-tuple-element.112), kind=kOutput, calls=%fused_computation.108 | convolution fusion | flops 818282496 | bytes 27549696 | tf_op jit(solution)/shard_map/hqk,khd->qhd/dot_general | solution.py:127
  143.1 3.7 fusion.93
  147.3 11.1 %fusion.86 = f32[1024,3072]{1,0:T(8,128)} fusion(bf16[768,3072]{1,0:T(8,128)(2,1)} %all-gather.10.cloned.1.call-done, f32[1024,768]{0,1:T(8,128)S(1)} %get-tuple-element.115, f32[768]{0:T(1024)S(1)} %convert_element_type.142, f32[1024]{0:T(1024)S(1)} %add_rsqrt_fusion, f32[1024]{0:T(1024)S(1)} %broadcast_multiply_fusion.4), kind=kOutput, calls=%fused_computation.148 | convolution fusion | flops 4834983936 | bytes 20458496 | tf_op jit(solution)/shard_map/dot_general | solution.py:137
  158.4 17.1 %fusion.94 = (bf16[3072]{0:T(1024)(128)(2,1)}, bf16[1024,3072]{1,0:T(8,128)(2,1)S(1)}) fusion(f32[1024,3072]{1,0:T(8,128)} %fusion.86, f32[3072]{0:T(1024)S(1)} %bitcast.132, bf16[3072,768]{1,0:T(8,128)(2,1)} %all-gather.12.cloned.1.call-done, bf16[1,1024,768]{2,1,0:T(8,128)(2,1)} %param.16), kind=kOutput, calls=%fused_computation.156 | convolution fusion | flops 4901041152 | bytes 25184256 | tf_op jit(solution)/shard_map/dot_general | solution.py:72
  175.6 6.1 multiply_reduce_fusion.2
  182.8 1.6 copy-done.6
  184.4 2.4 convolution_convert_fusion.4
  186.9 3.3 convolution_convert_fusion.3
  192.1 9.5 %fusion.15 = f32[12,64,1024]{2,1,0:T(8,128)S(1)} fusion(bf16[512,12,64]{0,2,1:T(8,128)(2,1)S(1)} %bitcast.130, f32[12,512,1024]{2,1,0:T(8,128)} %get-tuple-element.113, f32[12,512]{1,0:T(8,128)S(1)} %get-tuple-element.112), kind=kOutput, calls=%fused_computation.28 | convolution fusion | flops 817889280 | bytes 29122560 | tf_op jit(solution)/shard_map/hqk,qhd->khd/dot_general | solution.py:56
  201.5 16.8 %multiply_reduce_fusion = (f32[12,512]{1,0:T(8,128)S(1)}, f32[12,512,1024]{2,1,0:T(8,128)}) fusion(f32[12,512,1024]{2,1,0:T(8,128)} %get-tuple-element.113, f32[12,512]{1,0:T(8,128)S(1)} %get-tuple-element.112, bf16[512,12,64]{0,2,1:T(8,128)(2,1)} %bitcast.131, bf16[1024,12,64]{0,2,1:T(8,128)(2,1)} %bitcast.116), kind=kOutput, calls=%fused_computation.3 | convolution fusion | flops 824174592 | bytes 52740096 | tf_op jit(solution)/shard_map/qhd,khd->hqk/dot_general | solution.py:57
  219.8 10.8 %multiply_reduce_fusion.1 = (f32[12,512]{1,0:T(8,128)S(1)}, f32[12,512,512]{1,2,0:T(8,128)}) fusion(f32[12,512,512]{1,2,0:T(8,128)} %get-tuple-element.111, f32[12,512]{1,0:T(8,128)S(1)} %get-tuple-element.110, bf16[512,12,64]{0,2,1:T(8,128)(2,1)S(1)} %bitcast.128, bf16[512,12,64]{0,2,1:T(8,128)(2,1)S(1)} %bitcast.127), kind=kOutput, calls=%fused_computation.16 | convolution fusion | flops 412084224 | bytes 26787840 | tf_op jit(solution)/shard_map/qhd,khd->hqk/dot_general | solution.py:57
  232.0 2.2 fusion.47
  234.4 7.3 %multiply_convert_fusion.1 = bf16[12,512,512]{1,2,0:T(8,128)(2,1)S(1)} fusion(f32[12,512,512]{1,2,0:T(8,128)} %get-tuple-element.118, f32[12,512]{1,0:T(8,128)S(1)} %get-tuple-element.117, f32[12,512,512]{1,2,0:T(8,128)S(1)} %bitcast.114, f32[12,512]{1,0:T(8,128)S(1)} %get-tuple-element.110), kind=kLoop, calls=%fused_computation.15 | loop fusion | flops 12582912 | bytes 31506432 | tf_op jit(solution)/shard_map/convert_element_type | solution.py:59
  242.9 16.7 %multiply_convert_fusion = bf16[12,512,1024]{2,1,0:T(8,128)(2,1)S(1)} fusion(f32[12,512,1024]{2,1,0:T(8,128)} %get-tuple-element.120, f32[12,512]{1,0:T(8,128)S(1)} %get-tuple-element.119, f32[12,512,1024]{2,1,0:T(8,128)} %get-tuple-element.113, f32[12,512]{1,0:T(8,128)S(1)} %get-tuple-element.112), kind=kLoop, calls=%fused_computation.2 | loop fusion | flops 25165824 | bytes 62963712 | tf_op jit(solution)/shard_map/convert_element_type | solution.py:59
  259.7 2.3 multiply_bitcast_fusion
  262.1 2.2 copy-done
  264.2 2.1 fusion.48
  266.3 8.5 %multiply_bitcast_fusion.2 = f32[512,12,64]{0,2,1:T(8,128)S(1)} fusion(bf16[12,512,1024]{2,1,0:T(8,128)(2,1)} %copy-done, bf16[1024,12,32]{0,2,1:T(8,128)(2,1)S(1)} %copy-done.10, bf16[1024,12,32]{0,2,1:T(8,128)(2,1)S(1)} %copy-done.8), kind=kOutput, calls=%fused_computation.98 | convolution fusion | flops 808845312 | bytes 15728640 | tf_op jit(solution)/shard_map/hqk,khd->qhd/dot_general | solution.py:60
  278.1 9.1 %convolution_convert_fusion.2 = bf16[768,2304]{1,0:T(8,128)(2,1)} fusion(bf16[1024,768]{0,1:T(8,128)(2,1)S(1)} %bitcast.124, bf16[1024,768]{0,1:T(8,128)(2,1)S(1)} %bitcast.120, bf16[1024,768]{0,1:T(8,128)(2,1)S(1)} %bitcast.118, bf16[1,1024,768]{1,2,0:T(8,128)(2,1)S(1)} %copy-done.4, f32[768]{0:T(1024)S(1)} %copy-done.43, f32[1024]{0:T(1024)S(1)} %copy-done.45, ...), kind=kOutput, calls=%fused_computation.35 | convolution fusion | flops 3643736064 | bytes 9841664 | tf_op jit(solution)/shard_map/dot_general | solution.py:66
  288.5 12.2 %convolution_convert_fusion = bf16[3072,768]{1,0:T(8,128)(2,1)} fusion(bf16[1,1024,768]{2,1,0:T(8,128)(2,1)S(1)} %copy-done.16, f32[1024,3072]{1,0:T(8,128)} %fusion.86, f32[3072]{0:T(1024)S(1)} %bitcast.133), kind=kOutput, calls=%fused_computation.33 | convolution fusion | flops 4865654784 | bytes 18886656 | tf_op jit(solution)/shard_map/dot_general | solution.py:66
  300.8 1.8 copy-done.2
  302.6 9.9 %convolution_convert_fusion.1 = bf16[768,3072]{1,0:T(8,128)(2,1)} fusion(bf16[1024,3072]{1,0:T(8,128)(2,1)} %copy-done.56, f32[1024,768]{0,1:T(8,128)S(1)} %copy-done.2, f32[768]{0:T(1024)S(1)} %copy-done.36, f32[1024]{0:T(1024)S(1)} %copy-done.38, f32[1024]{0:T(1024)S(1)} %copy-done.34), kind=kOutput, calls=%fused_computation.34 | convolution fusion | flops 4837343232 | bytes 14167040 | tf_op jit(solution)/shard_map/dot_general | solution.py:66
  313.8 1.7 reduce_sum.170
  315.8 9.8 %fusion.34 = (bf16[768]{0:T(1024)(128)(2,1)S(1)}, f32[1024]{0:T(1024)S(1)}, f32[1024]{0:T(1024)S(1)}, f32[1024,768]{0,1:T(8,128)}) fusion(bf16[1,1024,768]{1,2,0:T(8,128)(2,1)} %copy-done.3, f32[1024]{0:T(1024)S(1)} %copy-done.45, f32[1024]{0:T(1024)S(1)} %copy-done.41, f32[768]{0:T(1024)S(1)} %copy-done.43, ...), kind=kOutput, calls=%fused_computation.53 | convolution fusion | flops 3645109504 | bytes 12997120 | tf_op jit(solution)/shard_map/dot_general | solution.py:72
  325.6 10.6 %all-reduce.8 = (bf16[768]{0:T(1024)(128)(2,1)S(1)}, bf16[768]{0:T(1024)(128)(2,1)S(1)}, bf16[768]{0:T(1024)(128)(2,1)S(1)}, bf16[3072]{0:T(1024)(128)(2,1)S(1)}, bf16[768]{0:T(1024)(128)(2,1)S(1)}) all-reduce(bf16[768]{0:T(1024)(128)(2,1)S(1)} %dynamic-update-slice.8, ...), channel_id=1, replica_groups=mesh['wide'=8,'narrow'=4] {'narrow'}, use_global_device_ids=true, to_apply=%add.2 | all-reduce | flops 6144 | bytes 24576
  336.2 13.1 %fusion.51 = bf16[1,1024,768]{1,2,0:T(8,128)(2,1)} fusion(f32[768]{0:T(1024)S(1)} %convert_element_type.146, f32[1024,768]{0,1:T(8,128)S(1)} %copy-done.2, bf16[3072,768]{1,0:T(8,128)(2,1)} %all-gather.12.cloned.1.call-done, f32[1024,3072]{1,0:T(8,128)} %fusion.86, f32[3072]{0:T(1024)S(1)} %bitcast.134), kind=kOutput, calls=%fused_computation.104 | convolution fusion | flops 4865654784 | bytes 22035456 | tf_op jit(solution)/shard_map/dot_general | solution.py:142
  349.3 3.0 copy.65
  352.4 3.9 fusion.45
  358.1 20.5 %reduce-scatter.11.cloned.1.call-done = bf16[768,768]{1,0:T(8,128)(2,1)} async-done(((bf16[3072,768]{1,0:T(8,128)(2,1)}), bf16[768,768]{1,0:T(8,128)(2,1)}) %reduce-scatter.11.cloned.1.call-update) | async-done | bytes 1179664 | tf_op jit(solution)/shard_map/reduce_scatter | solution.py:209
  378.6 50.6 %reduce-scatter.9.cloned.1.call-done = bf16[192,3072]{1,0:T(8,128)(2,1)} async-done(((bf16[768,3072]{1,0:T(8,128)(2,1)}), bf16[192,3072]{1,0:T(8,128)(2,1)}) %reduce-scatter.9.cloned.1.call-update) | async-done | bytes 1179664 | tf_op jit(solution)/shard_map/reduce_scatter | solution.py:203
  429.2 278.9 %all-reduce.11 = (f32[192]{0:T(256)}, f32[192,2304]{1,0:T(8,128)}, f32[192,768]{1,0:T(8,128)}, f32[192]{0:T(256)}, f32[192,3072]{1,0:T(8,128)}, /*index=5*/f32[768]{0:T(1024)}, f32[768,768]{1,0:T(8,128)}, f32[192]{0:T(256)}) all-reduce(f32[192]{0:T(256)S(1)} %dynamic-slice_convert_fusion.3, ...), channel_id=1, replica_groups=mesh['wide'=8,'narrow'=4] {'wide'}, use_global_device_ids=true, to_apply=%region_16.17 | all-reduce | flops 1770816 | bytes 10627584 | tf_op jit(solution)/shard_map/psum | solution.py:216
  (184 shorter events, 27.2 us)
Async XLA Ops:
  7.2 3.6 copy-start.50
  7.2 4.8 copy-start.53
  7.2 5.1 copy-start.54
  7.2 13.7 %copy-start.51 = (bf16[768]{0:T(1024)(128)(2,1)S(1)}, bf16[768]{0:T(1024)(128)(2,1)}, u32[]{:S(2)}) copy-start(bf16[768]{0:T(1024)(128)(2,1)} %param.23) | copy-start | bytes 4612
  7.2 36.0 %all-gather.6.cloned.1.call-start = ((), (), s32[]{:S(2)}) async-start(), calls=%async_computation.4 | async-start | bytes 4423680 | tf_op jit(solution)/shard_map/all_gather | solution.py:92
  8.0 135.1 %all-gather.8.cloned.1.call-start = ((), (), s32[]{:S(2)}) async-start(), calls=%async_computation.5 | async-start | bytes 1474560 | tf_op jit(solution)/shard_map/all_gather | solution.py:93
  8.7 138.6 %all-gather.10.cloned.1.call-start = ((), (), s32[]{:S(2)}) async-start(), calls=%async_computation.6 | async-start | bytes 5898240 | tf_op jit(solution)/shard_map/all_gather | solution.py:95
  9.4 149.0 %all-gather.12.cloned.1.call-start = ((), (), s32[]{:S(2)}) async-start(), calls=%async_computation.7 | async-start | bytes 5898240 | tf_op jit(solution)/shard_map/all_gather | solution.py:97
  10.0 348.1 %reduce-scatter.7.cloned.1.call-start = ((), (), s32[]{:S(2)}) async-start(), calls=%async_computation.9 | async-start | bytes 1474560 | tf_op jit(solution)/shard_map/reduce_scatter | solution.py:197
  20.9 22.3 %copy-start.42 = (f32[768]{0:T(1024)}, f32[768]{0:T(1024)S(1)}, u32[]{:S(2)}) copy-start(f32[768]{0:T(1024)S(1)} %convert_element_type.134) | copy-start | bytes 9220
  20.9 160.8 %copy-start.35 = (f32[768]{0:T(1024)}, f32[768]{0:T(1024)S(1)}, u32[]{:S(2)}) copy-start(f32[768]{0:T(1024)S(1)} %convert_element_type.142) | copy-start | bytes 9220
  26.1 132.3 %copy-start.46 = (f32[4,1,768]{2,1,0:T(1,128)}, f32[4,1,768]{2,1,0:T(1,128)S(1)}, u32[]{:S(2)}) copy-start(f32[4,1,768]{2,1,0:T(1,128)S(1)} %convert_element_type.170) | copy-start | bytes 36868
  28.6 2.6 copy-start.15
  30.4 12.8 %copy-start.3 = (bf16[1,1024,768]{1,2,0:T(8,128)(2,1)}, bf16[1,1024,768]{1,2,0:T(8,128)(2,1)S(1)}, u32[]{:S(2)}) copy-start(bf16[1,1024,768]{1,2,0:T(8,128)(2,1)S(1)} %copy.53) | copy-start | bytes 4718596
  30.7 18.6 %copy-start.40 = (f32[1024]{0:T(1024)}, f32[1024]{0:T(1024)S(1)}, u32[]{:S(2)}) copy-start(f32[1024]{0:T(1024)S(1)} %broadcast_multiply_fusion.5) | copy-start | bytes 12292
  31.2 18.1 %copy-start.44 = (f32[1024]{0:T(1024)}, f32[1024]{0:T(1024)S(1)}, u32[]{:S(2)}) copy-start(f32[1024]{0:T(1024)S(1)} %add_rsqrt_fusion.1) | copy-start | bytes 12292
  33.4 32.0 %copy-start.24 = (f32[1024,32]{0,1:T(8,128)}, f32[1024,32]{0,1:T(8,128)S(1)}, u32[]{:S(2)}) copy-start(f32[1024,32]{0,1:T(8,128)S(1)} %get-tuple-element.101) | copy-start | bytes 393220
  33.4 32.0 %copy-start.26 = (f32[1024,32]{0,1:T(8,128)}, f32[1024,32]{0,1:T(8,128)S(1)}, u32[]{:S(2)}) copy-start(f32[1024,32]{0,1:T(8,128)S(1)} %get-tuple-element.102) | copy-start | bytes 393220
  70.0 10.8 %copy-start.39 = (pred[512,512]{0,1:T(8,128)(4,1)S(1)}, pred[512,512]{0,1:T(8,128)(4,1)}, u32[]{:S(2)}) copy-start(pred[512,512]{0,1:T(8,128)(4,1)} %copy.58) | copy-start | bytes 786436
  80.8 10.6 %copy-start.32 = (pred[512,1024]{1,0:T(8,128)(4,1)S(1)}, pred[512,1024]{1,0:T(8,128)(4,1)}, u32[]{:S(2)}) copy-start(pred[512,1024]{1,0:T(8,128)(4,1)} %pad_add_fusion) | copy-start | bytes 1572868
  91.4 33.6 %copy-start.28 = (bf16[512,768]{0,1:T(8,128)(2,1)S(1)}, bf16[512,768]{0,1:T(8,128)(2,1)}, u32[]{:S(2)}) copy-start(bf16[512,768]{0,1:T(8,128)(2,1)} %copy.57) | copy-start | bytes 2359300
  124.9 6.0 copy-start.19
  146.8 34.9 %copy-start.1 = (f32[1024,768]{0,1:T(8,128)}, f32[1024,768]{0,1:T(8,128)S(1)}, u32[]{:S(2)}) copy-start(f32[1024,768]{0,1:T(8,128)S(1)} %get-tuple-element.115) | copy-start | bytes 9437188
  146.9 34.8 %copy-start.33 = (f32[1024]{0:T(1024)}, f32[1024]{0:T(1024)S(1)}, u32[]{:S(2)}) copy-start(f32[1024]{0:T(1024)S(1)} %broadcast_multiply_fusion.4) | copy-start | bytes 12292
  147.3 34.4 %copy-start.37 = (f32[1024]{0:T(1024)}, f32[1024]{0:T(1024)S(1)}, u32[]{:S(2)}) copy-start(f32[1024]{0:T(1024)S(1)} %add_rsqrt_fusion) | copy-start | bytes 12292
  158.4 17.1 %copy-start.18 = (bf16[768,3072]{1,0:T(8,128)(2,1)S(1)}, bf16[768,3072]{1,0:T(8,128)(2,1)}, u32[]{:S(2)}) copy-start(bf16[768,3072]{1,0:T(8,128)(2,1)} %all-gather.10.cloned.1.call-done) | copy-start | bytes 14155780
  175.6 6.1 copy-start.56
  175.6 6.2 copy-start.17
  181.7 2.7 copy-start.22
  184.4 2.5 copy-start.52
  218.3 139.8 %reduce-scatter.5.cloned.1.call-start = ((), (), s32[]{:S(2)}) async-start(), calls=%async_computation.8 | async-start | bytes 4423680 | tf_op jit(solution)/shard_map/reduce_scatter | solution.py:194
  218.4 12.1 %slice-start = ((s8[12582912]{0:T(1024)(128)(4,1)}), s8[4194304]{0:T(1024)(128)(4,1)S(1)}, s32[]{:S(2)}) async-start(s8[12582912]{0:T(1024)(128)(4,1)} %bitcast.113), calls=%async_computation.12 | async-start | bytes 8388608
  219.7 10.8 %slice-start.1 = ((s8[12582912]{0:T(1024)(128)(4,1)}), s8[4194304]{0:T(1024)(128)(4,1)S(1)}, s32[]{:S(2)}) async-start(s8[12582912]{0:T(1024)(128)(4,1)} %bitcast.113), calls=%async_computation.13 | async-start | bytes 8388608
  219.8 12.2 %slice-start.2 = ((s8[12582912]{0:T(1024)(128)(4,1)}), s8[4194304]{0:T(1024)(128)(4,1)S(1)}, s32[]{:S(2)}) async-start(s8[12582912]{0:T(1024)(128)(4,1)} %bitcast.113), calls=%async_computation.14 | async-start | bytes 8388608
  234.4 42.0 %copy-start.23 = (bf16[1024,12,64]{0,2,1:T(8,128)(2,1)}, bf16[1024,12,64]{0,2,1:T(8,128)(2,1)S(1)}, u32[]{:S(2)}) copy-start(bf16[1024,12,64]{0,2,1:T(8,128)(2,1)S(1)} %convert.55) | copy-start | bytes 4718596
  234.4 7.4 %copy-start.8 = (bf16[1024,12,32]{0,2,1:T(8,128)(2,1)S(1)}, bf16[1024,12,32]{0,2,1:T(8,128)(2,1)}, u32[]{:S(2)}) copy-start(bf16[1024,12,32]{0,2,1:T(8,128)(2,1)} %copy-done.7) | copy-start | bytes 2359300
  234.4 7.4 %copy-start.10 = (bf16[1024,12,32]{0,2,1:T(8,128)(2,1)S(1)}, bf16[1024,12,32]{0,2,1:T(8,128)(2,1)}, u32[]{:S(2)}) copy-start(bf16[1024,12,32]{0,2,1:T(8,128)(2,1)} %copy-done.9) | copy-start | bytes 2359300
  242.9 16.8 %copy-start.12 = (bf16[1024,12,32]{0,2,1:T(8,128)(2,1)S(1)}, bf16[1024,12,32]{0,2,1:T(8,128)(2,1)}, u32[]{:S(2)}) copy-start(bf16[1024,12,32]{0,2,1:T(8,128)(2,1)} %copy-done.11) | copy-start | bytes 2359300
  242.9 16.8 %copy-start.14 = (bf16[1024,12,32]{0,2,1:T(8,128)(2,1)S(1)}, bf16[1024,12,32]{0,2,1:T(8,128)(2,1)}, u32[]{:S(2)}) copy-start(bf16[1024,12,32]{0,2,1:T(8,128)(2,1)} %copy-done.13) | copy-start | bytes 2359300
  259.7 4.5 copy-start
  266.3 8.6 %copy-start.25 = (f32[1024,32]{0,1:T(8,128)S(1)}, f32[1024,32]{0,1:T(8,128)}, u32[]{:S(2)}) copy-start(f32[1024,32]{0,1:T(8,128)} %copy-done.24) | copy-start | bytes 393220
  266.3 8.6 %copy-start.27 = (f32[1024,32]{0,1:T(8,128)S(1)}, f32[1024,32]{0,1:T(8,128)}, u32[]{:S(2)}) copy-start(f32[1024,32]{0,1:T(8,128)} %copy-done.26) | copy-start | bytes 393220
  287.1 91.5 %reduce-scatter.11.cloned.1.call-start = ((), (), s32[]{:S(2)}) async-start(), calls=%async_computation.11 | async-start | bytes 5898240 | tf_op jit(solution)/shard_map/reduce_scatter | solution.py:209
  300.7 128.5 %reduce-scatter.9.cloned.1.call-start = ((), (), s32[]{:S(2)}) async-start(), calls=%async_computation.10 | async-start | bytes 5898240 | tf_op jit(solution)/shard_map/reduce_scatter | solution.py:203
  312.5 3.0 copy-start.55
  315.8 9.8 %copy-start.48 = (bf16[3072]{0:T(1024)(128)(2,1)S(1)}, bf16[3072]{0:T(1024)(128)(2,1)}, u32[]{:S(2)}) copy-start(bf16[3072]{0:T(1024)(128)(2,1)} %get-tuple-element.122) | copy-start | bytes 18436
  315.8 9.8 %copy-start.49 = (bf16[768]{0:T(1024)(128)(2,1)S(1)}, bf16[768]{0:T(1024)(128)(2,1)}, u32[]{:S(2)}) copy-start(bf16[768]{0:T(1024)(128)(2,1)} %get-tuple-element.64) | copy-start | bytes 4612
  349.3 3.0 copy-start.5
  (20 other events, 31.5 us)
Sparse Core Ops, SparseCore 0:
  9.6 33.5 all-gather.5
  44.7 17.4 all-gather.7
  63.8 37.4 all-gather.9
  102.7 37.4 all-gather.11
  218.4 26.1 reduce-scatter.6
  287.3 40.9 reduce-scatter.4
  330.8 47.8 reduce-scatter.10
  381.3 47.8 reduce-scatter.8
where the time goes:
time: 725 us; the launch traced here: 715 us
  blocking collectives  303 us (42%)
  matrix products  195 us (27%)
  waiting for transfers between devices  81.6 us (11%)
  other arithmetic  75.5 us (10%)
  local copies, waits for them, and re-layouts  41.6 us (6%)
  between operations  17.7 us (2%)
    psum x1, blocking collectives, shards(): lax.psum((shares[0], shares[1], shares[2], shares[3], shares[4], shares[5...  279 us
    reduce_scatter x1, waiting for transfers between devices, shards(): lax.psum_scatter(grad_up.astype(jnp.bfloat16), 'narrow', scatter_dimensio...  50.6 us
    dot_general x4, matrix products, inner_prod(): lax.dot_general(left, right, (((1,), (1,)), ((), ())), preferred_element_...  36.3 us
    dot_general x4, matrix products, outer_sum(): lax.dot_general(left, right, (((0,), (0,)), ((), ())), preferred_element_...  33.6 us
    sub x1, other arithmetic, probs_of(): expo = jnp.exp(scores - jnp.max(scores, axis=-1, keepdims=True))  33.6 us
    dot_general x2, matrix products, part_back(): jnp.einsum('qhd,khd->hqk', d_out, v_part, preferred_element_type=jnp.floa...  27.5 us
    convert_element_type x2, other arithmetic, part_back(): d_low = d_scores.astype(jnp.bfloat16)  24.1 us
    unnamed x133, local copies, waits for them, and re-layouts  23.5 us
  transfers between devices with their start and end apart: 8, of which 3 were waited for; matrix products, arithmetic and copies ran while one was open for 34% of the time, Pallas kernels for 0%

commit v1 on v0

v1 whole, which is shorter than its diff:
```python
import functools
import math

import jax
import jax.numpy as jnp
from jax import lax
from jax.experimental import pallas as pl
from jax.experimental.pallas import tpu as pltpu
from jax.sharding import PartitionSpec as P

HEAD = 64
PAIR = 2 * HEAD
TILE = 128
SPAN = 256
LOG2E = 1.4426950408889634
LN2 = 0.6931471805599453
f32 = jnp.float32
bf16 = jnp.bfloat16
MIB = 1 << 20


def nn(left, right):
    return jnp.dot(left, right, preferred_element_type=f32)


def nt(left, right):
    return lax.dot_general(left, right, (((1,), (1,)), ((), ())), preferred_element_type=f32)


def norm_rows(values):
    centre = values - jnp.mean(values, axis=-1, keepdims=True)
    inverse = lax.rsqrt(jnp.mean(centre * centre, axis=-1, keepdims=True) + 1e-05)
    return centre * inverse, inverse


def norm_back(d_norm, scaled, inverse, gain):
    d_scaled = d_norm * gain
    return inverse * (
        d_scaled
        - jnp.mean(d_scaled, axis=-1, keepdims=True)
        - scaled * jnp.mean(d_scaled * scaled, axis=-1, keepdims=True)
    )


def swap_halves(tile):
    lane = lax.broadcasted_iota(jnp.int32, (1, PAIR), 1) % HEAD
    return jnp.where(
        lane < HEAD // 2,
        pltpu.roll(tile, PAIR - HEAD // 2, 1),
        pltpu.roll(tile, HEAD // 2, 1),
    )


class Weight:
    def __init__(self, pieces):
        self.arrays = [array for array, _, _ in pieces]
        self.plan = [(rows, place) for _, rows, place in pieces]
        self.rows = sum(rows for rows, _ in self.plan)
        self.cols = self.arrays[0].shape[1]

    def specs(self):
        return [pl.BlockSpec(memory_space=pltpu.HBM)] * len(self.plan)

    def whole(self):
        return pltpu.VMEM((self.rows, self.cols), bf16)

    def sems(self):
        return [pltpu.SemaphoreType.DMA((len(self.plan),))]

    def scratch(self):
        return [pltpu.VMEM((self.rows, self.cols), bf16), pltpu.SemaphoreType.DMA((len(self.plan),))]


def fetches(at_ref, plan, parts, whole, sems):
    copies = []
    for i, ((rows, place), part) in enumerate(zip(plan, parts)):
        start = pl.multiple_of(at_ref[place], math.gcd(rows, 256))
        copies.append(pltpu.make_async_copy(part.at[pl.ds(0, rows)], whole.at[pl.ds(start, rows)], sems.at[i]))
    return copies


def fetch(at_ref, *weights):
    @pl.when(pl.program_id(0) == 0)
    def _():
        for weight in weights:
            for copy in fetches(at_ref, *weight):
                copy.start()


def arrive(at_ref, weight):
    @pl.when(pl.program_id(0) == 0)
    def _():
        for copy in fetches(at_ref, *weight):
            copy.wait()


def step_rows(step):
    return pl.ds(pl.multiple_of(pl.program_id(0) * step, step), step)


def take(refs, *groups):
    out, at = [], 0
    for group in groups:
        out.append(refs[at : at + len(group)])
        at += len(group)
    return out + [refs[at:]]


def fixed(shape):
    return pl.BlockSpec(shape, lambda *_: (0,) * len(shape), pipeline_mode=pl.Buffered(1))


def call(body, name, grid, in_specs, out_specs, out_shape, scratch, limit, cost, near=(), aliases=None, moved=1 << 20):
    fun = pl.pallas_call(
        body,
        name=name,
        out_shape=out_shape,
        input_output_aliases=aliases or {},
        grid_spec=pltpu.PrefetchScalarGridSpec(
            num_scalar_prefetch=1,
            grid=grid,
            in_specs=in_specs,
            out_specs=out_specs,
            scratch_shapes=scratch,
        ),
        compiler_params=pltpu.CompilerParams(
            dimension_semantics=("arbitrary",) * len(grid), vmem_limit_bytes=limit * MIB
        ),
        cost_estimate=pl.CostEstimate(
            flops=int(cost * 1e12), bytes_accessed=moved, transcendentals=0
        ),
    )

    def run(index, *args):
        args = [
            pltpu.with_memory_space_constraint(arg, pltpu.VMEM if i in near else pltpu.HBM)
            for i, arg in enumerate(args)
        ]
        return fun(index, *args)

    return run


def hbm(shape, dtype):
    return pltpu.HBM(shape, dtype)


def vmem(shape, dtype):
    return pltpu.VMEM(shape, dtype)


def sds(shape, dtype):
    return jax.ShapeDtypeStruct(shape, dtype)


def first_body(idx_ref, w_ref, gain1_ref, gain2_ref, down_ref, up_ref, first_ref, second_ref, near_ref):
    rows, cols = w_ref.shape
    size = rows // 3

    def lanes(*refs):
        values = [ref[...].astype(f32).reshape(1, -1) for ref in refs]
        return jnp.concatenate(
            [v for v in values for _ in range(cols // (len(refs) * v.shape[1]))], axis=1
        )

    row = lax.broadcasted_iota(jnp.int32, (8, cols), 0)
    small = jnp.where(row == 0, lanes(gain1_ref, gain2_ref, down_ref), lanes(up_ref)).astype(bf16)
    start = pl.multiple_of(idx_ref[1] * size, math.gcd(size, 256))
    first_ref[:size, :] = w_ref[pl.ds(start, size), :]
    first_ref[size:, :] = small
    second_ref[...] = w_ref[2 * size :, :]
    near_ref[:rows, :] = w_ref[...]
    near_ref[rows:, :] = small


def first_call(index, w_qkv, gain1, gain2, down, up):
    rows, cols = w_qkv.shape
    size = rows // 3
    shapes = [(size + 8, cols), (size, cols), (rows + 8, cols)]
    return call(
        first_body,
        "first_messages",
        (1,),
        [fixed(array.shape) for array in (w_qkv, gain1, gain2, down, up)],
        [fixed(shape) for shape in shapes],
        [sds(shape, bf16) for shape in shapes],
        [],
        8,
        1.5,
    )(index, w_qkv, gain1, gain2, down, up)


def qkv_body(plan, n, idx_ref, x_ref, cos_ref, sin_ref, *refs):
    smalls, parts, refs = take(refs, range(n), plan)
    qkv_ref, a1t_ref, vec_ref, whole, sems = refs
    weight = (plan, parts, whole, sems)
    fetch(idx_ref, weight)
    width = x_ref.shape[1]

    @pl.when(pl.program_id(0) == 0)
    def _():
        lane = lax.broadcasted_iota(jnp.int32, (1, width), 1) // (width // n)
        values = [ref[...].astype(f32) for ref in smalls]
        vec_ref[...] = jnp.zeros_like(vec_ref)
        for i in range(3):
            vec_ref[i : i + 1, :width] = sum(
                jnp.where(lane == (idx_ref[0] ^ j), v[0:1, i * width : (i + 1) * width], 0.0)
                for j, v in enumerate(values)
            )
        size = vec_ref.shape[1] // n
        for c in range(n):
            vec_ref[3:4, c * size : (c + 1) * size] = sum(
                jnp.where((idx_ref[0] ^ j) == c, v[1:2, :size], 0.0) for j, v in enumerate(values)
            )

    scaled, _ = norm_rows(x_ref[...].astype(f32))
    a1 = (scaled * vec_ref[0:1, :width]).astype(bf16)
    a1t_ref[...] = a1.T
    cosine, sine = cos_ref[...], sin_ref[...]
    arrive(idx_ref, weight)
    for part in range(3):
        y = nn(a1, whole[:, part * width : (part + 1) * width])
        if part == 2:
            qkv_ref[:, part * width :] = y.astype(bf16)
            continue
        for t in range(width // PAIR):
            tile = y[:, t * PAIR : (t + 1) * PAIR]
            tile = tile * cosine + swap_halves(tile) * sine
            if part == 0:
                tile = tile * (LOG2E / 8.0)
            at = part * width + t * PAIR
            qkv_ref[:, at : at + PAIR] = tile.astype(bf16)


def qkv_call(index, x, weight, smalls, ff, cosine, sine):
    rows, width = x.shape
    wide = weight.cols
    step = 256
    per = cosine.shape[0] // step

    def vector(array):
        return pl.BlockSpec((8, wide), lambda i, s: (array.shape[0] // 8 - 1, 0))

    return call(
        functools.partial(qkv_body, weight.plan, len(smalls)),
        "norm_qkv",
        (rows // step,),
        [
            pl.BlockSpec((step, width), lambda i, s: (i, 0)),
            pl.BlockSpec((step, PAIR), lambda i, s: (i % per, 0)),
            pl.BlockSpec((step, PAIR), lambda i, s: (i % per, 0)),
        ]
        + [vector(array) for array in smalls]
        + weight.specs(),
        [
            pl.BlockSpec((step, wide), lambda i, s: (i, 0)),
            pl.BlockSpec((width, step), lambda i, s: (0, i)),
            pl.BlockSpec((8, ff), lambda i, s: (0, 0)),
        ],
        [hbm((rows, wide), bf16), hbm((width, rows), bf16), hbm((8, ff), f32)],
        weight.scratch(),
        14,
        7,
    )(index, x, cosine, sine, *smalls, *weight.arrays)


def head_masks():
    lane = lax.broadcasted_iota(jnp.int32, (1, PAIR), 1)
    return lane < HEAD, lane >= HEAD


def widen(tile, allowed):
    count = SPAN // TILE
    never = jnp.full(tile.shape, -1e30, f32)
    before = jnp.zeros(tile.shape, f32) if allowed else never
    return jnp.concatenate(
        [
            jnp.concatenate([tile if a == b else (before if a < b else never) for b in range(count)], axis=1)
            for a in range(count)
        ],
        axis=0,
    )


def att_body(seq, idx_ref, q_ref, k_ref, v_ref, same_ref, less_ref, upto_ref, *refs):
    o_ref, ot_ref, lse_ref = refs[-3:]
    k_all = k_ref[...]
    keys = [jnp.where(m, k_all, jnp.zeros_like(k_all)) for m in head_masks()]
    v_t = v_ref[...].T
    ones = jnp.ones((16, 2 * seq), bf16)
    vals = [jnp.concatenate([v_t[h * HEAD : (h + 1) * HEAD], ones], axis=0) for h in range(2)]
    same, less, upto = widen(same_ref[...], False), widen(less_ref[...], True), widen(upto_ref[...], True)

    def scores(lo, clean, h):
        hi = lo + SPAN
        row = lo + seq if clean else lo
        query = q_ref[row : row + SPAN, :]
        pieces = [nt(keys[h][seq + lo : seq + hi], query) + (upto if clean else less)]
        if lo > 0:
            pieces.append(nt(keys[h][seq : seq + lo], query))
        if not clean:
            pieces.append(nt(keys[h][lo:hi], query) + same)
        return pieces

    def soften(pieces):
        top = functools.reduce(jnp.maximum, [jnp.max(p, axis=0, keepdims=True) for p in pieces])
        return top, [jnp.exp2(p - top).astype(bf16) for p in pieces]

    def mix(lo, clean, h, weights):
        hi = lo + SPAN
        out = nn(vals[h][:, seq + lo : seq + hi], weights[0])
        if lo > 0:
            out = out + nn(vals[h][:, seq : seq + lo], weights[1])
        if not clean:
            out = out + nn(vals[h][:, lo:hi], weights[-1])
        return out

    def finish(lo, clean, softened):
        row = lo + seq if clean else lo
        outs = [mix(lo, clean, h, softened[h][1]) for h in range(2)]
        out = jnp.concatenate([o[:HEAD] / o[HEAD : HEAD + 1] for o in outs], axis=0)
        ot_ref[:, row : row + SPAN] = out.astype(bf16)
        o_ref[row : row + SPAN, :] = out.T.astype(bf16)
        for h in range(2):
            lse_ref[0, h : h + 1, row : row + SPAN] = softened[h][0] + jnp.log2(outs[h][HEAD : HEAD + 1])

    work = [(lo, clean) for lo in range(0, seq, SPAN) for clean in (False, True)]
    ahead = [scores(*work[0], h) for h in range(2)]
    behind = None
    for i, item in enumerate(work):
        now = ahead
        if i + 1 < len(work):
            ahead = [scores(*work[i + 1], h) for h in range(2)]
        softened = [soften(pieces) for pieces in now]
        if behind is not None:
            finish(*behind)
        behind = (*item, softened)
    finish(*behind)


def att_call(index, qkv, masks, start, count, held=()):
    rows = qkv.shape[0]
    width = qkv.shape[1] // 3
    pairs = width // PAIR

    def column(part):
        return pl.BlockSpec((rows, PAIR), lambda p, s: (0, part * pairs + start + p))

    return call(
        functools.partial(att_body, rows // 2),
        "attention",
        (count,),
        [column(0), column(1), column(2)] + [fixed((TILE, TILE))] * 3
        + [pl.BlockSpec(memory_space=pltpu.HBM)] * len(held),
        [
            pl.BlockSpec((rows, PAIR), lambda p, s: (0, start + p)),
            pl.BlockSpec((PAIR, rows), lambda p, s: (start + p, 0)),
            pl.BlockSpec((1, 2, rows), lambda p, s: (start + p, 0, 0)),
        ],
        [hbm((rows, width), bf16), hbm((width, rows), bf16), hbm((pairs, 2, rows), f32)],
        [],
        20,
        2.0 * count,
        aliases={7 + i: i for i in range(len(held))},
    )(index, qkv, qkv, qkv, *masks, *held)


def att_back_body(
    seq, idx_ref, q_ref, k_ref, v_ref, do_ref, o_ref, lse_ref, same_ref, less_ref, upto_ref,
    cos_ref, sin_ref, dq_ref, dk_ref, dv_ref, dqt_ref,
):
    first, second = head_masks()
    q_all, k_all, v_all, do_all = q_ref[...], k_ref[...], v_ref[...], do_ref[...]

    def split(array):
        return [jnp.where(m, array, jnp.zeros_like(array)) for m in (first, second)]

    queries, keys, vals, dos = split(q_all), split(k_all), split(v_all), split(do_all)
    keys_t = k_all.T
    product = do_all.astype(f32) * o_ref[...].astype(f32)
    high = product.astype(bf16)
    rest = (product - high.astype(f32)).astype(bf16)
    picked = lax.broadcasted_iota(jnp.int32, (8, PAIR), 0)
    picked = jnp.where(picked == lax.broadcasted_iota(jnp.int32, (8, PAIR), 1) // HEAD, 1.0, 0.0).astype(bf16)
    delta = nt(picked, high) + nt(picked, rest)
    same, less, upto = widen(same_ref[...], False), widen(less_ref[...], True), widen(upto_ref[...], True)
    dqt_ref[...] = jnp.zeros_like(dqt_ref)

    def products(unit):
        return [
            (nt(keys[h][k : k + SPAN], q_all[q:end]), nt(vals[h][k : k + SPAN], do_all[q:end]))
            for h, k, q, end, _ in unit[0]
        ]

    def soften(unit, values):
        out = []
        for (h, _, q, end, mask), (scores, d_probs) in zip(unit[0], values):
            scores = scores - lse_ref[0, h : h + 1, q:end]
            probs = jnp.exp2(scores[:, :SPAN] + mask)
            if end - q > SPAN:
                probs = jnp.concatenate([probs, jnp.exp2(scores[:, SPAN:])], axis=1)
            d_scores = probs * (d_probs - delta[h : h + 1, q:end])
            out.append((probs.astype(bf16), d_scores.astype(bf16)))
        return out

    def rotate_back(tile, row):
        at = row % seq
        cosine, sine = cos_ref[at : at + SPAN, :], sin_ref[at : at + SPAN, :]
        return tile * cosine - swap_halves(tile) * sine

    def gather(unit, values, sums):
        items, last = unit
        d_vals, d_keys = sums
        for (h, k, q, end, _), (probs, d_scores) in zip(items, values):
            d_vals = d_vals + nn(probs, dos[h][q:end])
            d_keys = d_keys + nn(d_scores, queries[h][q:end])
            at = slice(h * HEAD, (h + 1) * HEAD)
            dqt_ref[at, q:end] += nn(keys_t[at, k : k + SPAN], d_scores)
        if not last:
            return d_vals, d_keys
        k = items[0][1]
        dv_ref[k : k + SPAN, :] = d_vals.astype(bf16)
        dk_ref[k : k + SPAN, :] = rotate_back(d_keys * LN2, k).astype(bf16)
        return 0.0, 0.0

    units = []
    for lo in range(0, seq, SPAN):
        units.append(([(h, lo, lo, lo + SPAN, same) for h in range(2)], True))
        for base, mask in ((0, less), (seq, upto)):
            units.append(([(h, seq + lo, base + lo, base + seq, mask) for h in range(2)], base > 0))
    ahead, behind, sums = products(units[0]), None, (0.0, 0.0)
    for i, unit in enumerate(units):
        now = ahead
        if i + 1 < len(units):
            ahead = products(units[i + 1])
        values = soften(unit, now)
        if behind is not None:
            sums = gather(*behind, sums)
        behind = (unit, values)
    gather(*behind, sums)
    for r in range(0, 2 * seq, SPAN):
        tile = dqt_ref[:, r : r + SPAN].T * 0.125
        dq_ref[r : r + SPAN, :] = rotate_back(tile, r).astype(bf16)


def att_back_call(index, qkv, d_o, o, lse, masks, cosine, sine, start, count):
    rows = qkv.shape[0]
    width = qkv.shape[1] // 3
    pairs = width // PAIR
    seq = rows // 2

    def column(part):
        return pl.BlockSpec((rows, PAIR), lambda p, s: (0, part * pairs + start + p))

    out = pl.BlockSpec((rows, PAIR), lambda p, s: (0, p))
    return call(
        functools.partial(att_back_body, seq),
        "attention_back",
        (count,),
        [column(0), column(1), column(2), column(0), column(0)]
        + [pl.BlockSpec((1, 2, rows), lambda p, s: (start + p, 0, 0))]
        + [fixed((TILE, TILE))] * 3
        + [fixed((seq, PAIR))] * 2,
        [out] * 3,
        [vmem((rows, count * PAIR), bf16)] * 3,
        [pltpu.VMEM((PAIR, rows), f32)],
        20,
        3.6 * count,
    )(index, qkv, qkv, qkv, d_o, o, lse, *masks, cosine, sine)


def up_body(out_at, up_at, idx_ref, x_ref, o_ref, vec_ref, *refs):
    outs, ups, refs = take(refs, out_at, up_at)
    x1_ref, a2t_ref, h_ref, g_ref, w_out, w_up, out_sems, up_sems = refs
    out_weight, up_weight = (out_at, outs, w_out, out_sems), (up_at, ups, w_up, up_sems)
    fetch(idx_ref, out_weight, up_weight)
    arrive(idx_ref, out_weight)
    width = x_ref.shape[1]
    here = step_rows(x_ref.shape[0])
    x1 = x_ref[...].astype(f32) + nn(o_ref[...], w_out[...])
    x1_ref[here, :] = x1
    scaled, _ = norm_rows(x1)
    a2 = (scaled * vec_ref[1:2, :width]).astype(bf16)
    a2t_ref[:, here] = a2.T
    arrive(idx_ref, up_weight)
    c0 = math.sqrt(2.0 / math.pi)
    c1 = c0 * 0.044715
    chunk = 512
    for at in range(0, w_up.shape[1], chunk):
        u = nn(a2, w_up[:, at : at + chunk]) + vec_ref[3:4, at : at + chunk]
        square = u * u
        t = jnp.tanh(u * (c1 * square + c0))
        half = 0.5 * t + 0.5
        h_ref[here, at : at + chunk] = (u * half).astype(bf16)
        slope = u * (1.5 * c1 * square + 0.5 * c0)
        g_ref[here, at : at + chunk] = (half + slope * (1.0 - t * t)).astype(bf16)


def up_call(index, x, o, vec, w_out, w_up):
    rows, width = x.shape
    ff = w_up.cols
    step = 256

    def row(cols):
        return pl.BlockSpec((step, cols), lambda i, s: (i, 0))

    outs = [
        vmem((rows, width), f32), vmem((width, rows), bf16), vmem((rows, ff), bf16), vmem((rows, ff), bf16),
        w_out.whole(), w_up.whole(),
    ]
    return call(
        functools.partial(up_body, w_out.plan, w_up.plan),
        "feed_up",
        (rows // step,),
        [row(width), row(width), fixed(vec.shape)] + w_out.specs() + w_up.specs(),
        [fixed(out.shape) for out in outs],
        outs,
        w_out.sems() + w_up.sems(),
        8,
        18,
    )(index, x, o, vec, *w_out.arrays, *w_up.arrays)


def down_body(down_at, idx_ref, dy_ref, x1_ref, g_ref, vec_ref, w_up, w_out, *refs):
    downs, refs = take(refs, down_at)
    du_ref, dx1_ref, dx1r_ref, do_ref, bias_ref, w_down, down_sems = refs
    weight = (down_at, downs, w_down, down_sems)
    fetch(idx_ref, weight)

    @pl.when(pl.program_id(0) == 0)
    def _():
        bias_ref[...] = jnp.zeros_like(bias_ref)

    width = dy_ref.shape[1]
    here = step_rows(dy_ref.shape[0])
    low = dy_ref[...]
    d_y = low.astype(f32)
    bias_ref[1:2, :width] += jnp.sum(d_y, axis=0, keepdims=True)
    arrive(idx_ref, weight)
    chunk = 512
    d_a2 = 0.0
    for at in range(0, w_up.shape[1], chunk):
        d_u = nt(low, w_down[at : at + chunk, :]) * g_ref[here, at : at + chunk].astype(f32)
        bias_ref[0:1, at : at + chunk] += jnp.sum(d_u, axis=0, keepdims=True)
        d_u = d_u.astype(bf16)
        du_ref[here, at : at + chunk] = d_u
        d_a2 = d_a2 + nt(d_u, w_up[:, at : at + chunk])
    scaled, inverse = norm_rows(x1_ref[here, :])
    d_x1 = d_y + norm_back(d_a2, scaled, inverse, vec_ref[1:2, :width])
    dx1_ref[here, :] = d_x1
    d_x1 = d_x1.astype(bf16)
    dx1r_ref[here, :] = d_x1
    do_ref[...] = nt(d_x1, w_out[...]).astype(bf16)


def down_call(index, d_y, x1, g, vec, w_up, w_out, w_down):
    rows, width = d_y.shape
    ff = w_up.shape[1]
    step = 256

    def row(cols):
        return pl.BlockSpec((step, cols), lambda i, s: (i, 0))

    return call(
        functools.partial(down_body, w_down.plan),
        "feed_back",
        (rows // step,),
        [row(width)] + [fixed(array.shape) for array in (x1, g, vec, w_up, w_out)] + w_down.specs(),
        [fixed((rows, ff)), fixed((rows, width)), fixed((rows, width)), row(width), fixed((2, ff)),
         fixed((ff, width))],
        [
            vmem((rows, ff), bf16), vmem((rows, width), f32), vmem((rows, width), bf16),
            hbm((rows, width), bf16), vmem((2, ff), f32), w_down.whole(),
        ],
        w_down.sems(),
        10,
        20,
        near=(1, 2, 4, 5),
    )(index, d_y, x1, g, vec, w_up, w_out, *w_down.arrays)


def grad_down_body(offsets, idx_ref, dyt_ref, h_ref, out_ref):
    base, step = offsets
    cols = out_ref.shape[2]
    shard = idx_ref[0] ^ (base + step * pl.program_id(0))
    columns = pl.ds(pl.multiple_of(shard * cols, cols), cols)
    out_ref[pl.program_id(0)] = nn(dyt_ref[...], h_ref[:, columns]).astype(bf16)


def grad_down_call(index, dyt, h, offsets, shards):
    width, rows = dyt.shape
    cols = h.shape[1] // shards
    return call(
        functools.partial(grad_down_body, offsets),
        "grad_down",
        (2,),
        [fixed(dyt.shape), fixed(h.shape)],
        fixed((2, width, cols)),
        vmem((2, width, cols), bf16),
        [],
        6,
        3,
        near=(0, 1),
    )(index, dyt, h)


def shard_rows(idx_ref, offsets, rows):
    base, step = offsets
    return [
        pl.ds(pl.multiple_of((idx_ref[0] ^ (base + step * j)) * rows, math.gcd(rows, 256)), rows) for j in range(2)
    ]


def grad_up_body(chunks, offsets, idx_ref, a_ref, o_ref, du_ref, dx_ref, bias_ref, out_ref):
    rows = out_ref.shape[1]
    width = dx_ref.shape[1]
    i = pl.program_id(0)
    columns = pl.ds(pl.multiple_of(i * width, width), width)
    shards_at = shard_rows(idx_ref, offsets, rows)

    def write(left, right):
        y = nn(jnp.concatenate([left[at, :] for at in shards_at], axis=0), right).astype(bf16)
        out_ref[0, :, columns] = y[:rows]
        out_ref[1, :, columns] = y[rows:]

    @pl.when(i < chunks)
    def _():
        write(a_ref, du_ref[:, columns])

    @pl.when(i == chunks)
    def _():
        write(o_ref, dx_ref[...])
        at = (chunks + 1) * width
        lanes = out_ref.shape[2] - at
        base, step = offsets
        shards = width // rows
        pad = jnp.zeros((1, 2 * lanes - rows), f32)
        for j in range(2):
            shard = idx_ref[0] ^ (base + step * j)
            tiles = [
                bias_ref[0:1, pl.ds(pl.multiple_of(shard * width + k * lanes, lanes), lanes)]
                for k in range(width // lanes)
            ]
            own = sum(
                jnp.where(shard == k, bias_ref[1:2, k * rows : (k + 1) * rows], 0.0) for k in range(shards)
            )
            own = jnp.concatenate([own, pad], axis=1)
            tiles += [own[:, :lanes], own[:, lanes:]]
            block = jnp.concatenate(tiles + [jnp.zeros((16 - len(tiles), lanes), f32)], axis=0)
            out_ref[j, :16, at:] = block.astype(bf16)
            out_ref[j, 16:, at:] = jnp.zeros((rows - 16, lanes), bf16)


def grad_up_call(index, a2t, ot, d_u, dx1r, biases, offsets, shards):
    width, rows = a2t.shape
    own = width // shards
    ff = d_u.shape[1]
    chunks = ff // width
    cols = ff + width + TILE
    return call(
        functools.partial(grad_up_body, chunks, offsets),
        "grad_up_out",
        (chunks + 1,),
        [fixed(array.shape) for array in (a2t, ot, d_u, dx1r, biases)],
        fixed((2, own, cols)),
        vmem((2, own, cols), bf16),
        [],
        8,
        4.7,
        near=range(5),
    )(index, a2t, ot, d_u, dx1r, biases)


def grad_qkv_body(offsets, idx_ref, a_ref, *refs):
    rights, out_ref = refs[:-1], refs[-1]
    rows = out_ref.shape[1]
    left = jnp.concatenate([a_ref[at, :] for at in shard_rows(idx_ref, offsets, rows)], axis=0)
    at = 0
    for right in rights:
        cols = right.shape[1]
        y = nn(left, right[...]).astype(bf16)
        out_ref[0, :, at : at + cols] = y[:rows]
        out_ref[1, :, at : at + cols] = y[rows:]
        at += cols


def grad_qkv_call(index, a1t, rights, offsets, shards):
    own = a1t.shape[0] // shards
    cols = sum(right.shape[1] for right in rights)
    return call(
        functools.partial(grad_qkv_body, offsets),
        "grad_qkv",
        (1,),
        [fixed(array.shape) for array in (a1t, *rights)],
        fixed((2, own, cols)),
        vmem((2, own, cols), bf16),
        [],
        8,
        1.0 + cols / 1000.0,
        near=range(1 + len(rights)),
    )(index, a1t, *rights)


def input_body(plan, groups, idx_ref, x_ref, dx1_ref, vec_ref, *refs):
    grads, parts, refs = take(refs, range(3 * groups), plan)
    dx_ref, whole, sems = refs
    weight = (plan, parts, whole, sems)
    fetch(idx_ref, weight)
    width = x_ref.shape[1]
    here = step_rows(x_ref.shape[0])
    scaled, inverse = norm_rows(x_ref[...].astype(f32))
    arrive(idx_ref, weight)
    d_a1 = 0.0
    for part in range(3):
        at = part * width
        for g in range(groups):
            ref = grads[3 * g + part]
            cols = ref.shape[1]
            d_a1 = d_a1 + nt(ref[here, :], whole[:, at : at + cols])
            at += cols
    d_x = dx1_ref[here, :] + norm_back(d_a1, scaled, inverse, vec_ref[0:1, :width])
    dx_ref[...] = d_x.astype(bf16)


def input_call(index, x, dx1, vec, d_groups, weight):
    rows, width = x.shape
    step = 256

    def row(cols):
        return pl.BlockSpec((step, cols), lambda i, s: (i, 0))

    flat = [array for group in d_groups for array in group]
    return call(
        functools.partial(input_body, weight.plan, len(d_groups)),
        "grad_input",
        (rows // step,),
        [row(width), fixed(dx1.shape), fixed(vec.shape)] + [fixed(array.shape) for array in flat] + weight.specs(),
        row(width),
        hbm((rows, width), bf16),
        weight.scratch(),
        12,
        9,
        near=(1, *range(3, 3 + len(flat))),
    )(index, x, dx1, vec, *flat, *weight.arrays)


def output_body(idx_ref, x1_ref, h_ref, vec_ref, w_ref, out_ref):
    here = step_rows(out_ref.shape[0])
    y = x1_ref[here, :] + nn(h_ref[here, :], w_ref[...]) + vec_ref[2:3, : x1_ref.shape[1]]
    out_ref[...] = y.astype(bf16)


def output_call(index, x1, h, vec, weight):
    rows, width = x1.shape
    step = 256
    return call(
        output_body,
        "layer_output",
        (rows // step,),
        [fixed(array.shape) for array in (x1, h, vec, weight)],
        pl.BlockSpec((step, width), lambda i, s: (i, 0)),
        hbm((rows, width), bf16),
        [],
        6,
        8,
        near=(0, 1, 3),
    )(index, x1, h, vec, weight)


def whole_call(name, body, arrays, outs, place=None):
    def run(*refs):
        body(refs[: len(arrays)], refs[len(arrays) :])

    return pl.pallas_call(
        run,
        name=name,
        in_specs=[pl.BlockSpec(memory_space=pltpu.VMEM)] * len(arrays),
        out_specs=[pl.BlockSpec(memory_space=pltpu.VMEM)] * len(outs),
        out_shape=[(place or vmem)(shape, dtype) for shape, dtype in outs],
        compiler_params=pltpu.CompilerParams(vmem_limit_bytes=8 * MIB),
        cost_estimate=pl.CostEstimate(
            flops=0,
            bytes_accessed=sum(array.size * array.dtype.itemsize for array in arrays),
            transcendentals=0,
        ),
    )(*(pltpu.with_memory_space_constraint(array, pltpu.VMEM) for array in arrays))


def half_of(bit, flip, rows):
    mine = (lax.axis_index("wide") // bit) % 2
    return pl.ds(pl.multiple_of((1 - mine if flip else mine) * rows, math.gcd(rows, 256)), rows)


def add_call(terms, rows, cols):
    def body(ins, outs):
        outs[0][...] = sum(
            (ref[...] if lead is None else ref[lead]).astype(f32) for ref, (_, lead) in zip(ins, terms)
        ).astype(bf16)

    return whole_call("add_terms", body, [a for a, _ in terms], [((rows, cols), bf16)])[0]


def halve_call(terms, rows, cols, bit):
    def body(ins, outs):
        for flip, out in ((1, outs[0]), (0, outs[1])):
            half = half_of(bit, flip, rows)
            out[...] = sum(
                (ref[half, :] if lead is None else ref[lead, half, :]).astype(f32)
                for ref, (_, lead) in zip(ins, terms)
            ).astype(out.dtype)

    return whole_call(
        "add_halves", body, [a for a, _ in terms], [((rows, cols), bf16), ((rows, cols), f32)]
    )


def fork_call(keep, core, rows, cols, left):
    def body(ins, outs):
        kept, got = ins
        outs[0][...] = (kept[1, :, :left].astype(f32) + got[1, :, :left].astype(f32)).astype(bf16)
        half = half_of(1, 1, rows // 2)
        for j in range(2):
            outs[1][j] = (kept[j, half, left:].astype(f32) + got[j, half, left:].astype(f32)).astype(bf16)

    return whole_call(
        "add_fork", body, [keep, core], [((rows, left), bf16), ((2, rows // 2, cols - left), bf16)]
    )


def cross_call(keep, core, got_left, got_right, rows, cols, left):
    rows //= 2

    def body(ins, outs):
        kept, got, from_left, from_right = ins
        mine, other = half_of(1, 0, rows), half_of(1, 1, rows)
        for half, out in ((other, outs[0]), (mine, outs[2])):
            out[...] = (
                kept[0, half, :left].astype(f32) + got[0, half, :left].astype(f32) + from_left[half, :].astype(f32)
            ).astype(out.dtype)
        for j, out in ((1, outs[1]), (0, outs[3])):
            out[...] = (
                kept[j, mine, left:].astype(f32) + got[j, mine, left:].astype(f32) + from_right[j].astype(f32)
            ).astype(out.dtype)

    shapes = [(rows, left), (rows, cols - left)]
    return whole_call(
        "add_cross", body, [keep, core, got_left, got_right],
        [(shape, dtype) for dtype in (bf16, f32) for shape in shapes],
    )


def merge_call(lefts, rights, rows, cols, left, bit):
    def body(ins, outs):
        for flip, out in ((1, outs[0]), (0, outs[1])):
            half = half_of(bit, flip, rows)
            out[:, :left] = (ins[0][half, :].astype(f32) + ins[1][half, :].astype(f32)).astype(out.dtype)
            out[:, left:] = (ins[2][half, :].astype(f32) + ins[3][half, :].astype(f32)).astype(out.dtype)

    return whole_call(
        "add_merge", body, [*lefts, *rights], [((rows, cols), bf16), ((rows, cols), f32)]
    )


def join_call(mine, other, bit):
    rows, cols = mine.shape

    def body(ins, outs):
        for flip in (0, 1):
            outs[0][half_of(bit, flip, rows), :] = ins[flip][...]

    return whole_call("join_halves", body, [mine, other], [((2 * rows, cols), bf16)])[0]


def turn_call(mine, other, bit):
    rows, cols = mine.shape

    def body(ins, outs):
        for flip in (0, 1):
            outs[0][:, half_of(bit, flip, rows)] = ins[flip][...].astype(f32).T

    return whole_call("last_down", body, [mine, other], [((cols, 2 * rows), f32)], hbm)[0]


def spread_body(plans, w_ref, gain_ref, *refs):
    ins, outs = refs[: 2 * len(plans)], refs[2 * len(plans) :]
    for c, plan in enumerate(plans):
        mine_ref, other_ref = ins[2 * c], ins[2 * c + 1]
        rows = mine_ref.shape[0]
        for flip, ref in ((0, mine_ref), (1, other_ref)):
            for begin, length, out, to in plan:
                outs[out][half_of(1, flip, rows), to : to + length] = ref[:, begin : begin + length].astype(f32)
    share = jnp.sum(outs[0][...] * w_ref[...].astype(f32), axis=1, keepdims=True)
    share = jnp.broadcast_to(share, (share.shape[0], PAIR)).T[0:1]
    outs[-1][...] = (share / gain_ref[...].astype(f32).reshape(1, -1)).reshape(-1)


def spread_call(weight, gain, sums, plans, shapes):
    arrays = [array for pair in sums for array in pair]
    return whole_call(
        "last_grads",
        lambda ins, outs: spread_body(plans, *ins, *outs),
        [weight, gain, *arrays],
        [(shape, f32) for shape in (*shapes, gain.shape)],
        hbm,
    )


def after(value, *deps):
    return lax.optimization_barrier((value, *deps))[0] if deps else value


class Moves:
    def __init__(self, narrow, wide):
        self.narrow, self.wide = narrow, wide
        self.n = lax.axis_index("narrow")
        self.w = lax.axis_index("wide")
        self.starts = [self.n, self.w % 2, (self.w // 2) % 2]

    def swap(self, value, axis, bit):
        size = self.narrow if axis == "narrow" else self.wide
        return lax.ppermute(value, axis, [(i, i ^ bit) for i in range(size)])

    def place(self, start):
        self.starts.append(start)
        return len(self.starts) - 1

    def reduce(self, send, keep, left):
        rows, cols = send.shape[1:]
        core = self.swap(send, "narrow", 1)
        deps = yield (send,)
        core = after(core, *deps)
        to_left, to_right = fork_call(keep, core, rows, cols, left)
        got_left, got_right = self.swap(to_left, "narrow", 2), self.swap(to_right, "wide", 1)
        deps = yield to_left, to_right
        to_left, to_right, mine_left, mine_right = cross_call(
            keep, core, after(got_left, *deps), after(got_right, *deps), rows, cols, left
        )
        got_left, got_right = self.swap(to_left, "wide", 1), self.swap(to_right, "narrow", 2)
        deps = yield to_left, to_right
        rows //= 4
        total, mine = merge_call(
            (mine_left, after(got_left, *deps)), (mine_right, after(got_right, *deps)), rows, cols, left, 2
        )
        got = self.swap(total, "wide", 2)
        deps = yield (total,)
        terms = [(mine, None), (after(got, *deps), None)]
        bit = 4
        while bit < self.wide:
            total = add_call(terms, rows, cols)
            got = self.swap(total, "wide", bit)
            deps = (yield (total,)) if bit == 4 else ()
            terms = [(total, None), (after(got, *deps), None)]
            bit *= 2
        total = add_call(terms, rows, cols)
        got = self.swap(total, "wide", 2)
        deps = yield (total,)
        total = join_call(total, after(got, *deps), 2)
        got = self.swap(total, "wide", 1)
        deps = yield (total,)
        yield total, after(got, *deps)


def begin(steps):
    return next(steps)


def step(steps, *deps):
    return steps.send(deps)


def advance(chains, *deps):
    return [array for chain in chains for array in step(chain, *deps)]


def shards(narrow, wide, layer_input, cotangent, block_size, gain_attn, w_qkv, w_out, gain_mlp, w_up, b_up, w_down, b_down):
    moves = Moves(narrow, wide)
    x, d_y = layer_input[0], cotangent[0]
    rows, width = x.shape
    seq = rows // 2
    pairs = width // PAIR
    ff = w_up.shape[1]
    n, bit = moves.n, moves.w % 2

    size = w_qkv.shape[0] // 3
    at_qkv = [
        moves.place((n ^ j) * w_qkv.shape[0] + extra)
        for j, extra in (
            (0, 0), (1, 0), (2, bit * size), (2, 2 * size), (2, (1 - bit) * size),
            (3, bit * size), (3, 2 * size), (3, (1 - bit) * size),
        )
    ]
    at_row = [moves.place((n ^ j) * w_out.shape[0]) for j in range(4)]

    def half_places(shard):
        half = shard.shape[0] // 2
        return [
            moves.place((n ^ j) * shard.shape[0] + extra)
            for j, extra in (
                (0, 0), (1, 0), (2, bit * half), (2, (1 - bit) * half), (3, bit * half), (3, (1 - bit) * half)
            )
        ]

    def own_half(shard):
        half = shard.shape[0] // 2
        return lax.dynamic_slice_in_dim(shard, bit * half, half, 0)

    def by_halves(shard, near, pieces, places):
        rows = shard.shape[0]
        return Weight(
            [(a, r, p) for a, r, p in zip((shard, near, *pieces), (rows, rows) + (rows // 2,) * 4, places)]
        )

    at_up = half_places(w_up)
    at_down = [moves.place((n ^ j) * w_down.shape[0]) for j in range(4)]
    index = jnp.stack(moves.starts).astype(jnp.int32)

    def ready(*deps):
        return after(index, *deps)

    first, second, near = first_call(index, w_qkv, gain_attn, gain_mlp, b_down, b_up)
    got_first = moves.swap(first, "narrow", 2)
    got_near = moves.swap(near, "narrow", 1)
    got_cross = moves.swap(got_first, "wide", 1)
    got_second = moves.swap(after(second, got_first), "narrow", 2)
    far_first, far_second, far_cross = (moves.swap(v, "narrow", 1) for v in (got_first, got_second, got_cross))
    count = w_qkv.shape[0]
    qkv_w = Weight(
        [
            (array, rows_of, place)
            for (array, rows_of), place in zip(
                (
                    (w_qkv, count), (got_near, count), (got_first, size), (got_second, size), (got_cross, size),
                    (far_first, size), (far_second, size), (far_cross, size),
                ),
                at_qkv,
            )
        ]
    )
    smalls = [near, got_near, got_first, far_first]
    up_far = moves.swap(after(own_half(w_up), got_second), "narrow", 2)
    out_near, up_near, down_near = (moves.swap(v, "narrow", 1) for v in (w_out, w_up, w_down))

    freq = 10000.0 ** (-jnp.arange(HEAD // 2).astype(f32) / (HEAD // 2))
    angles = jnp.arange(seq).astype(f32)[:, None] * freq[None, :]
    cosine, sine = jnp.cos(angles), jnp.sin(angles)
    cosine = jnp.tile(cosine, (1, 4))
    sine = jnp.concatenate([-sine, sine, -sine, sine], axis=1)
    block = jnp.arange(TILE, dtype=jnp.int32) // block_size[0]
    row_block, col_block = block[:, None], block[None, :]
    same, less, upto, less_t, upto_t = (
        jnp.where(ok, 0.0, -1e30).astype(f32)
        for ok in (
            row_block == col_block, col_block < row_block, col_block <= row_block,
            row_block < col_block, row_block <= col_block,
        )
    )
    dyt = d_y.T

    qkv, a1t, vec = qkv_call(index, x, qkv_w, smalls, ff, cosine, sine)
    up_far = after(up_far, vec)
    up_cross = moves.swap(up_far, "wide", 1)
    out_far = moves.swap(after(w_out, up_far), "narrow", 2)
    down_far = moves.swap(after(w_down, up_far), "narrow", 2)
    o, ot, lse = att_call(ready(up_far), qkv, (same, less_t, upto_t), 0, pairs)
    up_cross, out_far = after(up_cross, lse), after(out_far, lse)
    up_last = [moves.swap(v, "narrow", 1) for v in (after(up_far, lse), up_cross)]
    out_last = moves.swap(out_far, "narrow", 1)
    out_w = Weight([(a, w_out.shape[0], p) for a, p in zip((w_out, out_near, out_far, out_last), at_row)])
    up_w = by_halves(w_up, up_near, (up_far, up_cross, *up_last), at_up)
    x1, a2t, h, g, out_full, up_full = up_call(ready(lse), x, o, vec, out_w, up_w)
    send = grad_down_call(index, dyt, h, (1, 2), narrow)
    down_far = after(down_far, send)
    down_last = moves.swap(down_far, "narrow", 1)
    down_w = Weight([(a, w_down.shape[0], p) for a, p in zip((w_down, down_near, down_far, down_last), at_down)])
    keep = grad_down_call(ready(send, down_far), dyt, h, (0, 2), narrow)
    chain_a = moves.reduce(send, keep, width // 2)
    begin(chain_a)
    d_u, dx1, dx1r, d_o, biases, down_full = down_call(
        ready(keep, *advance([chain_a], keep)), d_y, x1, g, vec, up_full, out_full, down_w
    )
    send = grad_up_call(index, a2t, ot, d_u, dx1r, biases, (1, 2), narrow)
    keep = grad_up_call(ready(send), a2t, ot, d_u, dx1r, biases, (0, 2), narrow)
    chain_b = moves.reduce(send, keep, 2048)
    begin(chain_b)

    def back(start, count, *deps):
        return att_back_call(
            ready(*deps), qkv, d_o, o, lse, (same, less_t, upto_t), cosine, sine, start, count
        )

    g0 = back(0, 2, keep, *advance([chain_a, chain_b], keep))
    g1 = back(2, 2, g0[0], *advance([chain_a], g0[0]))
    g2 = back(4, 2, g1[0], *advance([chain_a, chain_b], g1[0]))
    groups = [g0, g1, g2]
    rights = [array for group in groups for array in group]
    send = grad_qkv_call(ready(*advance([chain_a, chain_b], g2[0])), a1t, rights, (1, 2), narrow)
    keep = grad_qkv_call(ready(send), a1t, rights, (0, 2), narrow)
    chain_c = moves.reduce(send, keep, 1152)
    begin(chain_c)
    sent = advance([chain_a, chain_b, chain_c], keep)
    output = output_call(ready(keep, *sent), x1, h, vec, down_full)
    sum_a = step(chain_a, output)
    sent = advance([chain_b, chain_c], output)
    d_input = input_call(ready(output, *sum_a, *sent), x, dx1, vec, groups, qkv_w)
    grad_down = turn_call(*sum_a, 1)
    sent = advance([chain_b, chain_c], d_input)
    sent = advance([chain_c], *sent)
    sum_b = step(chain_b, *sent)
    sent = advance([chain_c], *sent)
    sent = advance([chain_c], *sent)
    sum_c = step(chain_c)

    own = width // narrow
    grad_up, grad_out, biases, grad_gain_mlp = spread_call(
        w_up, gain_mlp, [sum_b], [[(0, ff, 0, 0), (ff, width, 1, 0), (ff + width, TILE, 2, 0)]],
        [(own, ff), (own, width), (own, TILE)],
    )
    biases = biases[:8].reshape(-1)
    cols = 2 * PAIR
    columns = [((3 * g + part) * cols, cols, 0, part * width + g * cols) for g in range(3) for part in range(3)]
    grad_qkv, grad_gain_attn = spread_call(w_qkv, gain_attn, [sum_c], [columns], [(own, 3 * width)])
    return (
        output[None],
        d_input[None],
        grad_gain_attn,
        grad_qkv,
        grad_out,
        grad_gain_mlp,
        grad_up,
        biases[:width],
        grad_down,
        biases[width : width + own],
    )


def solution(mesh):
    return jax.shard_map(
        functools.partial(shards, mesh.shape["narrow"], mesh.shape["wide"]),
        mesh=mesh,
        in_specs=(
            P(("wide", "narrow"), None, None),
            P(("wide", "narrow"), None, None),
            P(("wide", "narrow")),
            P("narrow"),
            P("narrow", None),
            P("narrow", None),
            P("narrow"),
            P("narrow", None),
            P("narrow"),
            P("narrow", None),
            P("narrow"),
        ),
        out_specs=(
            P(("wide", "narrow"), None, None),
            P(("wide", "narrow"), None, None),
            P("narrow"),
            P("narrow", None),
            P("narrow", None),
            P("narrow"),
            P("narrow", None),
            P("narrow"),
            P("narrow", None),
            P("narrow"),
        ),
        check_vma=False,
    )
```

time: 725 us -> 286 us (0.39)
  blocking collectives: 303 us -> 0 us
  matrix products: 195 us -> 0 us
  Pallas kernels: 0 us -> 178 us
  other arithmetic: 75.5 us -> 2.86 us
  starting transfers between devices: 0.32 us -> 35.8 us
  waiting for transfers between devices: 81.6 us -> 49.9 us
  local copies, waits for them, and re-layouts: 41.6 us -> 13.7 us
  between operations: 17.7 us -> 2.01 us
    psum x1 -> x0, blocking collectives: 279 us -> none  [shards(): lax.psum((shares[0], shares[1], shares[2], shares[3], shares[4], shares[5...]
    dot_general x23 -> x0, matrix products: 185 us -> none  [the longest x4 36.3 us: inner_prod(): lax.dot_general(left, right, (((1,), (1,)), ((), ())), preferred_element_...]
    pallas_call x0 -> x37, Pallas kernels: none -> 178 us  [the longest x16 136 us: run(): return fun(index, *args)]
    reduce_scatter x4 -> x0, waiting for transfers between devices: 71.1 us -> none  [the longest x1 50.6 us: shards(): lax.psum_scatter(grad_up.astype(jnp.bfloat16), 'narrow', scatter_dimensio...]
    ppermute x0 -> x45, waiting for transfers between devices: none -> 49.9 us  [swap(): return lax.ppermute(value, axis, [(i, i ^ bit) for i in range(size)])]
    ppermute x0 -> x45, starting transfers between devices: none -> 35.8 us  [swap(): return lax.ppermute(value, axis, [(i, i ^ bit) for i in range(size)])]
    sub x1 -> x0, other arithmetic: 33.6 us -> none  [probs_of(): expo = jnp.exp(scores - jnp.max(scores, axis=-1, keepdims=True))]
    convert_element_type x11 -> x1, other arithmetic: 24.4 us -> 0.01 us  [shards(): angles = jnp.arange(seq).astype(f32)[:, None] * freq[None, :]]
  transfers between devices with their start and end apart: 8 -> 45, of which waited for: 3 -> 15; matrix products, arithmetic and copies ran while one was open for 34% -> 3% of each run, Pallas kernels for 0% -> 62%
where the time goes in v1:
time: 286 us; the launch traced here: 282 us
  Pallas kernels  178 us (62%)
  waiting for transfers between devices  49.9 us (17%)
  starting transfers between devices  35.8 us (13%)
  local copies, waits for them, and re-layouts  13.7 us (5%)
  other arithmetic  2.86 us (1%)
    pallas_call x16, Pallas kernels, run(): return fun(index, *args)  136 us
    ppermute x45, waiting for transfers between devices, swap(): return lax.ppermute(value, axis, [(i, i ^ bit) for i in range(size)])  49.9 us
    pallas_call x21, Pallas kernels, whole_call(): pl.pallas_call(run, name=name, in_specs=[pl.BlockSpec(memory_space=pltpu....  41.8 us
    ppermute x45, starting transfers between devices, swap(): return lax.ppermute(value, axis, [(i, i ^ bit) for i in range(size)])  35.8 us
    unnamed x54, local copies, waits for them, and re-layouts  6.95 us
  transfers between devices with their start and end apart: 45, of which 15 were waited for; matrix products, arithmetic and copies ran while one was open for 3% of the time, Pallas kernels for 62%

profile of v1, /device:TPU:0, one launch (start us, length us, event | category | flops | bytes accessed | tf_op | source)
XLA Modules:
  0.0 281.8 jit_solution(13677522714837505058)
XLA Ops:
  1.3 1.8 first_messages.1
  3.1 2.7 collective-permute-start
  11.0 3.3 %collective-permute-done.refs_2_.refs_6_.refs_11_ = bf16[72,2304]{1,0:T(8,128)(2,1)} collective-permute-done((bf16[72,2304]{1,0:T(8,128)(2,1)S(1)}, bf16[72,2304]{1,0:T(8,128)(2,1)}, u32[]{:S(2)}, u32[]{:S(2)}) %collective-permute-start) | collective-permute-done | bytes 331808 | tf_op jit(solution)/shard_map/ppermute | solution.py:921
  14.3 1.8 collective-permute-start.1
  18.4 4.6 %collective-permute-done.1.refs_7_.refs_12_ = bf16[64,2304]{1,0:T(8,128)(2,1)S(1)} collective-permute-done((bf16[64,2304]{1,0:T(8,128)(2,1)S(1)}, bf16[64,2304]{1,0:T(8,128)(2,1)S(1)}, u32[]{:S(2)}, u32[]{:S(2)}) %collective-permute-start.1) | collective-permute-done | bytes 294944 | tf_op jit(solution)/shard_map/ppermute | solution.py:921
  23.1 2.3 collective-permute-done.5.refs_8_.refs_13_
  27.7 11.3 %norm_qkv.1 = (bf16[1024,2304]{1,0:T(8,128)(2,1)}, bf16[768,1024]{1,0:T(8,128)(2,1)}, f32[8,3072]{1,0:T(8,128)}) custom-call(s32[25]{0:T(128)S(1)} %stack.91.idx_ref, bf16[1024,768]{1,0:T(8,128)(2,1)} %bitcast.38, f32[512,128]{1,0:T(8,128)} %copy.32.cos_ref, f32[512,128]{1,0:T(8,128)} %pad_maximum_fusion.sin_ref, bf16[200,2304]{1,0:T(8,128)(2,1)} %copy-done.11, ...), custom_call_target="tpu_custom_call" | custom-call | flops 6999999774720 | bytes 1048576 | tf_op jit(solution)/shard_map/norm_qkv/pallas_call | solution.py:139
  39.1 3.3 %collective-permute-done.2.refs_6_ = bf16[96,3072]{1,0:T(8,128)(2,1)} collective-permute-done((bf16[96,3072]{1,0:T(8,128)(2,1)}, bf16[96,3072]{1,0:T(8,128)(2,1)}, u32[]{:S(2)}, u32[]{:S(2)}) %collective-permute-start.2) | collective-permute-done | bytes 589856 | tf_op jit(solution)/shard_map/ppermute | solution.py:921
  44.3 11.6 %attention.1 = (bf16[1024,768]{1,0:T(8,128)(2,1)}, bf16[768,1024]{1,0:T(8,128)(2,1)}, f32[6,2,1024]{2,1,0:T(2,128)}) custom-call(s32[25]{0:T(128)S(1)} %stack.91.idx_ref, bf16[1024,2304]{1,0:T(8,128)(2,1)} %get-tuple-element.125.q_ref.k_ref.v_ref, bf16[1024,2304]{1,0:T(8,128)(2,1)} %get-tuple-element.125.q_ref.k_ref.v_ref, ...), custom_call_target="tpu_custom_call" | custom-call | flops 12000000212992 | bytes 1048576 | tf_op jit(solution)/shard_map/attention/pallas_call | solution.py:139
  55.9 1.6 collective-permute-done.12.refs_7_
  61.4 19.3 %feed_up.1 = (f32[1024,768]{1,0:T(8,128)S(1)}, bf16[768,1024]{1,0:T(8,128)(2,1)S(1)}, bf16[1024,3072]{1,0:T(8,128)(2,1)S(1)}, bf16[1024,3072]{1,0:T(8,128)(2,1)S...) custom-call(s32[25]{0:T(128)S(1)} %stack.91.idx_ref, bf16[1024,768]{1,0:T(8,128)(2,1)} %bitcast.39, ...), custom_call_target="tpu_custom_call" | custom-call | flops 18000000319488 | bytes 1048576 | tf_op jit(solution)/shard_map/feed_up/pallas_call | solution.py:139
  80.7 4.8 %grad_down.2 = bf16[2,768,768]{2,1,0:T(8,128)(2,1)} custom-call(s32[25]{0:T(128)S(1)} %stack.91.idx_ref, bf16[768,1024]{1,0:T(8,128)(2,1)S(1)} %copy.33.dyt_ref, bf16[1024,3072]{1,0:T(8,128)(2,1)S(1)} %get-tuple-element.133.h_ref), custom_call_target="tpu_custom_call" | custom-call | flops 3000000053248 | bytes 1048576 | tf_op jit(solution)/shard_map/grad_down/pallas_call | solution.py:139
  85.5 3.4 %collective-permute-done.15.refs_2_ = bf16[768,768]{1,0:T(8,128)(2,1)} collective-permute-done((bf16[768,768]{1,0:T(8,128)(2,1)}, bf16[768,768]{1,0:T(8,128)(2,1)}, u32[]{:S(2)}, u32[]{:S(2)}) %collective-permute-start.15) | collective-permute-done | bytes 1179680 | tf_op jit(solution)/shard_map/ppermute | solution.py:921
  89.4 3.4 %grad_down.3.refs_0_ = bf16[2,768,768]{2,1,0:T(8,128)(2,1)S(1)} custom-call(s32[25]{0:T(128)S(1)} %stack.91.idx_ref, bf16[768,1024]{1,0:T(8,128)(2,1)S(1)} %copy.33.dyt_ref, bf16[1024,3072]{1,0:T(8,128)(2,1)S(1)} %get-tuple-element.133.h_ref), custom_call_target="tpu_custom_call" | custom-call | flops 3000000053248 | bytes 1048576 | tf_op jit(solution)/shard_map/grad_down/pallas_call | solution.py:139
  92.8 2.6 collective-permute-done.16.refs_1_
  95.5 2.8 add_fork.3
  100.3 20.9 %feed_back.1 = (bf16[1024,3072]{1,0:T(8,128)(2,1)S(1)}, f32[1024,768]{1,0:T(8,128)S(1)}, bf16[1024,768]{1,0:T(8,128)(2,1)S(1)}, bf16[1024,768]{1,0:T(8,128)(2,1)...) custom-call(s32[25]{0:T(128)S(1)} %stack.91.idx_ref, bf16[1024,768]{1,0:T(8,128)(2,1)} %bitcast.35, ...), custom_call_target="tpu_custom_call" | custom-call | flops 19999999655936 | bytes 1048576 | tf_op jit(solution)/shard_map/feed_back/pallas_call | solution.py:139
  121.3 6.2 %grad_up_out.2 = bf16[2,192,3968]{2,1,0:T(8,128)(2,1)} custom-call(s32[25]{0:T(128)S(1)} %stack.91.idx_ref, bf16[768,1024]{1,0:T(8,128)(2,1)S(1)} %get-tuple-element.139.a_ref, bf16[768,1024]{1,0:T(8,128)(2,1)S(1)} %copy-done.15, bf16[1024,3072]{1,0:T(8,128)(2,1)S(1)} %get-tuple-element.147.du_ref, bf16[1024,768]{1,0:T(8,128)(2,1)S(1)} %get-tuple-element.148.dx_ref, ...), custom_call_target="tpu_custom_call" | custom-call | flops 4700000223232 | bytes 1048576 | tf_op jit(solution)/shard_map/grad_up_out/pallas_call | solution.py:139
  127.5 4.6 %grad_up_out.3.refs_0_ = bf16[2,192,3968]{2,1,0:T(8,128)(2,1)S(1)} custom-call(s32[25]{0:T(128)S(1)} %stack.91.idx_ref, bf16[768,1024]{1,0:T(8,128)(2,1)S(1)} %get-tuple-element.139.a_ref, bf16[768,1024]{1,0:T(8,128)(2,1)S(1)} %copy-done.15, bf16[1024,3072]{1,0:T(8,128)(2,1)S(1)} %get-tuple-element.147.du_ref, ...), custom_call_target="tpu_custom_call" | custom-call | flops 4700000223232 | bytes 1048576 | tf_op jit(solution)/shard_map/grad_up_out/pallas_call | solution.py:139
  132.2 4.1 %add_cross.3 = (bf16[384,384]{1,0:T(8,128)(2,1)}, bf16[384,384]{1,0:T(8,128)(2,1)}, f32[384,384]{1,0:T(8,128)S(1)}, f32[384,384]{1,0:T(8,128)S(1)}) custom-call(bf16[2,768,768]{2,1,0:T(8,128)(2,1)S(1)} %copy-done.3, bf16[2,768,768]{2,1,0:T(8,128)(2,1)} %collective-permute-done.16.refs_1_, bf16[768,384]{1,0:T(8,128)(2,1)} %collective-permute-done.17.refs_2_, ...), custom_call_target="tpu_custom_call" | custom-call | bytes 5898240 | tf_op jit(solution)/shard_map/add_cross/pallas_call | solution.py:774
  138.3 3.2 %add_fork.4 = (bf16[192,2048]{1,0:T(8,128)(2,1)}, bf16[2,96,1920]{2,1,0:T(8,128)(2,1)}) custom-call(bf16[2,192,3968]{2,1,0:T(8,128)(2,1)S(1)} %grad_up_out.3.refs_0_, bf16[2,192,3968]{2,1,0:T(8,128)(2,1)} %collective-permute-done.22.refs_1_), custom_call_target="tpu_custom_call" | custom-call | bytes 6094848 | tf_op jit(solution)/shard_map/add_fork/pallas_call | solution.py:774
  143.6 8.8 %attention_back.3 = (bf16[1024,256]{1,0:T(8,128)(2,1)S(1)}, bf16[1024,256]{1,0:T(8,128)(2,1)S(1)}, bf16[1024,256]{1,0:T(8,128)(2,1)S(1)}) custom-call(s32[25]{0:T(128)S(1)} %stack.91.idx_ref, bf16[1024,2304]{1,0:T(8,128)(2,1)} %get-tuple-element.125.q_ref.k_ref.v_ref, bf16[1024,2304]{1,0:T(8,128)(2,1)} %get-tuple-element.125.q_ref.k_ref.v_ref, ...), custom_call_target="tpu_custom_call" | custom-call | flops 7199999918080 | bytes 1048576 | tf_op jit(solution)/shard_map/attention_back/pallas_call | solution.py:139
  152.4 1.8 add_merge.3
  155.8 9.0 %attention_back.4 = (bf16[1024,256]{1,0:T(8,128)(2,1)S(1)}, bf16[1024,256]{1,0:T(8,128)(2,1)S(1)}, bf16[1024,256]{1,0:T(8,128)(2,1)S(1)}) custom-call(s32[25]{0:T(128)S(1)} %stack.91.idx_ref, bf16[1024,2304]{1,0:T(8,128)(2,1)} %get-tuple-element.125.q_ref.k_ref.v_ref, bf16[1024,2304]{1,0:T(8,128)(2,1)} %get-tuple-element.125.q_ref.k_ref.v_ref, ...), custom_call_target="tpu_custom_call" | custom-call | flops 7199999918080 | bytes 1048576 | tf_op jit(solution)/shard_map/attention_back/pallas_call | solution.py:139
  164.8 1.8 add_terms.6.refs_0_
  166.6 2.6 collective-permute-start.25
  169.3 1.9 copy-done.1
  171.1 3.4 %add_cross.4 = (bf16[96,2048]{1,0:T(8,128)(2,1)}, bf16[96,1920]{1,0:T(8,128)(2,1)}, f32[96,2048]{1,0:T(8,128)S(1)}, f32[96,1920]{1,0:T(8,128)S(1)}) custom-call(bf16[2,192,3968]{2,1,0:T(8,128)(2,1)S(1)} %copy-done.1, bf16[2,192,3968]{2,1,0:T(8,128)(2,1)} %collective-permute-done.22.refs_1_, bf16[192,2048]{1,0:T(8,128)(2,1)} %collective-permute-done.26.refs_2_, ...), custom_call_target="tpu_custom_call" | custom-call | bytes 7618560 | tf_op jit(solution)/shard_map/add_cross/pallas_call | solution.py:774
  176.6 8.8 %attention_back.5 = (bf16[1024,256]{1,0:T(8,128)(2,1)S(1)}, bf16[1024,256]{1,0:T(8,128)(2,1)S(1)}, bf16[1024,256]{1,0:T(8,128)(2,1)S(1)}) custom-call(s32[25]{0:T(128)S(1)} %stack.91.idx_ref, bf16[1024,2304]{1,0:T(8,128)(2,1)} %get-tuple-element.125.q_ref.k_ref.v_ref, bf16[1024,2304]{1,0:T(8,128)(2,1)} %get-tuple-element.125.q_ref.k_ref.v_ref, ...), custom_call_target="tpu_custom_call" | custom-call | flops 7199999918080 | bytes 1048576 | tf_op jit(solution)/shard_map/attention_back/pallas_call | solution.py:139
  185.4 2.2 add_terms.7.refs_0_
  188.1 2.0 add_merge.4
  191.7 3.8 %grad_qkv.2 = bf16[2,192,2304]{2,1,0:T(8,128)(2,1)} custom-call(s32[25]{0:T(128)S(1)} %stack.91.idx_ref, bf16[768,1024]{1,0:T(8,128)(2,1)S(1)} %copy-done.14, bf16[1024,256]{1,0:T(8,128)(2,1)S(1)} %get-tuple-element.161.refs_0_, bf16[1024,256]{1,0:T(8,128)(2,1)S(1)} %get-tuple-element.184.refs_1_, bf16[1024,256]{1,0:T(8,128)(2,1)S(1)} %get-tuple-element.185.refs_2_, ...), custom_call_target="tpu_custom_call" | custom-call | flops 3304000061440 | bytes 1048576 | tf_op jit(solution)/shard_map/grad_qkv/pallas_call | solution.py:139
  195.4 2.6 grad_qkv.3.refs_0_
  198.0 2.4 join_halves.3.refs_0_
  203.3 1.8 add_terms.8.refs_0_
  205.5 2.5 add_fork.5
  210.0 2.8 copy-done.13
  212.8 8.1 %layer_output.1 = bf16[1024,768]{1,0:T(8,128)(2,1)} custom-call(s32[25]{0:T(128)S(1)} %stack.91.idx_ref, f32[1024,768]{1,0:T(8,128)S(1)} %get-tuple-element.143.x1_ref, bf16[1024,3072]{1,0:T(8,128)(2,1)S(1)} %copy-done.13, f32[8,3072]{1,0:T(8,128)} %get-tuple-element.122.vec_ref, bf16[3072,768]{1,0:T(8,128)(2,1)S(1)} %get-tuple-element.198.w_ref), custom_call_target="tpu_custom_call" | custom-call | flops 7999999967232 | bytes 1048576 | tf_op jit(solution)/shard_map/layer_output/pallas_call | solution.py:139
  220.8 3.1 %collective-permute-done.34.refs_1_ = bf16[48,3968]{1,0:T(8,128)(2,1)} collective-permute-done((bf16[48,3968]{1,0:T(8,128)(2,1)}, bf16[48,3968]{1,0:T(8,128)(2,1)}, u32[]{:S(2)}, u32[]{:S(2)}) %collective-permute-start.34) | collective-permute-done | bytes 380960 | tf_op jit(solution)/shard_map/ppermute | solution.py:921
  224.0 2.0 add_terms.9.refs_0_
  227.5 2.6 add_cross.5
  232.0 10.7 %grad_input.1 = bf16[1024,768]{1,0:T(8,128)(2,1)} custom-call(s32[25]{0:T(128)S(1)} %stack.91.idx_ref, bf16[1024,768]{1,0:T(8,128)(2,1)} %bitcast.40, f32[1024,768]{1,0:T(8,128)S(1)} %get-tuple-element.206.dx1_ref, f32[8,3072]{1,0:T(8,128)} %get-tuple-element.122.vec_ref, bf16[1024,256]{1,0:T(8,128)(2,1)S(1)} %get-tuple-element.161.refs_0_, ...), custom_call_target="tpu_custom_call" | custom-call | flops 9000000159744 | bytes 1048576 | tf_op jit(solution)/shard_map/grad_input/pallas_call | solution.py:139
  245.9 1.9 collective-permute-start.39
  247.8 4.5 %collective-permute-done.39.refs_1_ = bf16[48,2304]{1,0:T(8,128)(2,1)S(1)} collective-permute-done((bf16[48,2304]{1,0:T(8,128)(2,1)S(1)}, bf16[48,2304]{1,0:T(8,128)(2,1)S(1)}, u32[]{:S(2)}, u32[]{:S(2)}) %collective-permute-start.39) | collective-permute-done | bytes 221216 | tf_op jit(solution)/shard_map/ppermute | solution.py:921
  252.8 10.7 %collective-permute-done.41.refs_1_ = bf16[48,2304]{1,0:T(8,128)(2,1)S(1)} collective-permute-done((bf16[48,2304]{1,0:T(8,128)(2,1)S(1)}, bf16[48,2304]{1,0:T(8,128)(2,1)S(1)}, u32[]{:S(2)}, u32[]{:S(2)}) %collective-permute-start.41) | collective-permute-done | bytes 221216 | tf_op jit(solution)/shard_map/ppermute | solution.py:921
  263.6 3.1 %last_down.1 = f32[768,768]{1,0:T(8,128)} custom-call(bf16[384,768]{1,0:T(8,128)(2,1)} %join_halves.3.refs_0_, bf16[384,768]{1,0:T(8,128)(2,1)} %collective-permute-done.33.refs_1_), custom_call_target="tpu_custom_call" | custom-call | bytes 1179648 | tf_op jit(solution)/shard_map/last_down/pallas_call | solution.py:774
  266.8 2.0 last_grads.3
  273.7 6.3 %collective-permute-done.43.refs_3_ = bf16[96,2304]{1,0:T(8,128)(2,1)S(1)} collective-permute-done((bf16[96,2304]{1,0:T(8,128)(2,1)S(1)}, bf16[96,2304]{1,0:T(8,128)(2,1)S(1)}, u32[]{:S(2)}, u32[]{:S(2)}) %collective-permute-start.43) | collective-permute-done | bytes 442400 | tf_op jit(solution)/shard_map/ppermute | solution.py:921
  (148 shorter events, 47.0 us)
Async XLA Ops:
  0.6 60.0 %collective-permute-start.11 = (bf16[192,3072]{1,0:T(8,128)(2,1)}, bf16[192,3072]{1,0:T(8,128)(2,1)}, u32[]{:S(2)}, u32[]{:S(2)}) collective-permute-start(bf16[192,3072]{1,0:T(8,128)(2,1)} %refs_0_.7), channel_id=1, source_target_pairs={{0,1},{1,0},{2,3},{3,2},{4,5},{5,4},{6,7},{7,6},{8,9},{9,8},{10,11... | collective-permute-start | bytes 3538952 | tf_op jit(solution)/shard_map/ppermute | solution.py:921
  3.1 23.1 %copy-start.11 = (bf16[200,2304]{1,0:T(8,128)(2,1)}, bf16[200,2304]{1,0:T(8,128)(2,1)S(1)}, u32[]{:S(2)}) copy-start(bf16[200,2304]{1,0:T(8,128)(2,1)S(1)} %get-tuple-element.121.refs_0_) | copy-start | bytes 2764804
  3.1 22.2 %copy-start.6 = (bf16[192,3072]{1,0:T(8,128)(2,1)S(1)}, bf16[192,3072]{1,0:T(8,128)(2,1)}, u32[]{:S(2)}) copy-start(bf16[192,3072]{1,0:T(8,128)(2,1)} %refs_0_.7) | copy-start | bytes 3538948
  3.1 11.2 %collective-permute-start = (bf16[72,2304]{1,0:T(8,128)(2,1)S(1)}, bf16[72,2304]{1,0:T(8,128)(2,1)}, u32[]{:S(2)}, u32[]{:S(2)}) collective-permute-start(bf16[72,2304]{1,0:T(8,128)(2,1)S(1)} %get-tuple-element.118), channel_id=1, source_target_pairs={{0,2},{1,3},{2,0},{3,1},{4,6},{5,7},{6,4},{7,5},{8,10},{9,11},{10,... | collective-permute-start | bytes 995336 | tf_op jit(solution)/shard_map/ppermute | solution.py:921
  5.8 21.0 %collective-permute-start.3 = (bf16[200,2304]{1,0:T(8,128)(2,1)S(1)}, bf16[200,2304]{1,0:T(8,128)(2,1)}, u32[]{:S(2)}, u32[]{:S(2)}) collective-permute-start(bf16[200,2304]{1,0:T(8,128)(2,1)S(1)} %get-tuple-element.121.refs_0_), channel_id=1, source_target_pairs={{0,1},{1,0},{2,3},{3,2},{4,5},{5,4},{6,7},{7,6},{8,9},{9,8},{10,11... | collective-permute-start | bytes 2764808 | tf_op jit(solution)/shard_map/ppermute | solution.py:921
  14.3 8.8 %collective-permute-start.1 = (bf16[64,2304]{1,0:T(8,128)(2,1)S(1)}, bf16[64,2304]{1,0:T(8,128)(2,1)S(1)}, u32[]{:S(2)}, u32[]{:S(2)}) collective-permute-start(bf16[64,2304]{1,0:T(8,128)(2,1)S(1)} %get-tuple-element.119), channel_id=1, source_target_pairs={{0,2},{1,3},{2,0},{3,1},{4,6},{5,7},{6,4},{7,5},{8,10},{9,11},{10,... | collective-permute-start | bytes 884744 | tf_op jit(solution)/shard_map/ppermute | solution.py:921
  16.1 9.3 %collective-permute-start.5 = (bf16[72,2304]{1,0:T(8,128)(2,1)}, bf16[72,2304]{1,0:T(8,128)(2,1)S(1)}, u32[]{:S(2)}, u32[]{:S(2)}) collective-permute-start(bf16[72,2304]{1,0:T(8,128)(2,1)} %collective-permute-done.refs_2_.refs_6_.refs_11_), channel_id=1, source_target_pairs={{0,4},{4,0},{8,12},{12,8},{16,20},{20,16},{24,28},{28,24},{1,5},{5... | collective-permute-start | bytes 995336 | tf_op jit(solution)/shard_map/ppermute | solution.py:921
  18.4 7.8 %collective-permute-start.4 = (bf16[72,2304]{1,0:T(8,128)(2,1)}, bf16[72,2304]{1,0:T(8,128)(2,1)S(1)}, u32[]{:S(2)}, u32[]{:S(2)}) collective-permute-start(bf16[72,2304]{1,0:T(8,128)(2,1)} %collective-permute-done.refs_2_.refs_6_.refs_11_), channel_id=1, source_target_pairs={{0,1},{1,0},{2,3},{3,2},{4,5},{5,4},{6,7},{7,6},{8,9},{9,8},{10,11... | collective-permute-start | bytes 995336 | tf_op jit(solution)/shard_map/ppermute | solution.py:921
  23.1 3.7 %collective-permute-start.6 = (bf16[64,2304]{1,0:T(8,128)(2,1)S(1)}, bf16[64,2304]{1,0:T(8,128)(2,1)S(1)}, u32[]{:S(2)}, u32[]{:S(2)}) collective-permute-start(bf16[64,2304]{1,0:T(8,128)(2,1)S(1)} %collective-permute-done.1.refs_7_.refs_12_), channel_id=1, source_target_pairs={{0,1},{1,0},{2,3},{3,2},{4,5},{5,4},{6,7},{7,6},{8,9},{9,8},{10,11... | collective-permute-start | bytes 884744 | tf_op jit(solution)/shard_map/ppermute | solution.py:921
  25.3 1.6 collective-permute-start.7
  26.3 16.1 %collective-permute-start.2 = (bf16[96,3072]{1,0:T(8,128)(2,1)}, bf16[96,3072]{1,0:T(8,128)(2,1)}, u32[]{:S(2)}, u32[]{:S(2)}) collective-permute-start(bf16[96,3072]{1,0:T(8,128)(2,1)} %constant_dynamic-slice_fusion), channel_id=1, source_target_pairs={{0,2},{1,3},{2,0},{3,1},{4,6},{5,7},{6,4},{7,5},{8,10},{9,11},{10,... | collective-permute-start | bytes 1769480 | tf_op jit(solution)/shard_map/ppermute | solution.py:921
  42.3 15.2 %collective-permute-start.12 = (bf16[96,3072]{1,0:T(8,128)(2,1)}, bf16[96,3072]{1,0:T(8,128)(2,1)}, u32[]{:S(2)}, u32[]{:S(2)}) collective-permute-start(bf16[96,3072]{1,0:T(8,128)(2,1)} %collective-permute-done.2.refs_6_), channel_id=1, source_target_pairs={{0,4},{4,0},{8,12},{12,8},{16,20},{20,16},{24,28},{28,24},{1,5},{5... | collective-permute-start | bytes 1769480 | tf_op jit(solution)/shard_map/ppermute | solution.py:921
  43.8 14.2 %collective-permute-start.9 = (bf16[192,768]{1,0:T(8,128)(2,1)}, bf16[192,768]{1,0:T(8,128)(2,1)}, u32[]{:S(2)}, u32[]{:S(2)}) collective-permute-start(bf16[192,768]{1,0:T(8,128)(2,1)} %refs_0_.4), channel_id=1, source_target_pairs={{0,2},{1,3},{2,0},{3,1},{4,6},{5,7},{6,4},{7,5},{8,10},{9,11},{10,... | collective-permute-start | bytes 884744 | tf_op jit(solution)/shard_map/ppermute | solution.py:921
  55.9 5.4 %collective-permute-start.13 = (bf16[96,3072]{1,0:T(8,128)(2,1)}, bf16[96,3072]{1,0:T(8,128)(2,1)}, u32[]{:S(2)}, u32[]{:S(2)}) collective-permute-start(bf16[96,3072]{1,0:T(8,128)(2,1)} %collective-permute-done.2.refs_6_), channel_id=1, source_target_pairs={{0,1},{1,0},{2,3},{3,2},{4,5},{5,4},{6,7},{7,6},{8,9},{9,8},{10,11... | collective-permute-start | bytes 1769480 | tf_op jit(solution)/shard_map/ppermute | solution.py:921
  57.5 3.8 %collective-permute-start.14 = (bf16[96,3072]{1,0:T(8,128)(2,1)}, bf16[96,3072]{1,0:T(8,128)(2,1)}, u32[]{:S(2)}, u32[]{:S(2)}) collective-permute-start(bf16[96,3072]{1,0:T(8,128)(2,1)} %collective-permute-done.12.refs_7_), channel_id=1, source_target_pairs={{0,1},{1,0},{2,3},{3,2},{4,5},{5,4},{6,7},{7,6},{8,9},{9,8},{10,11... | collective-permute-start | bytes 1769480 | tf_op jit(solution)/shard_map/ppermute | solution.py:921
  57.5 2.7 collective-permute-start.8
  58.0 3.3 %collective-permute-start.10 = (bf16[192,768]{1,0:T(8,128)(2,1)}, bf16[192,768]{1,0:T(8,128)(2,1)}, u32[]{:S(2)}, u32[]{:S(2)}) collective-permute-start(bf16[192,768]{1,0:T(8,128)(2,1)} %collective-permute-done.9.refs_2_), channel_id=1, source_target_pairs={{0,1},{1,0},{2,3},{3,2},{4,5},{5,4},{6,7},{7,6},{8,9},{9,8},{10,11... | collective-permute-start | bytes 884744 | tf_op jit(solution)/shard_map/ppermute | solution.py:921
  60.2 40.1 %collective-permute-start.18 = (bf16[768,768]{1,0:T(8,128)(2,1)}, bf16[768,768]{1,0:T(8,128)(2,1)}, u32[]{:S(2)}, u32[]{:S(2)}) collective-permute-start(bf16[768,768]{1,0:T(8,128)(2,1)} %refs_0_.5), channel_id=1, source_target_pairs={{0,1},{1,0},{2,3},{3,2},{4,5},{5,4},{6,7},{7,6},{8,9},{9,8},{10,11... | collective-permute-start | bytes 3538952 | tf_op jit(solution)/shard_map/ppermute | solution.py:921
  60.6 28.3 %collective-permute-start.15 = (bf16[768,768]{1,0:T(8,128)(2,1)}, bf16[768,768]{1,0:T(8,128)(2,1)}, u32[]{:S(2)}, u32[]{:S(2)}) collective-permute-start(bf16[768,768]{1,0:T(8,128)(2,1)} %refs_0_.5), channel_id=1, source_target_pairs={{0,2},{1,3},{2,0},{3,1},{4,6},{5,7},{6,4},{7,5},{8,10},{9,11},{10,... | collective-permute-start | bytes 3538952 | tf_op jit(solution)/shard_map/ppermute | solution.py:921
  88.9 11.4 %collective-permute-start.19 = (bf16[768,768]{1,0:T(8,128)(2,1)}, bf16[768,768]{1,0:T(8,128)(2,1)}, u32[]{:S(2)}, u32[]{:S(2)}) collective-permute-start(bf16[768,768]{1,0:T(8,128)(2,1)} %collective-permute-done.15.refs_2_), channel_id=1, source_target_pairs={{0,1},{1,0},{2,3},{3,2},{4,5},{5,4},{6,7},{7,6},{8,9},{9,8},{10,11... | collective-permute-start | bytes 3538952 | tf_op jit(solution)/shard_map/ppermute | solution.py:921
  88.9 6.6 %collective-permute-start.16 = (bf16[2,768,768]{2,1,0:T(8,128)(2,1)}, bf16[2,768,768]{2,1,0:T(8,128)(2,1)}, u32[]{:S(2)}, u32[]{:S(2)}) collective-permute-start(bf16[2,768,768]{2,1,0:T(8,128)(2,1)} %grad_down.2), channel_id=1, source_target_pairs={{0,1},{1,0},{2,3},{3,2},{4,5},{5,4},{6,7},{7,6},{8,9},{9,8},{10,11... | collective-permute-start | bytes 7077896 | tf_op jit(solution)/shard_map/ppermute | solution.py:921
  98.3 33.9 %collective-permute-start.17 = (bf16[768,384]{1,0:T(8,128)(2,1)}, bf16[768,384]{1,0:T(8,128)(2,1)}, u32[]{:S(2)}, u32[]{:S(2)}) collective-permute-start(bf16[768,384]{1,0:T(8,128)(2,1)} %get-tuple-element.138), channel_id=1, source_target_pairs={{0,2},{1,3},{2,0},{3,1},{4,6},{5,7},{6,4},{7,5},{8,10},{9,11},{10,... | collective-permute-start | bytes 1769480 | tf_op jit(solution)/shard_map/ppermute | solution.py:921
  99.1 33.1 %collective-permute-start.20 = (bf16[2,384,384]{2,1,0:T(8,128)(2,1)}, bf16[2,384,384]{2,1,0:T(8,128)(2,1)}, u32[]{:S(2)}, u32[]{:S(2)}) collective-permute-start(bf16[2,384,384]{2,1,0:T(8,128)(2,1)} %get-tuple-element.141), channel_id=1, source_target_pairs={{0,4},{4,0},{8,12},{12,8},{16,20},{20,16},{24,28},{28,24},{1,5},{5... | collective-permute-start | bytes 1769480 | tf_op jit(solution)/shard_map/ppermute | solution.py:921
  100.3 21.0 %copy-start.15 = (bf16[768,1024]{1,0:T(8,128)(2,1)S(1)}, bf16[768,1024]{1,0:T(8,128)(2,1)}, u32[]{:S(2)}) copy-start(bf16[768,1024]{1,0:T(8,128)(2,1)} %get-tuple-element.140.o_ref) | copy-start | bytes 4718596
  127.5 10.8 %collective-permute-start.22 = (bf16[2,192,3968]{2,1,0:T(8,128)(2,1)}, bf16[2,192,3968]{2,1,0:T(8,128)(2,1)}, u32[]{:S(2)}, u32[]{:S(2)}) collective-permute-start(bf16[2,192,3968]{2,1,0:T(8,128)(2,1)} %grad_up_out.2), channel_id=1, source_target_pairs={{0,1},{1,0},{2,3},{3,2},{4,5},{5,4},{6,7},{7,6},{8,9},{9,8},{10,11... | collective-permute-start | bytes 9142280 | tf_op jit(solution)/shard_map/ppermute | solution.py:921
  136.3 16.1 %collective-permute-start.21 = (bf16[384,384]{1,0:T(8,128)(2,1)}, bf16[384,384]{1,0:T(8,128)(2,1)}, u32[]{:S(2)}, u32[]{:S(2)}) collective-permute-start(bf16[384,384]{1,0:T(8,128)(2,1)} %get-tuple-element.154), channel_id=1, source_target_pairs={{0,4},{4,0},{8,12},{12,8},{16,20},{20,16},{24,28},{28,24},{1,5},{5... | collective-permute-start | bytes 884744 | tf_op jit(solution)/shard_map/ppermute | solution.py:921
  137.1 15.3 %collective-permute-start.23 = (bf16[384,384]{1,0:T(8,128)(2,1)}, bf16[384,384]{1,0:T(8,128)(2,1)}, u32[]{:S(2)}, u32[]{:S(2)}) collective-permute-start(bf16[384,384]{1,0:T(8,128)(2,1)} %get-tuple-element.155), channel_id=1, source_target_pairs={{0,2},{1,3},{2,0},{3,1},{4,6},{5,7},{6,4},{7,5},{8,10},{9,11},{10,... | collective-permute-start | bytes 884744 | tf_op jit(solution)/shard_map/ppermute | solution.py:921
  141.6 27.7 %collective-permute-start.27 = (bf16[2,96,1920]{2,1,0:T(8,128)(2,1)}, bf16[2,96,1920]{2,1,0:T(8,128)(2,1)}, u32[]{:S(2)}, u32[]{:S(2)}) collective-permute-start(bf16[2,96,1920]{2,1,0:T(8,128)(2,1)} %get-tuple-element.158), channel_id=1, source_target_pairs={{0,4},{4,0},{8,12},{12,8},{16,20},{20,16},{24,28},{28,24},{1,5},{5... | collective-permute-start | bytes 2211848 | tf_op jit(solution)/shard_map/ppermute | solution.py:921
  143.1 26.2 %collective-permute-start.26 = (bf16[192,2048]{1,0:T(8,128)(2,1)}, bf16[192,2048]{1,0:T(8,128)(2,1)}, u32[]{:S(2)}, u32[]{:S(2)}) collective-permute-start(bf16[192,2048]{1,0:T(8,128)(2,1)} %get-tuple-element.157), channel_id=1, source_target_pairs={{0,2},{1,3},{2,0},{3,1},{4,6},{5,7},{6,4},{7,5},{8,10},{9,11},{10,... | collective-permute-start | bytes 2359304 | tf_op jit(solution)/shard_map/ppermute | solution.py:921
  154.2 10.6 %collective-permute-start.24 = (bf16[192,768]{1,0:T(8,128)(2,1)}, bf16[192,768]{1,0:T(8,128)(2,1)}, u32[]{:S(2)}, u32[]{:S(2)}) collective-permute-start(bf16[192,768]{1,0:T(8,128)(2,1)} %get-tuple-element.166), channel_id=1, source_target_pairs={{0,8},{4,12},{8,0},{12,4},{16,24},{20,28},{24,16},{28,20},{1,9},{5... | collective-permute-start | bytes 884744 | tf_op jit(solution)/shard_map/ppermute | solution.py:921
  166.6 18.8 %collective-permute-start.25 = (bf16[192,768]{1,0:T(8,128)(2,1)}, bf16[192,768]{1,0:T(8,128)(2,1)}, u32[]{:S(2)}, u32[]{:S(2)}) collective-permute-start(bf16[192,768]{1,0:T(8,128)(2,1)} %add_terms.6.refs_0_), channel_id=1, source_target_pairs={{0,16},{4,20},{8,24},{12,28},{16,0},{20,4},{24,8},{28,12},{1,17},{... | collective-permute-start | bytes 884744 | tf_op jit(solution)/shard_map/ppermute | solution.py:921
  174.5 13.6 %collective-permute-start.29 = (bf16[96,1920]{1,0:T(8,128)(2,1)}, bf16[96,1920]{1,0:T(8,128)(2,1)}, u32[]{:S(2)}, u32[]{:S(2)}) collective-permute-start(bf16[96,1920]{1,0:T(8,128)(2,1)} %get-tuple-element.173), channel_id=1, source_target_pairs={{0,2},{1,3},{2,0},{3,1},{4,6},{5,7},{6,4},{7,5},{8,10},{9,11},{10,... | collective-permute-start | bytes 1105928 | tf_op jit(solution)/shard_map/ppermute | solution.py:921
  176.0 12.1 %collective-permute-start.28 = (bf16[96,2048]{1,0:T(8,128)(2,1)}, bf16[96,2048]{1,0:T(8,128)(2,1)}, u32[]{:S(2)}, u32[]{:S(2)}) collective-permute-start(bf16[96,2048]{1,0:T(8,128)(2,1)} %get-tuple-element.172), channel_id=1, source_target_pairs={{0,4},{4,0},{8,12},{12,8},{16,20},{20,16},{24,28},{28,24},{1,5},{5... | collective-permute-start | bytes 1179656 | tf_op jit(solution)/shard_map/ppermute | solution.py:921
  187.7 10.3 %collective-permute-start.30 = (bf16[192,768]{1,0:T(8,128)(2,1)}, bf16[192,768]{1,0:T(8,128)(2,1)}, u32[]{:S(2)}, u32[]{:S(2)}) collective-permute-start(bf16[192,768]{1,0:T(8,128)(2,1)} %add_terms.7.refs_0_), channel_id=1, source_target_pairs={{0,8},{4,12},{8,0},{12,4},{16,24},{20,28},{24,16},{28,20},{1,9},{5... | collective-permute-start | bytes 884744 | tf_op jit(solution)/shard_map/ppermute | solution.py:921
  190.1 13.2 %collective-permute-start.31 = (bf16[48,3968]{1,0:T(8,128)(2,1)}, bf16[48,3968]{1,0:T(8,128)(2,1)}, u32[]{:S(2)}, u32[]{:S(2)}) collective-permute-start(bf16[48,3968]{1,0:T(8,128)(2,1)} %get-tuple-element.181), channel_id=1, source_target_pairs={{0,8},{4,12},{8,0},{12,4},{16,24},{20,28},{24,16},{28,20},{1,9},{5... | collective-permute-start | bytes 1142792 | tf_op jit(solution)/shard_map/ppermute | solution.py:921
  195.4 10.1 %collective-permute-start.32 = (bf16[2,192,2304]{2,1,0:T(8,128)(2,1)}, bf16[2,192,2304]{2,1,0:T(8,128)(2,1)}, u32[]{:S(2)}, u32[]{:S(2)}) collective-permute-start(bf16[2,192,2304]{2,1,0:T(8,128)(2,1)} %grad_qkv.2), channel_id=1, source_target_pairs={{0,1},{1,0},{2,3},{3,2},{4,5},{5,4},{6,7},{7,6},{8,9},{9,8},{10,11... | collective-permute-start | bytes 5308424 | tf_op jit(solution)/shard_map/ppermute | solution.py:921
  200.4 25.6 %collective-permute-start.33 = (bf16[384,768]{1,0:T(8,128)(2,1)}, bf16[384,768]{1,0:T(8,128)(2,1)}, u32[]{:S(2)}, u32[]{:S(2)}) collective-permute-start(bf16[384,768]{1,0:T(8,128)(2,1)} %join_halves.3.refs_0_), channel_id=1, source_target_pairs={{0,4},{4,0},{8,12},{12,8},{16,20},{20,16},{24,28},{28,24},{1,5},{5... | collective-permute-start | bytes 1769480 | tf_op jit(solution)/shard_map/ppermute | solution.py:921
  205.1 18.8 %collective-permute-start.34 = (bf16[48,3968]{1,0:T(8,128)(2,1)}, bf16[48,3968]{1,0:T(8,128)(2,1)}, u32[]{:S(2)}, u32[]{:S(2)}) collective-permute-start(bf16[48,3968]{1,0:T(8,128)(2,1)} %add_terms.8.refs_0_), channel_id=1, source_target_pairs={{0,16},{4,20},{8,24},{12,28},{16,0},{20,4},{24,8},{28,12},{1,17},{... | collective-permute-start | bytes 1142792 | tf_op jit(solution)/shard_map/ppermute | solution.py:921
  208.0 18.0 %collective-permute-start.35 = (bf16[192,1152]{1,0:T(8,128)(2,1)}, bf16[192,1152]{1,0:T(8,128)(2,1)}, u32[]{:S(2)}, u32[]{:S(2)}) collective-permute-start(bf16[192,1152]{1,0:T(8,128)(2,1)} %get-tuple-element.195), channel_id=1, source_target_pairs={{0,2},{1,3},{2,0},{3,1},{4,6},{5,7},{6,4},{7,5},{8,10},{9,11},{10,... | collective-permute-start | bytes 1327112 | tf_op jit(solution)/shard_map/ppermute | solution.py:921
  208.7 17.2 %collective-permute-start.36 = (bf16[2,96,1152]{2,1,0:T(8,128)(2,1)}, bf16[2,96,1152]{2,1,0:T(8,128)(2,1)}, u32[]{:S(2)}, u32[]{:S(2)}) collective-permute-start(bf16[2,96,1152]{2,1,0:T(8,128)(2,1)} %get-tuple-element.196), channel_id=1, source_target_pairs={{0,4},{4,0},{8,12},{12,8},{16,20},{20,16},{24,28},{28,24},{1,5},{5... | collective-permute-start | bytes 1327112 | tf_op jit(solution)/shard_map/ppermute | solution.py:921
  226.0 16.7 %collective-permute-start.40 = (bf16[48,3968]{1,0:T(8,128)(2,1)}, bf16[48,3968]{1,0:T(8,128)(2,1)}, u32[]{:S(2)}, u32[]{:S(2)}) collective-permute-start(bf16[48,3968]{1,0:T(8,128)(2,1)} %add_terms.9.refs_0_), channel_id=1, source_target_pairs={{0,8},{4,12},{8,0},{12,4},{16,24},{20,28},{24,16},{28,20},{1,9},{5... | collective-permute-start | bytes 1142792 | tf_op jit(solution)/shard_map/ppermute | solution.py:921
  230.1 14.7 %collective-permute-start.37 = (bf16[96,1152]{1,0:T(8,128)(2,1)}, bf16[96,1152]{1,0:T(8,128)(2,1)}, u32[]{:S(2)}, u32[]{:S(2)}) collective-permute-start(bf16[96,1152]{1,0:T(8,128)(2,1)} %get-tuple-element.203), channel_id=1, source_target_pairs={{0,4},{4,0},{8,12},{12,8},{16,20},{20,16},{24,28},{28,24},{1,5},{5... | collective-permute-start | bytes 663560 | tf_op jit(solution)/shard_map/ppermute | solution.py:921
  231.5 13.3 %collective-permute-start.38 = (bf16[96,1152]{1,0:T(8,128)(2,1)}, bf16[96,1152]{1,0:T(8,128)(2,1)}, u32[]{:S(2)}, u32[]{:S(2)}) collective-permute-start(bf16[96,1152]{1,0:T(8,128)(2,1)} %get-tuple-element.204), channel_id=1, source_target_pairs={{0,2},{1,3},{2,0},{3,1},{4,6},{5,7},{6,4},{7,5},{8,10},{9,11},{10,... | collective-permute-start | bytes 663560 | tf_op jit(solution)/shard_map/ppermute | solution.py:921
  243.9 22.8 %collective-permute-start.44 = (bf16[96,3968]{1,0:T(8,128)(2,1)S(1)}, bf16[96,3968]{1,0:T(8,128)(2,1)S(1)}, u32[]{:S(2)}, u32[]{:S(2)}) collective-permute-start(bf16[96,3968]{1,0:T(8,128)(2,1)S(1)} %join_halves.4.refs_2_), channel_id=1, source_target_pairs={{0,4},{4,0},{8,12},{12,8},{16,20},{20,16},{24,28},{28,24},{1,5},{5... | collective-permute-start | bytes 2285576 | tf_op jit(solution)/shard_map/ppermute | solution.py:921
  245.9 6.4 %collective-permute-start.39 = (bf16[48,2304]{1,0:T(8,128)(2,1)S(1)}, bf16[48,2304]{1,0:T(8,128)(2,1)S(1)}, u32[]{:S(2)}, u32[]{:S(2)}) collective-permute-start(bf16[48,2304]{1,0:T(8,128)(2,1)S(1)} %get-tuple-element.212), channel_id=1, source_target_pairs={{0,8},{4,12},{8,0},{12,4},{16,24},{20,28},{24,16},{28,20},{1,9},{5... | collective-permute-start | bytes 663560 | tf_op jit(solution)/shard_map/ppermute | solution.py:921
  252.4 11.1 %collective-permute-start.41 = (bf16[48,2304]{1,0:T(8,128)(2,1)S(1)}, bf16[48,2304]{1,0:T(8,128)(2,1)S(1)}, u32[]{:S(2)}, u32[]{:S(2)}) collective-permute-start(bf16[48,2304]{1,0:T(8,128)(2,1)S(1)} %add_terms.10.refs_0_), channel_id=1, source_target_pairs={{0,16},{4,20},{8,24},{12,28},{16,0},{20,4},{24,8},{28,12},{1,17},{... | collective-permute-start | bytes 663560 | tf_op jit(solution)/shard_map/ppermute | solution.py:921
  263.6 6.3 %collective-permute-start.42 = (bf16[48,2304]{1,0:T(8,128)(2,1)S(1)}, bf16[48,2304]{1,0:T(8,128)(2,1)S(1)}, u32[]{:S(2)}, u32[]{:S(2)}) collective-permute-start(bf16[48,2304]{1,0:T(8,128)(2,1)S(1)} %add_terms.11.refs_0_), channel_id=1, source_target_pairs={{0,8},{4,12},{8,0},{12,4},{16,24},{20,28},{24,16},{28,20},{1,9},{5... | collective-permute-start | bytes 663560 | tf_op jit(solution)/shard_map/ppermute | solution.py:921
  269.9 10.1 %collective-permute-start.43 = (bf16[96,2304]{1,0:T(8,128)(2,1)S(1)}, bf16[96,2304]{1,0:T(8,128)(2,1)S(1)}, u32[]{:S(2)}, u32[]{:S(2)}) collective-permute-start(bf16[96,2304]{1,0:T(8,128)(2,1)S(1)} %join_halves.5.refs_2_), channel_id=1, source_target_pairs={{0,4},{4,0},{8,12},{12,8},{16,20},{20,16},{24,28},{28,24},{1,5},{5... | collective-permute-start | bytes 1327112 | tf_op jit(solution)/shard_map/ppermute | solution.py:921
  (24 other events, 139.2 us)

commit v2 on v1

--- a/solution.py
+++ b/solution.py
@@ -11,6 +11,7 @@
 HEAD = 64
 PAIR = 2 * HEAD
 TILE = 128
+ORDER = (1, 3, 0, 2)
 SPAN = 256
 LOG2E = 1.4426950408889634
 LN2 = 0.6931471805599453
@@ -58,8 +59,12 @@
         self.rows = sum(rows for rows, _ in self.plan)
         self.cols = self.arrays[0].shape[1]
 
-    def specs(self):
-        return [pl.BlockSpec(memory_space=pltpu.HBM)] * len(self.plan)
+    def specs(self, near=True):
+        space = pltpu.VMEM if near else pltpu.HBM
+        return [pl.BlockSpec(memory_space=pltpu.HBM)] + [pl.BlockSpec(memory_space=space)] * (len(self.plan) - 1)
+
+    def near(self, at):
+        return list(range(at + 1, at + len(self.plan)))
 
     def whole(self):
         return pltpu.VMEM((self.rows, self.cols), bf16)
@@ -153,10 +158,7 @@
     return jax.ShapeDtypeStruct(shape, dtype)
 
 
-def first_body(idx_ref, w_ref, gain1_ref, gain2_ref, down_ref, up_ref, first_ref, second_ref, near_ref):
-    rows, cols = w_ref.shape
-    size = rows // 3
-
+def small_rows(cols, gain1_ref, gain2_ref, down_ref, up_ref):
     def lanes(*refs):
         values = [ref[...].astype(f32).reshape(1, -1) for ref in refs]
         return jnp.concatenate(
@@ -164,30 +166,52 @@
         )
 
     row = lax.broadcasted_iota(jnp.int32, (8, cols), 0)
-    small = jnp.where(row == 0, lanes(gain1_ref, gain2_ref, down_ref), lanes(up_ref)).astype(bf16)
-    start = pl.multiple_of(idx_ref[1] * size, math.gcd(size, 256))
-    first_ref[:size, :] = w_ref[pl.ds(start, size), :]
-    first_ref[size:, :] = small
-    second_ref[...] = w_ref[2 * size :, :]
-    near_ref[:rows, :] = w_ref[...]
-    near_ref[rows:, :] = small
-
-
-def first_call(index, w_qkv, gain1, gain2, down, up):
-    rows, cols = w_qkv.shape
-    size = rows // 3
-    shapes = [(size + 8, cols), (size, cols), (rows + 8, cols)]
+    return jnp.where(row == 0, lanes(gain1_ref, gain2_ref, down_ref), lanes(up_ref)).astype(bf16)
+
+
+def first_body(idx_ref, w_ref, gain1_ref, gain2_ref, down_ref, up_ref, out_ref, small_ref):
+    size = w_ref.shape[0]
+    small = small_rows(w_ref.shape[1], gain1_ref, gain2_ref, down_ref, up_ref)
+    out_ref[:size, :] = w_ref[...]
+    out_ref[size:, :] = small
+    small_ref[...] = small
+
+
+def first_call(index, weight, *vectors):
+    size, cols = weight.shape[0] // 3, weight.shape[1]
+    shapes = [(size + 8, cols), (8, cols)]
     return call(
         first_body,
-        "first_messages",
+        "first_message",
         (1,),
-        [fixed(array.shape) for array in (w_qkv, gain1, gain2, down, up)],
+        [pl.BlockSpec((size, cols), lambda i, s: (s[1], 0))] + [fixed(v.shape) for v in vectors],
         [fixed(shape) for shape in shapes],
-        [sds(shape, bf16) for shape in shapes],
+        [vmem(shape, bf16) for shape in shapes],
         [],
-        8,
+        6,
         1.5,
-    )(index, w_qkv, gain1, gain2, down, up)
+    )(index, weight, *vectors)
+
+
+def thirds_body(idx_ref, *refs):
+    count = len(refs) // 2
+    for ref, out_ref in zip(refs[:count], refs[count:]):
+        out_ref[...] = ref[...]
+
+
+def thirds_call(index, weight, places):
+    size, cols = weight.shape[0] // 3, weight.shape[1]
+    return call(
+        thirds_body,
+        "next_message",
+        (1,),
+        [pl.BlockSpec((size, cols), lambda i, s, p=p: (2 if p is None else s[p], 0)) for p in places],
+        [fixed((size, cols))] * len(places),
+        [vmem((size, cols), bf16)] * len(places),
+        [],
+        6,
+        1.5,
+    )(index, *[weight] * len(places))
 
 
 def qkv_body(plan, n, idx_ref, x_ref, cos_ref, sin_ref, *refs):
@@ -256,11 +280,13 @@
             pl.BlockSpec((step, wide), lambda i, s: (i, 0)),
             pl.BlockSpec((width, step), lambda i, s: (0, i)),
             pl.BlockSpec((8, ff), lambda i, s: (0, 0)),
+            fixed((weight.rows, wide)),
         ],
-        [hbm((rows, wide), bf16), hbm((width, rows), bf16), hbm((8, ff), f32)],
-        weight.scratch(),
-        14,
+        [hbm((rows, wide), bf16), hbm((width, rows), bf16), hbm((8, ff), f32), hbm((weight.rows, wide), bf16)],
+        weight.sems(),
+        16,
         7,
+        near=(*range(3, 3 + len(smalls)), *weight.near(3 + len(smalls))),
     )(index, x, cosine, sine, *smalls, *weight.arrays)
 
 
@@ -359,7 +385,7 @@
         ],
         [hbm((rows, width), bf16), hbm((width, rows), bf16), hbm((pairs, 2, rows), f32)],
         [],
-        20,
+        16,
         2.0 * count,
         aliases={7 + i: i for i in range(len(held))},
     )(index, qkv, qkv, qkv, *masks, *held)
@@ -464,7 +490,7 @@
         [out] * 3,
         [vmem((rows, count * PAIR), bf16)] * 3,
         [pltpu.VMEM((PAIR, rows), f32)],
-        20,
+        16,
         3.6 * count,
     )(index, qkv, qkv, qkv, d_o, o, lse, *masks, cosine, sine)
 
@@ -478,7 +504,7 @@
     width = x_ref.shape[1]
     here = step_rows(x_ref.shape[0])
     x1 = x_ref[...].astype(f32) + nn(o_ref[...], w_out[...])
-    x1_ref[here, :] = x1
+    x1_ref[...] = x1
     scaled, _ = norm_rows(x1)
     a2 = (scaled * vec_ref[1:2, :width]).astype(bf16)
     a2t_ref[:, here] = a2.T
@@ -505,7 +531,7 @@
         return pl.BlockSpec((step, cols), lambda i, s: (i, 0))
 
     outs = [
-        vmem((rows, width), f32), vmem((width, rows), bf16), vmem((rows, ff), bf16), vmem((rows, ff), bf16),
+        hbm((rows, width), f32), vmem((width, rows), bf16), vmem((rows, ff), bf16), vmem((rows, ff), bf16),
         w_out.whole(), w_up.whole(),
     ]
     return call(
@@ -513,11 +539,12 @@
         "feed_up",
         (rows // step,),
         [row(width), row(width), fixed(vec.shape)] + w_out.specs() + w_up.specs(),
-        [fixed(out.shape) for out in outs],
+        [row(width)] + [fixed(out.shape) for out in outs[1:]],
         outs,
         w_out.sems() + w_up.sems(),
-        8,
+        12,
         18,
+        near=w_out.near(3) + w_up.near(3 + len(w_out.plan)),
     )(index, x, o, vec, *w_out.arrays, *w_up.arrays)
 
 
@@ -545,9 +572,9 @@
         d_u = d_u.astype(bf16)
         du_ref[here, at : at + chunk] = d_u
         d_a2 = d_a2 + nt(d_u, w_up[:, at : at + chunk])
-    scaled, inverse = norm_rows(x1_ref[here, :])
+    scaled, inverse = norm_rows(x1_ref[...])
     d_x1 = d_y + norm_back(d_a2, scaled, inverse, vec_ref[1:2, :width])
-    dx1_ref[here, :] = d_x1
+    dx1_ref[...] = d_x1
     d_x1 = d_x1.astype(bf16)
     dx1r_ref[here, :] = d_x1
     do_ref[...] = nt(d_x1, w_out[...]).astype(bf16)
@@ -565,17 +592,17 @@
         functools.partial(down_body, w_down.plan),
         "feed_back",
         (rows // step,),
-        [row(width)] + [fixed(array.shape) for array in (x1, g, vec, w_up, w_out)] + w_down.specs(),
-        [fixed((rows, ff)), fixed((rows, width)), fixed((rows, width)), row(width), fixed((2, ff)),
+        [row(width), row(width)] + [fixed(array.shape) for array in (g, vec, w_up, w_out)] + w_down.specs(),
+        [fixed((rows, ff)), row(width), fixed((rows, width)), row(width), fixed((2, ff)),
          fixed((ff, width))],
         [
-            vmem((rows, ff), bf16), vmem((rows, width), f32), vmem((rows, width), bf16),
+            vmem((rows, ff), bf16), hbm((rows, width), f32), vmem((rows, width), bf16),
             hbm((rows, width), bf16), vmem((2, ff), f32), w_down.whole(),
         ],
         w_down.sems(),
-        10,
+        14,
         20,
-        near=(1, 2, 4, 5),
+        near=(2, 4, 5, *w_down.near(6)),
     )(index, d_y, x1, g, vec, w_up, w_out, *w_down.arrays)
 
 
@@ -598,30 +625,27 @@
         fixed((2, width, cols)),
         vmem((2, width, cols), bf16),
         [],
-        6,
+        8,
         3,
         near=(0, 1),
     )(index, dyt, h)
 
 
-def shard_rows(idx_ref, offsets, rows):
-    base, step = offsets
-    return [
-        pl.ds(pl.multiple_of((idx_ref[0] ^ (base + step * j)) * rows, math.gcd(rows, 256)), rows) for j in range(2)
-    ]
-
-
-def grad_up_body(chunks, offsets, idx_ref, a_ref, o_ref, du_ref, dx_ref, bias_ref, out_ref):
-    rows = out_ref.shape[1]
+def shard_rows(idx_ref, rows):
+    return [pl.ds(pl.multiple_of((idx_ref[0] ^ j) * rows, math.gcd(rows, 256)), rows) for j in ORDER]
+
+
+def grad_up_body(chunks, idx_ref, a_ref, o_ref, du_ref, dx_ref, bias_ref, send_ref, keep_ref):
+    rows = send_ref.shape[1]
     width = dx_ref.shape[1]
     i = pl.program_id(0)
     columns = pl.ds(pl.multiple_of(i * width, width), width)
-    shards_at = shard_rows(idx_ref, offsets, rows)
+    shards_at = shard_rows(idx_ref, rows)
 
     def write(left, right):
         y = nn(jnp.concatenate([left[at, :] for at in shards_at], axis=0), right).astype(bf16)
-        out_ref[0, :, columns] = y[:rows]
-        out_ref[1, :, columns] = y[rows:]
+        for k in range(4):
+            (send_ref if k < 2 else keep_ref)[k % 2, :, columns] = y[k * rows : (k + 1) * rows]
 
     @pl.when(i < chunks)
     def _():
@@ -631,94 +655,90 @@
     def _():
         write(o_ref, dx_ref[...])
         at = (chunks + 1) * width
-        lanes = out_ref.shape[2] - at
-        base, step = offsets
+        lanes = send_ref.shape[2] - at
         shards = width // rows
         pad = jnp.zeros((1, 2 * lanes - rows), f32)
-        for j in range(2):
-            shard = idx_ref[0] ^ (base + step * j)
+        for k, j in enumerate(ORDER):
+            shard = idx_ref[0] ^ j
+            out_ref = send_ref if k < 2 else keep_ref
             tiles = [
-                bias_ref[0:1, pl.ds(pl.multiple_of(shard * width + k * lanes, lanes), lanes)]
-                for k in range(width // lanes)
+                bias_ref[0:1, pl.ds(pl.multiple_of(shard * width + t * lanes, lanes), lanes)]
+                for t in range(width // lanes)
             ]
             own = sum(
-                jnp.where(shard == k, bias_ref[1:2, k * rows : (k + 1) * rows], 0.0) for k in range(shards)
+                jnp.where(shard == t, bias_ref[1:2, t * rows : (t + 1) * rows], 0.0) for t in range(shards)
             )
             own = jnp.concatenate([own, pad], axis=1)
             tiles += [own[:, :lanes], own[:, lanes:]]
             block = jnp.concatenate(tiles + [jnp.zeros((16 - len(tiles), lanes), f32)], axis=0)
-            out_ref[j, :16, at:] = block.astype(bf16)
-            out_ref[j, 16:, at:] = jnp.zeros((rows - 16, lanes), bf16)
-
-
-def grad_up_call(index, a2t, ot, d_u, dx1r, biases, offsets, shards):
+            out_ref[k % 2, :16, at:] = block.astype(bf16)
+            out_ref[k % 2, 16:, at:] = jnp.zeros((rows - 16, lanes), bf16)
+
+
+def grad_up_call(index, a2t, ot, d_u, dx1r, biases, shards):
     width, rows = a2t.shape
     own = width // shards
     ff = d_u.shape[1]
     chunks = ff // width
     cols = ff + width + TILE
     return call(
-        functools.partial(grad_up_body, chunks, offsets),
+        functools.partial(grad_up_body, chunks),
         "grad_up_out",
         (chunks + 1,),
         [fixed(array.shape) for array in (a2t, ot, d_u, dx1r, biases)],
-        fixed((2, own, cols)),
-        vmem((2, own, cols), bf16),
+        [fixed((2, own, cols))] * 2,
+        [vmem((2, own, cols), bf16)] * 2,
         [],
-        8,
+        10,
         4.7,
         near=range(5),
     )(index, a2t, ot, d_u, dx1r, biases)
 
 
-def grad_qkv_body(offsets, idx_ref, a_ref, *refs):
-    rights, out_ref = refs[:-1], refs[-1]
-    rows = out_ref.shape[1]
-    left = jnp.concatenate([a_ref[at, :] for at in shard_rows(idx_ref, offsets, rows)], axis=0)
+def grad_qkv_body(idx_ref, a_ref, *refs):
+    rights, send_ref, keep_ref = refs[:-2], refs[-2], refs[-1]
+    rows = send_ref.shape[1]
+    left = jnp.concatenate([a_ref[at, :] for at in shard_rows(idx_ref, rows)], axis=0)
     at = 0
     for right in rights:
         cols = right.shape[1]
         y = nn(left, right[...]).astype(bf16)
-        out_ref[0, :, at : at + cols] = y[:rows]
-        out_ref[1, :, at : at + cols] = y[rows:]
+        for k in range(4):
+            (send_ref if k < 2 else keep_ref)[k % 2, :, at : at + cols] = y[k * rows : (k + 1) * rows]
         at += cols
 
 
-def grad_qkv_call(index, a1t, rights, offsets, shards):
+def grad_qkv_call(index, a1t, rights, shards):
     own = a1t.shape[0] // shards
     cols = sum(right.shape[1] for right in rights)
     return call(
-        functools.partial(grad_qkv_body, offsets),
+        grad_qkv_body,
         "grad_qkv",
         (1,),
         [fixed(array.shape) for array in (a1t, *rights)],
-        fixed((2, own, cols)),
-        vmem((2, own, cols), bf16),
+        [fixed((2, own, cols))] * 2,
+        [vmem((2, own, cols), bf16)] * 2,
         [],
-        8,
+        10,
         1.0 + cols / 1000.0,
         near=range(1 + len(rights)),
     )(index, a1t, *rights)
 
 
-def input_body(plan, groups, idx_ref, x_ref, dx1_ref, vec_ref, *refs):
-    grads, parts, refs = take(refs, range(3 * groups), plan)
-    dx_ref, whole, sems = refs
-    weight = (plan, parts, whole, sems)
-    fetch(idx_ref, weight)
+def input_body(groups, idx_ref, x_ref, dx1_ref, vec_ref, w_ref, *refs):
+    grads, (dx_ref,) = refs[: 3 * groups], refs[3 * groups :]
     width = x_ref.shape[1]
     here = step_rows(x_ref.shape[0])
     scaled, inverse = norm_rows(x_ref[...].astype(f32))
-    arrive(idx_ref, weight)
     d_a1 = 0.0
     for part in range(3):
         at = part * width
         for g in range(groups):
             ref = grads[3 * g + part]
             cols = ref.shape[1]
-            d_a1 = d_a1 + nt(ref[here, :], whole[:, at : at + cols])
+            d_a1 = d_a1 + nt(ref[here, :], w_ref[:, at : at + cols])
             at += cols
-    d_x = dx1_ref[here, :] + norm_back(d_a1, scaled, inverse, vec_ref[0:1, :width])
+    d_x = dx1_ref[...] + norm_back(d_a1, scaled, inverse, vec_ref[0:1, :width])
     dx_ref[...] = d_x.astype(bf16)
 
 
@@ -731,59 +751,92 @@
 
     flat = [array for group in d_groups for array in group]
     return call(
-        functools.partial(input_body, weight.plan, len(d_groups)),
+        functools.partial(input_body, len(d_groups)),
         "grad_input",
         (rows // step,),
-        [row(width), fixed(dx1.shape), fixed(vec.shape)] + [fixed(array.shape) for array in flat] + weight.specs(),
+        [row(width), row(width)] + [fixed(array.shape) for array in (vec, weight, *flat)],
         row(width),
         hbm((rows, width), bf16),
-        weight.scratch(),
-        12,
+        [],
+        14,
         9,
-        near=(1, *range(3, 3 + len(flat))),
-    )(index, x, dx1, vec, *flat, *weight.arrays)
+        near=range(4, 4 + len(flat)),
+    )(index, x, dx1, vec, weight, *flat)
 
 
 def output_body(idx_ref, x1_ref, h_ref, vec_ref, w_ref, out_ref):
-    here = step_rows(out_ref.shape[0])
-    y = x1_ref[here, :] + nn(h_ref[here, :], w_ref[...]) + vec_ref[2:3, : x1_ref.shape[1]]
+    y = x1_ref[...] + nn(h_ref[...], w_ref[...]) + vec_ref[2:3, : x1_ref.shape[1]]
     out_ref[...] = y.astype(bf16)
 
 
 def output_call(index, x1, h, vec, weight):
     rows, width = x1.shape
-    step = 256
+
+    def row(cols):
+        return pl.BlockSpec((256, cols), lambda i, s: (i, 0))
+
     return call(
         output_body,
         "layer_output",
-        (rows // step,),
-        [fixed(array.shape) for array in (x1, h, vec, weight)],
-        pl.BlockSpec((step, width), lambda i, s: (i, 0)),
+        (rows // 256,),
+        [row(width), row(h.shape[1]), fixed(vec.shape), fixed(weight.shape)],
+        row(width),
         hbm((rows, width), bf16),
         [],
-        6,
+        14,
         8,
-        near=(0, 1, 3),
+        near=(3,),
     )(index, x1, h, vec, weight)
 
 
-def whole_call(name, body, arrays, outs, place=None):
+def pace_body(idx_ref, tile_ref, out_ref):
+    out_ref[...] = tile_ref[:8, :]
+
+
+def pace_call(index, tile):
+    return call(
+        pace_body,
+        "pace",
+        (1,),
+        [fixed(tile.shape)],
+        fixed((8, tile.shape[1])),
+        vmem((8, tile.shape[1]), f32),
+        [],
+        2,
+        5,
+        near=(0,),
+    )(index, tile)
+
+
+def whole_call(name, jobs):
+    arrays = [array for _, ins, _, _ in jobs for array in ins]
+    results = [place(shape, dtype) for _, _, outs, place in jobs for shape, dtype in outs]
+
     def run(*refs):
-        body(refs[: len(arrays)], refs[len(arrays) :])
-
-    return pl.pallas_call(
+        ins, outs = refs[: len(arrays)], refs[len(arrays) :]
+        at, to = 0, 0
+        for body, job_ins, job_outs, _ in jobs:
+            body(ins[at : at + len(job_ins)], outs[to : to + len(job_outs)])
+            at, to = at + len(job_ins), to + len(job_outs)
+
+    flat = pl.pallas_call(
         run,
         name=name,
         in_specs=[pl.BlockSpec(memory_space=pltpu.VMEM)] * len(arrays),
-        out_specs=[pl.BlockSpec(memory_space=pltpu.VMEM)] * len(outs),
-        out_shape=[(place or vmem)(shape, dtype) for shape, dtype in outs],
-        compiler_params=pltpu.CompilerParams(vmem_limit_bytes=8 * MIB),
+        out_specs=[pl.BlockSpec(memory_space=pltpu.VMEM)] * len(results),
+        out_shape=results,
+        compiler_params=pltpu.CompilerParams(vmem_limit_bytes=10 * MIB),
         cost_estimate=pl.CostEstimate(
             flops=0,
             bytes_accessed=sum(array.size * array.dtype.itemsize for array in arrays),
             transcendentals=0,
         ),
     )(*(pltpu.with_memory_space_constraint(array, pltpu.VMEM) for array in arrays))
+    groups, at = [], 0
+    for _, _, outs, _ in jobs:
+        groups.append(flat[at : at + len(outs)])
+        at += len(outs)
+    return groups
 
 
 def half_of(bit, flip, rows):
@@ -791,16 +844,16 @@
     return pl.ds(pl.multiple_of((1 - mine if flip else mine) * rows, math.gcd(rows, 256)), rows)
 
 
-def add_call(terms, rows, cols):
+def add_job(terms, rows, cols):
     def body(ins, outs):
         outs[0][...] = sum(
             (ref[...] if lead is None else ref[lead]).astype(f32) for ref, (_, lead) in zip(ins, terms)
         ).astype(bf16)
 
-    return whole_call("add_terms", body, [a for a, _ in terms], [((rows, cols), bf16)])[0]
-
-
-def halve_call(terms, rows, cols, bit):
+    return body, [a for a, _ in terms], [((rows, cols), bf16)], vmem
+
+
+def halve_job(terms, rows, cols, bit):
     def body(ins, outs):
         for flip, out in ((1, outs[0]), (0, outs[1])):
             half = half_of(bit, flip, rows)
@@ -809,76 +862,80 @@
                 for ref, (_, lead) in zip(ins, terms)
             ).astype(out.dtype)
 
-    return whole_call(
-        "add_halves", body, [a for a, _ in terms], [((rows, cols), bf16), ((rows, cols), f32)]
-    )
-
-
-def fork_call(keep, core, rows, cols, left):
+    return body, [a for a, _ in terms], [((rows, cols), bf16), ((rows, cols), f32)], vmem
+
+
+def part_job(keep, core, rows, cols):
     def body(ins, outs):
         kept, got = ins
-        outs[0][...] = (kept[1, :, :left].astype(f32) + got[1, :, :left].astype(f32)).astype(bf16)
-        half = half_of(1, 1, rows // 2)
-        for j in range(2):
-            outs[1][j] = (kept[j, half, left:].astype(f32) + got[j, half, left:].astype(f32)).astype(bf16)
-
-    return whole_call(
-        "add_fork", body, [keep, core], [((rows, left), bf16), ((2, rows // 2, cols - left), bf16)]
+        for j, out in ((1, outs[0]), (0, outs[1])):
+            out[...] = (kept[j].astype(f32) + got[j].astype(f32)).astype(out.dtype)
+
+    return body, [keep, core], [((rows, cols), bf16), ((rows, cols), f32)], vmem
+
+
+def fork_job(keep, core, rows, cols, left):
+    rest = cols - left
+
+    def body(ins, outs):
+        kept, got = ins
+        for j, out in ((1, outs[0]), (0, outs[2])):
+            out[...] = (kept[j, :, :left].astype(f32) + got[j, :, :left].astype(f32)).astype(out.dtype)
+        for flip, out in ((1, outs[1]), (0, outs[3])):
+            half = half_of(1, flip, rows // 2)
+            for j in range(2):
+                out[j] = (kept[j, half, left:].astype(f32) + got[j, half, left:].astype(f32)).astype(out.dtype)
+
+    shapes = [(rows, left), (2, rows // 2, rest)]
+    return body, [keep, core], [(shape, dtype) for dtype in (bf16, f32) for shape in shapes], vmem
+
+
+def cross_job(own_left, own_right, got_left, got_right, rows, cols, left):
+    rows //= 2
+
+    def body(ins, outs):
+        lefts, rights, from_left, from_right = ins
+        for flip, out in ((1, outs[0]), (0, outs[2])):
+            half = half_of(1, flip, rows)
+            out[...] = (lefts[half, :] + from_left[half, :].astype(f32)).astype(out.dtype)
+        for j, out in ((1, outs[1]), (0, outs[3])):
+            out[...] = (rights[j] + from_right[j].astype(f32)).astype(out.dtype)
+
+    shapes = [(rows, left), (rows, cols - left)]
+    return (
+        body, [own_left, own_right, got_left, got_right], [(shape, dtype) for dtype in (bf16, f32) for shape in shapes],
+        vmem,
     )
 
 
-def cross_call(keep, core, got_left, got_right, rows, cols, left):
-    rows //= 2
-
-    def body(ins, outs):
-        kept, got, from_left, from_right = ins
-        mine, other = half_of(1, 0, rows), half_of(1, 1, rows)
-        for half, out in ((other, outs[0]), (mine, outs[2])):
-            out[...] = (
-                kept[0, half, :left].astype(f32) + got[0, half, :left].astype(f32) + from_left[half, :].astype(f32)
-            ).astype(out.dtype)
-        for j, out in ((1, outs[1]), (0, outs[3])):
-            out[...] = (
-                kept[j, mine, left:].astype(f32) + got[j, mine, left:].astype(f32) + from_right[j].astype(f32)
-            ).astype(out.dtype)
-
-    shapes = [(rows, left), (rows, cols - left)]
-    return whole_call(
-        "add_cross", body, [keep, core, got_left, got_right],
-        [(shape, dtype) for dtype in (bf16, f32) for shape in shapes],
-    )
-
-
-def merge_call(lefts, rights, rows, cols, left, bit):
+def merge_job(lefts, rights, rows, cols, left, bit):
     def body(ins, outs):
         for flip, out in ((1, outs[0]), (0, outs[1])):
             half = half_of(bit, flip, rows)
             out[:, :left] = (ins[0][half, :].astype(f32) + ins[1][half, :].astype(f32)).astype(out.dtype)
             out[:, left:] = (ins[2][half, :].astype(f32) + ins[3][half, :].astype(f32)).astype(out.dtype)
 
-    return whole_call(
-        "add_merge", body, [*lefts, *rights], [((rows, cols), bf16), ((rows, cols), f32)]
-    )
-
-
-def join_call(mine, other, bit):
+    return body, [*lefts, *rights], [((rows, cols), bf16), ((rows, cols), f32)], vmem
+
+
+def join_job(mine, other, bit):
     rows, cols = mine.shape
 
     def body(ins, outs):
         for flip in (0, 1):
             outs[0][half_of(bit, flip, rows), :] = ins[flip][...]
 
-    return whole_call("join_halves", body, [mine, other], [((2 * rows, cols), bf16)])[0]
-
-
-def turn_call(mine, other, bit):
+    return body, [mine, other], [((2 * rows, cols), bf16)], vmem
+
+
+def turn_job(mine, other, bit):
     rows, cols = mine.shape
 
     def body(ins, outs):
         for flip in (0, 1):
             outs[0][:, half_of(bit, flip, rows)] = ins[flip][...].astype(f32).T
 
-    return whole_call("last_down", body, [mine, other], [((cols, 2 * rows), f32)], hbm)[0]
+    return body, [mine, other], [((cols, 2 * rows), f32)], hbm
 
 
 def spread_body(plans, w_ref, gain_ref, *refs):
@@ -894,15 +951,10 @@
     outs[-1][...] = (share / gain_ref[...].astype(f32).reshape(1, -1)).reshape(-1)
 
 
-def spread_call(weight, gain, sums, plans, shapes):
+def spread_job(weight, gain, sums, plans, shapes):
     arrays = [array for pair in sums for array in pair]
-    return whole_call(
-        "last_grads",
-        lambda ins, outs: spread_body(plans, *ins, *outs),
-        [weight, gain, *arrays],
-        [(shape, f32) for shape in (*shapes, gain.shape)],
-        hbm,
-    )
+    outs = [(shape, f32) for shape in (*shapes, gain.shape)]
+    return lambda ins, outs: spread_body(plans, *ins, *outs), [weight, gain, *arrays], outs, hbm
 
 
 def after(value, *deps):
@@ -924,52 +976,67 @@
         self.starts.append(start)
         return len(self.starts) - 1
 
-    def reduce(self, send, keep, left):
+    def reduce(self, send, keep, left=0):
         rows, cols = send.shape[1:]
         core = self.swap(send, "narrow", 1)
         deps = yield (send,)
         core = after(core, *deps)
-        to_left, to_right = fork_call(keep, core, rows, cols, left)
-        got_left, got_right = self.swap(to_left, "narrow", 2), self.swap(to_right, "wide", 1)
-        deps = yield to_left, to_right
-        to_left, to_right, mine_left, mine_right = cross_call(
-            keep, core, after(got_left, *deps), after(got_right, *deps), rows, cols, left
-        )
-        got_left, got_right = self.swap(to_left, "wide", 1), self.swap(to_right, "narrow", 2)
-        deps = yield to_left, to_right
-        rows //= 4
-        total, mine = merge_call(
-            (mine_left, after(got_left, *deps)), (mine_right, after(got_right, *deps)), rows, cols, left, 2
-        )
+        if left:
+            to_left, to_right, mine_left, mine_right = yield fork_job(keep, core, rows, cols, left)
+            got_left, got_right = self.swap(to_left, "narrow", 2), self.swap(to_right, "wide", 1)
+            deps = yield to_left, to_right
+            to_left, to_right, mine_left, mine_right = yield cross_job(
+                mine_left, mine_right, after(got_left, *deps), after(got_right, *deps), rows, cols, left
+            )
+            got_left, got_right = self.swap(to_left, "wide", 1), self.swap(to_right, "narrow", 2)
+            deps = yield to_left, to_right
+            rows //= 4
+            total, mine = yield merge_job(
+                (mine_left, after(got_left, *deps)), (mine_right, after(got_right, *deps)), rows, cols, left, 2
+            )
+        else:
+            total, mine = yield part_job(keep, core, rows, cols)
+            got = self.swap(total, "narrow", 2)
+            deps = yield (total,)
+            total, mine = yield halve_job([(mine, None), (after(got, *deps), None)], rows // 2, cols, 1)
+            got = self.swap(total, "wide", 1)
+            deps = yield (total,)
+            rows //= 4
+            total, mine = yield halve_job([(mine, None), (after(got, *deps), None)], rows, cols, 2)
         got = self.swap(total, "wide", 2)
         deps = yield (total,)
         terms = [(mine, None), (after(got, *deps), None)]
         bit = 4
         while bit < self.wide:
-            total = add_call(terms, rows, cols)
+            if bit == 4:
+                (total,) = yield add_job(terms, rows, cols)
+            else:
+                total = whole_call("add_terms", [add_job(terms, rows, cols)])[0][0]
             got = self.swap(total, "wide", bit)
             deps = (yield (total,)) if bit == 4 else ()
             terms = [(total, None), (after(got, *deps), None)]
             bit *= 2
-        total = add_call(terms, rows, cols)
+        (total,) = yield add_job(terms, rows, cols)
         got = self.swap(total, "wide", 2)
         deps = yield (total,)
-        total = join_call(total, after(got, *deps), 2)
+        (total,) = yield join_job(total, after(got, *deps), 2)
         got = self.swap(total, "wide", 1)
         deps = yield (total,)
         yield total, after(got, *deps)
 
 
-def begin(steps):
-    return next(steps)
-
-
-def step(steps, *deps):
-    return steps.send(deps)
+def begin(chain):
+    return next(chain)
+
+
+def close(chain, *deps):
+    return chain.send(deps)
 
 
 def advance(chains, *deps):
-    return [array for chain in chains for array in step(chain, *deps)]
+    jobs = [chain.send(deps) for chain in chains]
+    results = whole_call("gradient_sums", jobs)
+    return [array for chain, result in zip(chains, results) for array in chain.send(result)]
 
 
 def shards(narrow, wide, layer_input, cotangent, block_size, gain_attn, w_qkv, w_out, gain_mlp, w_up, b_up, w_down, b_down):
@@ -991,38 +1058,43 @@
     ]
     at_row = [moves.place((n ^ j) * w_out.shape[0]) for j in range(4)]
 
-    def half_places(shard):
-        half = shard.shape[0] // 2
-        return [
-            moves.place((n ^ j) * shard.shape[0] + extra)
-            for j, extra in (
-                (0, 0), (1, 0), (2, bit * half), (2, (1 - bit) * half), (3, bit * half), (3, (1 - bit) * half)
-            )
-        ]
-
-    def own_half(shard):
-        half = shard.shape[0] // 2
-        return lax.dynamic_slice_in_dim(shard, bit * half, half, 0)
-
-    def by_halves(shard, near, pieces, places):
-        rows = shard.shape[0]
-        return Weight(
-            [(a, r, p) for a, r, p in zip((shard, near, *pieces), (rows, rows) + (rows // 2,) * 4, places)]
+    at_down = [moves.place((n ^ j) * w_down.shape[0]) for j in range(4)]
+    size_up = w_up.shape[0] // 3
+    at_up = [
+        moves.place((n ^ j) * w_up.shape[0] + extra)
+        for j, extra in (
+            (0, 0), (1, 0), (2, bit * size_up), (2, 2 * size_up), (2, (1 - bit) * size_up),
+            (3, bit * size_up), (3, 2 * size_up), (3, (1 - bit) * size_up),
         )
-
-    at_up = half_places(w_up)
-    at_down = [moves.place((n ^ j) * w_down.shape[0]) for j in range(4)]
+    ]
     index = jnp.stack(moves.starts).astype(jnp.int32)
 
     def ready(*deps):
         return after(index, *deps)
 
-    first, second, near = first_call(index, w_qkv, gain_attn, gain_mlp, b_down, b_up)
+    freq = 10000.0 ** (-jnp.arange(HEAD // 2).astype(f32) / (HEAD // 2))
+    angles = jnp.arange(seq).astype(f32)[:, None] * freq[None, :]
+    cosine, sine = jnp.cos(angles), jnp.sin(angles)
+    cosine = jnp.tile(cosine, (1, 4))
+    sine = jnp.concatenate([-sine, sine, -sine, sine], axis=1)
+
+    first, small = first_call(index, w_qkv, gain_attn, gain_mlp, b_down, b_up)
     got_first = moves.swap(first, "narrow", 2)
-    got_near = moves.swap(near, "narrow", 1)
+    (second,) = thirds_call(ready(first), w_qkv, (None,))
+    got_second = moves.swap(second, "narrow", 2)
+    up_first, up_second = thirds_call(ready(second), w_up, (1, None))
+    got_near, got_small, up_near, out_near = (
+        moves.swap(after(v, first), "narrow", 1) for v in (w_qkv, small, w_up, w_out)
+    )
+    up_far, up_more = moves.swap(up_first, "narrow", 2), moves.swap(up_second, "narrow", 2)
+    paced = pace_call(ready(up_first), cosine)
+    got_first, got_near, got_small, up_near, out_near, _ = lax.optimization_barrier(
+        (got_first, got_near, got_small, up_near, out_near, paced)
+    )
     got_cross = moves.swap(got_first, "wide", 1)
-    got_second = moves.swap(after(second, got_first), "narrow", 2)
-    far_first, far_second, far_cross = (moves.swap(v, "narrow", 1) for v in (got_first, got_second, got_cross))
+    far_first = moves.swap(got_first, "narrow", 1)
+    out_far = moves.swap(after(w_out, got_first), "narrow", 2)
+    far_second, far_cross = (moves.swap(v, "narrow", 1) for v in (got_second, got_cross))
     count = w_qkv.shape[0]
     qkv_w = Weight(
         [
@@ -1036,15 +1108,8 @@
             )
         ]
     )
-    smalls = [near, got_near, got_first, far_first]
-    up_far = moves.swap(after(own_half(w_up), got_second), "narrow", 2)
-    out_near, up_near, down_near = (moves.swap(v, "narrow", 1) for v in (w_out, w_up, w_down))
-
-    freq = 10000.0 ** (-jnp.arange(HEAD // 2).astype(f32) / (HEAD // 2))
-    angles = jnp.arange(seq).astype(f32)[:, None] * freq[None, :]
-    cosine, sine = jnp.cos(angles), jnp.sin(angles)
-    cosine = jnp.tile(cosine, (1, 4))
-    sine = jnp.concatenate([-sine, sine, -sine, sine], axis=1)
+    smalls = [small, got_small, got_first, far_first]
+
     block = jnp.arange(TILE, dtype=jnp.int32) // block_size[0]
     row_block, col_block = block[:, None], block[None, :]
     same, less, upto, less_t, upto_t = (
@@ -1056,30 +1121,37 @@
     )
     dyt = d_y.T
 
-    qkv, a1t, vec = qkv_call(index, x, qkv_w, smalls, ff, cosine, sine)
+    qkv, a1t, vec, qkv_full = qkv_call(index, x, qkv_w, smalls, ff, cosine, sine)
     up_far = after(up_far, vec)
     up_cross = moves.swap(up_far, "wide", 1)
-    out_far = moves.swap(after(w_out, up_far), "narrow", 2)
     down_far = moves.swap(after(w_down, up_far), "narrow", 2)
     o, ot, lse = att_call(ready(up_far), qkv, (same, less_t, upto_t), 0, pairs)
-    up_cross, out_far = after(up_cross, lse), after(out_far, lse)
-    up_last = [moves.swap(v, "narrow", 1) for v in (after(up_far, lse), up_cross)]
+    up_pieces = [after(v, lse) for v in (up_far, up_more, up_cross)]
+    up_last = [moves.swap(v, "narrow", 1) for v in up_pieces]
+    out_far = after(out_far, lse)
     out_last = moves.swap(out_far, "narrow", 1)
     out_w = Weight([(a, w_out.shape[0], p) for a, p in zip((w_out, out_near, out_far, out_last), at_row)])
-    up_w = by_halves(w_up, up_near, (up_far, up_cross, *up_last), at_up)
+    up_w = Weight(
+        [
+            (a, r, p)
+            for a, r, p in zip(
+                (w_up, up_near, *up_pieces, *up_last), (w_up.shape[0],) * 2 + (size_up,) * 6, at_up
+            )
+        ]
+    )
     x1, a2t, h, g, out_full, up_full = up_call(ready(lse), x, o, vec, out_w, up_w)
     send = grad_down_call(index, dyt, h, (1, 2), narrow)
-    down_far = after(down_far, send)
+    keep = grad_down_call(ready(send), dyt, h, (0, 2), narrow)
+    down_far = after(down_far, keep)
     down_last = moves.swap(down_far, "narrow", 1)
+    down_near = moves.swap(after(w_down, send), "narrow", 1)
     down_w = Weight([(a, w_down.shape[0], p) for a, p in zip((w_down, down_near, down_far, down_last), at_down)])
-    keep = grad_down_call(ready(send, down_far), dyt, h, (0, 2), narrow)
     chain_a = moves.reduce(send, keep, width // 2)
     begin(chain_a)
     d_u, dx1, dx1r, d_o, biases, down_full = down_call(
         ready(keep, *advance([chain_a], keep)), d_y, x1, g, vec, up_full, out_full, down_w
     )
-    send = grad_up_call(index, a2t, ot, d_u, dx1r, biases, (1, 2), narrow)
-    keep = grad_up_call(ready(send), a2t, ot, d_u, dx1r, biases, (0, 2), narrow)
+    send, keep = grad_up_call(ready(*advance([chain_a], dx1r)), a2t, ot, d_u, dx1r, biases, narrow)
     chain_b = moves.reduce(send, keep, 2048)
     begin(chain_b)
 
@@ -1088,37 +1160,48 @@
             ready(*deps), qkv, d_o, o, lse, (same, less_t, upto_t), cosine, sine, start, count
         )
 
-    g0 = back(0, 2, keep, *advance([chain_a, chain_b], keep))
+    paced = pace_call(ready(send), same)
+    g0 = back(0, 2, keep, *advance([chain_a, chain_b], keep, paced))
     g1 = back(2, 2, g0[0], *advance([chain_a], g0[0]))
-    g2 = back(4, 2, g1[0], *advance([chain_a, chain_b], g1[0]))
+    g2 = back(4, 2, g1[0], *advance([chain_b], g1[0]))
     groups = [g0, g1, g2]
     rights = [array for group in groups for array in group]
-    send = grad_qkv_call(ready(*advance([chain_a, chain_b], g2[0])), a1t, rights, (1, 2), narrow)
-    keep = grad_qkv_call(ready(send), a1t, rights, (0, 2), narrow)
+    send, keep = grad_qkv_call(ready(*advance([chain_a, chain_b], g2[0])), a1t, rights, narrow)
     chain_c = moves.reduce(send, keep, 1152)
     begin(chain_c)
-    sent = advance([chain_a, chain_b, chain_c], keep)
+    paced = pace_call(ready(send), same)
+    sent = advance([chain_b, chain_c], keep, paced)
     output = output_call(ready(keep, *sent), x1, h, vec, down_full)
-    sum_a = step(chain_a, output)
-    sent = advance([chain_b, chain_c], output)
-    d_input = input_call(ready(output, *sum_a, *sent), x, dx1, vec, groups, qkv_w)
-    grad_down = turn_call(*sum_a, 1)
+    sent = advance([chain_a, chain_b, chain_c], output)
+    d_input = input_call(ready(output, *sent), x, dx1, vec, groups, qkv_full)
     sent = advance([chain_b, chain_c], d_input)
+    sum_a = close(chain_a, *sent)
+    (grad_down,) = whole_call("last_down", [turn_job(*sum_a, 1)])[0]
+    sent = advance([chain_c], *sent, grad_down)
     sent = advance([chain_c], *sent)
-    sum_b = step(chain_b, *sent)
+    sum_b = close(chain_b, *sent)
     sent = advance([chain_c], *sent)
-    sent = advance([chain_c], *sent)
-    sum_c = step(chain_c)
+    sum_c = close(chain_c)
 
     own = width // narrow
-    grad_up, grad_out, biases, grad_gain_mlp = spread_call(
-        w_up, gain_mlp, [sum_b], [[(0, ff, 0, 0), (ff, width, 1, 0), (ff + width, TILE, 2, 0)]],
-        [(own, ff), (own, width), (own, TILE)],
-    )
+    grad_up, grad_out, biases, grad_gain_mlp = whole_call(
+        "last_up",
+        [
+            spread_job(
+                w_up, gain_mlp, [sum_b], [[(0, ff, 0, 0), (ff, width, 1, 0), (ff + width, TILE, 2, 0)]],
+                [(own, ff), (own, width), (own, TILE)],
+            )
+        ],
+    )[0]
     biases = biases[:8].reshape(-1)
-    cols = 2 * PAIR
-    columns = [((3 * g + part) * cols, cols, 0, part * width + g * cols) for g in range(3) for part in range(3)]
-    grad_qkv, grad_gain_attn = spread_call(w_qkv, gain_attn, [sum_c], [columns], [(own, 3 * width)])
+    plan, begin_at, to = [], 0, 0
+    for group in groups:
+        cols = group[0].shape[1]
+        for part in range(3):
+            plan.append((begin_at, cols, 0, part * width + to))
+            begin_at += cols
+        to += cols
+    grad_qkv, grad_gain_attn = whole_call("last_qkv", [spread_job(w_qkv, gain_attn, [sum_c], [plan], [(own, 3 * width)])])[0]
     return (
         output[None],
         d_input[None],

time: 286 us -> 268 us (0.937)
  Pallas kernels: 178 us -> 165 us
  local copies, waits for them, and re-layouts: 13.7 us -> 5.33 us
    pallas_call x21 -> x15, Pallas kernels: 41.8 us -> 29.8 us  [whole_call(): pl.pallas_call(run, name=name, in_specs=[pl.BlockSpec(memory_space=pltpu....]
    unnamed x54 -> x12, local copies, waits for them, and re-layouts: 6.95 us -> 0.03 us
    ppermute x45 -> x48, waiting for transfers between devices: 49.9 us -> 52.4 us  [swap(): return lax.ppermute(value, axis, [(i, i ^ bit) for i in range(size)])]
    ppermute x45 -> x48, starting transfers between devices: 35.8 us -> 36.7 us  [swap(): return lax.ppermute(value, axis, [(i, i ^ bit) for i in range(size)])]
  transfers between devices with their start and end apart: 45 -> 48, of which waited for: 15 -> 12; matrix products, arithmetic and copies ran while one was open for 3% -> 3% of each run, Pallas kernels for 62% -> 57%
where the time goes in v2:
time: 268 us; the launch traced here: 264 us
  Pallas kernels  165 us (62%)
  waiting for transfers between devices  52.4 us (20%)
  starting transfers between devices  36.7 us (14%)
  local copies, waits for them, and re-layouts  5.33 us (2%)
  other arithmetic  2.9 us (1%)
    pallas_call x16, Pallas kernels, run(): return fun(index, *args)  135 us
    ppermute x48, waiting for transfers between devices, swap(): return lax.ppermute(value, axis, [(i, i ^ bit) for i in range(size)])  52.4 us
    ppermute x48, starting transfers between devices, swap(): return lax.ppermute(value, axis, [(i, i ^ bit) for i in range(size)])  36.7 us
    pallas_call x15, Pallas kernels, whole_call(): pl.pallas_call(run, name=name, in_specs=[pl.BlockSpec(memory_space=pltpu....  29.8 us
  transfers between devices with their start and end apart: 48, of which 12 were waited for; matrix products, arithmetic and copies ran while one was open for 3% of the time, Pallas kernels for 57%

profile of v2, /device:TPU:0, one launch (start us, length us, event | category | flops | bytes accessed | tf_op | source)
XLA Modules:
  0.0 263.9 jit_solution(9003187217140439926)
XLA Ops:
  0.8 2.4 first_message.1
  3.2 3.0 %collective-permute-start.1 = (bf16[72,2304]{1,0:T(8,128)(2,1)}, bf16[72,2304]{1,0:T(8,128)(2,1)}, u32[]{:S(2)}, u32[]{:S(2)}) collective-permute-start(bf16[72,2304]{1,0:T(8,128)(2,1)} %get-tuple-element.146), channel_id=1, source_target_pairs={{0,2},{1,3},{2,0},{3,1},{4,6},{5,7},{6,4},{7,5},{8,10},{9,11},{10,... | collective-permute-start | bytes 995336 | tf_op jit(solution)/shard_map/ppermute | solution.py:973
  7.2 1.5 next_message.2
  8.7 2.6 next_message.3
  12.0 2.0 collective-permute-start
  14.5 2.5 collective-permute-start.13
  22.4 2.2 collective-permute-done.8.refs_8_
  26.2 11.1 %norm_qkv.1 = (bf16[1024,2304]{1,0:T(8,128)(2,1)}, bf16[768,1024]{1,0:T(8,128)(2,1)}, f32[8,3072]{1,0:T(8,128)}, bf16[768,2304]{1,0:T(8,128)(2,1)}) custom-call(s32[27]{0:T(128)S(1)} %stack.81.idx_ref, bf16[1024,768]{1,0:T(8,128)(2,1)} %bitcast.34, f32[512,128]{1,0:T(8,128)} %copy.32.cos_ref, f32[512,128]{1,0:T(8,128)} %pad_maximum_fusion.sin_ref, ...), custom_call_target="tpu_custom_call" | custom-call | flops 6999999774720 | bytes 1048576 | tf_op jit(solution)/shard_map/norm_qkv/pallas_call | solution.py:144
  37.4 1.6 collective-permute-start.14
  39.0 11.6 %attention.1 = (bf16[1024,768]{1,0:T(8,128)(2,1)}, bf16[768,1024]{1,0:T(8,128)(2,1)}, f32[6,2,1024]{2,1,0:T(2,128)}) custom-call(s32[27]{0:T(128)S(1)} %stack.81.idx_ref, bf16[1024,2304]{1,0:T(8,128)(2,1)} %get-tuple-element.161.q_ref.k_ref.v_ref, bf16[1024,2304]{1,0:T(8,128)(2,1)} %get-tuple-element.161.q_ref.k_ref.v_ref, ...), custom_call_target="tpu_custom_call" | custom-call | flops 12000000212992 | bytes 1048576 | tf_op jit(solution)/shard_map/attention/pallas_call | solution.py:144
  51.7 1.7 copy.33.dyt_ref
  53.4 1.4 collective-permute-start.21
  54.8 19.4 %feed_up.1 = (f32[1024,768]{1,0:T(8,128)}, bf16[768,1024]{1,0:T(8,128)(2,1)S(1)}, bf16[1024,3072]{1,0:T(8,128)(2,1)S(1)}, bf16[1024,3072]{1,0:T(8,128)(2,1)S(1)}...) custom-call(s32[27]{0:T(128)S(1)} %stack.81.idx_ref, bf16[1024,768]{1,0:T(8,128)(2,1)} %bitcast.35, ...), custom_call_target="tpu_custom_call" | custom-call | flops 18000000319488 | bytes 1048576 | tf_op jit(solution)/shard_map/feed_up/pallas_call | solution.py:144
  74.3 4.8 %grad_down.2 = bf16[2,768,768]{2,1,0:T(8,128)(2,1)} custom-call(s32[27]{0:T(128)S(1)} %stack.81.idx_ref, bf16[768,1024]{1,0:T(8,128)(2,1)S(1)} %copy.33.dyt_ref, bf16[1024,3072]{1,0:T(8,128)(2,1)S(1)} %get-tuple-element.173.h_ref), custom_call_target="tpu_custom_call" | custom-call | flops 3000000053248 | bytes 1048576 | tf_op jit(solution)/shard_map/grad_down/pallas_call | solution.py:144
  79.1 3.4 %grad_down.3.refs_0_ = bf16[2,768,768]{2,1,0:T(8,128)(2,1)S(1)} custom-call(s32[27]{0:T(128)S(1)} %stack.81.idx_ref, bf16[768,1024]{1,0:T(8,128)(2,1)S(1)} %copy.33.dyt_ref, bf16[1024,3072]{1,0:T(8,128)(2,1)S(1)} %get-tuple-element.173.h_ref), custom_call_target="tpu_custom_call" | custom-call | flops 3000000053248 | bytes 1048576 | tf_op jit(solution)/shard_map/grad_down/pallas_call | solution.py:144
  83.9 3.0 %gradient_sums.12 = (bf16[768,384]{1,0:T(8,128)(2,1)}, bf16[2,384,384]{2,1,0:T(8,128)(2,1)}, f32[768,384]{1,0:T(8,128)S(1)}, f32[2,384,384]{2,1,0:T(8,128)S(1)}) custom-call(bf16[2,768,768]{2,1,0:T(8,128)(2,1)S(1)} %grad_down.3.refs_0_, bf16[2,768,768]{2,1,0:T(8,128)(2,1)} %collective-permute-done.18.refs_1_), custom_call_target="tpu_custom_call" | custom-call | bytes 4718592 | tf_op jit(solution)/shard_map/gradient_sums/pallas_call | solution.py:822
  88.1 20.6 %feed_back.1 = (bf16[1024,3072]{1,0:T(8,128)(2,1)S(1)}, f32[1024,768]{1,0:T(8,128)}, bf16[1024,768]{1,0:T(8,128)(2,1)S(1)}, bf16[1024,768]{1,0:T(8,128)(2,1)}, f...) custom-call(s32[27]{0:T(128)S(1)} %stack.81.idx_ref, bf16[1024,768]{1,0:T(8,128)(2,1)} %bitcast.32, ...), custom_call_target="tpu_custom_call" | custom-call | flops 19999999655936 | bytes 1048576 | tf_op jit(solution)/shard_map/feed_back/pallas_call | solution.py:144
  108.8 2.3 gradient_sums.13
  111.1 1.5 collective-permute-start.24
  113.9 7.7 %grad_up_out.1 = (bf16[2,192,3968]{2,1,0:T(8,128)(2,1)S(1)}, bf16[2,192,3968]{2,1,0:T(8,128)(2,1)S(1)}) custom-call(s32[27]{0:T(128)S(1)} %stack.81.idx_ref, bf16[768,1024]{1,0:T(8,128)(2,1)S(1)} %get-tuple-element.195.a_ref, bf16[768,1024]{1,0:T(8,128)(2,1)S(1)} %copy-done.4, bf16[1024,3072]{1,0:T(8,128)(2,1)S(1)} %get-tuple-element.197.du_ref, ...), custom_call_target="tpu_custom_call" | custom-call | flops 4700000223232 | bytes 1048576 | tf_op jit(solution)/shard_map/grad_up_out/pallas_call | solution.py:144
  121.7 5.5 %collective-permute-done.26.refs_5_ = bf16[2,192,3968]{2,1,0:T(8,128)(2,1)S(1)} collective-permute-done((bf16[2,192,3968]{2,1,0:T(8,128)(2,1)S(1)}, bf16[2,192,3968]{2,1,0:T(8,128)(2,1)S(1)}, u32[]{:S(2)}, u32[]{:S(2)}) %collective-permute-start.26) | collective-permute-done | bytes 3047456 | tf_op jit(solution)/shard_map/ppermute | solution.py:973
  127.1 2.7 %gradient_sums.14 = (bf16[192,768]{1,0:T(8,128)(2,1)}, f32[192,768]{1,0:T(8,128)S(1)}, bf16[192,2048]{1,0:T(8,128)(2,1)}, bf16[2,96,1920]{2,1,0:T(8,128)(2,1)}, ...) custom-call(f32[384,384]{1,0:T(8,128)S(1)} %get-tuple-element.191.refs_0_, ...), custom_call_target="tpu_custom_call" | custom-call | bytes 7864320 | tf_op jit(solution)/shard_map/gradient_sums/pallas_call | solution.py:822
  129.8 1.6 collective-permute-start.27
  132.6 8.8 %attention_back.3 = (bf16[1024,256]{1,0:T(8,128)(2,1)S(1)}, bf16[1024,256]{1,0:T(8,128)(2,1)S(1)}, bf16[1024,256]{1,0:T(8,128)(2,1)S(1)}) custom-call(s32[27]{0:T(128)S(1)} %stack.81.idx_ref, bf16[1024,2304]{1,0:T(8,128)(2,1)} %get-tuple-element.161.q_ref.k_ref.v_ref, bf16[1024,2304]{1,0:T(8,128)(2,1)} %get-tuple-element.161.q_ref.k_ref.v_ref, ...), custom_call_target="tpu_custom_call" | custom-call | flops 7199999918080 | bytes 1048576 | tf_op jit(solution)/shard_map/attention_back/pallas_call | solution.py:144
  141.4 1.8 gradient_sums.15.refs_0_
  143.2 2.6 collective-permute-start.28
  145.8 9.0 %attention_back.4 = (bf16[1024,256]{1,0:T(8,128)(2,1)S(1)}, bf16[1024,256]{1,0:T(8,128)(2,1)S(1)}, bf16[1024,256]{1,0:T(8,128)(2,1)S(1)}) custom-call(s32[27]{0:T(128)S(1)} %stack.81.idx_ref, bf16[1024,2304]{1,0:T(8,128)(2,1)} %get-tuple-element.161.q_ref.k_ref.v_ref, bf16[1024,2304]{1,0:T(8,128)(2,1)} %get-tuple-element.161.q_ref.k_ref.v_ref, ...), custom_call_target="tpu_custom_call" | custom-call | flops 7199999918080 | bytes 1048576 | tf_op jit(solution)/shard_map/attention_back/pallas_call | solution.py:144
  154.8 2.3 gradient_sums.16
  158.5 1.5 collective-permute-start.31
  160.0 8.8 %attention_back.5 = (bf16[1024,256]{1,0:T(8,128)(2,1)S(1)}, bf16[1024,256]{1,0:T(8,128)(2,1)S(1)}, bf16[1024,256]{1,0:T(8,128)(2,1)S(1)}) custom-call(s32[27]{0:T(128)S(1)} %stack.81.idx_ref, bf16[1024,2304]{1,0:T(8,128)(2,1)} %get-tuple-element.161.q_ref.k_ref.v_ref, bf16[1024,2304]{1,0:T(8,128)(2,1)} %get-tuple-element.161.q_ref.k_ref.v_ref, ...), custom_call_target="tpu_custom_call" | custom-call | flops 7199999918080 | bytes 1048576 | tf_op jit(solution)/shard_map/attention_back/pallas_call | solution.py:144
  168.9 2.4 gradient_sums.17
  171.7 1.6 collective-permute-start.33
  173.3 4.4 %grad_qkv.1 = (bf16[2,192,2304]{2,1,0:T(8,128)(2,1)S(1)}, bf16[2,192,2304]{2,1,0:T(8,128)(2,1)S(1)}) custom-call(s32[27]{0:T(128)S(1)} %stack.81.idx_ref, bf16[768,1024]{1,0:T(8,128)(2,1)S(1)} %copy-done.3, bf16[1024,256]{1,0:T(8,128)(2,1)S(1)} %get-tuple-element.212.refs_0_, bf16[1024,256]{1,0:T(8,128)(2,1)S(1)} %get-tuple-element.233.refs_1_, ...), custom_call_target="tpu_custom_call" | custom-call | flops 3304000061440 | bytes 1048576 | tf_op jit(solution)/shard_map/grad_qkv/pallas_call | solution.py:144
  177.7 9.4 %collective-permute-done.33.refs_1_ = bf16[48,3968]{1,0:T(8,128)(2,1)} collective-permute-done((bf16[48,3968]{1,0:T(8,128)(2,1)}, bf16[48,3968]{1,0:T(8,128)(2,1)}, u32[]{:S(2)}, u32[]{:S(2)}) %collective-permute-start.33) | collective-permute-done | bytes 380960 | tf_op jit(solution)/shard_map/ppermute | solution.py:973
  187.1 2.2 gradient_sums.18
  190.9 9.4 %layer_output.1 = bf16[1024,768]{1,0:T(8,128)(2,1)} custom-call(s32[27]{0:T(128)S(1)} %stack.81.idx_ref, f32[1024,768]{1,0:T(8,128)} %get-tuple-element.181.x1_ref, bf16[1024,3072]{1,0:T(8,128)(2,1)} %copy-done.2, f32[8,3072]{1,0:T(8,128)} %get-tuple-element.158.vec_ref, bf16[3072,768]{1,0:T(8,128)(2,1)S(1)} %get-tuple-element.249.w_ref), custom_call_target="tpu_custom_call" | custom-call | flops 7999999967232 | bytes 1048576 | tf_op jit(solution)/shard_map/layer_output/pallas_call | solution.py:144
  200.3 6.6 %collective-permute-done.36.refs_3_ = bf16[48,3968]{1,0:T(8,128)(2,1)} collective-permute-done((bf16[48,3968]{1,0:T(8,128)(2,1)}, bf16[48,3968]{1,0:T(8,128)(2,1)}, u32[]{:S(2)}, u32[]{:S(2)}) %collective-permute-start.36) | collective-permute-done | bytes 380960 | tf_op jit(solution)/shard_map/ppermute | solution.py:973
  206.9 2.8 %gradient_sums.19 = (bf16[384,768]{1,0:T(8,128)(2,1)}, bf16[48,3968]{1,0:T(8,128)(2,1)}, bf16[96,1152]{1,0:T(8,128)(2,1)}, bf16[96,1152]{1,0:T(8,128)(2,1)}, f32...) custom-call(bf16[192,768]{1,0:T(8,128)(2,1)} %get-tuple-element.229.refs_0_, ...), custom_call_target="tpu_custom_call" | custom-call | bytes 4005888 | tf_op jit(solution)/shard_map/gradient_sums/pallas_call | solution.py:822
  210.3 2.0 collective-permute-start.43
  212.3 9.3 %grad_input.1 = bf16[1024,768]{1,0:T(8,128)(2,1)} custom-call(s32[27]{0:T(128)S(1)} %stack.81.idx_ref, bf16[1024,768]{1,0:T(8,128)(2,1)} %bitcast.36, f32[1024,768]{1,0:T(8,128)} %get-tuple-element.261.dx1_ref, f32[8,3072]{1,0:T(8,128)} %get-tuple-element.158.vec_ref, bf16[768,2304]{1,0:T(8,128)(2,1)} %get-tuple-element.262.w_ref, ...), custom_call_target="tpu_custom_call" | custom-call | flops 9000000159744 | bytes 1048576 | tf_op jit(solution)/shard_map/grad_input/pallas_call | solution.py:144
  221.7 1.4 gradient_sums.20
  225.2 5.7 %collective-permute-done.43.refs_1_ = bf16[384,768]{1,0:T(8,128)(2,1)} collective-permute-done((bf16[384,768]{1,0:T(8,128)(2,1)}, bf16[384,768]{1,0:T(8,128)(2,1)}, u32[]{:S(2)}, u32[]{:S(2)}) %collective-permute-start.43) | collective-permute-done | bytes 589856 | tf_op jit(solution)/shard_map/ppermute | solution.py:973
  230.9 3.0 %last_down.1 = f32[768,768]{1,0:T(8,128)} custom-call(bf16[384,768]{1,0:T(8,128)(2,1)} %get-tuple-element.256.refs_0_, bf16[384,768]{1,0:T(8,128)(2,1)} %collective-permute-done.43.refs_1_), custom_call_target="tpu_custom_call" | custom-call | bytes 1179648 | tf_op jit(solution)/shard_map/last_down/pallas_call | solution.py:822
  234.1 8.8 %collective-permute-done.44.refs_1_ = bf16[48,2304]{1,0:T(8,128)(2,1)S(1)} collective-permute-done((bf16[48,2304]{1,0:T(8,128)(2,1)S(1)}, bf16[48,2304]{1,0:T(8,128)(2,1)S(1)}, u32[]{:S(2)}, u32[]{:S(2)}) %collective-permute-start.44) | collective-permute-done | bytes 221216 | tf_op jit(solution)/shard_map/ppermute | solution.py:973
  243.0 7.0 %collective-permute-done.45.refs_1_ = bf16[48,2304]{1,0:T(8,128)(2,1)S(1)} collective-permute-done((bf16[48,2304]{1,0:T(8,128)(2,1)S(1)}, bf16[48,2304]{1,0:T(8,128)(2,1)S(1)}, u32[]{:S(2)}, u32[]{:S(2)}) %collective-permute-start.45) | collective-permute-done | bytes 221216 | tf_op jit(solution)/shard_map/ppermute | solution.py:973
  250.2 3.2 %last_up.1 = (f32[192,3072]{1,0:T(8,128)}, f32[192,768]{1,0:T(8,128)}, f32[192,128]{1,0:T(8,128)}, f32[192]{0:T(256)}) custom-call(bf16[192,3072]{1,0:T(8,128)(2,1)} %refs_0_.11, bf16[192]{0:T(256)(128)(2,1)S(1)} %copy-done, bf16[96,3968]{1,0:T(8,128)(2,1)S(1)} %get-tuple-element.270.refs_2_, bf16[96,3968]{1,0:T(8,128)(2,1)S(1)} %collective-permute-done.47.refs_3_), custom_call_target="tpu_custom_call" | custom-call | bytes 2703744 | tf_op jit(solution)/shard_map/last_up/pallas_call | solution.py:822
  255.9 5.1 %collective-permute-done.46.refs_3_ = bf16[96,2304]{1,0:T(8,128)(2,1)S(1)} collective-permute-done((bf16[96,2304]{1,0:T(8,128)(2,1)S(1)}, bf16[96,2304]{1,0:T(8,128)(2,1)S(1)}, u32[]{:S(2)}, u32[]{:S(2)}) %collective-permute-start.46) | collective-permute-done | bytes 442400 | tf_op jit(solution)/shard_map/ppermute | solution.py:973
  261.0 2.6 %last_qkv.1 = (f32[192,2304]{1,0:T(8,128)}, f32[192]{0:T(256)}) custom-call(bf16[192,2304]{1,0:T(8,128)(2,1)} %refs_0_.10, bf16[192]{0:T(256)(128)(2,1)S(1)} %copy-done.1, bf16[96,2304]{1,0:T(8,128)(2,1)S(1)} %gradient_sums.23.refs_2_, bf16[96,2304]{1,0:T(8,128)(2,1)S(1)} %collective-permute-done.46.refs_3_), custom_call_target="tpu_custom_call" | custom-call | bytes 1769856 | tf_op jit(solution)/shard_map/last_qkv/pallas_call | solution.py:822
  (105 shorter events, 24.4 us)
Async XLA Ops:
  3.2 11.3 %collective-permute-start.1 = (bf16[72,2304]{1,0:T(8,128)(2,1)}, bf16[72,2304]{1,0:T(8,128)(2,1)}, u32[]{:S(2)}, u32[]{:S(2)}) collective-permute-start(bf16[72,2304]{1,0:T(8,128)(2,1)} %get-tuple-element.146), channel_id=1, source_target_pairs={{0,2},{1,3},{2,0},{3,1},{4,6},{5,7},{6,4},{7,5},{8,10},{9,11},{10,... | collective-permute-start | bytes 995336 | tf_op jit(solution)/shard_map/ppermute | solution.py:973
  6.2 5.8 %collective-permute-start.3 = (bf16[8,2304]{1,0:T(8,128)(2,1)}, bf16[8,2304]{1,0:T(8,128)(2,1)}, u32[]{:S(2)}, u32[]{:S(2)}) collective-permute-start(bf16[8,2304]{1,0:T(8,128)(2,1)} %get-tuple-element.152.refs_0_), channel_id=1, source_target_pairs={{0,1},{1,0},{2,3},{3,2},{4,5},{5,4},{6,7},{7,6},{8,9},{9,8},{10,11... | collective-permute-start | bytes 110600 | tf_op jit(solution)/shard_map/ppermute | solution.py:973
  6.2 5.9 %collective-permute-start.5 = (bf16[192,768]{1,0:T(8,128)(2,1)}, bf16[192,768]{1,0:T(8,128)(2,1)}, u32[]{:S(2)}, u32[]{:S(2)}) collective-permute-start(bf16[192,768]{1,0:T(8,128)(2,1)} %refs_0_.8), channel_id=1, source_target_pairs={{0,1},{1,0},{2,3},{3,2},{4,5},{5,4},{6,7},{7,6},{8,9},{9,8},{10,11... | collective-permute-start | bytes 884744 | tf_op jit(solution)/shard_map/ppermute | solution.py:973
  6.7 10.3 %collective-permute-start.2 = (bf16[192,2304]{1,0:T(8,128)(2,1)}, bf16[192,2304]{1,0:T(8,128)(2,1)}, u32[]{:S(2)}, u32[]{:S(2)}) collective-permute-start(bf16[192,2304]{1,0:T(8,128)(2,1)} %refs_0_.10), channel_id=1, source_target_pairs={{0,1},{1,0},{2,3},{3,2},{4,5},{5,4},{6,7},{7,6},{8,9},{9,8},{10,11... | collective-permute-start | bytes 2654216 | tf_op jit(solution)/shard_map/ppermute | solution.py:973
  6.7 10.3 %collective-permute-start.4 = (bf16[192,3072]{1,0:T(8,128)(2,1)}, bf16[192,3072]{1,0:T(8,128)(2,1)}, u32[]{:S(2)}, u32[]{:S(2)}) collective-permute-start(bf16[192,3072]{1,0:T(8,128)(2,1)} %refs_0_.11), channel_id=1, source_target_pairs={{0,1},{1,0},{2,3},{3,2},{4,5},{5,4},{6,7},{7,6},{8,9},{9,8},{10,11... | collective-permute-start | bytes 3538952 | tf_op jit(solution)/shard_map/ppermute | solution.py:973
  11.9 9.9 %collective-permute-start.7 = (bf16[64,2304]{1,0:T(8,128)(2,1)S(1)}, bf16[64,2304]{1,0:T(8,128)(2,1)S(1)}, u32[]{:S(2)}, u32[]{:S(2)}) collective-permute-start(bf16[64,2304]{1,0:T(8,128)(2,1)S(1)} %next_message.2), channel_id=1, source_target_pairs={{0,2},{1,3},{2,0},{3,1},{4,6},{5,7},{6,4},{7,5},{8,10},{9,11},{10,... | collective-permute-start | bytes 884744 | tf_op jit(solution)/shard_map/ppermute | solution.py:973
  12.0 25.4 %collective-permute-start = (bf16[64,3072]{1,0:T(8,128)(2,1)}, bf16[64,3072]{1,0:T(8,128)(2,1)}, u32[]{:S(2)}, u32[]{:S(2)}) collective-permute-start(bf16[64,3072]{1,0:T(8,128)(2,1)} %get-tuple-element.149), channel_id=1, source_target_pairs={{0,2},{1,3},{2,0},{3,1},{4,6},{5,7},{6,4},{7,5},{8,10},{9,11},{10,... | collective-permute-start | bytes 1179656 | tf_op jit(solution)/shard_map/ppermute | solution.py:973
  14.5 36.1 %collective-permute-start.13 = (bf16[64,3072]{1,0:T(8,128)(2,1)}, bf16[64,3072]{1,0:T(8,128)(2,1)}, u32[]{:S(2)}, u32[]{:S(2)}) collective-permute-start(bf16[64,3072]{1,0:T(8,128)(2,1)} %get-tuple-element.170), channel_id=1, source_target_pairs={{0,2},{1,3},{2,0},{3,1},{4,6},{5,7},{6,4},{7,5},{8,10},{9,11},{10,... | collective-permute-start | bytes 1179656 | tf_op jit(solution)/shard_map/ppermute | solution.py:973
  17.0 7.7 %collective-permute-start.8 = (bf16[72,2304]{1,0:T(8,128)(2,1)}, bf16[72,2304]{1,0:T(8,128)(2,1)S(1)}, u32[]{:S(2)}, u32[]{:S(2)}) collective-permute-start(bf16[72,2304]{1,0:T(8,128)(2,1)} %collective-permute-done.1.refs_2_.refs_6_), channel_id=1, source_target_pairs={{0,4},{4,0},{8,12},{12,8},{16,20},{20,16},{24,28},{28,24},{1,5},{5... | collective-permute-start | bytes 995336 | tf_op jit(solution)/shard_map/ppermute | solution.py:973
  21.9 3.7 %collective-permute-start.9 = (bf16[64,2304]{1,0:T(8,128)(2,1)S(1)}, bf16[64,2304]{1,0:T(8,128)(2,1)S(1)}, u32[]{:S(2)}, u32[]{:S(2)}) collective-permute-start(bf16[64,2304]{1,0:T(8,128)(2,1)S(1)} %collective-permute-done.7.refs_7_), channel_id=1, source_target_pairs={{0,1},{1,0},{2,3},{3,2},{4,5},{5,4},{6,7},{7,6},{8,9},{9,8},{10,11... | collective-permute-start | bytes 884744 | tf_op jit(solution)/shard_map/ppermute | solution.py:973
  21.9 4.3 %collective-permute-start.6 = (bf16[72,2304]{1,0:T(8,128)(2,1)}, bf16[72,2304]{1,0:T(8,128)(2,1)S(1)}, u32[]{:S(2)}, u32[]{:S(2)}) collective-permute-start(bf16[72,2304]{1,0:T(8,128)(2,1)} %collective-permute-done.1.refs_2_.refs_6_), channel_id=1, source_target_pairs={{0,1},{1,0},{2,3},{3,2},{4,5},{5,4},{6,7},{7,6},{8,9},{9,8},{10,11... | collective-permute-start | bytes 995336 | tf_op jit(solution)/shard_map/ppermute | solution.py:973
  24.6 1.6 collective-permute-start.10
  25.5 25.7 %collective-permute-start.11 = (bf16[192,768]{1,0:T(8,128)(2,1)}, bf16[192,768]{1,0:T(8,128)(2,1)}, u32[]{:S(2)}, u32[]{:S(2)}) collective-permute-start(bf16[192,768]{1,0:T(8,128)(2,1)} %refs_0_.8), channel_id=1, source_target_pairs={{0,2},{1,3},{2,0},{3,1},{4,6},{5,7},{6,4},{7,5},{8,10},{9,11},{10,... | collective-permute-start | bytes 884744 | tf_op jit(solution)/shard_map/ppermute | solution.py:973
  37.4 13.8 %collective-permute-start.14 = (bf16[64,3072]{1,0:T(8,128)(2,1)}, bf16[64,3072]{1,0:T(8,128)(2,1)}, u32[]{:S(2)}, u32[]{:S(2)}) collective-permute-start(bf16[64,3072]{1,0:T(8,128)(2,1)} %collective-permute-done.refs_6_), channel_id=1, source_target_pairs={{0,4},{4,0},{8,12},{12,8},{16,20},{20,16},{24,28},{28,24},{1,5},{5... | collective-permute-start | bytes 1179656 | tf_op jit(solution)/shard_map/ppermute | solution.py:973
  50.6 4.2 %collective-permute-start.15 = (bf16[64,3072]{1,0:T(8,128)(2,1)}, bf16[64,3072]{1,0:T(8,128)(2,1)S(1)}, u32[]{:S(2)}, u32[]{:S(2)}) collective-permute-start(bf16[64,3072]{1,0:T(8,128)(2,1)} %collective-permute-done.refs_6_), channel_id=1, source_target_pairs={{0,1},{1,0},{2,3},{3,2},{4,5},{5,4},{6,7},{7,6},{8,9},{9,8},{10,11... | collective-permute-start | bytes 1179656 | tf_op jit(solution)/shard_map/ppermute | solution.py:973
  50.7 4.1 %collective-permute-start.16 = (bf16[64,3072]{1,0:T(8,128)(2,1)}, bf16[64,3072]{1,0:T(8,128)(2,1)S(1)}, u32[]{:S(2)}, u32[]{:S(2)}) collective-permute-start(bf16[64,3072]{1,0:T(8,128)(2,1)} %collective-permute-done.13.refs_7_), channel_id=1, source_target_pairs={{0,1},{1,0},{2,3},{3,2},{4,5},{5,4},{6,7},{7,6},{8,9},{9,8},{10,11... | collective-permute-start | bytes 1179656 | tf_op jit(solution)/shard_map/ppermute | solution.py:973
  51.2 3.6 %collective-permute-start.17 = (bf16[64,3072]{1,0:T(8,128)(2,1)}, bf16[64,3072]{1,0:T(8,128)(2,1)S(1)}, u32[]{:S(2)}, u32[]{:S(2)}) collective-permute-start(bf16[64,3072]{1,0:T(8,128)(2,1)} %collective-permute-done.14.refs_8_), channel_id=1, source_target_pairs={{0,1},{1,0},{2,3},{3,2},{4,5},{5,4},{6,7},{7,6},{8,9},{9,8},{10,11... | collective-permute-start | bytes 1179656 | tf_op jit(solution)/shard_map/ppermute | solution.py:973
  51.3 3.5 %collective-permute-start.12 = (bf16[192,768]{1,0:T(8,128)(2,1)}, bf16[192,768]{1,0:T(8,128)(2,1)S(1)}, u32[]{:S(2)}, u32[]{:S(2)}) collective-permute-start(bf16[192,768]{1,0:T(8,128)(2,1)} %collective-permute-done.11.refs_2_), channel_id=1, source_target_pairs={{0,1},{1,0},{2,3},{3,2},{4,5},{5,4},{6,7},{7,6},{8,9},{9,8},{10,11... | collective-permute-start | bytes 884744 | tf_op jit(solution)/shard_map/ppermute | solution.py:973
  53.4 29.6 %collective-permute-start.21 = (bf16[768,768]{1,0:T(8,128)(2,1)}, bf16[768,768]{1,0:T(8,128)(2,1)}, u32[]{:S(2)}, u32[]{:S(2)}) collective-permute-start(bf16[768,768]{1,0:T(8,128)(2,1)} %refs_0_.9), channel_id=1, source_target_pairs={{0,2},{1,3},{2,0},{3,1},{4,6},{5,7},{6,4},{7,5},{8,10},{9,11},{10,... | collective-permute-start | bytes 3538952 | tf_op jit(solution)/shard_map/ppermute | solution.py:973
  79.1 4.9 %collective-permute-start.18 = (bf16[2,768,768]{2,1,0:T(8,128)(2,1)}, bf16[2,768,768]{2,1,0:T(8,128)(2,1)}, u32[]{:S(2)}, u32[]{:S(2)}) collective-permute-start(bf16[2,768,768]{2,1,0:T(8,128)(2,1)} %grad_down.2), channel_id=1, source_target_pairs={{0,1},{1,0},{2,3},{3,2},{4,5},{5,4},{6,7},{7,6},{8,9},{9,8},{10,11... | collective-permute-start | bytes 7077896 | tf_op jit(solution)/shard_map/ppermute | solution.py:973
  82.5 5.7 %collective-permute-start.20 = (bf16[768,768]{1,0:T(8,128)(2,1)S(1)}, bf16[768,768]{1,0:T(8,128)(2,1)S(1)}, u32[]{:S(2)}, u32[]{:S(2)}) collective-permute-start(bf16[768,768]{1,0:T(8,128)(2,1)S(1)} %copy-done.5), channel_id=1, source_target_pairs={{0,1},{1,0},{2,3},{3,2},{4,5},{5,4},{6,7},{7,6},{8,9},{9,8},{10,11... | collective-permute-start | bytes 3538952 | tf_op jit(solution)/shard_map/ppermute | solution.py:973
  83.0 5.1 %collective-permute-start.22 = (bf16[768,768]{1,0:T(8,128)(2,1)}, bf16[768,768]{1,0:T(8,128)(2,1)S(1)}, u32[]{:S(2)}, u32[]{:S(2)}) collective-permute-start(bf16[768,768]{1,0:T(8,128)(2,1)} %collective-permute-done.21.refs_2_), channel_id=1, source_target_pairs={{0,1},{1,0},{2,3},{3,2},{4,5},{5,4},{6,7},{7,6},{8,9},{9,8},{10,11... | collective-permute-start | bytes 3538952 | tf_op jit(solution)/shard_map/ppermute | solution.py:973
  86.9 21.9 %collective-permute-start.19 = (bf16[768,384]{1,0:T(8,128)(2,1)}, bf16[768,384]{1,0:T(8,128)(2,1)}, u32[]{:S(2)}, u32[]{:S(2)}) collective-permute-start(bf16[768,384]{1,0:T(8,128)(2,1)} %get-tuple-element.178), channel_id=1, source_target_pairs={{0,2},{1,3},{2,0},{3,1},{4,6},{5,7},{6,4},{7,5},{8,10},{9,11},{10,... | collective-permute-start | bytes 1769480 | tf_op jit(solution)/shard_map/ppermute | solution.py:973
  87.6 21.2 %collective-permute-start.23 = (bf16[2,384,384]{2,1,0:T(8,128)(2,1)}, bf16[2,384,384]{2,1,0:T(8,128)(2,1)}, u32[]{:S(2)}, u32[]{:S(2)}) collective-permute-start(bf16[2,384,384]{2,1,0:T(8,128)(2,1)} %get-tuple-element.179), channel_id=1, source_target_pairs={{0,4},{4,0},{8,12},{12,8},{16,20},{20,16},{24,28},{28,24},{1,5},{5... | collective-permute-start | bytes 1769480 | tf_op jit(solution)/shard_map/ppermute | solution.py:973
  111.1 10.6 %collective-permute-start.24 = (bf16[384,384]{1,0:T(8,128)(2,1)}, bf16[384,384]{1,0:T(8,128)(2,1)}, u32[]{:S(2)}, u32[]{:S(2)}) collective-permute-start(bf16[384,384]{1,0:T(8,128)(2,1)} %get-tuple-element.192), channel_id=1, source_target_pairs={{0,4},{4,0},{8,12},{12,8},{16,20},{20,16},{24,28},{28,24},{1,5},{5... | collective-permute-start | bytes 884744 | tf_op jit(solution)/shard_map/ppermute | solution.py:973
  112.6 9.1 %collective-permute-start.25 = (bf16[384,384]{1,0:T(8,128)(2,1)}, bf16[384,384]{1,0:T(8,128)(2,1)}, u32[]{:S(2)}, u32[]{:S(2)}) collective-permute-start(bf16[384,384]{1,0:T(8,128)(2,1)} %get-tuple-element.193), channel_id=1, source_target_pairs={{0,2},{1,3},{2,0},{3,1},{4,6},{5,7},{6,4},{7,5},{8,10},{9,11},{10,... | collective-permute-start | bytes 884744 | tf_op jit(solution)/shard_map/ppermute | solution.py:973
  121.6 5.6 %collective-permute-start.26 = (bf16[2,192,3968]{2,1,0:T(8,128)(2,1)S(1)}, bf16[2,192,3968]{2,1,0:T(8,128)(2,1)S(1)}, u32[]{:S(2)}, u32[]{:S(2)}) collective-permute-start(bf16[2,192,3968]{2,1,0:T(8,128)(2,1)S(1)} %get-tuple-element.200), channel_id=1, source_target_pairs={{0,1},{1,0},{2,3},{3,2},{4,5},{5,4},{6,7},{7,6},{8,9},{9,8},{10,11... | collective-permute-start | bytes 9142280 | tf_op jit(solution)/shard_map/ppermute | solution.py:973
  129.8 11.6 %collective-permute-start.27 = (bf16[192,768]{1,0:T(8,128)(2,1)}, bf16[192,768]{1,0:T(8,128)(2,1)}, u32[]{:S(2)}, u32[]{:S(2)}) collective-permute-start(bf16[192,768]{1,0:T(8,128)(2,1)} %get-tuple-element.207), channel_id=1, source_target_pairs={{0,8},{4,12},{8,0},{12,4},{16,24},{20,28},{24,16},{28,20},{1,9},{5... | collective-permute-start | bytes 884744 | tf_op jit(solution)/shard_map/ppermute | solution.py:973
  131.4 23.4 %collective-permute-start.30 = (bf16[2,96,1920]{2,1,0:T(8,128)(2,1)}, bf16[2,96,1920]{2,1,0:T(8,128)(2,1)}, u32[]{:S(2)}, u32[]{:S(2)}) collective-permute-start(bf16[2,96,1920]{2,1,0:T(8,128)(2,1)} %get-tuple-element.209), channel_id=1, source_target_pairs={{0,4},{4,0},{8,12},{12,8},{16,20},{20,16},{24,28},{28,24},{1,5},{5... | collective-permute-start | bytes 2211848 | tf_op jit(solution)/shard_map/ppermute | solution.py:973
  131.9 22.9 %collective-permute-start.29 = (bf16[192,2048]{1,0:T(8,128)(2,1)}, bf16[192,2048]{1,0:T(8,128)(2,1)}, u32[]{:S(2)}, u32[]{:S(2)}) collective-permute-start(bf16[192,2048]{1,0:T(8,128)(2,1)} %get-tuple-element.208), channel_id=1, source_target_pairs={{0,2},{1,3},{2,0},{3,1},{4,6},{5,7},{6,4},{7,5},{8,10},{9,11},{10,... | collective-permute-start | bytes 2359304 | tf_op jit(solution)/shard_map/ppermute | solution.py:973
  143.2 25.7 %collective-permute-start.28 = (bf16[192,768]{1,0:T(8,128)(2,1)}, bf16[192,768]{1,0:T(8,128)(2,1)}, u32[]{:S(2)}, u32[]{:S(2)}) collective-permute-start(bf16[192,768]{1,0:T(8,128)(2,1)} %gradient_sums.15.refs_0_), channel_id=1, source_target_pairs={{0,16},{4,20},{8,24},{12,28},{16,0},{20,4},{24,8},{28,12},{1,17},{... | collective-permute-start | bytes 884744 | tf_op jit(solution)/shard_map/ppermute | solution.py:973
  157.2 11.7 %collective-permute-start.32 = (bf16[96,1920]{1,0:T(8,128)(2,1)}, bf16[96,1920]{1,0:T(8,128)(2,1)}, u32[]{:S(2)}, u32[]{:S(2)}) collective-permute-start(bf16[96,1920]{1,0:T(8,128)(2,1)} %get-tuple-element.221), channel_id=1, source_target_pairs={{0,2},{1,3},{2,0},{3,1},{4,6},{5,7},{6,4},{7,5},{8,10},{9,11},{10,... | collective-permute-start | bytes 1105928 | tf_op jit(solution)/shard_map/ppermute | solution.py:973
  158.5 10.4 %collective-permute-start.31 = (bf16[96,2048]{1,0:T(8,128)(2,1)}, bf16[96,2048]{1,0:T(8,128)(2,1)}, u32[]{:S(2)}, u32[]{:S(2)}) collective-permute-start(bf16[96,2048]{1,0:T(8,128)(2,1)} %get-tuple-element.220), channel_id=1, source_target_pairs={{0,4},{4,0},{8,12},{12,8},{16,20},{20,16},{24,28},{28,24},{1,5},{5... | collective-permute-start | bytes 1179656 | tf_op jit(solution)/shard_map/ppermute | solution.py:973
  171.3 29.0 %collective-permute-start.35 = (bf16[192,768]{1,0:T(8,128)(2,1)}, bf16[192,768]{1,0:T(8,128)(2,1)}, u32[]{:S(2)}, u32[]{:S(2)}) collective-permute-start(bf16[192,768]{1,0:T(8,128)(2,1)} %get-tuple-element.229.refs_0_), channel_id=1, source_target_pairs={{0,8},{4,12},{8,0},{12,4},{16,24},{20,28},{24,16},{28,20},{1,9},{5... | collective-permute-start | bytes 884744 | tf_op jit(solution)/shard_map/ppermute | solution.py:973
  171.7 15.4 %collective-permute-start.33 = (bf16[48,3968]{1,0:T(8,128)(2,1)}, bf16[48,3968]{1,0:T(8,128)(2,1)}, u32[]{:S(2)}, u32[]{:S(2)}) collective-permute-start(bf16[48,3968]{1,0:T(8,128)(2,1)} %get-tuple-element.230), channel_id=1, source_target_pairs={{0,8},{4,12},{8,0},{12,4},{16,24},{20,28},{24,16},{28,20},{1,9},{5... | collective-permute-start | bytes 1142792 | tf_op jit(solution)/shard_map/ppermute | solution.py:973
  177.7 9.5 %collective-permute-start.34 = (bf16[2,192,2304]{2,1,0:T(8,128)(2,1)S(1)}, bf16[2,192,2304]{2,1,0:T(8,128)(2,1)S(1)}, u32[]{:S(2)}, u32[]{:S(2)}) collective-permute-start(bf16[2,192,2304]{2,1,0:T(8,128)(2,1)S(1)} %get-tuple-element.241), channel_id=1, source_target_pairs={{0,1},{1,0},{2,3},{3,2},{4,5},{5,4},{6,7},{7,6},{8,9},{9,8},{10,11... | collective-permute-start | bytes 5308424 | tf_op jit(solution)/shard_map/ppermute | solution.py:973
  189.3 17.6 %collective-permute-start.36 = (bf16[48,3968]{1,0:T(8,128)(2,1)}, bf16[48,3968]{1,0:T(8,128)(2,1)}, u32[]{:S(2)}, u32[]{:S(2)}) collective-permute-start(bf16[48,3968]{1,0:T(8,128)(2,1)} %get-tuple-element.245.refs_2_), channel_id=1, source_target_pairs={{0,16},{4,20},{8,24},{12,28},{16,0},{20,4},{24,8},{28,12},{1,17},{... | collective-permute-start | bytes 1142792 | tf_op jit(solution)/shard_map/ppermute | solution.py:973
  189.7 17.2 %collective-permute-start.37 = (bf16[192,1152]{1,0:T(8,128)(2,1)}, bf16[192,1152]{1,0:T(8,128)(2,1)}, u32[]{:S(2)}, u32[]{:S(2)}) collective-permute-start(bf16[192,1152]{1,0:T(8,128)(2,1)} %get-tuple-element.246), channel_id=1, source_target_pairs={{0,2},{1,3},{2,0},{3,1},{4,6},{5,7},{6,4},{7,5},{8,10},{9,11},{10,... | collective-permute-start | bytes 1327112 | tf_op jit(solution)/shard_map/ppermute | solution.py:973
  190.3 16.5 %collective-permute-start.38 = (bf16[2,96,1152]{2,1,0:T(8,128)(2,1)}, bf16[2,96,1152]{2,1,0:T(8,128)(2,1)}, u32[]{:S(2)}, u32[]{:S(2)}) collective-permute-start(bf16[2,96,1152]{2,1,0:T(8,128)(2,1)} %get-tuple-element.247), channel_id=1, source_target_pairs={{0,4},{4,0},{8,12},{12,8},{16,20},{20,16},{24,28},{28,24},{1,5},{5... | collective-permute-start | bytes 1327112 | tf_op jit(solution)/shard_map/ppermute | solution.py:973
  209.7 12.0 %collective-permute-start.40 = (bf16[96,1152]{1,0:T(8,128)(2,1)}, bf16[96,1152]{1,0:T(8,128)(2,1)}, u32[]{:S(2)}, u32[]{:S(2)}) collective-permute-start(bf16[96,1152]{1,0:T(8,128)(2,1)} %get-tuple-element.258), channel_id=1, source_target_pairs={{0,4},{4,0},{8,12},{12,8},{16,20},{20,16},{24,28},{28,24},{1,5},{5... | collective-permute-start | bytes 663560 | tf_op jit(solution)/shard_map/ppermute | solution.py:973
  209.7 12.0 %collective-permute-start.41 = (bf16[96,1152]{1,0:T(8,128)(2,1)}, bf16[96,1152]{1,0:T(8,128)(2,1)}, u32[]{:S(2)}, u32[]{:S(2)}) collective-permute-start(bf16[96,1152]{1,0:T(8,128)(2,1)} %get-tuple-element.259), channel_id=1, source_target_pairs={{0,2},{1,3},{2,0},{3,1},{4,6},{5,7},{6,4},{7,5},{8,10},{9,11},{10,... | collective-permute-start | bytes 663560 | tf_op jit(solution)/shard_map/ppermute | solution.py:973
  210.3 11.3 %collective-permute-start.39 = (bf16[48,3968]{1,0:T(8,128)(2,1)}, bf16[48,3968]{1,0:T(8,128)(2,1)}, u32[]{:S(2)}, u32[]{:S(2)}) collective-permute-start(bf16[48,3968]{1,0:T(8,128)(2,1)} %get-tuple-element.257.refs_0_), channel_id=1, source_target_pairs={{0,8},{4,12},{8,0},{12,4},{16,24},{20,28},{24,16},{28,20},{1,9},{5... | collective-permute-start | bytes 1142792 | tf_op jit(solution)/shard_map/ppermute | solution.py:973
  210.3 20.5 %collective-permute-start.43 = (bf16[384,768]{1,0:T(8,128)(2,1)}, bf16[384,768]{1,0:T(8,128)(2,1)}, u32[]{:S(2)}, u32[]{:S(2)}) collective-permute-start(bf16[384,768]{1,0:T(8,128)(2,1)} %get-tuple-element.256.refs_0_), channel_id=1, source_target_pairs={{0,4},{4,0},{8,12},{12,8},{16,20},{20,16},{24,28},{28,24},{1,5},{5... | collective-permute-start | bytes 1769480 | tf_op jit(solution)/shard_map/ppermute | solution.py:973
  223.1 27.1 %collective-permute-start.47 = (bf16[96,3968]{1,0:T(8,128)(2,1)S(1)}, bf16[96,3968]{1,0:T(8,128)(2,1)S(1)}, u32[]{:S(2)}, u32[]{:S(2)}) collective-permute-start(bf16[96,3968]{1,0:T(8,128)(2,1)S(1)} %get-tuple-element.270.refs_2_), channel_id=1, source_target_pairs={{0,4},{4,0},{8,12},{12,8},{16,20},{20,16},{24,28},{28,24},{1,5},{5... | collective-permute-start | bytes 2285576 | tf_op jit(solution)/shard_map/ppermute | solution.py:973
  224.3 9.6 %collective-permute-start.42 = (bf16[48,2304]{1,0:T(8,128)(2,1)S(1)}, bf16[48,2304]{1,0:T(8,128)(2,1)S(1)}, u32[]{:S(2)}, u32[]{:S(2)}) collective-permute-start(bf16[48,2304]{1,0:T(8,128)(2,1)S(1)} %get-tuple-element.269), channel_id=1, source_target_pairs={{0,8},{4,12},{8,0},{12,4},{16,24},{20,28},{24,16},{28,20},{1,9},{5... | collective-permute-start | bytes 663560 | tf_op jit(solution)/shard_map/ppermute | solution.py:973
  234.0 8.9 %collective-permute-start.44 = (bf16[48,2304]{1,0:T(8,128)(2,1)S(1)}, bf16[48,2304]{1,0:T(8,128)(2,1)S(1)}, u32[]{:S(2)}, u32[]{:S(2)}) collective-permute-start(bf16[48,2304]{1,0:T(8,128)(2,1)S(1)} %gradient_sums.21.refs_0_), channel_id=1, source_target_pairs={{0,16},{4,20},{8,24},{12,28},{16,0},{20,4},{24,8},{28,12},{1,17},{... | collective-permute-start | bytes 663560 | tf_op jit(solution)/shard_map/ppermute | solution.py:973
  243.0 7.1 %collective-permute-start.45 = (bf16[48,2304]{1,0:T(8,128)(2,1)S(1)}, bf16[48,2304]{1,0:T(8,128)(2,1)S(1)}, u32[]{:S(2)}, u32[]{:S(2)}) collective-permute-start(bf16[48,2304]{1,0:T(8,128)(2,1)S(1)} %gradient_sums.22.refs_0_), channel_id=1, source_target_pairs={{0,8},{4,12},{8,0},{12,4},{16,24},{20,28},{24,16},{28,20},{1,9},{5... | collective-permute-start | bytes 663560 | tf_op jit(solution)/shard_map/ppermute | solution.py:973
  250.1 10.9 %collective-permute-start.46 = (bf16[96,2304]{1,0:T(8,128)(2,1)S(1)}, bf16[96,2304]{1,0:T(8,128)(2,1)S(1)}, u32[]{:S(2)}, u32[]{:S(2)}) collective-permute-start(bf16[96,2304]{1,0:T(8,128)(2,1)S(1)} %gradient_sums.23.refs_2_), channel_id=1, source_target_pairs={{0,4},{4,0},{8,12},{12,8},{16,20},{20,16},{24,28},{28,24},{1,5},{5... | collective-permute-start | bytes 1327112 | tf_op jit(solution)/shard_map/ppermute | solution.py:973
  (6 other events, 52.1 us)

commit v3 on v2

--- a/solution.py
+++ b/solution.py
@@ -73,7 +73,7 @@
         return [pltpu.SemaphoreType.DMA((len(self.plan),))]
 
     def scratch(self):
-        return [pltpu.VMEM((self.rows, self.cols), bf16), pltpu.SemaphoreType.DMA((len(self.plan),))]
+        return [self.whole(), *self.sems()]
 
 
 def fetches(at_ref, plan, parts, whole, sems):
@@ -169,7 +169,7 @@
     return jnp.where(row == 0, lanes(gain1_ref, gain2_ref, down_ref), lanes(up_ref)).astype(bf16)
 
 
-def first_body(idx_ref, w_ref, gain1_ref, gain2_ref, down_ref, up_ref, out_ref, small_ref):
+def vector_body(idx_ref, w_ref, gain1_ref, gain2_ref, down_ref, up_ref, out_ref, small_ref):
     size = w_ref.shape[0]
     small = small_rows(w_ref.shape[1], gain1_ref, gain2_ref, down_ref, up_ref)
     out_ref[:size, :] = w_ref[...]
@@ -177,14 +177,14 @@
     small_ref[...] = small
 
 
-def first_call(index, weight, *vectors):
+def vector_call(index, weight, *vectors):
     size, cols = weight.shape[0] // 3, weight.shape[1]
     shapes = [(size + 8, cols), (8, cols)]
     return call(
-        first_body,
-        "first_message",
+        vector_body,
+        "vector_message",
         (1,),
-        [pl.BlockSpec((size, cols), lambda i, s: (s[1], 0))] + [fixed(v.shape) for v in vectors],
+        [pl.BlockSpec((size, cols), lambda i, s: (2, 0))] + [fixed(v.shape) for v in vectors],
         [fixed(shape) for shape in shapes],
         [vmem(shape, bf16) for shape in shapes],
         [],
@@ -220,6 +220,7 @@
     weight = (plan, parts, whole, sems)
     fetch(idx_ref, weight)
     width = x_ref.shape[1]
+    here = step_rows(x_ref.shape[0])
 
     @pl.when(pl.program_id(0) == 0)
     def _():
@@ -245,7 +246,7 @@
     for part in range(3):
         y = nn(a1, whole[:, part * width : (part + 1) * width])
         if part == 2:
-            qkv_ref[:, part * width :] = y.astype(bf16)
+            qkv_ref[here, part * width :] = y.astype(bf16)
             continue
         for t in range(width // PAIR):
             tile = y[:, t * PAIR : (t + 1) * PAIR]
@@ -253,7 +254,7 @@
             if part == 0:
                 tile = tile * (LOG2E / 8.0)
             at = part * width + t * PAIR
-            qkv_ref[:, at : at + PAIR] = tile.astype(bf16)
+            qkv_ref[here, at : at + PAIR] = tile.astype(bf16)
 
 
 def qkv_call(index, x, weight, smalls, ff, cosine, sine):
@@ -277,12 +278,12 @@
         + [vector(array) for array in smalls]
         + weight.specs(),
         [
-            pl.BlockSpec((step, wide), lambda i, s: (i, 0)),
+            fixed((rows, wide)),
             pl.BlockSpec((width, step), lambda i, s: (0, i)),
             pl.BlockSpec((8, ff), lambda i, s: (0, 0)),
             fixed((weight.rows, wide)),
         ],
-        [hbm((rows, wide), bf16), hbm((width, rows), bf16), hbm((8, ff), f32), hbm((weight.rows, wide), bf16)],
+        [vmem((rows, wide), bf16), hbm((width, rows), bf16), hbm((8, ff), f32), hbm((weight.rows, wide), bf16)],
         weight.sems(),
         16,
         7,
@@ -308,11 +309,14 @@
     )
 
 
-def att_body(seq, idx_ref, q_ref, k_ref, v_ref, same_ref, less_ref, upto_ref, *refs):
-    o_ref, ot_ref, lse_ref = refs[-3:]
-    k_all = k_ref[...]
+def att_body(seq, idx_ref, qkv_ref, same_ref, less_ref, upto_ref, o_ref, ot_ref, lse_ref):
+    def columns(part):
+        start = part * (qkv_ref.shape[1] // 3) + pl.program_id(0) * PAIR
+        return pl.ds(pl.multiple_of(start, PAIR), PAIR)
+
+    queries, k_all = columns(0), qkv_ref[:, columns(1)]
     keys = [jnp.where(m, k_all, jnp.zeros_like(k_all)) for m in head_masks()]
-    v_t = v_ref[...].T
+    v_t = qkv_ref[:, columns(2)].T
     ones = jnp.ones((16, 2 * seq), bf16)
     vals = [jnp.concatenate([v_t[h * HEAD : (h + 1) * HEAD], ones], axis=0) for h in range(2)]
     same, less, upto = widen(same_ref[...], False), widen(less_ref[...], True), widen(upto_ref[...], True)
@@ -320,7 +324,7 @@
     def scores(lo, clean, h):
         hi = lo + SPAN
         row = lo + seq if clean else lo
-        query = q_ref[row : row + SPAN, :]
+        query = qkv_ref[row : row + SPAN, queries]
         pieces = [nt(keys[h][seq + lo : seq + hi], query) + (upto if clean else less)]
         if lo > 0:
             pieces.append(nt(keys[h][seq : seq + lo], query))
@@ -364,31 +368,26 @@
     finish(*behind)
 
 
-def att_call(index, qkv, masks, start, count, held=()):
+def att_call(index, qkv, masks):
     rows = qkv.shape[0]
     width = qkv.shape[1] // 3
     pairs = width // PAIR
-
-    def column(part):
-        return pl.BlockSpec((rows, PAIR), lambda p, s: (0, part * pairs + start + p))
-
     return call(
         functools.partial(att_body, rows // 2),
         "attention",
-        (count,),
-        [column(0), column(1), column(2)] + [fixed((TILE, TILE))] * 3
-        + [pl.BlockSpec(memory_space=pltpu.HBM)] * len(held),
+        (pairs,),
+        [fixed(qkv.shape)] + [fixed((TILE, TILE))] * 3,
         [
-            pl.BlockSpec((rows, PAIR), lambda p, s: (0, start + p)),
-            pl.BlockSpec((PAIR, rows), lambda p, s: (start + p, 0)),
-            pl.BlockSpec((1, 2, rows), lambda p, s: (start + p, 0, 0)),
+            pl.BlockSpec((rows, PAIR), lambda p, s: (0, p)),
+            pl.BlockSpec((PAIR, rows), lambda p, s: (p, 0)),
+            pl.BlockSpec((1, 2, rows), lambda p, s: (p, 0, 0)),
         ],
         [hbm((rows, width), bf16), hbm((width, rows), bf16), hbm((pairs, 2, rows), f32)],
         [],
         16,
-        2.0 * count,
-        aliases={7 + i: i for i in range(len(held))},
-    )(index, qkv, qkv, qkv, *masks, *held)
+        12.0,
+        near=(0,),
+    )(index, qkv, *masks)
 
 
 def att_back_body(
@@ -1078,9 +1077,9 @@
     cosine = jnp.tile(cosine, (1, 4))
     sine = jnp.concatenate([-sine, sine, -sine, sine], axis=1)
 
-    first, small = first_call(index, w_qkv, gain_attn, gain_mlp, b_down, b_up)
+    first = lax.dynamic_slice_in_dim(w_qkv, bit * size, size, 0)
     got_first = moves.swap(first, "narrow", 2)
-    (second,) = thirds_call(ready(first), w_qkv, (None,))
+    second, small = vector_call(ready(first), w_qkv, gain_attn, gain_mlp, b_down, b_up)
     got_second = moves.swap(second, "narrow", 2)
     up_first, up_second = thirds_call(ready(second), w_up, (1, None))
     got_near, got_small, up_near, out_near = (
@@ -1108,7 +1107,7 @@
             )
         ]
     )
-    smalls = [small, got_small, got_first, far_first]
+    smalls = [small, got_small, got_second, far_second]
 
     block = jnp.arange(TILE, dtype=jnp.int32) // block_size[0]
     row_block, col_block = block[:, None], block[None, :]
@@ -1125,7 +1124,7 @@
     up_far = after(up_far, vec)
     up_cross = moves.swap(up_far, "wide", 1)
     down_far = moves.swap(after(w_down, up_far), "narrow", 2)
-    o, ot, lse = att_call(ready(up_far), qkv, (same, less_t, upto_t), 0, pairs)
+    o, ot, lse = att_call(ready(up_far), qkv, (same, less_t, upto_t))
     up_pieces = [after(v, lse) for v in (up_far, up_more, up_cross)]
     up_last = [moves.swap(v, "narrow", 1) for v in up_pieces]
     out_far = after(out_far, lse)
@@ -1166,21 +1165,22 @@
     g2 = back(4, 2, g1[0], *advance([chain_b], g1[0]))
     groups = [g0, g1, g2]
     rights = [array for group in groups for array in group]
-    send, keep = grad_qkv_call(ready(*advance([chain_a, chain_b], g2[0])), a1t, rights, narrow)
+    send, keep = grad_qkv_call(ready(*advance([chain_b], g2[0])), a1t, rights, narrow)
     chain_c = moves.reduce(send, keep, 1152)
     begin(chain_c)
     paced = pace_call(ready(send), same)
-    sent = advance([chain_b, chain_c], keep, paced)
+    sent = advance([chain_a], keep)
+    sent = advance([chain_b, chain_c], keep, paced, *sent)
     output = output_call(ready(keep, *sent), x1, h, vec, down_full)
-    sent = advance([chain_a, chain_b, chain_c], output)
+    sent = advance([chain_a, chain_c], output)
     d_input = input_call(ready(output, *sent), x, dx1, vec, groups, qkv_full)
     sent = advance([chain_b, chain_c], d_input)
+    sent = advance([chain_b, chain_c], *sent)
     sum_a = close(chain_a, *sent)
     (grad_down,) = whole_call("last_down", [turn_job(*sum_a, 1)])[0]
     sent = advance([chain_c], *sent, grad_down)
     sent = advance([chain_c], *sent)
     sum_b = close(chain_b, *sent)
-    sent = advance([chain_c], *sent)
     sum_c = close(chain_c)
 
     own = width // narrow

time: 268 us -> 257 us (0.959)
  waiting for transfers between devices: 52.4 us -> 37.1 us
  starting transfers between devices: 36.7 us -> 41.1 us
    ppermute x48, waiting for transfers between devices: 52.4 us -> 37.1 us  [swap(): return lax.ppermute(value, axis, [(i, i ^ bit) for i in range(size)])]
    ppermute x48, starting transfers between devices: 36.7 us -> 41.1 us  [swap(): return lax.ppermute(value, axis, [(i, i ^ bit) for i in range(size)])]
    pallas_call x16 -> x15, Pallas kernels: 135 us -> 133 us  [run(): return fun(index, *args)]
    pallas_call x15 -> x16, Pallas kernels: 29.8 us -> 30.1 us  [whole_call(): pl.pallas_call(run, name=name, in_specs=[pl.BlockSpec(memory_space=pltpu....]
  transfers between devices with their start and end apart: 48 -> 48, of which waited for: 12 -> 12; matrix products, arithmetic and copies ran while one was open for 3% -> 3% of each run, Pallas kernels for 57% -> 61%
where the time goes in v3:
time: 257 us; the launch traced here: 254 us
  Pallas kernels  163 us (63%)
  starting transfers between devices  41.1 us (16%)
  waiting for transfers between devices  37.1 us (14%)
  local copies, waits for them, and re-layouts  7.09 us (3%)
  other arithmetic  2.9 us (1%)
    pallas_call x15, Pallas kernels, run(): return fun(index, *args)  133 us
    ppermute x48, starting transfers between devices, swap(): return lax.ppermute(value, axis, [(i, i ^ bit) for i in range(size)])  41.1 us
    ppermute x48, waiting for transfers between devices, swap(): return lax.ppermute(value, axis, [(i, i ^ bit) for i in range(size)])  37.1 us
    pallas_call x16, Pallas kernels, whole_call(): pl.pallas_call(run, name=name, in_specs=[pl.BlockSpec(memory_space=pltpu....  30.1 us
  transfers between devices with their start and end apart: 48, of which 12 were waited for; matrix products, arithmetic and copies ran while one was open for 3% of the time, Pallas kernels for 61%

profile of v3, /device:TPU:0, one launch (start us, length us, event | category | flops | bytes accessed | tf_op | source)
XLA Modules:
  0.0 253.6 jit_solution(1823150636385081251)
XLA Ops:
  0.7 1.7 constant_dynamic-slice_fusion
  2.4 3.0 %collective-permute-start.1 = (bf16[64,2304]{1,0:T(8,128)(2,1)}, bf16[64,2304]{1,0:T(8,128)(2,1)}, u32[]{:S(2)}, u32[]{:S(2)}) collective-permute-start(bf16[64,2304]{1,0:T(8,128)(2,1)} %constant_dynamic-slice_fusion), channel_id=1, source_target_pairs={{0,2},{1,3},{2,0},{3,1},{4,6},{5,7},{6,4},{7,5},{8,10},{9,11},{10,... | collective-permute-start | bytes 884744 | tf_op jit(solution)/shard_map/ppermute | solution.py:972
  5.4 2.3 vector_message.1
  8.7 2.6 %next_message.1 = (bf16[64,3072]{1,0:T(8,128)(2,1)}, bf16[64,3072]{1,0:T(8,128)(2,1)}) custom-call(s32[27]{0:T(128)S(1)} %stack.81.idx_ref, bf16[192,3072]{1,0:T(8,128)(2,1)} %refs_0_.9, bf16[192,3072]{1,0:T(8,128)(2,1)} %refs_0_.9), custom_call_target="tpu_custom_call" | custom-call | flops 1500000026624 | bytes 1048576 | tf_op jit(solution)/shard_map/next_message/pallas_call | solution.py:144
  12.0 2.0 collective-permute-start
  14.4 1.7 collective-permute-start.8
  19.0 3.6 %collective-permute-done.6.refs_2_.refs_7_ = bf16[72,2304]{1,0:T(8,128)(2,1)S(1)} collective-permute-done((bf16[72,2304]{1,0:T(8,128)(2,1)S(1)}, bf16[72,2304]{1,0:T(8,128)(2,1)S(1)}, u32[]{:S(2)}, u32[]{:S(2)}) %collective-permute-start.6) | collective-permute-done | bytes 331808 | tf_op jit(solution)/shard_map/ppermute | solution.py:972
  25.3 11.6 %norm_qkv.1 = (bf16[1024,2304]{1,0:T(8,128)(2,1)S(1)}, bf16[768,1024]{1,0:T(8,128)(2,1)}, f32[8,3072]{1,0:T(8,128)}, bf16[768,2304]{1,0:T(8,128)(2,1)}) custom-call(s32[27]{0:T(128)S(1)} %stack.81.idx_ref, bf16[1024,768]{1,0:T(8,128)(2,1)} %bitcast.34, f32[512,128]{1,0:T(8,128)} %copy.32.cos_ref, f32[512,128]{1,0:T(8,128)} %pad_maximum_fusion.sin_ref, ...), custom_call_target="tpu_custom_call" | custom-call | flops 6999999774720 | bytes 1048576 | tf_op jit(solution)/shard_map/norm_qkv/pallas_call | solution.py:144
  36.9 1.6 collective-permute-start.14
  38.5 11.3 %attention.1 = (bf16[1024,768]{1,0:T(8,128)(2,1)}, bf16[768,1024]{1,0:T(8,128)(2,1)}, f32[6,2,1024]{2,1,0:T(2,128)}) custom-call(s32[27]{0:T(128)S(1)} %stack.81.idx_ref, bf16[1024,2304]{1,0:T(8,128)(2,1)S(1)} %get-tuple-element.161.qkv_ref.q_ref.k_ref.v_ref, f32[128,128]{1,0:T(8,128)} %get-tuple-element.286.same_ref, ...), custom_call_target="tpu_custom_call" | custom-call | flops 12000000212992 | bytes 1048576 | tf_op jit(solution)/shard_map/attention/pallas_call | solution.py:144
  50.9 1.7 copy.33.dyt_ref
  52.6 1.6 collective-permute-start.21
  54.2 19.4 %feed_up.1 = (f32[1024,768]{1,0:T(8,128)}, bf16[768,1024]{1,0:T(8,128)(2,1)S(1)}, bf16[1024,3072]{1,0:T(8,128)(2,1)S(1)}, bf16[1024,3072]{1,0:T(8,128)(2,1)S(1)}...) custom-call(s32[27]{0:T(128)S(1)} %stack.81.idx_ref, bf16[1024,768]{1,0:T(8,128)(2,1)} %bitcast.35, ...), custom_call_target="tpu_custom_call" | custom-call | flops 18000000319488 | bytes 1048576 | tf_op jit(solution)/shard_map/feed_up/pallas_call | solution.py:144
  73.7 4.8 %grad_down.2 = bf16[2,768,768]{2,1,0:T(8,128)(2,1)} custom-call(s32[27]{0:T(128)S(1)} %stack.81.idx_ref, bf16[768,1024]{1,0:T(8,128)(2,1)S(1)} %copy.33.dyt_ref, bf16[1024,3072]{1,0:T(8,128)(2,1)S(1)} %get-tuple-element.173.h_ref), custom_call_target="tpu_custom_call" | custom-call | flops 3000000053248 | bytes 1048576 | tf_op jit(solution)/shard_map/grad_down/pallas_call | solution.py:144
  78.5 3.4 %grad_down.3.refs_0_ = bf16[2,768,768]{2,1,0:T(8,128)(2,1)S(1)} custom-call(s32[27]{0:T(128)S(1)} %stack.81.idx_ref, bf16[768,1024]{1,0:T(8,128)(2,1)S(1)} %copy.33.dyt_ref, bf16[1024,3072]{1,0:T(8,128)(2,1)S(1)} %get-tuple-element.173.h_ref), custom_call_target="tpu_custom_call" | custom-call | flops 3000000053248 | bytes 1048576 | tf_op jit(solution)/shard_map/grad_down/pallas_call | solution.py:144
  83.3 3.0 %gradient_sums.13 = (bf16[768,384]{1,0:T(8,128)(2,1)}, bf16[2,384,384]{2,1,0:T(8,128)(2,1)}, f32[768,384]{1,0:T(8,128)S(1)}, f32[2,384,384]{2,1,0:T(8,128)S(1)}) custom-call(bf16[2,768,768]{2,1,0:T(8,128)(2,1)S(1)} %grad_down.3.refs_0_, bf16[2,768,768]{2,1,0:T(8,128)(2,1)} %collective-permute-done.18.refs_1_), custom_call_target="tpu_custom_call" | custom-call | bytes 4718592 | tf_op jit(solution)/shard_map/gradient_sums/pallas_call | solution.py:821
  87.7 20.6 %feed_back.1 = (bf16[1024,3072]{1,0:T(8,128)(2,1)S(1)}, f32[1024,768]{1,0:T(8,128)}, bf16[1024,768]{1,0:T(8,128)(2,1)S(1)}, bf16[1024,768]{1,0:T(8,128)(2,1)}, f...) custom-call(s32[27]{0:T(128)S(1)} %stack.81.idx_ref, bf16[1024,768]{1,0:T(8,128)(2,1)} %bitcast.32, ...), custom_call_target="tpu_custom_call" | custom-call | flops 19999999655936 | bytes 1048576 | tf_op jit(solution)/shard_map/feed_back/pallas_call | solution.py:144
  108.4 2.3 gradient_sums.14
  111.9 1.4 collective-permute-start.25
  113.3 7.7 %grad_up_out.1 = (bf16[2,192,3968]{2,1,0:T(8,128)(2,1)S(1)}, bf16[2,192,3968]{2,1,0:T(8,128)(2,1)S(1)}) custom-call(s32[27]{0:T(128)S(1)} %stack.81.idx_ref, bf16[768,1024]{1,0:T(8,128)(2,1)S(1)} %get-tuple-element.195.a_ref, bf16[768,1024]{1,0:T(8,128)(2,1)S(1)} %copy-done.5, bf16[1024,3072]{1,0:T(8,128)(2,1)S(1)} %get-tuple-element.197.du_ref, ...), custom_call_target="tpu_custom_call" | custom-call | flops 4700000223232 | bytes 1048576 | tf_op jit(solution)/shard_map/grad_up_out/pallas_call | solution.py:144
  121.1 5.5 %collective-permute-done.26.refs_5_ = bf16[2,192,3968]{2,1,0:T(8,128)(2,1)S(1)} collective-permute-done((bf16[2,192,3968]{2,1,0:T(8,128)(2,1)S(1)}, bf16[2,192,3968]{2,1,0:T(8,128)(2,1)S(1)}, u32[]{:S(2)}, u32[]{:S(2)}) %collective-permute-start.26) | collective-permute-done | bytes 3047456 | tf_op jit(solution)/shard_map/ppermute | solution.py:972
  126.5 2.7 %gradient_sums.15 = (bf16[192,768]{1,0:T(8,128)(2,1)}, f32[192,768]{1,0:T(8,128)S(1)}, bf16[192,2048]{1,0:T(8,128)(2,1)}, bf16[2,96,1920]{2,1,0:T(8,128)(2,1)}, ...) custom-call(f32[384,384]{1,0:T(8,128)S(1)} %get-tuple-element.191.refs_0_, ...), custom_call_target="tpu_custom_call" | custom-call | bytes 7864320 | tf_op jit(solution)/shard_map/gradient_sums/pallas_call | solution.py:821
  129.2 1.6 collective-permute-start.28
  132.2 8.8 %attention_back.3 = (bf16[1024,256]{1,0:T(8,128)(2,1)S(1)}, bf16[1024,256]{1,0:T(8,128)(2,1)S(1)}, bf16[1024,256]{1,0:T(8,128)(2,1)S(1)}) custom-call(s32[27]{0:T(128)S(1)} %stack.81.idx_ref, bf16[1024,2304]{1,0:T(8,128)(2,1)} %copy-done.4, bf16[1024,2304]{1,0:T(8,128)(2,1)} %copy-done.4, bf16[1024,2304]{1,0:T(8,128)(2,1)} %copy-done.4, ...), custom_call_target="tpu_custom_call" | custom-call | flops 7199999918080 | bytes 1048576 | tf_op jit(solution)/shard_map/attention_back/pallas_call | solution.py:144
  141.0 1.7 gradient_sums.16.refs_0_
  142.8 2.6 %collective-permute-start.33 = (bf16[192,768]{1,0:T(8,128)(2,1)}, bf16[192,768]{1,0:T(8,128)(2,1)}, u32[]{:S(2)}, u32[]{:S(2)}) collective-permute-start(bf16[192,768]{1,0:T(8,128)(2,1)} %gradient_sums.16.refs_0_), channel_id=1, source_target_pairs={{0,16},{4,20},{8,24},{12,28},{16,0},{20,4},{24,8},{28,12},{1,17},{... | collective-permute-start | bytes 884744 | tf_op jit(solution)/shard_map/ppermute | solution.py:972
  145.4 9.0 %attention_back.4 = (bf16[1024,256]{1,0:T(8,128)(2,1)S(1)}, bf16[1024,256]{1,0:T(8,128)(2,1)S(1)}, bf16[1024,256]{1,0:T(8,128)(2,1)S(1)}) custom-call(s32[27]{0:T(128)S(1)} %stack.81.idx_ref, bf16[1024,2304]{1,0:T(8,128)(2,1)} %copy-done.4, bf16[1024,2304]{1,0:T(8,128)(2,1)} %copy-done.4, bf16[1024,2304]{1,0:T(8,128)(2,1)} %copy-done.4, ...), custom_call_target="tpu_custom_call" | custom-call | flops 7199999918080 | bytes 1048576 | tf_op jit(solution)/shard_map/attention_back/pallas_call | solution.py:144
  154.4 2.3 gradient_sums.17
  156.8 1.4 collective-permute-start.31
  159.4 8.8 %attention_back.5 = (bf16[1024,256]{1,0:T(8,128)(2,1)S(1)}, bf16[1024,256]{1,0:T(8,128)(2,1)S(1)}, bf16[1024,256]{1,0:T(8,128)(2,1)S(1)}) custom-call(s32[27]{0:T(128)S(1)} %stack.81.idx_ref, bf16[1024,2304]{1,0:T(8,128)(2,1)} %copy-done.4, bf16[1024,2304]{1,0:T(8,128)(2,1)} %copy-done.4, bf16[1024,2304]{1,0:T(8,128)(2,1)} %copy-done.4, ...), custom_call_target="tpu_custom_call" | custom-call | flops 7199999918080 | bytes 1048576 | tf_op jit(solution)/shard_map/attention_back/pallas_call | solution.py:144
  168.3 2.5 %gradient_sums.18 = (bf16[48,3968]{1,0:T(8,128)(2,1)}, f32[48,3968]{1,0:T(8,128)S(1)}) custom-call(f32[96,2048]{1,0:T(8,128)S(1)} %get-tuple-element.220.refs_0_, bf16[96,2048]{1,0:T(8,128)(2,1)} %collective-permute-done.30.refs_1_, f32[96,1920]{1,0:T(8,128)S(1)} %get-tuple-element.226.refs_2_, bf16[96,1920]{1,0:T(8,128)(2,1)} %collective-permute-done.31.refs_3_), custom_call_target="tpu_custom_call" | custom-call | bytes 2285568 | tf_op jit(solution)/shard_map/gradient_sums/pallas_call | solution.py:821
  171.3 4.4 %grad_qkv.1 = (bf16[2,192,2304]{2,1,0:T(8,128)(2,1)S(1)}, bf16[2,192,2304]{2,1,0:T(8,128)(2,1)S(1)}) custom-call(s32[27]{0:T(128)S(1)} %stack.81.idx_ref, bf16[768,1024]{1,0:T(8,128)(2,1)S(1)} %copy-done.3, bf16[1024,256]{1,0:T(8,128)(2,1)S(1)} %get-tuple-element.213.refs_0_, bf16[1024,256]{1,0:T(8,128)(2,1)S(1)} %get-tuple-element.231.refs_1_, ...), custom_call_target="tpu_custom_call" | custom-call | flops 3304000061440 | bytes 1048576 | tf_op jit(solution)/shard_map/grad_qkv/pallas_call | solution.py:144
  175.8 1.9 gradient_sums.19.refs_0_
  177.6 1.6 collective-permute-start.35
  180.3 2.2 gradient_sums.20
  184.3 9.3 %layer_output.1 = bf16[1024,768]{1,0:T(8,128)(2,1)} custom-call(s32[27]{0:T(128)S(1)} %stack.81.idx_ref, f32[1024,768]{1,0:T(8,128)} %get-tuple-element.181.x1_ref, bf16[1024,3072]{1,0:T(8,128)(2,1)} %copy-done.2, f32[8,3072]{1,0:T(8,128)} %get-tuple-element.158.vec_ref, bf16[3072,768]{1,0:T(8,128)(2,1)S(1)} %get-tuple-element.248.w_ref), custom_call_target="tpu_custom_call" | custom-call | flops 7999999967232 | bytes 1048576 | tf_op jit(solution)/shard_map/layer_output/pallas_call | solution.py:144
  194.6 2.2 gradient_sums.21
  199.4 9.3 %grad_input.1 = bf16[1024,768]{1,0:T(8,128)(2,1)} custom-call(s32[27]{0:T(128)S(1)} %stack.81.idx_ref, bf16[1024,768]{1,0:T(8,128)(2,1)} %bitcast.36, f32[1024,768]{1,0:T(8,128)} %get-tuple-element.258.dx1_ref, f32[8,3072]{1,0:T(8,128)} %get-tuple-element.158.vec_ref, bf16[768,2304]{1,0:T(8,128)(2,1)} %get-tuple-element.259.w_ref, ...), custom_call_target="tpu_custom_call" | custom-call | flops 9000000159744 | bytes 1048576 | tf_op jit(solution)/shard_map/grad_input/pallas_call | solution.py:144
  208.7 1.4 gradient_sums.22
  210.1 1.6 collective-permute-start.41
  213.1 10.5 %collective-permute-done.42.refs_3_ = bf16[48,2304]{1,0:T(8,128)(2,1)S(1)} collective-permute-done((bf16[48,2304]{1,0:T(8,128)(2,1)S(1)}, bf16[48,2304]{1,0:T(8,128)(2,1)S(1)}, u32[]{:S(2)}, u32[]{:S(2)}) %collective-permute-start.42) | collective-permute-done | bytes 221216 | tf_op jit(solution)/shard_map/ppermute | solution.py:972
  224.7 2.6 %collective-permute-start.43 = (bf16[48,2304]{1,0:T(8,128)(2,1)S(1)}, bf16[48,2304]{1,0:T(8,128)(2,1)S(1)}, u32[]{:S(2)}, u32[]{:S(2)}) collective-permute-start(bf16[48,2304]{1,0:T(8,128)(2,1)S(1)} %get-tuple-element.270.refs_0_), channel_id=1, source_target_pairs={{0,16},{4,20},{8,24},{12,28},{16,0},{20,4},{24,8},{28,12},{1,17},{... | collective-permute-start | bytes 663560 | tf_op jit(solution)/shard_map/ppermute | solution.py:972
  227.3 1.8 last_down.1
  229.0 5.4 %collective-permute-done.43.refs_1_ = bf16[48,2304]{1,0:T(8,128)(2,1)S(1)} collective-permute-done((bf16[48,2304]{1,0:T(8,128)(2,1)S(1)}, bf16[48,2304]{1,0:T(8,128)(2,1)S(1)}, u32[]{:S(2)}, u32[]{:S(2)}) %collective-permute-start.43) | collective-permute-done | bytes 221216 | tf_op jit(solution)/shard_map/ppermute | solution.py:972
  235.2 5.3 %collective-permute-done.45.refs_1_ = bf16[48,2304]{1,0:T(8,128)(2,1)S(1)} collective-permute-done((bf16[48,2304]{1,0:T(8,128)(2,1)S(1)}, bf16[48,2304]{1,0:T(8,128)(2,1)S(1)}, u32[]{:S(2)}, u32[]{:S(2)}) %collective-permute-start.45) | collective-permute-done | bytes 221216 | tf_op jit(solution)/shard_map/ppermute | solution.py:972
  242.8 3.2 %last_up.1 = (f32[192,3072]{1,0:T(8,128)}, f32[192,768]{1,0:T(8,128)}, f32[192,128]{1,0:T(8,128)}, f32[192]{0:T(256)}) custom-call(bf16[192,3072]{1,0:T(8,128)(2,1)} %refs_0_.9, bf16[192]{0:T(256)(128)(2,1)S(1)} %copy-done, bf16[96,3968]{1,0:T(8,128)(2,1)S(1)} %get-tuple-element.271.refs_2_, bf16[96,3968]{1,0:T(8,128)(2,1)S(1)} %collective-permute-done.47.refs_3_), custom_call_target="tpu_custom_call" | custom-call | bytes 2703744 | tf_op jit(solution)/shard_map/last_up/pallas_call | solution.py:821
  248.6 2.1 collective-permute-done.46.refs_3_
  250.7 2.6 %last_qkv.1 = (f32[192,2304]{1,0:T(8,128)}, f32[192]{0:T(256)}) custom-call(bf16[192,2304]{1,0:T(8,128)(2,1)} %refs_0_.8, bf16[192]{0:T(256)(128)(2,1)S(1)} %copy-done.1, bf16[96,2304]{1,0:T(8,128)(2,1)S(1)} %gradient_sums.25.refs_2_, bf16[96,2304]{1,0:T(8,128)(2,1)S(1)} %collective-permute-done.46.refs_3_), custom_call_target="tpu_custom_call" | custom-call | bytes 1769856 | tf_op jit(solution)/shard_map/last_qkv/pallas_call | solution.py:821
  (120 shorter events, 30.1 us)
Async XLA Ops:
  2.4 11.7 %collective-permute-start.1 = (bf16[64,2304]{1,0:T(8,128)(2,1)}, bf16[64,2304]{1,0:T(8,128)(2,1)}, u32[]{:S(2)}, u32[]{:S(2)}) collective-permute-start(bf16[64,2304]{1,0:T(8,128)(2,1)} %constant_dynamic-slice_fusion), channel_id=1, source_target_pairs={{0,2},{1,3},{2,0},{3,1},{4,6},{5,7},{6,4},{7,5},{8,10},{9,11},{10,... | collective-permute-start | bytes 884744 | tf_op jit(solution)/shard_map/ppermute | solution.py:972
  5.3 6.7 %collective-permute-start.5 = (bf16[192,768]{1,0:T(8,128)(2,1)}, bf16[192,768]{1,0:T(8,128)(2,1)}, u32[]{:S(2)}, u32[]{:S(2)}) collective-permute-start(bf16[192,768]{1,0:T(8,128)(2,1)} %refs_0_.6), channel_id=1, source_target_pairs={{0,1},{1,0},{2,3},{3,2},{4,5},{5,4},{6,7},{7,6},{8,9},{9,8},{10,11... | collective-permute-start | bytes 884744 | tf_op jit(solution)/shard_map/ppermute | solution.py:972
  7.7 4.2 %collective-permute-start.3 = (bf16[8,2304]{1,0:T(8,128)(2,1)}, bf16[8,2304]{1,0:T(8,128)(2,1)}, u32[]{:S(2)}, u32[]{:S(2)}) collective-permute-start(bf16[8,2304]{1,0:T(8,128)(2,1)} %get-tuple-element.152.refs_0_), channel_id=1, source_target_pairs={{0,1},{1,0},{2,3},{3,2},{4,5},{5,4},{6,7},{7,6},{8,9},{9,8},{10,11... | collective-permute-start | bytes 110600 | tf_op jit(solution)/shard_map/ppermute | solution.py:972
  8.2 6.2 %collective-permute-start.2 = (bf16[192,2304]{1,0:T(8,128)(2,1)}, bf16[192,2304]{1,0:T(8,128)(2,1)}, u32[]{:S(2)}, u32[]{:S(2)}) collective-permute-start(bf16[192,2304]{1,0:T(8,128)(2,1)} %refs_0_.8), channel_id=1, source_target_pairs={{0,1},{1,0},{2,3},{3,2},{4,5},{5,4},{6,7},{7,6},{8,9},{9,8},{10,11... | collective-permute-start | bytes 2654216 | tf_op jit(solution)/shard_map/ppermute | solution.py:972
  8.2 6.2 %collective-permute-start.4 = (bf16[192,3072]{1,0:T(8,128)(2,1)}, bf16[192,3072]{1,0:T(8,128)(2,1)}, u32[]{:S(2)}, u32[]{:S(2)}) collective-permute-start(bf16[192,3072]{1,0:T(8,128)(2,1)} %refs_0_.9), channel_id=1, source_target_pairs={{0,1},{1,0},{2,3},{3,2},{4,5},{5,4},{6,7},{7,6},{8,9},{9,8},{10,11... | collective-permute-start | bytes 3538952 | tf_op jit(solution)/shard_map/ppermute | solution.py:972
  12.0 10.7 %collective-permute-start.6 = (bf16[72,2304]{1,0:T(8,128)(2,1)S(1)}, bf16[72,2304]{1,0:T(8,128)(2,1)S(1)}, u32[]{:S(2)}, u32[]{:S(2)}) collective-permute-start(bf16[72,2304]{1,0:T(8,128)(2,1)S(1)} %get-tuple-element.147), channel_id=1, source_target_pairs={{0,2},{1,3},{2,0},{3,1},{4,6},{5,7},{6,4},{7,5},{8,10},{9,11},{10,... | collective-permute-start | bytes 995336 | tf_op jit(solution)/shard_map/ppermute | solution.py:972
  12.0 24.9 %collective-permute-start = (bf16[64,3072]{1,0:T(8,128)(2,1)}, bf16[64,3072]{1,0:T(8,128)(2,1)}, u32[]{:S(2)}, u32[]{:S(2)}) collective-permute-start(bf16[64,3072]{1,0:T(8,128)(2,1)} %get-tuple-element.149), channel_id=1, source_target_pairs={{0,2},{1,3},{2,0},{3,1},{4,6},{5,7},{6,4},{7,5},{8,10},{9,11},{10,... | collective-permute-start | bytes 1179656 | tf_op jit(solution)/shard_map/ppermute | solution.py:972
  14.1 35.8 %collective-permute-start.13 = (bf16[64,3072]{1,0:T(8,128)(2,1)}, bf16[64,3072]{1,0:T(8,128)(2,1)}, u32[]{:S(2)}, u32[]{:S(2)}) collective-permute-start(bf16[64,3072]{1,0:T(8,128)(2,1)} %get-tuple-element.170), channel_id=1, source_target_pairs={{0,2},{1,3},{2,0},{3,1},{4,6},{5,7},{6,4},{7,5},{8,10},{9,11},{10,... | collective-permute-start | bytes 1179656 | tf_op jit(solution)/shard_map/ppermute | solution.py:972
  14.4 8.8 %collective-permute-start.8 = (bf16[64,2304]{1,0:T(8,128)(2,1)}, bf16[64,2304]{1,0:T(8,128)(2,1)S(1)}, u32[]{:S(2)}, u32[]{:S(2)}) collective-permute-start(bf16[64,2304]{1,0:T(8,128)(2,1)} %collective-permute-done.1.refs_6_), channel_id=1, source_target_pairs={{0,4},{4,0},{8,12},{12,8},{16,20},{20,16},{24,28},{28,24},{1,5},{5... | collective-permute-start | bytes 884744 | tf_op jit(solution)/shard_map/ppermute | solution.py:972
  22.7 2.1 collective-permute-start.7
  22.7 2.6 %collective-permute-start.9 = (bf16[64,2304]{1,0:T(8,128)(2,1)}, bf16[64,2304]{1,0:T(8,128)(2,1)S(1)}, u32[]{:S(2)}, u32[]{:S(2)}) collective-permute-start(bf16[64,2304]{1,0:T(8,128)(2,1)} %collective-permute-done.1.refs_6_), channel_id=1, source_target_pairs={{0,1},{1,0},{2,3},{3,2},{4,5},{5,4},{6,7},{7,6},{8,9},{9,8},{10,11... | collective-permute-start | bytes 884744 | tf_op jit(solution)/shard_map/ppermute | solution.py:972
  23.2 2.1 collective-permute-start.10
  24.7 25.8 %collective-permute-start.11 = (bf16[192,768]{1,0:T(8,128)(2,1)}, bf16[192,768]{1,0:T(8,128)(2,1)}, u32[]{:S(2)}, u32[]{:S(2)}) collective-permute-start(bf16[192,768]{1,0:T(8,128)(2,1)} %refs_0_.6), channel_id=1, source_target_pairs={{0,2},{1,3},{2,0},{3,1},{4,6},{5,7},{6,4},{7,5},{8,10},{9,11},{10,... | collective-permute-start | bytes 884744 | tf_op jit(solution)/shard_map/ppermute | solution.py:972
  36.9 13.5 %collective-permute-start.14 = (bf16[64,3072]{1,0:T(8,128)(2,1)}, bf16[64,3072]{1,0:T(8,128)(2,1)}, u32[]{:S(2)}, u32[]{:S(2)}) collective-permute-start(bf16[64,3072]{1,0:T(8,128)(2,1)} %collective-permute-done.refs_6_), channel_id=1, source_target_pairs={{0,4},{4,0},{8,12},{12,8},{16,20},{20,16},{24,28},{28,24},{1,5},{5... | collective-permute-start | bytes 1179656 | tf_op jit(solution)/shard_map/ppermute | solution.py:972
  49.8 4.4 %collective-permute-start.15 = (bf16[64,3072]{1,0:T(8,128)(2,1)}, bf16[64,3072]{1,0:T(8,128)(2,1)S(1)}, u32[]{:S(2)}, u32[]{:S(2)}) collective-permute-start(bf16[64,3072]{1,0:T(8,128)(2,1)} %collective-permute-done.refs_6_), channel_id=1, source_target_pairs={{0,1},{1,0},{2,3},{3,2},{4,5},{5,4},{6,7},{7,6},{8,9},{9,8},{10,11... | collective-permute-start | bytes 1179656 | tf_op jit(solution)/shard_map/ppermute | solution.py:972
  49.9 4.3 %collective-permute-start.16 = (bf16[64,3072]{1,0:T(8,128)(2,1)}, bf16[64,3072]{1,0:T(8,128)(2,1)S(1)}, u32[]{:S(2)}, u32[]{:S(2)}) collective-permute-start(bf16[64,3072]{1,0:T(8,128)(2,1)} %collective-permute-done.13.refs_7_), channel_id=1, source_target_pairs={{0,1},{1,0},{2,3},{3,2},{4,5},{5,4},{6,7},{7,6},{8,9},{9,8},{10,11... | collective-permute-start | bytes 1179656 | tf_op jit(solution)/shard_map/ppermute | solution.py:972
  50.4 3.8 %collective-permute-start.17 = (bf16[64,3072]{1,0:T(8,128)(2,1)}, bf16[64,3072]{1,0:T(8,128)(2,1)S(1)}, u32[]{:S(2)}, u32[]{:S(2)}) collective-permute-start(bf16[64,3072]{1,0:T(8,128)(2,1)} %collective-permute-done.14.refs_8_), channel_id=1, source_target_pairs={{0,1},{1,0},{2,3},{3,2},{4,5},{5,4},{6,7},{7,6},{8,9},{9,8},{10,11... | collective-permute-start | bytes 1179656 | tf_op jit(solution)/shard_map/ppermute | solution.py:972
  50.5 3.7 %collective-permute-start.12 = (bf16[192,768]{1,0:T(8,128)(2,1)}, bf16[192,768]{1,0:T(8,128)(2,1)S(1)}, u32[]{:S(2)}, u32[]{:S(2)}) collective-permute-start(bf16[192,768]{1,0:T(8,128)(2,1)} %collective-permute-done.11.refs_2_), channel_id=1, source_target_pairs={{0,1},{1,0},{2,3},{3,2},{4,5},{5,4},{6,7},{7,6},{8,9},{9,8},{10,11... | collective-permute-start | bytes 884744 | tf_op jit(solution)/shard_map/ppermute | solution.py:972
  52.6 29.8 %collective-permute-start.21 = (bf16[768,768]{1,0:T(8,128)(2,1)}, bf16[768,768]{1,0:T(8,128)(2,1)}, u32[]{:S(2)}, u32[]{:S(2)}) collective-permute-start(bf16[768,768]{1,0:T(8,128)(2,1)} %refs_0_.7), channel_id=1, source_target_pairs={{0,2},{1,3},{2,0},{3,1},{4,6},{5,7},{6,4},{7,5},{8,10},{9,11},{10,... | collective-permute-start | bytes 3538952 | tf_op jit(solution)/shard_map/ppermute | solution.py:972
  78.5 4.9 %collective-permute-start.18 = (bf16[2,768,768]{2,1,0:T(8,128)(2,1)}, bf16[2,768,768]{2,1,0:T(8,128)(2,1)}, u32[]{:S(2)}, u32[]{:S(2)}) collective-permute-start(bf16[2,768,768]{2,1,0:T(8,128)(2,1)} %grad_down.2), channel_id=1, source_target_pairs={{0,1},{1,0},{2,3},{3,2},{4,5},{5,4},{6,7},{7,6},{8,9},{9,8},{10,11... | collective-permute-start | bytes 7077896 | tf_op jit(solution)/shard_map/ppermute | solution.py:972
  81.9 5.9 %collective-permute-start.20 = (bf16[768,768]{1,0:T(8,128)(2,1)S(1)}, bf16[768,768]{1,0:T(8,128)(2,1)S(1)}, u32[]{:S(2)}, u32[]{:S(2)}) collective-permute-start(bf16[768,768]{1,0:T(8,128)(2,1)S(1)} %copy-done.12), channel_id=1, source_target_pairs={{0,1},{1,0},{2,3},{3,2},{4,5},{5,4},{6,7},{7,6},{8,9},{9,8},{10,11... | collective-permute-start | bytes 3538952 | tf_op jit(solution)/shard_map/ppermute | solution.py:972
  82.4 5.3 %collective-permute-start.22 = (bf16[768,768]{1,0:T(8,128)(2,1)}, bf16[768,768]{1,0:T(8,128)(2,1)S(1)}, u32[]{:S(2)}, u32[]{:S(2)}) collective-permute-start(bf16[768,768]{1,0:T(8,128)(2,1)} %collective-permute-done.21.refs_2_), channel_id=1, source_target_pairs={{0,1},{1,0},{2,3},{3,2},{4,5},{5,4},{6,7},{7,6},{8,9},{9,8},{10,11... | collective-permute-start | bytes 3538952 | tf_op jit(solution)/shard_map/ppermute | solution.py:972
  86.3 22.1 %collective-permute-start.19 = (bf16[768,384]{1,0:T(8,128)(2,1)}, bf16[768,384]{1,0:T(8,128)(2,1)}, u32[]{:S(2)}, u32[]{:S(2)}) collective-permute-start(bf16[768,384]{1,0:T(8,128)(2,1)} %get-tuple-element.178), channel_id=1, source_target_pairs={{0,2},{1,3},{2,0},{3,1},{4,6},{5,7},{6,4},{7,5},{8,10},{9,11},{10,... | collective-permute-start | bytes 1769480 | tf_op jit(solution)/shard_map/ppermute | solution.py:972
  87.0 21.4 %collective-permute-start.23 = (bf16[2,384,384]{2,1,0:T(8,128)(2,1)}, bf16[2,384,384]{2,1,0:T(8,128)(2,1)}, u32[]{:S(2)}, u32[]{:S(2)}) collective-permute-start(bf16[2,384,384]{2,1,0:T(8,128)(2,1)} %get-tuple-element.179), channel_id=1, source_target_pairs={{0,4},{4,0},{8,12},{12,8},{16,20},{20,16},{24,28},{28,24},{1,5},{5... | collective-permute-start | bytes 1769480 | tf_op jit(solution)/shard_map/ppermute | solution.py:972
  110.7 10.4 %collective-permute-start.24 = (bf16[384,384]{1,0:T(8,128)(2,1)}, bf16[384,384]{1,0:T(8,128)(2,1)}, u32[]{:S(2)}, u32[]{:S(2)}) collective-permute-start(bf16[384,384]{1,0:T(8,128)(2,1)} %get-tuple-element.192), channel_id=1, source_target_pairs={{0,4},{4,0},{8,12},{12,8},{16,20},{20,16},{24,28},{28,24},{1,5},{5... | collective-permute-start | bytes 884744 | tf_op jit(solution)/shard_map/ppermute | solution.py:972
  111.9 9.1 %collective-permute-start.25 = (bf16[384,384]{1,0:T(8,128)(2,1)}, bf16[384,384]{1,0:T(8,128)(2,1)}, u32[]{:S(2)}, u32[]{:S(2)}) collective-permute-start(bf16[384,384]{1,0:T(8,128)(2,1)} %get-tuple-element.193), channel_id=1, source_target_pairs={{0,2},{1,3},{2,0},{3,1},{4,6},{5,7},{6,4},{7,5},{8,10},{9,11},{10,... | collective-permute-start | bytes 884744 | tf_op jit(solution)/shard_map/ppermute | solution.py:972
  121.0 5.6 %collective-permute-start.26 = (bf16[2,192,3968]{2,1,0:T(8,128)(2,1)S(1)}, bf16[2,192,3968]{2,1,0:T(8,128)(2,1)S(1)}, u32[]{:S(2)}, u32[]{:S(2)}) collective-permute-start(bf16[2,192,3968]{2,1,0:T(8,128)(2,1)S(1)} %get-tuple-element.200), channel_id=1, source_target_pairs={{0,1},{1,0},{2,3},{3,2},{4,5},{5,4},{6,7},{7,6},{8,9},{9,8},{10,11... | collective-permute-start | bytes 9142280 | tf_op jit(solution)/shard_map/ppermute | solution.py:972
  129.2 11.8 %collective-permute-start.28 = (bf16[192,768]{1,0:T(8,128)(2,1)}, bf16[192,768]{1,0:T(8,128)(2,1)}, u32[]{:S(2)}, u32[]{:S(2)}) collective-permute-start(bf16[192,768]{1,0:T(8,128)(2,1)} %get-tuple-element.209), channel_id=1, source_target_pairs={{0,8},{4,12},{8,0},{12,4},{16,24},{20,28},{24,16},{28,20},{1,9},{5... | collective-permute-start | bytes 884744 | tf_op jit(solution)/shard_map/ppermute | solution.py:972
  130.8 23.6 %collective-permute-start.29 = (bf16[2,96,1920]{2,1,0:T(8,128)(2,1)}, bf16[2,96,1920]{2,1,0:T(8,128)(2,1)}, u32[]{:S(2)}, u32[]{:S(2)}) collective-permute-start(bf16[2,96,1920]{2,1,0:T(8,128)(2,1)} %get-tuple-element.210), channel_id=1, source_target_pairs={{0,4},{4,0},{8,12},{12,8},{16,20},{20,16},{24,28},{28,24},{1,5},{5... | collective-permute-start | bytes 2211848 | tf_op jit(solution)/shard_map/ppermute | solution.py:972
  131.6 22.9 %collective-permute-start.27 = (bf16[192,2048]{1,0:T(8,128)(2,1)}, bf16[192,2048]{1,0:T(8,128)(2,1)}, u32[]{:S(2)}, u32[]{:S(2)}) collective-permute-start(bf16[192,2048]{1,0:T(8,128)(2,1)} %get-tuple-element.208), channel_id=1, source_target_pairs={{0,2},{1,3},{2,0},{3,1},{4,6},{5,7},{6,4},{7,5},{8,10},{9,11},{10,... | collective-permute-start | bytes 2359304 | tf_op jit(solution)/shard_map/ppermute | solution.py:972
  142.8 33.0 %collective-permute-start.33 = (bf16[192,768]{1,0:T(8,128)(2,1)}, bf16[192,768]{1,0:T(8,128)(2,1)}, u32[]{:S(2)}, u32[]{:S(2)}) collective-permute-start(bf16[192,768]{1,0:T(8,128)(2,1)} %gradient_sums.16.refs_0_), channel_id=1, source_target_pairs={{0,16},{4,20},{8,24},{12,28},{16,0},{20,4},{24,8},{28,12},{1,17},{... | collective-permute-start | bytes 884744 | tf_op jit(solution)/shard_map/ppermute | solution.py:972
  156.8 11.5 %collective-permute-start.31 = (bf16[96,1920]{1,0:T(8,128)(2,1)}, bf16[96,1920]{1,0:T(8,128)(2,1)}, u32[]{:S(2)}, u32[]{:S(2)}) collective-permute-start(bf16[96,1920]{1,0:T(8,128)(2,1)} %get-tuple-element.222), channel_id=1, source_target_pairs={{0,2},{1,3},{2,0},{3,1},{4,6},{5,7},{6,4},{7,5},{8,10},{9,11},{10,... | collective-permute-start | bytes 1105928 | tf_op jit(solution)/shard_map/ppermute | solution.py:972
  158.1 10.2 %collective-permute-start.30 = (bf16[96,2048]{1,0:T(8,128)(2,1)}, bf16[96,2048]{1,0:T(8,128)(2,1)}, u32[]{:S(2)}, u32[]{:S(2)}) collective-permute-start(bf16[96,2048]{1,0:T(8,128)(2,1)} %get-tuple-element.221), channel_id=1, source_target_pairs={{0,4},{4,0},{8,12},{12,8},{16,20},{20,16},{24,28},{28,24},{1,5},{5... | collective-permute-start | bytes 1179656 | tf_op jit(solution)/shard_map/ppermute | solution.py:972
  170.8 9.5 %collective-permute-start.32 = (bf16[48,3968]{1,0:T(8,128)(2,1)}, bf16[48,3968]{1,0:T(8,128)(2,1)}, u32[]{:S(2)}, u32[]{:S(2)}) collective-permute-start(bf16[48,3968]{1,0:T(8,128)(2,1)} %get-tuple-element.228), channel_id=1, source_target_pairs={{0,8},{4,12},{8,0},{12,4},{16,24},{20,28},{24,16},{28,20},{1,9},{5... | collective-permute-start | bytes 1142792 | tf_op jit(solution)/shard_map/ppermute | solution.py:972
  175.7 4.7 %collective-permute-start.34 = (bf16[2,192,2304]{2,1,0:T(8,128)(2,1)S(1)}, bf16[2,192,2304]{2,1,0:T(8,128)(2,1)S(1)}, u32[]{:S(2)}, u32[]{:S(2)}) collective-permute-start(bf16[2,192,2304]{2,1,0:T(8,128)(2,1)S(1)} %get-tuple-element.239), channel_id=1, source_target_pairs={{0,1},{1,0},{2,3},{3,2},{4,5},{5,4},{6,7},{7,6},{8,9},{9,8},{10,11... | collective-permute-start | bytes 5308424 | tf_op jit(solution)/shard_map/ppermute | solution.py:972
  177.6 16.1 %collective-permute-start.35 = (bf16[192,768]{1,0:T(8,128)(2,1)}, bf16[192,768]{1,0:T(8,128)(2,1)}, u32[]{:S(2)}, u32[]{:S(2)}) collective-permute-start(bf16[192,768]{1,0:T(8,128)(2,1)} %gradient_sums.19.refs_0_), channel_id=1, source_target_pairs={{0,8},{4,12},{8,0},{12,4},{16,24},{20,28},{24,16},{28,20},{1,9},{5... | collective-permute-start | bytes 884744 | tf_op jit(solution)/shard_map/ppermute | solution.py:972
  182.6 26.1 %collective-permute-start.38 = (bf16[48,3968]{1,0:T(8,128)(2,1)}, bf16[48,3968]{1,0:T(8,128)(2,1)}, u32[]{:S(2)}, u32[]{:S(2)}) collective-permute-start(bf16[48,3968]{1,0:T(8,128)(2,1)} %get-tuple-element.244.refs_0_), channel_id=1, source_target_pairs={{0,16},{4,20},{8,24},{12,28},{16,0},{20,4},{24,8},{28,12},{1,17},{... | collective-permute-start | bytes 1142792 | tf_op jit(solution)/shard_map/ppermute | solution.py:972
  182.9 11.3 %collective-permute-start.36 = (bf16[192,1152]{1,0:T(8,128)(2,1)}, bf16[192,1152]{1,0:T(8,128)(2,1)}, u32[]{:S(2)}, u32[]{:S(2)}) collective-permute-start(bf16[192,1152]{1,0:T(8,128)(2,1)} %get-tuple-element.245), channel_id=1, source_target_pairs={{0,2},{1,3},{2,0},{3,1},{4,6},{5,7},{6,4},{7,5},{8,10},{9,11},{10,... | collective-permute-start | bytes 1327112 | tf_op jit(solution)/shard_map/ppermute | solution.py:972
  183.5 11.1 %collective-permute-start.37 = (bf16[2,96,1152]{2,1,0:T(8,128)(2,1)}, bf16[2,96,1152]{2,1,0:T(8,128)(2,1)}, u32[]{:S(2)}, u32[]{:S(2)}) collective-permute-start(bf16[2,96,1152]{2,1,0:T(8,128)(2,1)} %get-tuple-element.246), channel_id=1, source_target_pairs={{0,4},{4,0},{8,12},{12,8},{16,20},{20,16},{24,28},{28,24},{1,5},{5... | collective-permute-start | bytes 1327112 | tf_op jit(solution)/shard_map/ppermute | solution.py:972
  196.8 11.8 %collective-permute-start.39 = (bf16[96,1152]{1,0:T(8,128)(2,1)}, bf16[96,1152]{1,0:T(8,128)(2,1)}, u32[]{:S(2)}, u32[]{:S(2)}) collective-permute-start(bf16[96,1152]{1,0:T(8,128)(2,1)} %get-tuple-element.255), channel_id=1, source_target_pairs={{0,4},{4,0},{8,12},{12,8},{16,20},{20,16},{24,28},{28,24},{1,5},{5... | collective-permute-start | bytes 663560 | tf_op jit(solution)/shard_map/ppermute | solution.py:972
  198.0 10.7 %collective-permute-start.40 = (bf16[96,1152]{1,0:T(8,128)(2,1)}, bf16[96,1152]{1,0:T(8,128)(2,1)}, u32[]{:S(2)}, u32[]{:S(2)}) collective-permute-start(bf16[96,1152]{1,0:T(8,128)(2,1)} %get-tuple-element.256), channel_id=1, source_target_pairs={{0,2},{1,3},{2,0},{3,1},{4,6},{5,7},{6,4},{7,5},{8,10},{9,11},{10,... | collective-permute-start | bytes 663560 | tf_op jit(solution)/shard_map/ppermute | solution.py:972
  210.1 13.5 %collective-permute-start.41 = (bf16[48,3968]{1,0:T(8,128)(2,1)S(1)}, bf16[48,3968]{1,0:T(8,128)(2,1)S(1)}, u32[]{:S(2)}, u32[]{:S(2)}) collective-permute-start(bf16[48,3968]{1,0:T(8,128)(2,1)S(1)} %get-tuple-element.265.refs_0_), channel_id=1, source_target_pairs={{0,8},{4,12},{8,0},{12,4},{16,24},{20,28},{24,16},{28,20},{1,9},{5... | collective-permute-start | bytes 1142792 | tf_op jit(solution)/shard_map/ppermute | solution.py:972
  211.8 11.9 %collective-permute-start.42 = (bf16[48,2304]{1,0:T(8,128)(2,1)S(1)}, bf16[48,2304]{1,0:T(8,128)(2,1)S(1)}, u32[]{:S(2)}, u32[]{:S(2)}) collective-permute-start(bf16[48,2304]{1,0:T(8,128)(2,1)S(1)} %get-tuple-element.266), channel_id=1, source_target_pairs={{0,8},{4,12},{8,0},{12,4},{16,24},{20,28},{24,16},{28,20},{1,9},{5... | collective-permute-start | bytes 663560 | tf_op jit(solution)/shard_map/ppermute | solution.py:972
  212.2 15.0 %collective-permute-start.44 = (bf16[384,768]{1,0:T(8,128)(2,1)S(1)}, bf16[384,768]{1,0:T(8,128)(2,1)S(1)}, u32[]{:S(2)}, u32[]{:S(2)}) collective-permute-start(bf16[384,768]{1,0:T(8,128)(2,1)S(1)} %get-tuple-element.254.refs_0_), channel_id=1, source_target_pairs={{0,4},{4,0},{8,12},{12,8},{16,20},{20,16},{24,28},{28,24},{1,5},{5... | collective-permute-start | bytes 1769480 | tf_op jit(solution)/shard_map/ppermute | solution.py:972
  223.7 19.1 %collective-permute-start.47 = (bf16[96,3968]{1,0:T(8,128)(2,1)S(1)}, bf16[96,3968]{1,0:T(8,128)(2,1)S(1)}, u32[]{:S(2)}, u32[]{:S(2)}) collective-permute-start(bf16[96,3968]{1,0:T(8,128)(2,1)S(1)} %get-tuple-element.271.refs_2_), channel_id=1, source_target_pairs={{0,4},{4,0},{8,12},{12,8},{16,20},{20,16},{24,28},{28,24},{1,5},{5... | collective-permute-start | bytes 2285576 | tf_op jit(solution)/shard_map/ppermute | solution.py:972
  224.7 9.7 %collective-permute-start.43 = (bf16[48,2304]{1,0:T(8,128)(2,1)S(1)}, bf16[48,2304]{1,0:T(8,128)(2,1)S(1)}, u32[]{:S(2)}, u32[]{:S(2)}) collective-permute-start(bf16[48,2304]{1,0:T(8,128)(2,1)S(1)} %get-tuple-element.270.refs_0_), channel_id=1, source_target_pairs={{0,16},{4,20},{8,24},{12,28},{16,0},{20,4},{24,8},{28,12},{1,17},{... | collective-permute-start | bytes 663560 | tf_op jit(solution)/shard_map/ppermute | solution.py:972
  234.5 6.0 %collective-permute-start.45 = (bf16[48,2304]{1,0:T(8,128)(2,1)S(1)}, bf16[48,2304]{1,0:T(8,128)(2,1)S(1)}, u32[]{:S(2)}, u32[]{:S(2)}) collective-permute-start(bf16[48,2304]{1,0:T(8,128)(2,1)S(1)} %gradient_sums.24.refs_0_), channel_id=1, source_target_pairs={{0,8},{4,12},{8,0},{12,4},{16,24},{20,28},{24,16},{28,20},{1,9},{5... | collective-permute-start | bytes 663560 | tf_op jit(solution)/shard_map/ppermute | solution.py:972
  240.5 10.2 %collective-permute-start.46 = (bf16[96,2304]{1,0:T(8,128)(2,1)S(1)}, bf16[96,2304]{1,0:T(8,128)(2,1)S(1)}, u32[]{:S(2)}, u32[]{:S(2)}) collective-permute-start(bf16[96,2304]{1,0:T(8,128)(2,1)S(1)} %gradient_sums.25.refs_2_), channel_id=1, source_target_pairs={{0,4},{4,0},{8,12},{12,8},{16,20},{20,16},{24,28},{28,24},{1,5},{5... | collective-permute-start | bytes 1327112 | tf_op jit(solution)/shard_map/ppermute | solution.py:972
  (13 other events, 103.7 us)

commit v4 on v3

--- a/solution.py
+++ b/solution.py
@@ -549,7 +549,7 @@
 
 def down_body(down_at, idx_ref, dy_ref, x1_ref, g_ref, vec_ref, w_up, w_out, *refs):
     downs, refs = take(refs, down_at)
-    du_ref, dx1_ref, dx1r_ref, do_ref, bias_ref, w_down, down_sems = refs
+    du_ref, dx1_ref, do_ref, bias_ref, w_down, down_sems = refs
     weight = (down_at, downs, w_down, down_sems)
     fetch(idx_ref, weight)
 
@@ -575,7 +575,7 @@
     d_x1 = d_y + norm_back(d_a2, scaled, inverse, vec_ref[1:2, :width])
     dx1_ref[...] = d_x1
     d_x1 = d_x1.astype(bf16)
-    dx1r_ref[here, :] = d_x1
+    du_ref[here, w_up.shape[1] :] = d_x1
     do_ref[...] = nt(d_x1, w_out[...]).astype(bf16)
 
 
@@ -592,11 +592,11 @@
         "feed_back",
         (rows // step,),
         [row(width), row(width)] + [fixed(array.shape) for array in (g, vec, w_up, w_out)] + w_down.specs(),
-        [fixed((rows, ff)), row(width), fixed((rows, width)), row(width), fixed((2, ff)),
+        [fixed((rows, ff + width)), row(width), row(width), fixed((2, ff)),
          fixed((ff, width))],
         [
-            vmem((rows, ff), bf16), hbm((rows, width), f32), vmem((rows, width), bf16),
-            hbm((rows, width), bf16), vmem((2, ff), f32), w_down.whole(),
+            vmem((rows, ff + width), bf16), hbm((rows, width), f32), hbm((rows, width), bf16),
+            vmem((2, ff), f32), w_down.whole(),
         ],
         w_down.sems(),
         14,
@@ -634,25 +634,24 @@
     return [pl.ds(pl.multiple_of((idx_ref[0] ^ j) * rows, math.gcd(rows, 256)), rows) for j in ORDER]
 
 
-def grad_up_body(chunks, idx_ref, a_ref, o_ref, du_ref, dx_ref, bias_ref, send_ref, keep_ref):
+def grad_up_body(chunks, idx_ref, a_ref, o_ref, du_ref, bias_ref, send_ref, keep_ref, left_ref):
     rows = send_ref.shape[1]
-    width = dx_ref.shape[1]
+    width = a_ref.shape[0]
     i = pl.program_id(0)
     columns = pl.ds(pl.multiple_of(i * width, width), width)
-    shards_at = shard_rows(idx_ref, rows)
-
-    def write(left, right):
-        y = nn(jnp.concatenate([left[at, :] for at in shards_at], axis=0), right).astype(bf16)
-        for k in range(4):
-            (send_ref if k < 2 else keep_ref)[k % 2, :, columns] = y[k * rows : (k + 1) * rows]
-
-    @pl.when(i < chunks)
-    def _():
-        write(a_ref, du_ref[:, columns])
+    for step, ref in ((0, a_ref), (chunks, o_ref)):
+
+        @pl.when(i == step)
+        def _(ref=ref):
+            for k, at in enumerate(shard_rows(idx_ref, rows)):
+                left_ref[k * rows : (k + 1) * rows, :] = ref[at, :]
+
+    y = nn(left_ref[...], du_ref[:, columns]).astype(bf16)
+    for k in range(4):
+        (send_ref if k < 2 else keep_ref)[k % 2, :, columns] = y[k * rows : (k + 1) * rows]
 
     @pl.when(i == chunks)
     def _():
-        write(o_ref, dx_ref[...])
         at = (chunks + 1) * width
         lanes = send_ref.shape[2] - at
         shards = width // rows
@@ -674,24 +673,24 @@
             out_ref[k % 2, 16:, at:] = jnp.zeros((rows - 16, lanes), bf16)
 
 
-def grad_up_call(index, a2t, ot, d_u, dx1r, biases, shards):
+def grad_up_call(index, a2t, ot, d_u, biases, shards):
     width, rows = a2t.shape
     own = width // shards
-    ff = d_u.shape[1]
+    ff = d_u.shape[1] - width
     chunks = ff // width
     cols = ff + width + TILE
     return call(
         functools.partial(grad_up_body, chunks),
         "grad_up_out",
         (chunks + 1,),
-        [fixed(array.shape) for array in (a2t, ot, d_u, dx1r, biases)],
+        [fixed(array.shape) for array in (a2t, ot, d_u, biases)],
         [fixed((2, own, cols))] * 2,
         [vmem((2, own, cols), bf16)] * 2,
-        [],
+        [pltpu.VMEM((width, rows), bf16)],
         10,
         4.7,
-        near=range(5),
-    )(index, a2t, ot, d_u, dx1r, biases)
+        near=range(4),
+    )(index, a2t, ot, d_u, biases)
 
 
 def grad_qkv_body(idx_ref, a_ref, *refs):
@@ -1147,10 +1146,10 @@
     down_w = Weight([(a, w_down.shape[0], p) for a, p in zip((w_down, down_near, down_far, down_last), at_down)])
     chain_a = moves.reduce(send, keep, width // 2)
     begin(chain_a)
-    d_u, dx1, dx1r, d_o, biases, down_full = down_call(
+    d_u, dx1, d_o, biases, down_full = down_call(
         ready(keep, *advance([chain_a], keep)), d_y, x1, g, vec, up_full, out_full, down_w
     )
-    send, keep = grad_up_call(ready(*advance([chain_a], dx1r)), a2t, ot, d_u, dx1r, biases, narrow)
+    send, keep = grad_up_call(ready(*advance([chain_a], biases)), a2t, ot, d_u, biases, narrow)
     chain_b = moves.reduce(send, keep, 2048)
     begin(chain_b)
 
@@ -1160,12 +1159,12 @@
         )
 
     paced = pace_call(ready(send), same)
-    g0 = back(0, 2, keep, *advance([chain_a, chain_b], keep, paced))
-    g1 = back(2, 2, g0[0], *advance([chain_a], g0[0]))
-    g2 = back(4, 2, g1[0], *advance([chain_b], g1[0]))
-    groups = [g0, g1, g2]
+    sent = advance([chain_a], keep, pace_call(ready(keep), same))
+    g0 = back(0, 4, keep, *sent, *advance([chain_b], keep, paced, *sent))
+    g1 = back(4, pairs - 4, g0[0], *advance([chain_a, chain_b], g0[0]))
+    groups = [g0, g1]
     rights = [array for group in groups for array in group]
-    send, keep = grad_qkv_call(ready(*advance([chain_b], g2[0])), a1t, rights, narrow)
+    send, keep = grad_qkv_call(ready(*advance([chain_b], g1[0])), a1t, rights, narrow)
     chain_c = moves.reduce(send, keep, 1152)
     begin(chain_c)
     paced = pace_call(ready(send), same)

time: 257 us -> 250 us (0.973); the launches traced: 254 us -> 249 us
  Pallas kernels: 163 us -> 159 us
    pallas_call x15 -> x14, Pallas kernels: 133 us -> 130 us  [run(): return fun(index, *args)]
  transfers between devices with their start and end apart: 48 -> 48, of which waited for: 12 -> 14; matrix products, arithmetic and copies ran while one was open for 3% -> 3% of each run, Pallas kernels for 61% -> 60%
where the time goes in v4:
time: 250 us; the launch traced here: 249 us
  Pallas kernels  159 us (64%)
  starting transfers between devices  40.8 us (16%)
  waiting for transfers between devices  38 us (15%)
  local copies, waits for them, and re-layouts  7.07 us (3%)
  other arithmetic  2.9 us (1%)
    pallas_call x14, Pallas kernels, run(): return fun(index, *args)  130 us
    ppermute x48, starting transfers between devices, swap(): return lax.ppermute(value, axis, [(i, i ^ bit) for i in range(size)])  40.8 us
    ppermute x48, waiting for transfers between devices, swap(): return lax.ppermute(value, axis, [(i, i ^ bit) for i in range(size)])  38 us
    pallas_call x16, Pallas kernels, whole_call(): pl.pallas_call(run, name=name, in_specs=[pl.BlockSpec(memory_space=pltpu....  28.7 us
  transfers between devices with their start and end apart: 48, of which 14 were waited for; matrix products, arithmetic and copies ran while one was open for 3% of the time, Pallas kernels for 60%

profile of v4, /device:TPU:0, one launch (start us, length us, event | category | flops | bytes accessed | tf_op | source)
XLA Modules:
  0.0 249.4 jit_solution(2569767055285302675)
XLA Ops:
  0.7 1.7 constant_dynamic-slice_fusion
  2.4 3.0 %collective-permute-start.1 = (bf16[64,2304]{1,0:T(8,128)(2,1)}, bf16[64,2304]{1,0:T(8,128)(2,1)}, u32[]{:S(2)}, u32[]{:S(2)}) collective-permute-start(bf16[64,2304]{1,0:T(8,128)(2,1)} %constant_dynamic-slice_fusion), channel_id=1, source_target_pairs={{0,2},{1,3},{2,0},{3,1},{4,6},{5,7},{6,4},{7,5},{8,10},{9,11},{10,... | collective-permute-start | bytes 884744 | tf_op jit(solution)/shard_map/ppermute | solution.py:971
  5.4 2.3 vector_message.1
  8.7 2.6 %next_message.1 = (bf16[64,3072]{1,0:T(8,128)(2,1)}, bf16[64,3072]{1,0:T(8,128)(2,1)}) custom-call(s32[27]{0:T(128)S(1)} %stack.81.idx_ref, bf16[192,3072]{1,0:T(8,128)(2,1)} %refs_0_.9, bf16[192,3072]{1,0:T(8,128)(2,1)} %refs_0_.9), custom_call_target="tpu_custom_call" | custom-call | flops 1500000026624 | bytes 1048576 | tf_op jit(solution)/shard_map/next_message/pallas_call | solution.py:144
  12.0 2.0 collective-permute-start
  14.4 1.7 collective-permute-start.8
  19.0 3.6 %collective-permute-done.6.refs_2_.refs_7_ = bf16[72,2304]{1,0:T(8,128)(2,1)S(1)} collective-permute-done((bf16[72,2304]{1,0:T(8,128)(2,1)S(1)}, bf16[72,2304]{1,0:T(8,128)(2,1)S(1)}, u32[]{:S(2)}, u32[]{:S(2)}) %collective-permute-start.6) | collective-permute-done | bytes 331808 | tf_op jit(solution)/shard_map/ppermute | solution.py:971
  25.3 11.3 %norm_qkv.1 = (bf16[1024,2304]{1,0:T(8,128)(2,1)S(1)}, bf16[768,1024]{1,0:T(8,128)(2,1)}, f32[8,3072]{1,0:T(8,128)}, bf16[768,2304]{1,0:T(8,128)(2,1)}) custom-call(s32[27]{0:T(128)S(1)} %stack.81.idx_ref, bf16[1024,768]{1,0:T(8,128)(2,1)} %bitcast.34, f32[512,128]{1,0:T(8,128)} %copy.31.cos_ref, f32[512,128]{1,0:T(8,128)} %pad_maximum_fusion.sin_ref, ...), custom_call_target="tpu_custom_call" | custom-call | flops 6999999774720 | bytes 1048576 | tf_op jit(solution)/shard_map/norm_qkv/pallas_call | solution.py:144
  36.6 1.6 collective-permute-start.14
  38.2 11.3 %attention.1 = (bf16[1024,768]{1,0:T(8,128)(2,1)}, bf16[768,1024]{1,0:T(8,128)(2,1)}, f32[6,2,1024]{2,1,0:T(2,128)}) custom-call(s32[27]{0:T(128)S(1)} %stack.81.idx_ref, bf16[1024,2304]{1,0:T(8,128)(2,1)S(1)} %get-tuple-element.157.qkv_ref.q_ref.k_ref.v_ref, f32[128,128]{1,0:T(8,128)} %get-tuple-element.278.same_ref, ...), custom_call_target="tpu_custom_call" | custom-call | flops 12000000212992 | bytes 1048576 | tf_op jit(solution)/shard_map/attention/pallas_call | solution.py:144
  50.6 1.7 copy.32.dyt_ref
  52.3 1.6 collective-permute-start.21
  53.9 19.3 %feed_up.1 = (f32[1024,768]{1,0:T(8,128)}, bf16[768,1024]{1,0:T(8,128)(2,1)S(1)}, bf16[1024,3072]{1,0:T(8,128)(2,1)S(1)}, bf16[1024,3072]{1,0:T(8,128)(2,1)S(1)}...) custom-call(s32[27]{0:T(128)S(1)} %stack.81.idx_ref, bf16[1024,768]{1,0:T(8,128)(2,1)} %bitcast.35, ...), custom_call_target="tpu_custom_call" | custom-call | flops 18000000319488 | bytes 1048576 | tf_op jit(solution)/shard_map/feed_up/pallas_call | solution.py:144
  73.2 4.8 %grad_down.2 = bf16[2,768,768]{2,1,0:T(8,128)(2,1)} custom-call(s32[27]{0:T(128)S(1)} %stack.81.idx_ref, bf16[768,1024]{1,0:T(8,128)(2,1)S(1)} %copy.32.dyt_ref, bf16[1024,3072]{1,0:T(8,128)(2,1)S(1)} %get-tuple-element.169.h_ref), custom_call_target="tpu_custom_call" | custom-call | flops 3000000053248 | bytes 1048576 | tf_op jit(solution)/shard_map/grad_down/pallas_call | solution.py:144
  78.0 3.4 %grad_down.3.refs_0_ = bf16[2,768,768]{2,1,0:T(8,128)(2,1)S(1)} custom-call(s32[27]{0:T(128)S(1)} %stack.81.idx_ref, bf16[768,1024]{1,0:T(8,128)(2,1)S(1)} %copy.32.dyt_ref, bf16[1024,3072]{1,0:T(8,128)(2,1)S(1)} %get-tuple-element.169.h_ref), custom_call_target="tpu_custom_call" | custom-call | flops 3000000053248 | bytes 1048576 | tf_op jit(solution)/shard_map/grad_down/pallas_call | solution.py:144
  82.9 2.9 %gradient_sums.13 = (bf16[768,384]{1,0:T(8,128)(2,1)}, bf16[2,384,384]{2,1,0:T(8,128)(2,1)}, f32[768,384]{1,0:T(8,128)S(1)}, f32[2,384,384]{2,1,0:T(8,128)S(1)}) custom-call(bf16[2,768,768]{2,1,0:T(8,128)(2,1)S(1)} %grad_down.3.refs_0_, bf16[2,768,768]{2,1,0:T(8,128)(2,1)} %collective-permute-done.18.refs_1_), custom_call_target="tpu_custom_call" | custom-call | bytes 4718592 | tf_op jit(solution)/shard_map/gradient_sums/pallas_call | solution.py:820
  87.2 20.4 %feed_back.1 = (bf16[1024,3840]{1,0:T(8,128)(2,1)S(1)}, f32[1024,768]{1,0:T(8,128)}, bf16[1024,768]{1,0:T(8,128)(2,1)}, f32[2,3072]{1,0:T(2,128)S(1)}, bf16[3072,768]{1,0:T(8,128)(2,1)S(1)}) custom-call(s32[27]{0:T(128)S(1)} %stack.81.idx_ref, bf16[1024,768]{1,0:T(8,128)(2,1)} %bitcast.32, f32[1024,768]{1,0:T(8,128)} %get-tuple-element.177.x1_ref, ...), custom_call_target="tpu_custom_call" | custom-call | flops 19999999655936 | bytes 1048576 | tf_op jit(solution)/shard_map/feed_back/pallas_call | solution.py:144
  107.7 2.2 gradient_sums.14
  112.6 7.9 %grad_up_out.1 = (bf16[2,192,3968]{2,1,0:T(8,128)(2,1)S(1)}, bf16[2,192,3968]{2,1,0:T(8,128)(2,1)S(1)}) custom-call(s32[27]{0:T(128)S(1)} %stack.81.idx_ref, bf16[768,1024]{1,0:T(8,128)(2,1)S(1)} %get-tuple-element.191.a_ref, bf16[768,1024]{1,0:T(8,128)(2,1)S(1)} %copy-done.7, bf16[1024,3840]{1,0:T(8,128)(2,1)S(1)} %get-tuple-element.193.du_ref, ...), custom_call_target="tpu_custom_call" | custom-call | flops 4700000223232 | bytes 1048576 | tf_op jit(solution)/shard_map/grad_up_out/pallas_call | solution.py:144
  120.5 1.8 gradient_sums.15
  122.4 1.6 collective-permute-start.26
  124.0 2.1 collective-permute-done.27.refs_1_
  126.0 1.4 gradient_sums.16
  128.9 15.3 %attention_back.2 = (bf16[1024,512]{1,0:T(8,128)(2,1)S(1)}, bf16[1024,512]{1,0:T(8,128)(2,1)S(1)}, bf16[1024,512]{1,0:T(8,128)(2,1)S(1)}) custom-call(s32[27]{0:T(128)S(1)} %stack.81.idx_ref, bf16[1024,2304]{1,0:T(8,128)(2,1)} %copy-done.4, bf16[1024,2304]{1,0:T(8,128)(2,1)} %copy-done.4, bf16[1024,2304]{1,0:T(8,128)(2,1)} %copy-done.4, ...), custom_call_target="tpu_custom_call" | custom-call | flops 14399999836160 | bytes 1048576 | tf_op jit(solution)/shard_map/attention_back/pallas_call | solution.py:144
  144.2 2.1 collective-permute-done.29.refs_5_
  146.3 1.5 collective-permute-done.28.refs_4_
  147.8 2.5 %gradient_sums.17 = (bf16[192,768]{1,0:T(8,128)(2,1)}, bf16[96,2048]{1,0:T(8,128)(2,1)}, bf16[96,1920]{1,0:T(8,128)(2,1)}, f32[96,2048]{1,0:T(8,128)S(1)}, f32[96,1920]{1,0:T(8,128)S(1)}) custom-call(f32[192,768]{1,0:T(8,128)S(1)} %get-tuple-element.199.refs_0_, bf16[192,768]{1,0:T(8,128)(2,1)} %collective-permute-done.26.refs_1_, ...), custom_call_target="tpu_custom_call" | custom-call | bytes 5455872 | tf_op jit(solution)/shard_map/gradient_sums/pallas_call | solution.py:820
  150.4 2.6 %collective-permute-start.33 = (bf16[192,768]{1,0:T(8,128)(2,1)}, bf16[192,768]{1,0:T(8,128)(2,1)}, u32[]{:S(2)}, u32[]{:S(2)}) collective-permute-start(bf16[192,768]{1,0:T(8,128)(2,1)} %get-tuple-element.215.refs_0_), channel_id=1, source_target_pairs={{0,16},{4,20},{8,24},{12,28},{16,0},{20,4},{24,8},{28,12},{1,17},{... | collective-permute-start | bytes 884744 | tf_op jit(solution)/shard_map/ppermute | solution.py:971
  154.9 9.1 %attention_back.3 = (bf16[1024,256]{1,0:T(8,128)(2,1)S(1)}, bf16[1024,256]{1,0:T(8,128)(2,1)S(1)}, bf16[1024,256]{1,0:T(8,128)(2,1)S(1)}) custom-call(s32[27]{0:T(128)S(1)} %stack.81.idx_ref, bf16[1024,2304]{1,0:T(8,128)(2,1)} %copy-done.4, bf16[1024,2304]{1,0:T(8,128)(2,1)} %copy-done.4, bf16[1024,2304]{1,0:T(8,128)(2,1)} %copy-done.4, ...), custom_call_target="tpu_custom_call" | custom-call | flops 7199999918080 | bytes 1048576 | tf_op jit(solution)/shard_map/attention_back/pallas_call | solution.py:144
  164.0 2.2 gradient_sums.18
  166.2 1.6 collective-permute-start.32
  167.8 4.4 %grad_qkv.1 = (bf16[2,192,2304]{2,1,0:T(8,128)(2,1)S(1)}, bf16[2,192,2304]{2,1,0:T(8,128)(2,1)S(1)}) custom-call(s32[27]{0:T(128)S(1)} %stack.81.idx_ref, bf16[768,1024]{1,0:T(8,128)(2,1)S(1)} %copy-done.3, bf16[1024,512]{1,0:T(8,128)(2,1)S(1)} %get-tuple-element.207.refs_0_, bf16[1024,512]{1,0:T(8,128)(2,1)S(1)} %get-tuple-element.225.refs_1_, ...), custom_call_target="tpu_custom_call" | custom-call | flops 3304000061440 | bytes 1048576 | tf_op jit(solution)/shard_map/grad_qkv/pallas_call | solution.py:144
  172.2 1.8 gradient_sums.19.refs_0_
  175.9 2.2 gradient_sums.20
  178.4 1.4 collective-permute-start.36
  180.5 9.0 %layer_output.1 = bf16[1024,768]{1,0:T(8,128)(2,1)} custom-call(s32[27]{0:T(128)S(1)} %stack.81.idx_ref, f32[1024,768]{1,0:T(8,128)} %get-tuple-element.177.x1_ref, bf16[1024,3072]{1,0:T(8,128)(2,1)} %copy-done.2, f32[8,3072]{1,0:T(8,128)} %get-tuple-element.154.vec_ref, bf16[3072,768]{1,0:T(8,128)(2,1)S(1)} %get-tuple-element.240.w_ref), custom_call_target="tpu_custom_call" | custom-call | flops 7999999967232 | bytes 1048576 | tf_op jit(solution)/shard_map/layer_output/pallas_call | solution.py:144
  191.8 2.2 gradient_sums.21
  195.4 9.2 %grad_input.1 = bf16[1024,768]{1,0:T(8,128)(2,1)} custom-call(s32[27]{0:T(128)S(1)} %stack.81.idx_ref, bf16[1024,768]{1,0:T(8,128)(2,1)} %bitcast.36, f32[1024,768]{1,0:T(8,128)} %get-tuple-element.250.dx1_ref, f32[8,3072]{1,0:T(8,128)} %get-tuple-element.154.vec_ref, bf16[768,2304]{1,0:T(8,128)(2,1)} %get-tuple-element.251.w_ref, ...), custom_call_target="tpu_custom_call" | custom-call | flops 9000000159744 | bytes 1048576 | tf_op jit(solution)/shard_map/grad_input/pallas_call | solution.py:144
  204.7 1.4 gradient_sums.22
  206.7 1.4 collective-permute-start.42
  209.4 10.3 %collective-permute-done.42.refs_3_ = bf16[48,2304]{1,0:T(8,128)(2,1)S(1)} collective-permute-done((bf16[48,2304]{1,0:T(8,128)(2,1)S(1)}, bf16[48,2304]{1,0:T(8,128)(2,1)S(1)}, u32[]{:S(2)}, u32[]{:S(2)}) %collective-permute-start.42) | collective-permute-done | bytes 221216 | tf_op jit(solution)/shard_map/ppermute | solution.py:971
  221.2 3.7 %collective-permute-start.43 = (bf16[48,2304]{1,0:T(8,128)(2,1)S(1)}, bf16[48,2304]{1,0:T(8,128)(2,1)S(1)}, u32[]{:S(2)}, u32[]{:S(2)}) collective-permute-start(bf16[48,2304]{1,0:T(8,128)(2,1)S(1)} %get-tuple-element.262.refs_0_), channel_id=1, source_target_pairs={{0,16},{4,20},{8,24},{12,28},{16,0},{20,4},{24,8},{28,12},{1,17},{... | collective-permute-start | bytes 663560 | tf_op jit(solution)/shard_map/ppermute | solution.py:971
  224.9 1.8 last_down.1
  226.7 4.2 %collective-permute-done.43.refs_1_ = bf16[48,2304]{1,0:T(8,128)(2,1)S(1)} collective-permute-done((bf16[48,2304]{1,0:T(8,128)(2,1)S(1)}, bf16[48,2304]{1,0:T(8,128)(2,1)S(1)}, u32[]{:S(2)}, u32[]{:S(2)}) %collective-permute-start.43) | collective-permute-done | bytes 221216 | tf_op jit(solution)/shard_map/ppermute | solution.py:971
  231.0 5.9 %collective-permute-done.45.refs_1_ = bf16[48,2304]{1,0:T(8,128)(2,1)S(1)} collective-permute-done((bf16[48,2304]{1,0:T(8,128)(2,1)S(1)}, bf16[48,2304]{1,0:T(8,128)(2,1)S(1)}, u32[]{:S(2)}, u32[]{:S(2)}) %collective-permute-start.45) | collective-permute-done | bytes 221216 | tf_op jit(solution)/shard_map/ppermute | solution.py:971
  237.8 3.2 %last_up.1 = (f32[192,3072]{1,0:T(8,128)}, f32[192,768]{1,0:T(8,128)}, f32[192,128]{1,0:T(8,128)}, f32[192]{0:T(256)}) custom-call(bf16[192,3072]{1,0:T(8,128)(2,1)} %refs_0_.9, bf16[192]{0:T(256)(128)(2,1)S(1)} %copy-done, bf16[96,3968]{1,0:T(8,128)(2,1)S(1)} %get-tuple-element.263.refs_2_, bf16[96,3968]{1,0:T(8,128)(2,1)S(1)} %collective-permute-done.47.refs_3_), custom_call_target="tpu_custom_call" | custom-call | bytes 2703744 | tf_op jit(solution)/shard_map/last_up/pallas_call | solution.py:820
  243.6 3.2 %collective-permute-done.46.refs_3_ = bf16[96,2304]{1,0:T(8,128)(2,1)S(1)} collective-permute-done((bf16[96,2304]{1,0:T(8,128)(2,1)S(1)}, bf16[96,2304]{1,0:T(8,128)(2,1)S(1)}, u32[]{:S(2)}, u32[]{:S(2)}) %collective-permute-start.46) | collective-permute-done | bytes 442400 | tf_op jit(solution)/shard_map/ppermute | solution.py:971
  246.8 2.6 %last_qkv.1 = (f32[192,2304]{1,0:T(8,128)}, f32[192]{0:T(256)}) custom-call(bf16[192,2304]{1,0:T(8,128)(2,1)} %refs_0_.8, bf16[192]{0:T(256)(128)(2,1)S(1)} %copy-done.1, bf16[96,2304]{1,0:T(8,128)(2,1)S(1)} %gradient_sums.25.refs_2_, bf16[96,2304]{1,0:T(8,128)(2,1)S(1)} %collective-permute-done.46.refs_3_), custom_call_target="tpu_custom_call" | custom-call | bytes 1769856 | tf_op jit(solution)/shard_map/last_qkv/pallas_call | solution.py:820
  (115 shorter events, 30.7 us)
Async XLA Ops:
  2.4 11.7 %collective-permute-start.1 = (bf16[64,2304]{1,0:T(8,128)(2,1)}, bf16[64,2304]{1,0:T(8,128)(2,1)}, u32[]{:S(2)}, u32[]{:S(2)}) collective-permute-start(bf16[64,2304]{1,0:T(8,128)(2,1)} %constant_dynamic-slice_fusion), channel_id=1, source_target_pairs={{0,2},{1,3},{2,0},{3,1},{4,6},{5,7},{6,4},{7,5},{8,10},{9,11},{10,... | collective-permute-start | bytes 884744 | tf_op jit(solution)/shard_map/ppermute | solution.py:971
  5.3 6.7 %collective-permute-start.5 = (bf16[192,768]{1,0:T(8,128)(2,1)}, bf16[192,768]{1,0:T(8,128)(2,1)}, u32[]{:S(2)}, u32[]{:S(2)}) collective-permute-start(bf16[192,768]{1,0:T(8,128)(2,1)} %refs_0_.6), channel_id=1, source_target_pairs={{0,1},{1,0},{2,3},{3,2},{4,5},{5,4},{6,7},{7,6},{8,9},{9,8},{10,11... | collective-permute-start | bytes 884744 | tf_op jit(solution)/shard_map/ppermute | solution.py:971
  7.7 4.2 %collective-permute-start.3 = (bf16[8,2304]{1,0:T(8,128)(2,1)}, bf16[8,2304]{1,0:T(8,128)(2,1)}, u32[]{:S(2)}, u32[]{:S(2)}) collective-permute-start(bf16[8,2304]{1,0:T(8,128)(2,1)} %get-tuple-element.148.refs_0_), channel_id=1, source_target_pairs={{0,1},{1,0},{2,3},{3,2},{4,5},{5,4},{6,7},{7,6},{8,9},{9,8},{10,11... | collective-permute-start | bytes 110600 | tf_op jit(solution)/shard_map/ppermute | solution.py:971
  8.2 6.2 %collective-permute-start.2 = (bf16[192,2304]{1,0:T(8,128)(2,1)}, bf16[192,2304]{1,0:T(8,128)(2,1)}, u32[]{:S(2)}, u32[]{:S(2)}) collective-permute-start(bf16[192,2304]{1,0:T(8,128)(2,1)} %refs_0_.8), channel_id=1, source_target_pairs={{0,1},{1,0},{2,3},{3,2},{4,5},{5,4},{6,7},{7,6},{8,9},{9,8},{10,11... | collective-permute-start | bytes 2654216 | tf_op jit(solution)/shard_map/ppermute | solution.py:971
  8.2 6.2 %collective-permute-start.4 = (bf16[192,3072]{1,0:T(8,128)(2,1)}, bf16[192,3072]{1,0:T(8,128)(2,1)}, u32[]{:S(2)}, u32[]{:S(2)}) collective-permute-start(bf16[192,3072]{1,0:T(8,128)(2,1)} %refs_0_.9), channel_id=1, source_target_pairs={{0,1},{1,0},{2,3},{3,2},{4,5},{5,4},{6,7},{7,6},{8,9},{9,8},{10,11... | collective-permute-start | bytes 3538952 | tf_op jit(solution)/shard_map/ppermute | solution.py:971
  12.0 10.7 %collective-permute-start.6 = (bf16[72,2304]{1,0:T(8,128)(2,1)S(1)}, bf16[72,2304]{1,0:T(8,128)(2,1)S(1)}, u32[]{:S(2)}, u32[]{:S(2)}) collective-permute-start(bf16[72,2304]{1,0:T(8,128)(2,1)S(1)} %get-tuple-element.143), channel_id=1, source_target_pairs={{0,2},{1,3},{2,0},{3,1},{4,6},{5,7},{6,4},{7,5},{8,10},{9,11},{10,... | collective-permute-start | bytes 995336 | tf_op jit(solution)/shard_map/ppermute | solution.py:971
  12.0 24.6 %collective-permute-start = (bf16[64,3072]{1,0:T(8,128)(2,1)}, bf16[64,3072]{1,0:T(8,128)(2,1)}, u32[]{:S(2)}, u32[]{:S(2)}) collective-permute-start(bf16[64,3072]{1,0:T(8,128)(2,1)} %get-tuple-element.145), channel_id=1, source_target_pairs={{0,2},{1,3},{2,0},{3,1},{4,6},{5,7},{6,4},{7,5},{8,10},{9,11},{10,... | collective-permute-start | bytes 1179656 | tf_op jit(solution)/shard_map/ppermute | solution.py:971
  14.1 35.4 %collective-permute-start.13 = (bf16[64,3072]{1,0:T(8,128)(2,1)}, bf16[64,3072]{1,0:T(8,128)(2,1)}, u32[]{:S(2)}, u32[]{:S(2)}) collective-permute-start(bf16[64,3072]{1,0:T(8,128)(2,1)} %get-tuple-element.166), channel_id=1, source_target_pairs={{0,2},{1,3},{2,0},{3,1},{4,6},{5,7},{6,4},{7,5},{8,10},{9,11},{10,... | collective-permute-start | bytes 1179656 | tf_op jit(solution)/shard_map/ppermute | solution.py:971
  14.4 8.8 %collective-permute-start.8 = (bf16[64,2304]{1,0:T(8,128)(2,1)}, bf16[64,2304]{1,0:T(8,128)(2,1)S(1)}, u32[]{:S(2)}, u32[]{:S(2)}) collective-permute-start(bf16[64,2304]{1,0:T(8,128)(2,1)} %collective-permute-done.1.refs_6_), channel_id=1, source_target_pairs={{0,4},{4,0},{8,12},{12,8},{16,20},{20,16},{24,28},{28,24},{1,5},{5... | collective-permute-start | bytes 884744 | tf_op jit(solution)/shard_map/ppermute | solution.py:971
  22.7 2.1 collective-permute-start.7
  22.7 2.6 %collective-permute-start.9 = (bf16[64,2304]{1,0:T(8,128)(2,1)}, bf16[64,2304]{1,0:T(8,128)(2,1)S(1)}, u32[]{:S(2)}, u32[]{:S(2)}) collective-permute-start(bf16[64,2304]{1,0:T(8,128)(2,1)} %collective-permute-done.1.refs_6_), channel_id=1, source_target_pairs={{0,1},{1,0},{2,3},{3,2},{4,5},{5,4},{6,7},{7,6},{8,9},{9,8},{10,11... | collective-permute-start | bytes 884744 | tf_op jit(solution)/shard_map/ppermute | solution.py:971
  23.2 2.1 collective-permute-start.10
  24.7 25.4 %collective-permute-start.11 = (bf16[192,768]{1,0:T(8,128)(2,1)}, bf16[192,768]{1,0:T(8,128)(2,1)}, u32[]{:S(2)}, u32[]{:S(2)}) collective-permute-start(bf16[192,768]{1,0:T(8,128)(2,1)} %refs_0_.6), channel_id=1, source_target_pairs={{0,2},{1,3},{2,0},{3,1},{4,6},{5,7},{6,4},{7,5},{8,10},{9,11},{10,... | collective-permute-start | bytes 884744 | tf_op jit(solution)/shard_map/ppermute | solution.py:971
  36.6 13.5 %collective-permute-start.14 = (bf16[64,3072]{1,0:T(8,128)(2,1)}, bf16[64,3072]{1,0:T(8,128)(2,1)}, u32[]{:S(2)}, u32[]{:S(2)}) collective-permute-start(bf16[64,3072]{1,0:T(8,128)(2,1)} %collective-permute-done.refs_6_), channel_id=1, source_target_pairs={{0,4},{4,0},{8,12},{12,8},{16,20},{20,16},{24,28},{28,24},{1,5},{5... | collective-permute-start | bytes 1179656 | tf_op jit(solution)/shard_map/ppermute | solution.py:971
  49.5 4.4 %collective-permute-start.15 = (bf16[64,3072]{1,0:T(8,128)(2,1)}, bf16[64,3072]{1,0:T(8,128)(2,1)S(1)}, u32[]{:S(2)}, u32[]{:S(2)}) collective-permute-start(bf16[64,3072]{1,0:T(8,128)(2,1)} %collective-permute-done.refs_6_), channel_id=1, source_target_pairs={{0,1},{1,0},{2,3},{3,2},{4,5},{5,4},{6,7},{7,6},{8,9},{9,8},{10,11... | collective-permute-start | bytes 1179656 | tf_op jit(solution)/shard_map/ppermute | solution.py:971
  49.6 4.3 %collective-permute-start.16 = (bf16[64,3072]{1,0:T(8,128)(2,1)}, bf16[64,3072]{1,0:T(8,128)(2,1)S(1)}, u32[]{:S(2)}, u32[]{:S(2)}) collective-permute-start(bf16[64,3072]{1,0:T(8,128)(2,1)} %collective-permute-done.13.refs_7_), channel_id=1, source_target_pairs={{0,1},{1,0},{2,3},{3,2},{4,5},{5,4},{6,7},{7,6},{8,9},{9,8},{10,11... | collective-permute-start | bytes 1179656 | tf_op jit(solution)/shard_map/ppermute | solution.py:971
  50.1 3.8 %collective-permute-start.17 = (bf16[64,3072]{1,0:T(8,128)(2,1)}, bf16[64,3072]{1,0:T(8,128)(2,1)S(1)}, u32[]{:S(2)}, u32[]{:S(2)}) collective-permute-start(bf16[64,3072]{1,0:T(8,128)(2,1)} %collective-permute-done.14.refs_8_), channel_id=1, source_target_pairs={{0,1},{1,0},{2,3},{3,2},{4,5},{5,4},{6,7},{7,6},{8,9},{9,8},{10,11... | collective-permute-start | bytes 1179656 | tf_op jit(solution)/shard_map/ppermute | solution.py:971
  50.2 3.7 %collective-permute-start.12 = (bf16[192,768]{1,0:T(8,128)(2,1)}, bf16[192,768]{1,0:T(8,128)(2,1)S(1)}, u32[]{:S(2)}, u32[]{:S(2)}) collective-permute-start(bf16[192,768]{1,0:T(8,128)(2,1)} %collective-permute-done.11.refs_2_), channel_id=1, source_target_pairs={{0,1},{1,0},{2,3},{3,2},{4,5},{5,4},{6,7},{7,6},{8,9},{9,8},{10,11... | collective-permute-start | bytes 884744 | tf_op jit(solution)/shard_map/ppermute | solution.py:971
  52.3 29.7 %collective-permute-start.21 = (bf16[768,768]{1,0:T(8,128)(2,1)}, bf16[768,768]{1,0:T(8,128)(2,1)}, u32[]{:S(2)}, u32[]{:S(2)}) collective-permute-start(bf16[768,768]{1,0:T(8,128)(2,1)} %refs_0_.7), channel_id=1, source_target_pairs={{0,2},{1,3},{2,0},{3,1},{4,6},{5,7},{6,4},{7,5},{8,10},{9,11},{10,... | collective-permute-start | bytes 3538952 | tf_op jit(solution)/shard_map/ppermute | solution.py:971
  78.0 4.9 %collective-permute-start.18 = (bf16[2,768,768]{2,1,0:T(8,128)(2,1)}, bf16[2,768,768]{2,1,0:T(8,128)(2,1)}, u32[]{:S(2)}, u32[]{:S(2)}) collective-permute-start(bf16[2,768,768]{2,1,0:T(8,128)(2,1)} %grad_down.2), channel_id=1, source_target_pairs={{0,1},{1,0},{2,3},{3,2},{4,5},{5,4},{6,7},{7,6},{8,9},{9,8},{10,11... | collective-permute-start | bytes 7077896 | tf_op jit(solution)/shard_map/ppermute | solution.py:971
  81.4 5.8 %collective-permute-start.20 = (bf16[768,768]{1,0:T(8,128)(2,1)S(1)}, bf16[768,768]{1,0:T(8,128)(2,1)S(1)}, u32[]{:S(2)}, u32[]{:S(2)}) collective-permute-start(bf16[768,768]{1,0:T(8,128)(2,1)S(1)} %copy-done.10), channel_id=1, source_target_pairs={{0,1},{1,0},{2,3},{3,2},{4,5},{5,4},{6,7},{7,6},{8,9},{9,8},{10,11... | collective-permute-start | bytes 3538952 | tf_op jit(solution)/shard_map/ppermute | solution.py:971
  82.0 5.2 %collective-permute-start.22 = (bf16[768,768]{1,0:T(8,128)(2,1)}, bf16[768,768]{1,0:T(8,128)(2,1)S(1)}, u32[]{:S(2)}, u32[]{:S(2)}) collective-permute-start(bf16[768,768]{1,0:T(8,128)(2,1)} %collective-permute-done.21.refs_2_), channel_id=1, source_target_pairs={{0,1},{1,0},{2,3},{3,2},{4,5},{5,4},{6,7},{7,6},{8,9},{9,8},{10,11... | collective-permute-start | bytes 3538952 | tf_op jit(solution)/shard_map/ppermute | solution.py:971
  85.8 21.9 %collective-permute-start.19 = (bf16[768,384]{1,0:T(8,128)(2,1)}, bf16[768,384]{1,0:T(8,128)(2,1)}, u32[]{:S(2)}, u32[]{:S(2)}) collective-permute-start(bf16[768,384]{1,0:T(8,128)(2,1)} %get-tuple-element.174), channel_id=1, source_target_pairs={{0,2},{1,3},{2,0},{3,1},{4,6},{5,7},{6,4},{7,5},{8,10},{9,11},{10,... | collective-permute-start | bytes 1769480 | tf_op jit(solution)/shard_map/ppermute | solution.py:971
  86.5 21.2 %collective-permute-start.23 = (bf16[2,384,384]{2,1,0:T(8,128)(2,1)}, bf16[2,384,384]{2,1,0:T(8,128)(2,1)}, u32[]{:S(2)}, u32[]{:S(2)}) collective-permute-start(bf16[2,384,384]{2,1,0:T(8,128)(2,1)} %get-tuple-element.175), channel_id=1, source_target_pairs={{0,4},{4,0},{8,12},{12,8},{16,20},{20,16},{24,28},{28,24},{1,5},{5... | collective-permute-start | bytes 1769480 | tf_op jit(solution)/shard_map/ppermute | solution.py:971
  109.9 10.6 %collective-permute-start.24 = (bf16[384,384]{1,0:T(8,128)(2,1)}, bf16[384,384]{1,0:T(8,128)(2,1)}, u32[]{:S(2)}, u32[]{:S(2)}) collective-permute-start(bf16[384,384]{1,0:T(8,128)(2,1)} %get-tuple-element.188), channel_id=1, source_target_pairs={{0,4},{4,0},{8,12},{12,8},{16,20},{20,16},{24,28},{28,24},{1,5},{5... | collective-permute-start | bytes 884744 | tf_op jit(solution)/shard_map/ppermute | solution.py:971
  111.2 9.3 %collective-permute-start.25 = (bf16[384,384]{1,0:T(8,128)(2,1)}, bf16[384,384]{1,0:T(8,128)(2,1)}, u32[]{:S(2)}, u32[]{:S(2)}) collective-permute-start(bf16[384,384]{1,0:T(8,128)(2,1)} %get-tuple-element.189), channel_id=1, source_target_pairs={{0,2},{1,3},{2,0},{3,1},{4,6},{5,7},{6,4},{7,5},{8,10},{9,11},{10,... | collective-permute-start | bytes 884744 | tf_op jit(solution)/shard_map/ppermute | solution.py:971
  120.4 5.6 %collective-permute-start.27 = (bf16[2,192,3968]{2,1,0:T(8,128)(2,1)S(1)}, bf16[2,192,3968]{2,1,0:T(8,128)(2,1)S(1)}, u32[]{:S(2)}, u32[]{:S(2)}) collective-permute-start(bf16[2,192,3968]{2,1,0:T(8,128)(2,1)S(1)} %get-tuple-element.201), channel_id=1, source_target_pairs={{0,1},{1,0},{2,3},{3,2},{4,5},{5,4},{6,7},{7,6},{8,9},{9,8},{10,11... | collective-permute-start | bytes 9142280 | tf_op jit(solution)/shard_map/ppermute | solution.py:971
  122.4 21.8 %collective-permute-start.26 = (bf16[192,768]{1,0:T(8,128)(2,1)}, bf16[192,768]{1,0:T(8,128)(2,1)}, u32[]{:S(2)}, u32[]{:S(2)}) collective-permute-start(bf16[192,768]{1,0:T(8,128)(2,1)} %get-tuple-element.200), channel_id=1, source_target_pairs={{0,8},{4,12},{8,0},{12,4},{16,24},{20,28},{24,16},{28,20},{1,9},{5... | collective-permute-start | bytes 884744 | tf_op jit(solution)/shard_map/ppermute | solution.py:971
  127.5 18.8 %collective-permute-start.29 = (bf16[2,96,1920]{2,1,0:T(8,128)(2,1)}, bf16[2,96,1920]{2,1,0:T(8,128)(2,1)}, u32[]{:S(2)}, u32[]{:S(2)}) collective-permute-start(bf16[2,96,1920]{2,1,0:T(8,128)(2,1)} %get-tuple-element.204), channel_id=1, source_target_pairs={{0,4},{4,0},{8,12},{12,8},{16,20},{20,16},{24,28},{28,24},{1,5},{5... | collective-permute-start | bytes 2211848 | tf_op jit(solution)/shard_map/ppermute | solution.py:971
  128.2 19.6 %collective-permute-start.28 = (bf16[192,2048]{1,0:T(8,128)(2,1)}, bf16[192,2048]{1,0:T(8,128)(2,1)}, u32[]{:S(2)}, u32[]{:S(2)}) collective-permute-start(bf16[192,2048]{1,0:T(8,128)(2,1)} %get-tuple-element.203), channel_id=1, source_target_pairs={{0,2},{1,3},{2,0},{3,1},{4,6},{5,7},{6,4},{7,5},{8,10},{9,11},{10,... | collective-permute-start | bytes 2359304 | tf_op jit(solution)/shard_map/ppermute | solution.py:971
  150.4 21.9 %collective-permute-start.33 = (bf16[192,768]{1,0:T(8,128)(2,1)}, bf16[192,768]{1,0:T(8,128)(2,1)}, u32[]{:S(2)}, u32[]{:S(2)}) collective-permute-start(bf16[192,768]{1,0:T(8,128)(2,1)} %get-tuple-element.215.refs_0_), channel_id=1, source_target_pairs={{0,16},{4,20},{8,24},{12,28},{16,0},{20,4},{24,8},{28,12},{1,17},{... | collective-permute-start | bytes 884744 | tf_op jit(solution)/shard_map/ppermute | solution.py:971
  153.0 11.0 %collective-permute-start.31 = (bf16[96,1920]{1,0:T(8,128)(2,1)}, bf16[96,1920]{1,0:T(8,128)(2,1)}, u32[]{:S(2)}, u32[]{:S(2)}) collective-permute-start(bf16[96,1920]{1,0:T(8,128)(2,1)} %get-tuple-element.216), channel_id=1, source_target_pairs={{0,2},{1,3},{2,0},{3,1},{4,6},{5,7},{6,4},{7,5},{8,10},{9,11},{10,... | collective-permute-start | bytes 1105928 | tf_op jit(solution)/shard_map/ppermute | solution.py:971
  153.6 10.4 %collective-permute-start.30 = (bf16[96,2048]{1,0:T(8,128)(2,1)}, bf16[96,2048]{1,0:T(8,128)(2,1)}, u32[]{:S(2)}, u32[]{:S(2)}) collective-permute-start(bf16[96,2048]{1,0:T(8,128)(2,1)} %get-tuple-element.214), channel_id=1, source_target_pairs={{0,4},{4,0},{8,12},{12,8},{16,20},{20,16},{24,28},{28,24},{1,5},{5... | collective-permute-start | bytes 1179656 | tf_op jit(solution)/shard_map/ppermute | solution.py:971
  166.2 9.2 %collective-permute-start.32 = (bf16[48,3968]{1,0:T(8,128)(2,1)}, bf16[48,3968]{1,0:T(8,128)(2,1)}, u32[]{:S(2)}, u32[]{:S(2)}) collective-permute-start(bf16[48,3968]{1,0:T(8,128)(2,1)} %get-tuple-element.222), channel_id=1, source_target_pairs={{0,8},{4,12},{8,0},{12,4},{16,24},{20,28},{24,16},{28,20},{1,9},{5... | collective-permute-start | bytes 1142792 | tf_op jit(solution)/shard_map/ppermute | solution.py:971
  172.1 3.8 %collective-permute-start.34 = (bf16[2,192,2304]{2,1,0:T(8,128)(2,1)S(1)}, bf16[2,192,2304]{2,1,0:T(8,128)(2,1)S(1)}, u32[]{:S(2)}, u32[]{:S(2)}) collective-permute-start(bf16[2,192,2304]{2,1,0:T(8,128)(2,1)S(1)} %get-tuple-element.231), channel_id=1, source_target_pairs={{0,1},{1,0},{2,3},{3,2},{4,5},{5,4},{6,7},{7,6},{8,9},{9,8},{10,11... | collective-permute-start | bytes 5308424 | tf_op jit(solution)/shard_map/ppermute | solution.py:971
  174.1 15.5 %collective-permute-start.35 = (bf16[192,768]{1,0:T(8,128)(2,1)}, bf16[192,768]{1,0:T(8,128)(2,1)}, u32[]{:S(2)}, u32[]{:S(2)}) collective-permute-start(bf16[192,768]{1,0:T(8,128)(2,1)} %gradient_sums.19.refs_0_), channel_id=1, source_target_pairs={{0,8},{4,12},{8,0},{12,4},{16,24},{20,28},{24,16},{28,20},{1,9},{5... | collective-permute-start | bytes 884744 | tf_op jit(solution)/shard_map/ppermute | solution.py:971
  178.1 26.6 %collective-permute-start.38 = (bf16[48,3968]{1,0:T(8,128)(2,1)}, bf16[48,3968]{1,0:T(8,128)(2,1)}, u32[]{:S(2)}, u32[]{:S(2)}) collective-permute-start(bf16[48,3968]{1,0:T(8,128)(2,1)} %get-tuple-element.236.refs_0_), channel_id=1, source_target_pairs={{0,16},{4,20},{8,24},{12,28},{16,0},{20,4},{24,8},{28,12},{1,17},{... | collective-permute-start | bytes 1142792 | tf_op jit(solution)/shard_map/ppermute | solution.py:971
  178.4 12.2 %collective-permute-start.36 = (bf16[192,1152]{1,0:T(8,128)(2,1)}, bf16[192,1152]{1,0:T(8,128)(2,1)}, u32[]{:S(2)}, u32[]{:S(2)}) collective-permute-start(bf16[192,1152]{1,0:T(8,128)(2,1)} %get-tuple-element.237), channel_id=1, source_target_pairs={{0,2},{1,3},{2,0},{3,1},{4,6},{5,7},{6,4},{7,5},{8,10},{9,11},{10,... | collective-permute-start | bytes 1327112 | tf_op jit(solution)/shard_map/ppermute | solution.py:971
  179.8 12.0 %collective-permute-start.37 = (bf16[2,96,1152]{2,1,0:T(8,128)(2,1)}, bf16[2,96,1152]{2,1,0:T(8,128)(2,1)}, u32[]{:S(2)}, u32[]{:S(2)}) collective-permute-start(bf16[2,96,1152]{2,1,0:T(8,128)(2,1)} %get-tuple-element.238), channel_id=1, source_target_pairs={{0,4},{4,0},{8,12},{12,8},{16,20},{20,16},{24,28},{28,24},{1,5},{5... | collective-permute-start | bytes 1327112 | tf_op jit(solution)/shard_map/ppermute | solution.py:971
  194.0 10.7 %collective-permute-start.39 = (bf16[96,1152]{1,0:T(8,128)(2,1)}, bf16[96,1152]{1,0:T(8,128)(2,1)}, u32[]{:S(2)}, u32[]{:S(2)}) collective-permute-start(bf16[96,1152]{1,0:T(8,128)(2,1)} %get-tuple-element.247), channel_id=1, source_target_pairs={{0,4},{4,0},{8,12},{12,8},{16,20},{20,16},{24,28},{28,24},{1,5},{5... | collective-permute-start | bytes 663560 | tf_op jit(solution)/shard_map/ppermute | solution.py:971
  194.7 9.9 %collective-permute-start.40 = (bf16[96,1152]{1,0:T(8,128)(2,1)}, bf16[96,1152]{1,0:T(8,128)(2,1)}, u32[]{:S(2)}, u32[]{:S(2)}) collective-permute-start(bf16[96,1152]{1,0:T(8,128)(2,1)} %get-tuple-element.248), channel_id=1, source_target_pairs={{0,2},{1,3},{2,0},{3,1},{4,6},{5,7},{6,4},{7,5},{8,10},{9,11},{10,... | collective-permute-start | bytes 663560 | tf_op jit(solution)/shard_map/ppermute | solution.py:971
  206.1 13.7 %collective-permute-start.41 = (bf16[48,3968]{1,0:T(8,128)(2,1)S(1)}, bf16[48,3968]{1,0:T(8,128)(2,1)S(1)}, u32[]{:S(2)}, u32[]{:S(2)}) collective-permute-start(bf16[48,3968]{1,0:T(8,128)(2,1)S(1)} %get-tuple-element.257.refs_0_), channel_id=1, source_target_pairs={{0,8},{4,12},{8,0},{12,4},{16,24},{20,28},{24,16},{28,20},{1,9},{5... | collective-permute-start | bytes 1142792 | tf_op jit(solution)/shard_map/ppermute | solution.py:971
  206.7 13.0 %collective-permute-start.42 = (bf16[48,2304]{1,0:T(8,128)(2,1)S(1)}, bf16[48,2304]{1,0:T(8,128)(2,1)S(1)}, u32[]{:S(2)}, u32[]{:S(2)}) collective-permute-start(bf16[48,2304]{1,0:T(8,128)(2,1)S(1)} %get-tuple-element.258), channel_id=1, source_target_pairs={{0,8},{4,12},{8,0},{12,4},{16,24},{20,28},{24,16},{28,20},{1,9},{5... | collective-permute-start | bytes 663560 | tf_op jit(solution)/shard_map/ppermute | solution.py:971
  208.2 16.7 %collective-permute-start.44 = (bf16[384,768]{1,0:T(8,128)(2,1)S(1)}, bf16[384,768]{1,0:T(8,128)(2,1)S(1)}, u32[]{:S(2)}, u32[]{:S(2)}) collective-permute-start(bf16[384,768]{1,0:T(8,128)(2,1)S(1)} %get-tuple-element.246.refs_0_), channel_id=1, source_target_pairs={{0,4},{4,0},{8,12},{12,8},{16,20},{20,16},{24,28},{28,24},{1,5},{5... | collective-permute-start | bytes 1769480 | tf_op jit(solution)/shard_map/ppermute | solution.py:971
  219.9 17.9 %collective-permute-start.47 = (bf16[96,3968]{1,0:T(8,128)(2,1)S(1)}, bf16[96,3968]{1,0:T(8,128)(2,1)S(1)}, u32[]{:S(2)}, u32[]{:S(2)}) collective-permute-start(bf16[96,3968]{1,0:T(8,128)(2,1)S(1)} %get-tuple-element.263.refs_2_), channel_id=1, source_target_pairs={{0,4},{4,0},{8,12},{12,8},{16,20},{20,16},{24,28},{28,24},{1,5},{5... | collective-permute-start | bytes 2285576 | tf_op jit(solution)/shard_map/ppermute | solution.py:971
  221.2 9.7 %collective-permute-start.43 = (bf16[48,2304]{1,0:T(8,128)(2,1)S(1)}, bf16[48,2304]{1,0:T(8,128)(2,1)S(1)}, u32[]{:S(2)}, u32[]{:S(2)}) collective-permute-start(bf16[48,2304]{1,0:T(8,128)(2,1)S(1)} %get-tuple-element.262.refs_0_), channel_id=1, source_target_pairs={{0,16},{4,20},{8,24},{12,28},{16,0},{20,4},{24,8},{28,12},{1,17},{... | collective-permute-start | bytes 663560 | tf_op jit(solution)/shard_map/ppermute | solution.py:971
  230.9 6.0 %collective-permute-start.45 = (bf16[48,2304]{1,0:T(8,128)(2,1)S(1)}, bf16[48,2304]{1,0:T(8,128)(2,1)S(1)}, u32[]{:S(2)}, u32[]{:S(2)}) collective-permute-start(bf16[48,2304]{1,0:T(8,128)(2,1)S(1)} %gradient_sums.24.refs_0_), channel_id=1, source_target_pairs={{0,8},{4,12},{8,0},{12,4},{16,24},{20,28},{24,16},{28,20},{1,9},{5... | collective-permute-start | bytes 663560 | tf_op jit(solution)/shard_map/ppermute | solution.py:971
  237.0 9.8 %collective-permute-start.46 = (bf16[96,2304]{1,0:T(8,128)(2,1)S(1)}, bf16[96,2304]{1,0:T(8,128)(2,1)S(1)}, u32[]{:S(2)}, u32[]{:S(2)}) collective-permute-start(bf16[96,2304]{1,0:T(8,128)(2,1)S(1)} %gradient_sums.25.refs_2_), channel_id=1, source_target_pairs={{0,4},{4,0},{8,12},{12,8},{16,20},{20,16},{24,28},{28,24},{1,5},{5... | collective-permute-start | bytes 1327112 | tf_op jit(solution)/shard_map/ppermute | solution.py:971
  (11 other events, 107.0 us)

commit v5 on v4

--- a/solution.py
+++ b/solution.py
@@ -1161,7 +1161,8 @@
     paced = pace_call(ready(send), same)
     sent = advance([chain_a], keep, pace_call(ready(keep), same))
     g0 = back(0, 4, keep, *sent, *advance([chain_b], keep, paced, *sent))
-    g1 = back(4, pairs - 4, g0[0], *advance([chain_a, chain_b], g0[0]))
+    sent = advance([chain_a], g0[0])
+    g1 = back(4, pairs - 4, g0[0], *sent, *advance([chain_b], g0[0], *sent))
     groups = [g0, g1]
     rights = [array for group in groups for array in group]
     send, keep = grad_qkv_call(ready(*advance([chain_b], g1[0])), a1t, rights, narrow)
@@ -1171,8 +1172,9 @@
     sent = advance([chain_a], keep)
     sent = advance([chain_b, chain_c], keep, paced, *sent)
     output = output_call(ready(keep, *sent), x1, h, vec, down_full)
-    sent = advance([chain_a, chain_c], output)
-    d_input = input_call(ready(output, *sent), x, dx1, vec, groups, qkv_full)
+    sent_a = advance([chain_a], output)
+    sent = advance([chain_c], output, *sent_a)
+    d_input = input_call(ready(output, *sent_a, *sent), x, dx1, vec, groups, qkv_full)
     sent = advance([chain_b, chain_c], d_input)
     sent = advance([chain_b, chain_c], *sent)
     sum_a = close(chain_a, *sent)

time: 250 us -> 250 us (level)
  waiting for transfers between devices: 38 us -> 34.5 us
  Pallas kernels: 159 us -> 162 us
    ppermute x48, waiting for transfers between devices: 38 us -> 34.5 us  [swap(): return lax.ppermute(value, axis, [(i, i ^ bit) for i in range(size)])]
    pallas_call x16 -> x18, Pallas kernels: 28.7 us -> 31.4 us  [whole_call(): pl.pallas_call(run, name=name, in_specs=[pl.BlockSpec(memory_space=pltpu....]
  transfers between devices with their start and end apart: 48 -> 48, of which waited for: 14 -> 10; matrix products, arithmetic and copies ran while one was open for 3% -> 3% of each run, Pallas kernels for 60% -> 62%
where the time goes in v5:
time: 250 us; the launch traced here: 249 us
  Pallas kernels  162 us (65%)
  starting transfers between devices  41 us (16%)
  waiting for transfers between devices  34.5 us (14%)
  local copies, waits for them, and re-layouts  7.12 us (3%)
  other arithmetic  2.89 us (1%)
    pallas_call x14, Pallas kernels, run(): return fun(index, *args)  130 us
    ppermute x48, starting transfers between devices, swap(): return lax.ppermute(value, axis, [(i, i ^ bit) for i in range(size)])  41 us
    ppermute x48, waiting for transfers between devices, swap(): return lax.ppermute(value, axis, [(i, i ^ bit) for i in range(size)])  34.5 us
    pallas_call x18, Pallas kernels, whole_call(): pl.pallas_call(run, name=name, in_specs=[pl.BlockSpec(memory_space=pltpu....  31.4 us
  transfers between devices with their start and end apart: 48, of which 10 were waited for; matrix products, arithmetic and copies ran while one was open for 3% of the time, Pallas kernels for 62%

profile of v5, /device:TPU:0, one launch (start us, length us, event | category | flops | bytes accessed | tf_op | source)
XLA Modules:
  0.0 248.9 jit_solution(18335383721121131132)
XLA Ops:
  0.7 1.7 constant_dynamic-slice_fusion
  2.4 3.0 %collective-permute-start.1 = (bf16[64,2304]{1,0:T(8,128)(2,1)}, bf16[64,2304]{1,0:T(8,128)(2,1)}, u32[]{:S(2)}, u32[]{:S(2)}) collective-permute-start(bf16[64,2304]{1,0:T(8,128)(2,1)} %constant_dynamic-slice_fusion), channel_id=1, source_target_pairs={{0,2},{1,3},{2,0},{3,1},{4,6},{5,7},{6,4},{7,5},{8,10},{9,11},{10,... | collective-permute-start | bytes 884744 | tf_op jit(solution)/shard_map/ppermute | solution.py:971
  5.4 2.3 vector_message.1
  8.7 2.6 %next_message.1 = (bf16[64,3072]{1,0:T(8,128)(2,1)}, bf16[64,3072]{1,0:T(8,128)(2,1)}) custom-call(s32[27]{0:T(128)S(1)} %stack.81.idx_ref, bf16[192,3072]{1,0:T(8,128)(2,1)} %refs_0_.9, bf16[192,3072]{1,0:T(8,128)(2,1)} %refs_0_.9), custom_call_target="tpu_custom_call" | custom-call | flops 1500000026624 | bytes 1048576 | tf_op jit(solution)/shard_map/next_message/pallas_call | solution.py:144
  12.0 2.0 collective-permute-start
  14.4 1.7 collective-permute-start.8
  19.1 3.6 %collective-permute-done.6.refs_2_.refs_7_ = bf16[72,2304]{1,0:T(8,128)(2,1)S(1)} collective-permute-done((bf16[72,2304]{1,0:T(8,128)(2,1)S(1)}, bf16[72,2304]{1,0:T(8,128)(2,1)S(1)}, u32[]{:S(2)}, u32[]{:S(2)}) %collective-permute-start.6) | collective-permute-done | bytes 331808 | tf_op jit(solution)/shard_map/ppermute | solution.py:971
  25.3 11.3 %norm_qkv.1 = (bf16[1024,2304]{1,0:T(8,128)(2,1)S(1)}, bf16[768,1024]{1,0:T(8,128)(2,1)}, f32[8,3072]{1,0:T(8,128)}, bf16[768,2304]{1,0:T(8,128)(2,1)}) custom-call(s32[27]{0:T(128)S(1)} %stack.81.idx_ref, bf16[1024,768]{1,0:T(8,128)(2,1)} %bitcast.34, f32[512,128]{1,0:T(8,128)} %copy.31.cos_ref, f32[512,128]{1,0:T(8,128)} %pad_maximum_fusion.sin_ref, ...), custom_call_target="tpu_custom_call" | custom-call | flops 6999999774720 | bytes 1048576 | tf_op jit(solution)/shard_map/norm_qkv/pallas_call | solution.py:144
  36.6 1.6 collective-permute-start.14
  38.2 11.3 %attention.1 = (bf16[1024,768]{1,0:T(8,128)(2,1)}, bf16[768,1024]{1,0:T(8,128)(2,1)}, f32[6,2,1024]{2,1,0:T(2,128)}) custom-call(s32[27]{0:T(128)S(1)} %stack.81.idx_ref, bf16[1024,2304]{1,0:T(8,128)(2,1)S(1)} %get-tuple-element.155.qkv_ref.q_ref.k_ref.v_ref, f32[128,128]{1,0:T(8,128)} %get-tuple-element.274.same_ref, ...), custom_call_target="tpu_custom_call" | custom-call | flops 12000000212992 | bytes 1048576 | tf_op jit(solution)/shard_map/attention/pallas_call | solution.py:144
  50.6 1.7 copy.32.dyt_ref
  52.3 1.6 collective-permute-start.21
  53.9 19.3 %feed_up.1 = (f32[1024,768]{1,0:T(8,128)}, bf16[768,1024]{1,0:T(8,128)(2,1)S(1)}, bf16[1024,3072]{1,0:T(8,128)(2,1)S(1)}, bf16[1024,3072]{1,0:T(8,128)(2,1)S(1)}...) custom-call(s32[27]{0:T(128)S(1)} %stack.81.idx_ref, bf16[1024,768]{1,0:T(8,128)(2,1)} %bitcast.35, ...), custom_call_target="tpu_custom_call" | custom-call | flops 18000000319488 | bytes 1048576 | tf_op jit(solution)/shard_map/feed_up/pallas_call | solution.py:144
  73.2 4.8 %grad_down.2 = bf16[2,768,768]{2,1,0:T(8,128)(2,1)} custom-call(s32[27]{0:T(128)S(1)} %stack.81.idx_ref, bf16[768,1024]{1,0:T(8,128)(2,1)S(1)} %copy.32.dyt_ref, bf16[1024,3072]{1,0:T(8,128)(2,1)S(1)} %get-tuple-element.167.h_ref), custom_call_target="tpu_custom_call" | custom-call | flops 3000000053248 | bytes 1048576 | tf_op jit(solution)/shard_map/grad_down/pallas_call | solution.py:144
  78.0 3.4 %grad_down.3.refs_0_ = bf16[2,768,768]{2,1,0:T(8,128)(2,1)S(1)} custom-call(s32[27]{0:T(128)S(1)} %stack.81.idx_ref, bf16[768,1024]{1,0:T(8,128)(2,1)S(1)} %copy.32.dyt_ref, bf16[1024,3072]{1,0:T(8,128)(2,1)S(1)} %get-tuple-element.167.h_ref), custom_call_target="tpu_custom_call" | custom-call | flops 3000000053248 | bytes 1048576 | tf_op jit(solution)/shard_map/grad_down/pallas_call | solution.py:144
  82.9 2.9 %gradient_sums.15 = (bf16[768,384]{1,0:T(8,128)(2,1)}, bf16[2,384,384]{2,1,0:T(8,128)(2,1)}, f32[768,384]{1,0:T(8,128)S(1)}, f32[2,384,384]{2,1,0:T(8,128)S(1)}) custom-call(bf16[2,768,768]{2,1,0:T(8,128)(2,1)S(1)} %grad_down.3.refs_0_, bf16[2,768,768]{2,1,0:T(8,128)(2,1)} %collective-permute-done.18.refs_1_), custom_call_target="tpu_custom_call" | custom-call | bytes 4718592 | tf_op jit(solution)/shard_map/gradient_sums/pallas_call | solution.py:820
  87.2 20.4 %feed_back.1 = (bf16[1024,3840]{1,0:T(8,128)(2,1)S(1)}, f32[1024,768]{1,0:T(8,128)}, bf16[1024,768]{1,0:T(8,128)(2,1)}, f32[2,3072]{1,0:T(2,128)S(1)}, bf16[3072,768]{1,0:T(8,128)(2,1)S(1)}) custom-call(s32[27]{0:T(128)S(1)} %stack.81.idx_ref, bf16[1024,768]{1,0:T(8,128)(2,1)} %bitcast.32, f32[1024,768]{1,0:T(8,128)} %get-tuple-element.175.x1_ref, ...), custom_call_target="tpu_custom_call" | custom-call | flops 19999999655936 | bytes 1048576 | tf_op jit(solution)/shard_map/feed_back/pallas_call | solution.py:144
  107.7 2.2 gradient_sums.16
  111.2 1.4 collective-permute-start.26
  112.6 7.9 %grad_up_out.1 = (bf16[2,192,3968]{2,1,0:T(8,128)(2,1)S(1)}, bf16[2,192,3968]{2,1,0:T(8,128)(2,1)S(1)}) custom-call(s32[27]{0:T(128)S(1)} %stack.81.idx_ref, bf16[768,1024]{1,0:T(8,128)(2,1)S(1)} %get-tuple-element.188.a_ref, bf16[768,1024]{1,0:T(8,128)(2,1)S(1)} %copy-done.7, bf16[1024,3840]{1,0:T(8,128)(2,1)S(1)} %get-tuple-element.190.du_ref, ...), custom_call_target="tpu_custom_call" | custom-call | flops 4700000223232 | bytes 1048576 | tf_op jit(solution)/shard_map/grad_up_out/pallas_call | solution.py:144
  120.5 1.8 gradient_sums.17
  122.4 1.6 collective-permute-start.28
  124.0 2.1 collective-permute-done.24.refs_1_
  126.0 1.4 gradient_sums.18
  128.9 15.3 %attention_back.2 = (bf16[1024,512]{1,0:T(8,128)(2,1)S(1)}, bf16[1024,512]{1,0:T(8,128)(2,1)S(1)}, bf16[1024,512]{1,0:T(8,128)(2,1)S(1)}) custom-call(s32[27]{0:T(128)S(1)} %stack.81.idx_ref, bf16[1024,2304]{1,0:T(8,128)(2,1)} %copy-done.4, bf16[1024,2304]{1,0:T(8,128)(2,1)} %copy-done.4, bf16[1024,2304]{1,0:T(8,128)(2,1)} %copy-done.4, ...), custom_call_target="tpu_custom_call" | custom-call | flops 14399999836160 | bytes 1048576 | tf_op jit(solution)/shard_map/attention_back/pallas_call | solution.py:144
  144.2 2.0 gradient_sums.19.refs_0_
  146.2 2.6 %collective-permute-start.33 = (bf16[192,768]{1,0:T(8,128)(2,1)}, bf16[192,768]{1,0:T(8,128)(2,1)}, u32[]{:S(2)}, u32[]{:S(2)}) collective-permute-start(bf16[192,768]{1,0:T(8,128)(2,1)} %gradient_sums.19.refs_0_), channel_id=1, source_target_pairs={{0,16},{4,20},{8,24},{12,28},{16,0},{20,4},{24,8},{28,12},{1,17},{... | collective-permute-start | bytes 884744 | tf_op jit(solution)/shard_map/ppermute | solution.py:971
  148.8 2.3 gradient_sums.20
  153.7 9.1 %attention_back.3 = (bf16[1024,256]{1,0:T(8,128)(2,1)S(1)}, bf16[1024,256]{1,0:T(8,128)(2,1)S(1)}, bf16[1024,256]{1,0:T(8,128)(2,1)S(1)}) custom-call(s32[27]{0:T(128)S(1)} %stack.81.idx_ref, bf16[1024,2304]{1,0:T(8,128)(2,1)} %copy-done.4, bf16[1024,2304]{1,0:T(8,128)(2,1)} %copy-done.4, bf16[1024,2304]{1,0:T(8,128)(2,1)} %copy-done.4, ...), custom_call_target="tpu_custom_call" | custom-call | flops 7199999918080 | bytes 1048576 | tf_op jit(solution)/shard_map/attention_back/pallas_call | solution.py:144
  162.9 2.2 gradient_sums.21
  165.0 1.6 collective-permute-start.32
  166.6 4.4 %grad_qkv.1 = (bf16[2,192,2304]{2,1,0:T(8,128)(2,1)S(1)}, bf16[2,192,2304]{2,1,0:T(8,128)(2,1)S(1)}) custom-call(s32[27]{0:T(128)S(1)} %stack.81.idx_ref, bf16[768,1024]{1,0:T(8,128)(2,1)S(1)} %copy-done.3, bf16[1024,512]{1,0:T(8,128)(2,1)S(1)} %get-tuple-element.206.refs_0_, bf16[1024,512]{1,0:T(8,128)(2,1)S(1)} %get-tuple-element.222.refs_1_, ...), custom_call_target="tpu_custom_call" | custom-call | flops 3304000061440 | bytes 1048576 | tf_op jit(solution)/shard_map/grad_qkv/pallas_call | solution.py:144
  171.1 1.8 gradient_sums.22.refs_0_
  173.4 1.5 collective-permute-done.32.refs_1_
  174.9 2.2 gradient_sums.23
  177.9 1.4 collective-permute-start.36
  180.2 9.0 %layer_output.1 = bf16[1024,768]{1,0:T(8,128)(2,1)} custom-call(s32[27]{0:T(128)S(1)} %stack.81.idx_ref, f32[1024,768]{1,0:T(8,128)} %get-tuple-element.175.x1_ref, bf16[1024,3072]{1,0:T(8,128)(2,1)} %copy-done.2, f32[8,3072]{1,0:T(8,128)} %get-tuple-element.152.vec_ref, bf16[3072,768]{1,0:T(8,128)(2,1)S(1)} %get-tuple-element.237.w_ref), custom_call_target="tpu_custom_call" | custom-call | flops 7999999967232 | bytes 1048576 | tf_op jit(solution)/shard_map/layer_output/pallas_call | solution.py:144
  191.2 2.0 gradient_sums.25
  194.8 9.2 %grad_input.1 = bf16[1024,768]{1,0:T(8,128)(2,1)} custom-call(s32[27]{0:T(128)S(1)} %stack.81.idx_ref, bf16[1024,768]{1,0:T(8,128)(2,1)} %bitcast.36, f32[1024,768]{1,0:T(8,128)} %get-tuple-element.246.dx1_ref, f32[8,3072]{1,0:T(8,128)} %get-tuple-element.152.vec_ref, bf16[768,2304]{1,0:T(8,128)(2,1)} %get-tuple-element.247.w_ref, ...), custom_call_target="tpu_custom_call" | custom-call | flops 9000000159744 | bytes 1048576 | tf_op jit(solution)/shard_map/grad_input/pallas_call | solution.py:144
  204.1 1.4 gradient_sums.26
  208.7 10.5 %collective-permute-done.42.refs_3_ = bf16[48,2304]{1,0:T(8,128)(2,1)S(1)} collective-permute-done((bf16[48,2304]{1,0:T(8,128)(2,1)S(1)}, bf16[48,2304]{1,0:T(8,128)(2,1)S(1)}, u32[]{:S(2)}, u32[]{:S(2)}) %collective-permute-start.42) | collective-permute-done | bytes 221216 | tf_op jit(solution)/shard_map/ppermute | solution.py:971
  220.4 2.4 collective-permute-start.43
  222.9 1.8 last_down.1
  224.7 5.6 %collective-permute-done.43.refs_1_ = bf16[48,2304]{1,0:T(8,128)(2,1)S(1)} collective-permute-done((bf16[48,2304]{1,0:T(8,128)(2,1)S(1)}, bf16[48,2304]{1,0:T(8,128)(2,1)S(1)}, u32[]{:S(2)}, u32[]{:S(2)}) %collective-permute-start.43) | collective-permute-done | bytes 221216 | tf_op jit(solution)/shard_map/ppermute | solution.py:971
  230.4 5.9 %collective-permute-done.45.refs_1_ = bf16[48,2304]{1,0:T(8,128)(2,1)S(1)} collective-permute-done((bf16[48,2304]{1,0:T(8,128)(2,1)S(1)}, bf16[48,2304]{1,0:T(8,128)(2,1)S(1)}, u32[]{:S(2)}, u32[]{:S(2)}) %collective-permute-start.45) | collective-permute-done | bytes 221216 | tf_op jit(solution)/shard_map/ppermute | solution.py:971
  237.3 3.2 %last_up.1 = (f32[192,3072]{1,0:T(8,128)}, f32[192,768]{1,0:T(8,128)}, f32[192,128]{1,0:T(8,128)}, f32[192]{0:T(256)}) custom-call(bf16[192,3072]{1,0:T(8,128)(2,1)} %refs_0_.9, bf16[192]{0:T(256)(128)(2,1)S(1)} %copy-done, bf16[96,3968]{1,0:T(8,128)(2,1)S(1)} %get-tuple-element.259.refs_2_, bf16[96,3968]{1,0:T(8,128)(2,1)S(1)} %collective-permute-done.47.refs_3_), custom_call_target="tpu_custom_call" | custom-call | bytes 2703744 | tf_op jit(solution)/shard_map/last_up/pallas_call | solution.py:820
  243.1 3.1 %collective-permute-done.46.refs_3_ = bf16[96,2304]{1,0:T(8,128)(2,1)S(1)} collective-permute-done((bf16[96,2304]{1,0:T(8,128)(2,1)S(1)}, bf16[96,2304]{1,0:T(8,128)(2,1)S(1)}, u32[]{:S(2)}, u32[]{:S(2)}) %collective-permute-start.46) | collective-permute-done | bytes 442400 | tf_op jit(solution)/shard_map/ppermute | solution.py:971
  246.2 2.6 %last_qkv.1 = (f32[192,2304]{1,0:T(8,128)}, f32[192]{0:T(256)}) custom-call(bf16[192,2304]{1,0:T(8,128)(2,1)} %refs_0_.8, bf16[192]{0:T(256)(128)(2,1)S(1)} %copy-done.1, bf16[96,2304]{1,0:T(8,128)(2,1)S(1)} %gradient_sums.29.refs_2_, bf16[96,2304]{1,0:T(8,128)(2,1)S(1)} %collective-permute-done.46.refs_3_), custom_call_target="tpu_custom_call" | custom-call | bytes 1769856 | tf_op jit(solution)/shard_map/last_qkv/pallas_call | solution.py:820
  (117 shorter events, 30.6 us)
Async XLA Ops:
  2.4 11.7 %collective-permute-start.1 = (bf16[64,2304]{1,0:T(8,128)(2,1)}, bf16[64,2304]{1,0:T(8,128)(2,1)}, u32[]{:S(2)}, u32[]{:S(2)}) collective-permute-start(bf16[64,2304]{1,0:T(8,128)(2,1)} %constant_dynamic-slice_fusion), channel_id=1, source_target_pairs={{0,2},{1,3},{2,0},{3,1},{4,6},{5,7},{6,4},{7,5},{8,10},{9,11},{10,... | collective-permute-start | bytes 884744 | tf_op jit(solution)/shard_map/ppermute | solution.py:971
  5.3 6.7 %collective-permute-start.5 = (bf16[192,768]{1,0:T(8,128)(2,1)}, bf16[192,768]{1,0:T(8,128)(2,1)}, u32[]{:S(2)}, u32[]{:S(2)}) collective-permute-start(bf16[192,768]{1,0:T(8,128)(2,1)} %refs_0_.6), channel_id=1, source_target_pairs={{0,1},{1,0},{2,3},{3,2},{4,5},{5,4},{6,7},{7,6},{8,9},{9,8},{10,11... | collective-permute-start | bytes 884744 | tf_op jit(solution)/shard_map/ppermute | solution.py:971
  7.7 4.2 %collective-permute-start.3 = (bf16[8,2304]{1,0:T(8,128)(2,1)}, bf16[8,2304]{1,0:T(8,128)(2,1)}, u32[]{:S(2)}, u32[]{:S(2)}) collective-permute-start(bf16[8,2304]{1,0:T(8,128)(2,1)} %get-tuple-element.146.refs_0_), channel_id=1, source_target_pairs={{0,1},{1,0},{2,3},{3,2},{4,5},{5,4},{6,7},{7,6},{8,9},{9,8},{10,11... | collective-permute-start | bytes 110600 | tf_op jit(solution)/shard_map/ppermute | solution.py:971
  8.2 6.2 %collective-permute-start.2 = (bf16[192,2304]{1,0:T(8,128)(2,1)}, bf16[192,2304]{1,0:T(8,128)(2,1)}, u32[]{:S(2)}, u32[]{:S(2)}) collective-permute-start(bf16[192,2304]{1,0:T(8,128)(2,1)} %refs_0_.8), channel_id=1, source_target_pairs={{0,1},{1,0},{2,3},{3,2},{4,5},{5,4},{6,7},{7,6},{8,9},{9,8},{10,11... | collective-permute-start | bytes 2654216 | tf_op jit(solution)/shard_map/ppermute | solution.py:971
  8.2 6.2 %collective-permute-start.4 = (bf16[192,3072]{1,0:T(8,128)(2,1)}, bf16[192,3072]{1,0:T(8,128)(2,1)}, u32[]{:S(2)}, u32[]{:S(2)}) collective-permute-start(bf16[192,3072]{1,0:T(8,128)(2,1)} %refs_0_.9), channel_id=1, source_target_pairs={{0,1},{1,0},{2,3},{3,2},{4,5},{5,4},{6,7},{7,6},{8,9},{9,8},{10,11... | collective-permute-start | bytes 3538952 | tf_op jit(solution)/shard_map/ppermute | solution.py:971
  12.0 10.7 %collective-permute-start.6 = (bf16[72,2304]{1,0:T(8,128)(2,1)S(1)}, bf16[72,2304]{1,0:T(8,128)(2,1)S(1)}, u32[]{:S(2)}, u32[]{:S(2)}) collective-permute-start(bf16[72,2304]{1,0:T(8,128)(2,1)S(1)} %get-tuple-element.141), channel_id=1, source_target_pairs={{0,2},{1,3},{2,0},{3,1},{4,6},{5,7},{6,4},{7,5},{8,10},{9,11},{10,... | collective-permute-start | bytes 995336 | tf_op jit(solution)/shard_map/ppermute | solution.py:971
  12.0 24.6 %collective-permute-start = (bf16[64,3072]{1,0:T(8,128)(2,1)}, bf16[64,3072]{1,0:T(8,128)(2,1)}, u32[]{:S(2)}, u32[]{:S(2)}) collective-permute-start(bf16[64,3072]{1,0:T(8,128)(2,1)} %get-tuple-element.143), channel_id=1, source_target_pairs={{0,2},{1,3},{2,0},{3,1},{4,6},{5,7},{6,4},{7,5},{8,10},{9,11},{10,... | collective-permute-start | bytes 1179656 | tf_op jit(solution)/shard_map/ppermute | solution.py:971
  14.1 35.5 %collective-permute-start.13 = (bf16[64,3072]{1,0:T(8,128)(2,1)}, bf16[64,3072]{1,0:T(8,128)(2,1)}, u32[]{:S(2)}, u32[]{:S(2)}) collective-permute-start(bf16[64,3072]{1,0:T(8,128)(2,1)} %get-tuple-element.164), channel_id=1, source_target_pairs={{0,2},{1,3},{2,0},{3,1},{4,6},{5,7},{6,4},{7,5},{8,10},{9,11},{10,... | collective-permute-start | bytes 1179656 | tf_op jit(solution)/shard_map/ppermute | solution.py:971
  14.4 8.8 %collective-permute-start.8 = (bf16[64,2304]{1,0:T(8,128)(2,1)}, bf16[64,2304]{1,0:T(8,128)(2,1)S(1)}, u32[]{:S(2)}, u32[]{:S(2)}) collective-permute-start(bf16[64,2304]{1,0:T(8,128)(2,1)} %collective-permute-done.1.refs_6_), channel_id=1, source_target_pairs={{0,4},{4,0},{8,12},{12,8},{16,20},{20,16},{24,28},{28,24},{1,5},{5... | collective-permute-start | bytes 884744 | tf_op jit(solution)/shard_map/ppermute | solution.py:971
  22.7 2.1 collective-permute-start.7
  22.7 2.6 %collective-permute-start.9 = (bf16[64,2304]{1,0:T(8,128)(2,1)}, bf16[64,2304]{1,0:T(8,128)(2,1)S(1)}, u32[]{:S(2)}, u32[]{:S(2)}) collective-permute-start(bf16[64,2304]{1,0:T(8,128)(2,1)} %collective-permute-done.1.refs_6_), channel_id=1, source_target_pairs={{0,1},{1,0},{2,3},{3,2},{4,5},{5,4},{6,7},{7,6},{8,9},{9,8},{10,11... | collective-permute-start | bytes 884744 | tf_op jit(solution)/shard_map/ppermute | solution.py:971
  23.2 2.1 collective-permute-start.10
  24.7 25.4 %collective-permute-start.11 = (bf16[192,768]{1,0:T(8,128)(2,1)}, bf16[192,768]{1,0:T(8,128)(2,1)}, u32[]{:S(2)}, u32[]{:S(2)}) collective-permute-start(bf16[192,768]{1,0:T(8,128)(2,1)} %refs_0_.6), channel_id=1, source_target_pairs={{0,2},{1,3},{2,0},{3,1},{4,6},{5,7},{6,4},{7,5},{8,10},{9,11},{10,... | collective-permute-start | bytes 884744 | tf_op jit(solution)/shard_map/ppermute | solution.py:971
  36.6 13.5 %collective-permute-start.14 = (bf16[64,3072]{1,0:T(8,128)(2,1)}, bf16[64,3072]{1,0:T(8,128)(2,1)}, u32[]{:S(2)}, u32[]{:S(2)}) collective-permute-start(bf16[64,3072]{1,0:T(8,128)(2,1)} %collective-permute-done.refs_6_), channel_id=1, source_target_pairs={{0,4},{4,0},{8,12},{12,8},{16,20},{20,16},{24,28},{28,24},{1,5},{5... | collective-permute-start | bytes 1179656 | tf_op jit(solution)/shard_map/ppermute | solution.py:971
  49.5 4.4 %collective-permute-start.15 = (bf16[64,3072]{1,0:T(8,128)(2,1)}, bf16[64,3072]{1,0:T(8,128)(2,1)S(1)}, u32[]{:S(2)}, u32[]{:S(2)}) collective-permute-start(bf16[64,3072]{1,0:T(8,128)(2,1)} %collective-permute-done.refs_6_), channel_id=1, source_target_pairs={{0,1},{1,0},{2,3},{3,2},{4,5},{5,4},{6,7},{7,6},{8,9},{9,8},{10,11... | collective-permute-start | bytes 1179656 | tf_op jit(solution)/shard_map/ppermute | solution.py:971
  49.6 4.3 %collective-permute-start.16 = (bf16[64,3072]{1,0:T(8,128)(2,1)}, bf16[64,3072]{1,0:T(8,128)(2,1)S(1)}, u32[]{:S(2)}, u32[]{:S(2)}) collective-permute-start(bf16[64,3072]{1,0:T(8,128)(2,1)} %collective-permute-done.13.refs_7_), channel_id=1, source_target_pairs={{0,1},{1,0},{2,3},{3,2},{4,5},{5,4},{6,7},{7,6},{8,9},{9,8},{10,11... | collective-permute-start | bytes 1179656 | tf_op jit(solution)/shard_map/ppermute | solution.py:971
  50.1 3.8 %collective-permute-start.17 = (bf16[64,3072]{1,0:T(8,128)(2,1)}, bf16[64,3072]{1,0:T(8,128)(2,1)S(1)}, u32[]{:S(2)}, u32[]{:S(2)}) collective-permute-start(bf16[64,3072]{1,0:T(8,128)(2,1)} %collective-permute-done.14.refs_8_), channel_id=1, source_target_pairs={{0,1},{1,0},{2,3},{3,2},{4,5},{5,4},{6,7},{7,6},{8,9},{9,8},{10,11... | collective-permute-start | bytes 1179656 | tf_op jit(solution)/shard_map/ppermute | solution.py:971
  50.2 3.7 %collective-permute-start.12 = (bf16[192,768]{1,0:T(8,128)(2,1)}, bf16[192,768]{1,0:T(8,128)(2,1)S(1)}, u32[]{:S(2)}, u32[]{:S(2)}) collective-permute-start(bf16[192,768]{1,0:T(8,128)(2,1)} %collective-permute-done.11.refs_2_), channel_id=1, source_target_pairs={{0,1},{1,0},{2,3},{3,2},{4,5},{5,4},{6,7},{7,6},{8,9},{9,8},{10,11... | collective-permute-start | bytes 884744 | tf_op jit(solution)/shard_map/ppermute | solution.py:971
  52.3 29.7 %collective-permute-start.21 = (bf16[768,768]{1,0:T(8,128)(2,1)}, bf16[768,768]{1,0:T(8,128)(2,1)}, u32[]{:S(2)}, u32[]{:S(2)}) collective-permute-start(bf16[768,768]{1,0:T(8,128)(2,1)} %refs_0_.7), channel_id=1, source_target_pairs={{0,2},{1,3},{2,0},{3,1},{4,6},{5,7},{6,4},{7,5},{8,10},{9,11},{10,... | collective-permute-start | bytes 3538952 | tf_op jit(solution)/shard_map/ppermute | solution.py:971
  78.0 4.9 %collective-permute-start.18 = (bf16[2,768,768]{2,1,0:T(8,128)(2,1)}, bf16[2,768,768]{2,1,0:T(8,128)(2,1)}, u32[]{:S(2)}, u32[]{:S(2)}) collective-permute-start(bf16[2,768,768]{2,1,0:T(8,128)(2,1)} %grad_down.2), channel_id=1, source_target_pairs={{0,1},{1,0},{2,3},{3,2},{4,5},{5,4},{6,7},{7,6},{8,9},{9,8},{10,11... | collective-permute-start | bytes 7077896 | tf_op jit(solution)/shard_map/ppermute | solution.py:971
  81.4 5.8 %collective-permute-start.20 = (bf16[768,768]{1,0:T(8,128)(2,1)S(1)}, bf16[768,768]{1,0:T(8,128)(2,1)S(1)}, u32[]{:S(2)}, u32[]{:S(2)}) collective-permute-start(bf16[768,768]{1,0:T(8,128)(2,1)S(1)} %copy-done.10), channel_id=1, source_target_pairs={{0,1},{1,0},{2,3},{3,2},{4,5},{5,4},{6,7},{7,6},{8,9},{9,8},{10,11... | collective-permute-start | bytes 3538952 | tf_op jit(solution)/shard_map/ppermute | solution.py:971
  82.0 5.2 %collective-permute-start.22 = (bf16[768,768]{1,0:T(8,128)(2,1)}, bf16[768,768]{1,0:T(8,128)(2,1)S(1)}, u32[]{:S(2)}, u32[]{:S(2)}) collective-permute-start(bf16[768,768]{1,0:T(8,128)(2,1)} %collective-permute-done.21.refs_2_), channel_id=1, source_target_pairs={{0,1},{1,0},{2,3},{3,2},{4,5},{5,4},{6,7},{7,6},{8,9},{9,8},{10,11... | collective-permute-start | bytes 3538952 | tf_op jit(solution)/shard_map/ppermute | solution.py:971
  85.8 21.9 %collective-permute-start.19 = (bf16[768,384]{1,0:T(8,128)(2,1)}, bf16[768,384]{1,0:T(8,128)(2,1)}, u32[]{:S(2)}, u32[]{:S(2)}) collective-permute-start(bf16[768,384]{1,0:T(8,128)(2,1)} %get-tuple-element.172), channel_id=1, source_target_pairs={{0,2},{1,3},{2,0},{3,1},{4,6},{5,7},{6,4},{7,5},{8,10},{9,11},{10,... | collective-permute-start | bytes 1769480 | tf_op jit(solution)/shard_map/ppermute | solution.py:971
  86.5 21.2 %collective-permute-start.23 = (bf16[2,384,384]{2,1,0:T(8,128)(2,1)}, bf16[2,384,384]{2,1,0:T(8,128)(2,1)}, u32[]{:S(2)}, u32[]{:S(2)}) collective-permute-start(bf16[2,384,384]{2,1,0:T(8,128)(2,1)} %get-tuple-element.173), channel_id=1, source_target_pairs={{0,4},{4,0},{8,12},{12,8},{16,20},{20,16},{24,28},{28,24},{1,5},{5... | collective-permute-start | bytes 1769480 | tf_op jit(solution)/shard_map/ppermute | solution.py:971
  109.9 10.6 %collective-permute-start.25 = (bf16[384,384]{1,0:T(8,128)(2,1)}, bf16[384,384]{1,0:T(8,128)(2,1)}, u32[]{:S(2)}, u32[]{:S(2)}) collective-permute-start(bf16[384,384]{1,0:T(8,128)(2,1)} %get-tuple-element.185), channel_id=1, source_target_pairs={{0,4},{4,0},{8,12},{12,8},{16,20},{20,16},{24,28},{28,24},{1,5},{5... | collective-permute-start | bytes 884744 | tf_op jit(solution)/shard_map/ppermute | solution.py:971
  111.2 9.3 %collective-permute-start.26 = (bf16[384,384]{1,0:T(8,128)(2,1)}, bf16[384,384]{1,0:T(8,128)(2,1)}, u32[]{:S(2)}, u32[]{:S(2)}) collective-permute-start(bf16[384,384]{1,0:T(8,128)(2,1)} %get-tuple-element.186), channel_id=1, source_target_pairs={{0,2},{1,3},{2,0},{3,1},{4,6},{5,7},{6,4},{7,5},{8,10},{9,11},{10,... | collective-permute-start | bytes 884744 | tf_op jit(solution)/shard_map/ppermute | solution.py:971
  120.4 5.6 %collective-permute-start.24 = (bf16[2,192,3968]{2,1,0:T(8,128)(2,1)S(1)}, bf16[2,192,3968]{2,1,0:T(8,128)(2,1)S(1)}, u32[]{:S(2)}, u32[]{:S(2)}) collective-permute-start(bf16[2,192,3968]{2,1,0:T(8,128)(2,1)S(1)} %get-tuple-element.192), channel_id=1, source_target_pairs={{0,1},{1,0},{2,3},{3,2},{4,5},{5,4},{6,7},{7,6},{8,9},{9,8},{10,11... | collective-permute-start | bytes 9142280 | tf_op jit(solution)/shard_map/ppermute | solution.py:971
  122.4 21.8 %collective-permute-start.28 = (bf16[192,768]{1,0:T(8,128)(2,1)}, bf16[192,768]{1,0:T(8,128)(2,1)}, u32[]{:S(2)}, u32[]{:S(2)}) collective-permute-start(bf16[192,768]{1,0:T(8,128)(2,1)} %get-tuple-element.198), channel_id=1, source_target_pairs={{0,8},{4,12},{8,0},{12,4},{16,24},{20,28},{24,16},{28,20},{1,9},{5... | collective-permute-start | bytes 884744 | tf_op jit(solution)/shard_map/ppermute | solution.py:971
  127.5 21.3 %collective-permute-start.29 = (bf16[2,96,1920]{2,1,0:T(8,128)(2,1)}, bf16[2,96,1920]{2,1,0:T(8,128)(2,1)}, u32[]{:S(2)}, u32[]{:S(2)}) collective-permute-start(bf16[2,96,1920]{2,1,0:T(8,128)(2,1)} %get-tuple-element.203), channel_id=1, source_target_pairs={{0,4},{4,0},{8,12},{12,8},{16,20},{20,16},{24,28},{28,24},{1,5},{5... | collective-permute-start | bytes 2211848 | tf_op jit(solution)/shard_map/ppermute | solution.py:971
  128.2 20.6 %collective-permute-start.27 = (bf16[192,2048]{1,0:T(8,128)(2,1)}, bf16[192,2048]{1,0:T(8,128)(2,1)}, u32[]{:S(2)}, u32[]{:S(2)}) collective-permute-start(bf16[192,2048]{1,0:T(8,128)(2,1)} %get-tuple-element.202), channel_id=1, source_target_pairs={{0,2},{1,3},{2,0},{3,1},{4,6},{5,7},{6,4},{7,5},{8,10},{9,11},{10,... | collective-permute-start | bytes 2359304 | tf_op jit(solution)/shard_map/ppermute | solution.py:971
  146.2 24.9 %collective-permute-start.33 = (bf16[192,768]{1,0:T(8,128)(2,1)}, bf16[192,768]{1,0:T(8,128)(2,1)}, u32[]{:S(2)}, u32[]{:S(2)}) collective-permute-start(bf16[192,768]{1,0:T(8,128)(2,1)} %gradient_sums.19.refs_0_), channel_id=1, source_target_pairs={{0,16},{4,20},{8,24},{12,28},{16,0},{20,4},{24,8},{28,12},{1,17},{... | collective-permute-start | bytes 884744 | tf_op jit(solution)/shard_map/ppermute | solution.py:971
  151.1 11.7 %collective-permute-start.31 = (bf16[96,1920]{1,0:T(8,128)(2,1)}, bf16[96,1920]{1,0:T(8,128)(2,1)}, u32[]{:S(2)}, u32[]{:S(2)}) collective-permute-start(bf16[96,1920]{1,0:T(8,128)(2,1)} %get-tuple-element.213), channel_id=1, source_target_pairs={{0,2},{1,3},{2,0},{3,1},{4,6},{5,7},{6,4},{7,5},{8,10},{9,11},{10,... | collective-permute-start | bytes 1105928 | tf_op jit(solution)/shard_map/ppermute | solution.py:971
  152.5 10.4 %collective-permute-start.30 = (bf16[96,2048]{1,0:T(8,128)(2,1)}, bf16[96,2048]{1,0:T(8,128)(2,1)}, u32[]{:S(2)}, u32[]{:S(2)}) collective-permute-start(bf16[96,2048]{1,0:T(8,128)(2,1)} %get-tuple-element.212), channel_id=1, source_target_pairs={{0,4},{4,0},{8,12},{12,8},{16,20},{20,16},{24,28},{28,24},{1,5},{5... | collective-permute-start | bytes 1179656 | tf_op jit(solution)/shard_map/ppermute | solution.py:971
  165.0 9.8 %collective-permute-start.32 = (bf16[48,3968]{1,0:T(8,128)(2,1)}, bf16[48,3968]{1,0:T(8,128)(2,1)}, u32[]{:S(2)}, u32[]{:S(2)}) collective-permute-start(bf16[48,3968]{1,0:T(8,128)(2,1)} %get-tuple-element.219), channel_id=1, source_target_pairs={{0,8},{4,12},{8,0},{12,4},{16,24},{20,28},{24,16},{28,20},{1,9},{5... | collective-permute-start | bytes 1142792 | tf_op jit(solution)/shard_map/ppermute | solution.py:971
  171.0 3.9 %collective-permute-start.34 = (bf16[2,192,2304]{2,1,0:T(8,128)(2,1)S(1)}, bf16[2,192,2304]{2,1,0:T(8,128)(2,1)S(1)}, u32[]{:S(2)}, u32[]{:S(2)}) collective-permute-start(bf16[2,192,2304]{2,1,0:T(8,128)(2,1)S(1)} %get-tuple-element.228), channel_id=1, source_target_pairs={{0,1},{1,0},{2,3},{3,2},{4,5},{5,4},{6,7},{7,6},{8,9},{9,8},{10,11... | collective-permute-start | bytes 5308424 | tf_op jit(solution)/shard_map/ppermute | solution.py:971
  172.9 16.4 %collective-permute-start.35 = (bf16[192,768]{1,0:T(8,128)(2,1)}, bf16[192,768]{1,0:T(8,128)(2,1)}, u32[]{:S(2)}, u32[]{:S(2)}) collective-permute-start(bf16[192,768]{1,0:T(8,128)(2,1)} %gradient_sums.22.refs_0_), channel_id=1, source_target_pairs={{0,8},{4,12},{8,0},{12,4},{16,24},{20,28},{24,16},{28,20},{1,9},{5... | collective-permute-start | bytes 884744 | tf_op jit(solution)/shard_map/ppermute | solution.py:971
  177.0 27.0 %collective-permute-start.38 = (bf16[48,3968]{1,0:T(8,128)(2,1)}, bf16[48,3968]{1,0:T(8,128)(2,1)}, u32[]{:S(2)}, u32[]{:S(2)}) collective-permute-start(bf16[48,3968]{1,0:T(8,128)(2,1)} %get-tuple-element.233.refs_0_), channel_id=1, source_target_pairs={{0,16},{4,20},{8,24},{12,28},{16,0},{20,4},{24,8},{28,12},{1,17},{... | collective-permute-start | bytes 1142792 | tf_op jit(solution)/shard_map/ppermute | solution.py:971
  177.9 12.7 %collective-permute-start.36 = (bf16[192,1152]{1,0:T(8,128)(2,1)}, bf16[192,1152]{1,0:T(8,128)(2,1)}, u32[]{:S(2)}, u32[]{:S(2)}) collective-permute-start(bf16[192,1152]{1,0:T(8,128)(2,1)} %get-tuple-element.234), channel_id=1, source_target_pairs={{0,2},{1,3},{2,0},{3,1},{4,6},{5,7},{6,4},{7,5},{8,10},{9,11},{10,... | collective-permute-start | bytes 1327112 | tf_op jit(solution)/shard_map/ppermute | solution.py:971
  179.3 12.0 %collective-permute-start.37 = (bf16[2,96,1152]{2,1,0:T(8,128)(2,1)}, bf16[2,96,1152]{2,1,0:T(8,128)(2,1)}, u32[]{:S(2)}, u32[]{:S(2)}) collective-permute-start(bf16[2,96,1152]{2,1,0:T(8,128)(2,1)} %get-tuple-element.235), channel_id=1, source_target_pairs={{0,4},{4,0},{8,12},{12,8},{16,20},{20,16},{24,28},{28,24},{1,5},{5... | collective-permute-start | bytes 1327112 | tf_op jit(solution)/shard_map/ppermute | solution.py:971
  193.2 10.9 %collective-permute-start.39 = (bf16[96,1152]{1,0:T(8,128)(2,1)}, bf16[96,1152]{1,0:T(8,128)(2,1)}, u32[]{:S(2)}, u32[]{:S(2)}) collective-permute-start(bf16[96,1152]{1,0:T(8,128)(2,1)} %get-tuple-element.243), channel_id=1, source_target_pairs={{0,4},{4,0},{8,12},{12,8},{16,20},{20,16},{24,28},{28,24},{1,5},{5... | collective-permute-start | bytes 663560 | tf_op jit(solution)/shard_map/ppermute | solution.py:971
  194.2 9.9 %collective-permute-start.40 = (bf16[96,1152]{1,0:T(8,128)(2,1)}, bf16[96,1152]{1,0:T(8,128)(2,1)}, u32[]{:S(2)}, u32[]{:S(2)}) collective-permute-start(bf16[96,1152]{1,0:T(8,128)(2,1)} %get-tuple-element.244), channel_id=1, source_target_pairs={{0,2},{1,3},{2,0},{3,1},{4,6},{5,7},{6,4},{7,5},{8,10},{9,11},{10,... | collective-permute-start | bytes 663560 | tf_op jit(solution)/shard_map/ppermute | solution.py:971
  205.5 13.7 %collective-permute-start.41 = (bf16[48,3968]{1,0:T(8,128)(2,1)S(1)}, bf16[48,3968]{1,0:T(8,128)(2,1)S(1)}, u32[]{:S(2)}, u32[]{:S(2)}) collective-permute-start(bf16[48,3968]{1,0:T(8,128)(2,1)S(1)} %get-tuple-element.253.refs_0_), channel_id=1, source_target_pairs={{0,8},{4,12},{8,0},{12,4},{16,24},{20,28},{24,16},{28,20},{1,9},{5... | collective-permute-start | bytes 1142792 | tf_op jit(solution)/shard_map/ppermute | solution.py:971
  206.3 12.9 %collective-permute-start.42 = (bf16[48,2304]{1,0:T(8,128)(2,1)S(1)}, bf16[48,2304]{1,0:T(8,128)(2,1)S(1)}, u32[]{:S(2)}, u32[]{:S(2)}) collective-permute-start(bf16[48,2304]{1,0:T(8,128)(2,1)S(1)} %get-tuple-element.254), channel_id=1, source_target_pairs={{0,8},{4,12},{8,0},{12,4},{16,24},{20,28},{24,16},{28,20},{1,9},{5... | collective-permute-start | bytes 663560 | tf_op jit(solution)/shard_map/ppermute | solution.py:971
  207.6 15.3 %collective-permute-start.44 = (bf16[384,768]{1,0:T(8,128)(2,1)S(1)}, bf16[384,768]{1,0:T(8,128)(2,1)S(1)}, u32[]{:S(2)}, u32[]{:S(2)}) collective-permute-start(bf16[384,768]{1,0:T(8,128)(2,1)S(1)} %gradient_sums.24.refs_0_), channel_id=1, source_target_pairs={{0,4},{4,0},{8,12},{12,8},{16,20},{20,16},{24,28},{28,24},{1,5},{5... | collective-permute-start | bytes 1769480 | tf_op jit(solution)/shard_map/ppermute | solution.py:971
  219.3 18.0 %collective-permute-start.47 = (bf16[96,3968]{1,0:T(8,128)(2,1)S(1)}, bf16[96,3968]{1,0:T(8,128)(2,1)S(1)}, u32[]{:S(2)}, u32[]{:S(2)}) collective-permute-start(bf16[96,3968]{1,0:T(8,128)(2,1)S(1)} %get-tuple-element.259.refs_2_), channel_id=1, source_target_pairs={{0,4},{4,0},{8,12},{12,8},{16,20},{20,16},{24,28},{28,24},{1,5},{5... | collective-permute-start | bytes 2285576 | tf_op jit(solution)/shard_map/ppermute | solution.py:971
  220.4 9.8 %collective-permute-start.43 = (bf16[48,2304]{1,0:T(8,128)(2,1)S(1)}, bf16[48,2304]{1,0:T(8,128)(2,1)S(1)}, u32[]{:S(2)}, u32[]{:S(2)}) collective-permute-start(bf16[48,2304]{1,0:T(8,128)(2,1)S(1)} %get-tuple-element.258.refs_0_), channel_id=1, source_target_pairs={{0,16},{4,20},{8,24},{12,28},{16,0},{20,4},{24,8},{28,12},{1,17},{... | collective-permute-start | bytes 663560 | tf_op jit(solution)/shard_map/ppermute | solution.py:971
  230.3 6.0 %collective-permute-start.45 = (bf16[48,2304]{1,0:T(8,128)(2,1)S(1)}, bf16[48,2304]{1,0:T(8,128)(2,1)S(1)}, u32[]{:S(2)}, u32[]{:S(2)}) collective-permute-start(bf16[48,2304]{1,0:T(8,128)(2,1)S(1)} %gradient_sums.28.refs_0_), channel_id=1, source_target_pairs={{0,8},{4,12},{8,0},{12,4},{16,24},{20,28},{24,16},{28,20},{1,9},{5... | collective-permute-start | bytes 663560 | tf_op jit(solution)/shard_map/ppermute | solution.py:971
  236.3 9.9 %collective-permute-start.46 = (bf16[96,2304]{1,0:T(8,128)(2,1)S(1)}, bf16[96,2304]{1,0:T(8,128)(2,1)S(1)}, u32[]{:S(2)}, u32[]{:S(2)}) collective-permute-start(bf16[96,2304]{1,0:T(8,128)(2,1)S(1)} %gradient_sums.29.refs_2_), channel_id=1, source_target_pairs={{0,4},{4,0},{8,12},{12,8},{16,20},{20,16},{24,28},{28,24},{1,5},{5... | collective-permute-start | bytes 1327112 | tf_op jit(solution)/shard_map/ppermute | solution.py:971
  (11 other events, 105.4 us)

commit v6 on v5

--- a/solution.py
+++ b/solution.py
@@ -1076,7 +1076,7 @@
     cosine = jnp.tile(cosine, (1, 4))
     sine = jnp.concatenate([-sine, sine, -sine, sine], axis=1)
 
-    first = lax.dynamic_slice_in_dim(w_qkv, bit * size, size, 0)
+    (first,) = thirds_call(index, w_qkv, (1,))
     got_first = moves.swap(first, "narrow", 2)
     second, small = vector_call(ready(first), w_qkv, gain_attn, gain_mlp, b_down, b_up)
     got_second = moves.swap(second, "narrow", 2)

time: 250 us -> 251 us (level)
  Pallas kernels: 162 us -> 165 us
    pallas_call x14 -> x15, Pallas kernels: 130 us -> 133 us  [run(): return fun(index, *args)]
where the time goes in v6:
time: 251 us; the launch traced here: 250 us
  Pallas kernels  165 us (66%)
  starting transfers between devices  41 us (16%)
  waiting for transfers between devices  34.5 us (14%)
  local copies, waits for them, and re-layouts  5.43 us (2%)
  other arithmetic  2.89 us (1%)
    pallas_call x15, Pallas kernels, run(): return fun(index, *args)  133 us
    ppermute x48, starting transfers between devices, swap(): return lax.ppermute(value, axis, [(i, i ^ bit) for i in range(size)])  41 us
    ppermute x48, waiting for transfers between devices, swap(): return lax.ppermute(value, axis, [(i, i ^ bit) for i in range(size)])  34.5 us
    pallas_call x18, Pallas kernels, whole_call(): pl.pallas_call(run, name=name, in_specs=[pl.BlockSpec(memory_space=pltpu....  31.6 us
  transfers between devices with their start and end apart: 48, of which 10 were waited for; matrix products, arithmetic and copies ran while one was open for 3% of the time, Pallas kernels for 62%

profile of v6, /device:TPU:0, one launch (start us, length us, event | category | flops | bytes accessed | tf_op | source)
XLA Modules:
  0.0 250.1 jit_solution(3969070149051128652)
XLA Ops:
  0.8 2.2 next_message.2
  3.0 3.0 %collective-permute-start.1 = (bf16[64,2304]{1,0:T(8,128)(2,1)}, bf16[64,2304]{1,0:T(8,128)(2,1)}, u32[]{:S(2)}, u32[]{:S(2)}) collective-permute-start(bf16[64,2304]{1,0:T(8,128)(2,1)} %next_message.2), channel_id=1, source_target_pairs={{0,2},{1,3},{2,0},{3,1},{4,6},{5,7},{6,4},{7,5},{8,10},{9,11},{10,... | collective-permute-start | bytes 884744 | tf_op jit(solution)/shard_map/ppermute | solution.py:971
  6.0 2.3 vector_message.1
  9.3 2.6 %next_message.3 = (bf16[64,3072]{1,0:T(8,128)(2,1)}, bf16[64,3072]{1,0:T(8,128)(2,1)}) custom-call(s32[27]{0:T(128)S(1)} %stack.81.idx_ref, bf16[192,3072]{1,0:T(8,128)(2,1)} %refs_0_.11, bf16[192,3072]{1,0:T(8,128)(2,1)} %refs_0_.11), custom_call_target="tpu_custom_call" | custom-call | flops 1500000026624 | bytes 1048576 | tf_op jit(solution)/shard_map/next_message/pallas_call | solution.py:144
  12.6 2.0 collective-permute-start
  15.1 1.5 collective-permute-start.8
  19.7 3.6 %collective-permute-done.6.refs_2_.refs_7_ = bf16[72,2304]{1,0:T(8,128)(2,1)S(1)} collective-permute-done((bf16[72,2304]{1,0:T(8,128)(2,1)S(1)}, bf16[72,2304]{1,0:T(8,128)(2,1)S(1)}, u32[]{:S(2)}, u32[]{:S(2)}) %collective-permute-start.6) | collective-permute-done | bytes 331808 | tf_op jit(solution)/shard_map/ppermute | solution.py:971
  25.9 11.3 %norm_qkv.1 = (bf16[1024,2304]{1,0:T(8,128)(2,1)S(1)}, bf16[768,1024]{1,0:T(8,128)(2,1)}, f32[8,3072]{1,0:T(8,128)}, bf16[768,2304]{1,0:T(8,128)(2,1)}) custom-call(s32[27]{0:T(128)S(1)} %stack.81.idx_ref, bf16[1024,768]{1,0:T(8,128)(2,1)} %bitcast.34, f32[512,128]{1,0:T(8,128)} %copy.31.cos_ref, f32[512,128]{1,0:T(8,128)} %pad_maximum_fusion.sin_ref, ...), custom_call_target="tpu_custom_call" | custom-call | flops 6999999774720 | bytes 1048576 | tf_op jit(solution)/shard_map/norm_qkv/pallas_call | solution.py:144
  37.2 1.6 collective-permute-start.14
  38.8 11.3 %attention.1 = (bf16[1024,768]{1,0:T(8,128)(2,1)}, bf16[768,1024]{1,0:T(8,128)(2,1)}, f32[6,2,1024]{2,1,0:T(2,128)}) custom-call(s32[27]{0:T(128)S(1)} %stack.81.idx_ref, bf16[1024,2304]{1,0:T(8,128)(2,1)S(1)} %get-tuple-element.155.qkv_ref.q_ref.k_ref.v_ref, f32[128,128]{1,0:T(8,128)} %get-tuple-element.274.same_ref, ...), custom_call_target="tpu_custom_call" | custom-call | flops 12000000212992 | bytes 1048576 | tf_op jit(solution)/shard_map/attention/pallas_call | solution.py:144
  51.2 1.7 copy.32.dyt_ref
  52.9 1.6 collective-permute-start.21
  54.5 19.4 %feed_up.1 = (f32[1024,768]{1,0:T(8,128)}, bf16[768,1024]{1,0:T(8,128)(2,1)S(1)}, bf16[1024,3072]{1,0:T(8,128)(2,1)S(1)}, bf16[1024,3072]{1,0:T(8,128)(2,1)S(1)}...) custom-call(s32[27]{0:T(128)S(1)} %stack.81.idx_ref, bf16[1024,768]{1,0:T(8,128)(2,1)} %bitcast.35, ...), custom_call_target="tpu_custom_call" | custom-call | flops 18000000319488 | bytes 1048576 | tf_op jit(solution)/shard_map/feed_up/pallas_call | solution.py:144
  73.9 4.8 %grad_down.2 = bf16[2,768,768]{2,1,0:T(8,128)(2,1)} custom-call(s32[27]{0:T(128)S(1)} %stack.81.idx_ref, bf16[768,1024]{1,0:T(8,128)(2,1)S(1)} %copy.32.dyt_ref, bf16[1024,3072]{1,0:T(8,128)(2,1)S(1)} %get-tuple-element.167.h_ref), custom_call_target="tpu_custom_call" | custom-call | flops 3000000053248 | bytes 1048576 | tf_op jit(solution)/shard_map/grad_down/pallas_call | solution.py:144
  78.7 3.4 %grad_down.3.refs_0_ = bf16[2,768,768]{2,1,0:T(8,128)(2,1)S(1)} custom-call(s32[27]{0:T(128)S(1)} %stack.81.idx_ref, bf16[768,1024]{1,0:T(8,128)(2,1)S(1)} %copy.32.dyt_ref, bf16[1024,3072]{1,0:T(8,128)(2,1)S(1)} %get-tuple-element.167.h_ref), custom_call_target="tpu_custom_call" | custom-call | flops 3000000053248 | bytes 1048576 | tf_op jit(solution)/shard_map/grad_down/pallas_call | solution.py:144
  83.6 3.0 %gradient_sums.15 = (bf16[768,384]{1,0:T(8,128)(2,1)}, bf16[2,384,384]{2,1,0:T(8,128)(2,1)}, f32[768,384]{1,0:T(8,128)S(1)}, f32[2,384,384]{2,1,0:T(8,128)S(1)}) custom-call(bf16[2,768,768]{2,1,0:T(8,128)(2,1)S(1)} %grad_down.3.refs_0_, bf16[2,768,768]{2,1,0:T(8,128)(2,1)} %collective-permute-done.18.refs_1_), custom_call_target="tpu_custom_call" | custom-call | bytes 4718592 | tf_op jit(solution)/shard_map/gradient_sums/pallas_call | solution.py:820
  88.0 20.7 %feed_back.1 = (bf16[1024,3840]{1,0:T(8,128)(2,1)S(1)}, f32[1024,768]{1,0:T(8,128)}, bf16[1024,768]{1,0:T(8,128)(2,1)}, f32[2,3072]{1,0:T(2,128)S(1)}, bf16[3072,768]{1,0:T(8,128)(2,1)S(1)}) custom-call(s32[27]{0:T(128)S(1)} %stack.81.idx_ref, bf16[1024,768]{1,0:T(8,128)(2,1)} %bitcast.32, f32[1024,768]{1,0:T(8,128)} %get-tuple-element.175.x1_ref, ...), custom_call_target="tpu_custom_call" | custom-call | flops 19999999655936 | bytes 1048576 | tf_op jit(solution)/shard_map/feed_back/pallas_call | solution.py:144
  108.7 2.3 gradient_sums.16
  112.2 1.4 collective-permute-start.26
  113.6 7.9 %grad_up_out.1 = (bf16[2,192,3968]{2,1,0:T(8,128)(2,1)S(1)}, bf16[2,192,3968]{2,1,0:T(8,128)(2,1)S(1)}) custom-call(s32[27]{0:T(128)S(1)} %stack.81.idx_ref, bf16[768,1024]{1,0:T(8,128)(2,1)S(1)} %get-tuple-element.188.a_ref, bf16[768,1024]{1,0:T(8,128)(2,1)S(1)} %copy-done.7, bf16[1024,3840]{1,0:T(8,128)(2,1)S(1)} %get-tuple-element.190.du_ref, ...), custom_call_target="tpu_custom_call" | custom-call | flops 4700000223232 | bytes 1048576 | tf_op jit(solution)/shard_map/grad_up_out/pallas_call | solution.py:144
  121.6 1.8 gradient_sums.17
  123.4 1.6 collective-permute-start.28
  125.0 2.1 collective-permute-done.24.refs_1_
  127.0 1.4 gradient_sums.18
  129.9 15.3 %attention_back.2 = (bf16[1024,512]{1,0:T(8,128)(2,1)S(1)}, bf16[1024,512]{1,0:T(8,128)(2,1)S(1)}, bf16[1024,512]{1,0:T(8,128)(2,1)S(1)}) custom-call(s32[27]{0:T(128)S(1)} %stack.81.idx_ref, bf16[1024,2304]{1,0:T(8,128)(2,1)} %copy-done.4, bf16[1024,2304]{1,0:T(8,128)(2,1)} %copy-done.4, bf16[1024,2304]{1,0:T(8,128)(2,1)} %copy-done.4, ...), custom_call_target="tpu_custom_call" | custom-call | flops 14399999836160 | bytes 1048576 | tf_op jit(solution)/shard_map/attention_back/pallas_call | solution.py:144
  145.3 2.0 gradient_sums.19.refs_0_
  147.2 2.6 %collective-permute-start.33 = (bf16[192,768]{1,0:T(8,128)(2,1)}, bf16[192,768]{1,0:T(8,128)(2,1)}, u32[]{:S(2)}, u32[]{:S(2)}) collective-permute-start(bf16[192,768]{1,0:T(8,128)(2,1)} %gradient_sums.19.refs_0_), channel_id=1, source_target_pairs={{0,16},{4,20},{8,24},{12,28},{16,0},{20,4},{24,8},{28,12},{1,17},{... | collective-permute-start | bytes 884744 | tf_op jit(solution)/shard_map/ppermute | solution.py:971
  149.9 2.3 gradient_sums.20
  154.8 9.1 %attention_back.3 = (bf16[1024,256]{1,0:T(8,128)(2,1)S(1)}, bf16[1024,256]{1,0:T(8,128)(2,1)S(1)}, bf16[1024,256]{1,0:T(8,128)(2,1)S(1)}) custom-call(s32[27]{0:T(128)S(1)} %stack.81.idx_ref, bf16[1024,2304]{1,0:T(8,128)(2,1)} %copy-done.4, bf16[1024,2304]{1,0:T(8,128)(2,1)} %copy-done.4, bf16[1024,2304]{1,0:T(8,128)(2,1)} %copy-done.4, ...), custom_call_target="tpu_custom_call" | custom-call | flops 7199999918080 | bytes 1048576 | tf_op jit(solution)/shard_map/attention_back/pallas_call | solution.py:144
  163.9 2.2 gradient_sums.21
  166.1 1.6 collective-permute-start.32
  167.7 4.4 %grad_qkv.1 = (bf16[2,192,2304]{2,1,0:T(8,128)(2,1)S(1)}, bf16[2,192,2304]{2,1,0:T(8,128)(2,1)S(1)}) custom-call(s32[27]{0:T(128)S(1)} %stack.81.idx_ref, bf16[768,1024]{1,0:T(8,128)(2,1)S(1)} %copy-done.3, bf16[1024,512]{1,0:T(8,128)(2,1)S(1)} %get-tuple-element.206.refs_0_, bf16[1024,512]{1,0:T(8,128)(2,1)S(1)} %get-tuple-element.222.refs_1_, ...), custom_call_target="tpu_custom_call" | custom-call | flops 3304000061440 | bytes 1048576 | tf_op jit(solution)/shard_map/grad_qkv/pallas_call | solution.py:144
  172.2 1.8 gradient_sums.22.refs_0_
  174.5 1.5 collective-permute-done.32.refs_1_
  175.9 2.2 gradient_sums.23
  179.0 1.3 collective-permute-start.36
  181.3 9.1 %layer_output.1 = bf16[1024,768]{1,0:T(8,128)(2,1)} custom-call(s32[27]{0:T(128)S(1)} %stack.81.idx_ref, f32[1024,768]{1,0:T(8,128)} %get-tuple-element.175.x1_ref, bf16[1024,3072]{1,0:T(8,128)(2,1)} %copy-done.2, f32[8,3072]{1,0:T(8,128)} %get-tuple-element.152.vec_ref, bf16[3072,768]{1,0:T(8,128)(2,1)S(1)} %get-tuple-element.237.w_ref), custom_call_target="tpu_custom_call" | custom-call | flops 7999999967232 | bytes 1048576 | tf_op jit(solution)/shard_map/layer_output/pallas_call | solution.py:144
  192.3 2.0 gradient_sums.25
  195.9 9.3 %grad_input.1 = bf16[1024,768]{1,0:T(8,128)(2,1)} custom-call(s32[27]{0:T(128)S(1)} %stack.81.idx_ref, bf16[1024,768]{1,0:T(8,128)(2,1)} %bitcast.36, f32[1024,768]{1,0:T(8,128)} %get-tuple-element.246.dx1_ref, f32[8,3072]{1,0:T(8,128)} %get-tuple-element.152.vec_ref, bf16[768,2304]{1,0:T(8,128)(2,1)} %get-tuple-element.247.w_ref, ...), custom_call_target="tpu_custom_call" | custom-call | flops 9000000159744 | bytes 1048576 | tf_op jit(solution)/shard_map/grad_input/pallas_call | solution.py:144
  205.3 1.4 gradient_sums.26
  209.8 10.7 %collective-permute-done.42.refs_3_ = bf16[48,2304]{1,0:T(8,128)(2,1)S(1)} collective-permute-done((bf16[48,2304]{1,0:T(8,128)(2,1)S(1)}, bf16[48,2304]{1,0:T(8,128)(2,1)S(1)}, u32[]{:S(2)}, u32[]{:S(2)}) %collective-permute-start.42) | collective-permute-done | bytes 221216 | tf_op jit(solution)/shard_map/ppermute | solution.py:971
  221.6 2.6 %collective-permute-start.43 = (bf16[48,2304]{1,0:T(8,128)(2,1)S(1)}, bf16[48,2304]{1,0:T(8,128)(2,1)S(1)}, u32[]{:S(2)}, u32[]{:S(2)}) collective-permute-start(bf16[48,2304]{1,0:T(8,128)(2,1)S(1)} %get-tuple-element.258.refs_0_), channel_id=1, source_target_pairs={{0,16},{4,20},{8,24},{12,28},{16,0},{20,4},{24,8},{28,12},{1,17},{... | collective-permute-start | bytes 663560 | tf_op jit(solution)/shard_map/ppermute | solution.py:971
  224.2 1.8 last_down.1
  226.0 5.5 %collective-permute-done.43.refs_1_ = bf16[48,2304]{1,0:T(8,128)(2,1)S(1)} collective-permute-done((bf16[48,2304]{1,0:T(8,128)(2,1)S(1)}, bf16[48,2304]{1,0:T(8,128)(2,1)S(1)}, u32[]{:S(2)}, u32[]{:S(2)}) %collective-permute-start.43) | collective-permute-done | bytes 221216 | tf_op jit(solution)/shard_map/ppermute | solution.py:971
  231.6 5.9 %collective-permute-done.45.refs_1_ = bf16[48,2304]{1,0:T(8,128)(2,1)S(1)} collective-permute-done((bf16[48,2304]{1,0:T(8,128)(2,1)S(1)}, bf16[48,2304]{1,0:T(8,128)(2,1)S(1)}, u32[]{:S(2)}, u32[]{:S(2)}) %collective-permute-start.45) | collective-permute-done | bytes 221216 | tf_op jit(solution)/shard_map/ppermute | solution.py:971
  238.7 3.2 %last_up.1 = (f32[192,3072]{1,0:T(8,128)}, f32[192,768]{1,0:T(8,128)}, f32[192,128]{1,0:T(8,128)}, f32[192]{0:T(256)}) custom-call(bf16[192,3072]{1,0:T(8,128)(2,1)} %refs_0_.11, bf16[192]{0:T(256)(128)(2,1)S(1)} %copy-done, bf16[96,3968]{1,0:T(8,128)(2,1)S(1)} %get-tuple-element.259.refs_2_, bf16[96,3968]{1,0:T(8,128)(2,1)S(1)} %collective-permute-done.47.refs_3_), custom_call_target="tpu_custom_call" | custom-call | bytes 2703744 | tf_op jit(solution)/shard_map/last_up/pallas_call | solution.py:820
  244.4 3.1 %collective-permute-done.46.refs_3_ = bf16[96,2304]{1,0:T(8,128)(2,1)S(1)} collective-permute-done((bf16[96,2304]{1,0:T(8,128)(2,1)S(1)}, bf16[96,2304]{1,0:T(8,128)(2,1)S(1)}, u32[]{:S(2)}, u32[]{:S(2)}) %collective-permute-start.46) | collective-permute-done | bytes 442400 | tf_op jit(solution)/shard_map/ppermute | solution.py:971
  247.5 2.6 %last_qkv.1 = (f32[192,2304]{1,0:T(8,128)}, f32[192]{0:T(256)}) custom-call(bf16[192,2304]{1,0:T(8,128)(2,1)} %refs_0_.10, bf16[192]{0:T(256)(128)(2,1)S(1)} %copy-done.1, bf16[96,2304]{1,0:T(8,128)(2,1)S(1)} %gradient_sums.29.refs_2_, bf16[96,2304]{1,0:T(8,128)(2,1)S(1)} %collective-permute-done.46.refs_3_), custom_call_target="tpu_custom_call" | custom-call | bytes 1769856 | tf_op jit(solution)/shard_map/last_qkv/pallas_call | solution.py:820
  (117 shorter events, 30.6 us)
Async XLA Ops:
  3.0 11.6 %collective-permute-start.1 = (bf16[64,2304]{1,0:T(8,128)(2,1)}, bf16[64,2304]{1,0:T(8,128)(2,1)}, u32[]{:S(2)}, u32[]{:S(2)}) collective-permute-start(bf16[64,2304]{1,0:T(8,128)(2,1)} %next_message.2), channel_id=1, source_target_pairs={{0,2},{1,3},{2,0},{3,1},{4,6},{5,7},{6,4},{7,5},{8,10},{9,11},{10,... | collective-permute-start | bytes 884744 | tf_op jit(solution)/shard_map/ppermute | solution.py:971
  6.0 6.6 %collective-permute-start.5 = (bf16[192,768]{1,0:T(8,128)(2,1)}, bf16[192,768]{1,0:T(8,128)(2,1)}, u32[]{:S(2)}, u32[]{:S(2)}) collective-permute-start(bf16[192,768]{1,0:T(8,128)(2,1)} %refs_0_.8), channel_id=1, source_target_pairs={{0,1},{1,0},{2,3},{3,2},{4,5},{5,4},{6,7},{7,6},{8,9},{9,8},{10,11... | collective-permute-start | bytes 884744 | tf_op jit(solution)/shard_map/ppermute | solution.py:971
  8.3 4.2 %collective-permute-start.3 = (bf16[8,2304]{1,0:T(8,128)(2,1)}, bf16[8,2304]{1,0:T(8,128)(2,1)}, u32[]{:S(2)}, u32[]{:S(2)}) collective-permute-start(bf16[8,2304]{1,0:T(8,128)(2,1)} %get-tuple-element.146.refs_0_), channel_id=1, source_target_pairs={{0,1},{1,0},{2,3},{3,2},{4,5},{5,4},{6,7},{7,6},{8,9},{9,8},{10,11... | collective-permute-start | bytes 110600 | tf_op jit(solution)/shard_map/ppermute | solution.py:971
  8.8 6.3 %collective-permute-start.2 = (bf16[192,2304]{1,0:T(8,128)(2,1)}, bf16[192,2304]{1,0:T(8,128)(2,1)}, u32[]{:S(2)}, u32[]{:S(2)}) collective-permute-start(bf16[192,2304]{1,0:T(8,128)(2,1)} %refs_0_.10), channel_id=1, source_target_pairs={{0,1},{1,0},{2,3},{3,2},{4,5},{5,4},{6,7},{7,6},{8,9},{9,8},{10,11... | collective-permute-start | bytes 2654216 | tf_op jit(solution)/shard_map/ppermute | solution.py:971
  8.8 6.3 %collective-permute-start.4 = (bf16[192,3072]{1,0:T(8,128)(2,1)}, bf16[192,3072]{1,0:T(8,128)(2,1)}, u32[]{:S(2)}, u32[]{:S(2)}) collective-permute-start(bf16[192,3072]{1,0:T(8,128)(2,1)} %refs_0_.11), channel_id=1, source_target_pairs={{0,1},{1,0},{2,3},{3,2},{4,5},{5,4},{6,7},{7,6},{8,9},{9,8},{10,11... | collective-permute-start | bytes 3538952 | tf_op jit(solution)/shard_map/ppermute | solution.py:971
  12.5 10.7 %collective-permute-start.6 = (bf16[72,2304]{1,0:T(8,128)(2,1)S(1)}, bf16[72,2304]{1,0:T(8,128)(2,1)S(1)}, u32[]{:S(2)}, u32[]{:S(2)}) collective-permute-start(bf16[72,2304]{1,0:T(8,128)(2,1)S(1)} %get-tuple-element.141), channel_id=1, source_target_pairs={{0,2},{1,3},{2,0},{3,1},{4,6},{5,7},{6,4},{7,5},{8,10},{9,11},{10,... | collective-permute-start | bytes 995336 | tf_op jit(solution)/shard_map/ppermute | solution.py:971
  12.6 24.6 %collective-permute-start = (bf16[64,3072]{1,0:T(8,128)(2,1)}, bf16[64,3072]{1,0:T(8,128)(2,1)}, u32[]{:S(2)}, u32[]{:S(2)}) collective-permute-start(bf16[64,3072]{1,0:T(8,128)(2,1)} %get-tuple-element.143), channel_id=1, source_target_pairs={{0,2},{1,3},{2,0},{3,1},{4,6},{5,7},{6,4},{7,5},{8,10},{9,11},{10,... | collective-permute-start | bytes 1179656 | tf_op jit(solution)/shard_map/ppermute | solution.py:971
  14.6 35.5 %collective-permute-start.13 = (bf16[64,3072]{1,0:T(8,128)(2,1)}, bf16[64,3072]{1,0:T(8,128)(2,1)}, u32[]{:S(2)}, u32[]{:S(2)}) collective-permute-start(bf16[64,3072]{1,0:T(8,128)(2,1)} %get-tuple-element.164), channel_id=1, source_target_pairs={{0,2},{1,3},{2,0},{3,1},{4,6},{5,7},{6,4},{7,5},{8,10},{9,11},{10,... | collective-permute-start | bytes 1179656 | tf_op jit(solution)/shard_map/ppermute | solution.py:971
  15.1 8.7 %collective-permute-start.8 = (bf16[64,2304]{1,0:T(8,128)(2,1)}, bf16[64,2304]{1,0:T(8,128)(2,1)S(1)}, u32[]{:S(2)}, u32[]{:S(2)}) collective-permute-start(bf16[64,2304]{1,0:T(8,128)(2,1)} %collective-permute-done.1.refs_6_), channel_id=1, source_target_pairs={{0,4},{4,0},{8,12},{12,8},{16,20},{20,16},{24,28},{28,24},{1,5},{5... | collective-permute-start | bytes 884744 | tf_op jit(solution)/shard_map/ppermute | solution.py:971
  23.3 2.1 collective-permute-start.7
  23.3 2.6 %collective-permute-start.9 = (bf16[64,2304]{1,0:T(8,128)(2,1)}, bf16[64,2304]{1,0:T(8,128)(2,1)S(1)}, u32[]{:S(2)}, u32[]{:S(2)}) collective-permute-start(bf16[64,2304]{1,0:T(8,128)(2,1)} %collective-permute-done.1.refs_6_), channel_id=1, source_target_pairs={{0,1},{1,0},{2,3},{3,2},{4,5},{5,4},{6,7},{7,6},{8,9},{9,8},{10,11... | collective-permute-start | bytes 884744 | tf_op jit(solution)/shard_map/ppermute | solution.py:971
  23.8 2.1 collective-permute-start.10
  25.3 25.4 %collective-permute-start.11 = (bf16[192,768]{1,0:T(8,128)(2,1)}, bf16[192,768]{1,0:T(8,128)(2,1)}, u32[]{:S(2)}, u32[]{:S(2)}) collective-permute-start(bf16[192,768]{1,0:T(8,128)(2,1)} %refs_0_.8), channel_id=1, source_target_pairs={{0,2},{1,3},{2,0},{3,1},{4,6},{5,7},{6,4},{7,5},{8,10},{9,11},{10,... | collective-permute-start | bytes 884744 | tf_op jit(solution)/shard_map/ppermute | solution.py:971
  37.2 13.5 %collective-permute-start.14 = (bf16[64,3072]{1,0:T(8,128)(2,1)}, bf16[64,3072]{1,0:T(8,128)(2,1)}, u32[]{:S(2)}, u32[]{:S(2)}) collective-permute-start(bf16[64,3072]{1,0:T(8,128)(2,1)} %collective-permute-done.refs_6_), channel_id=1, source_target_pairs={{0,4},{4,0},{8,12},{12,8},{16,20},{20,16},{24,28},{28,24},{1,5},{5... | collective-permute-start | bytes 1179656 | tf_op jit(solution)/shard_map/ppermute | solution.py:971
  50.1 4.4 %collective-permute-start.15 = (bf16[64,3072]{1,0:T(8,128)(2,1)}, bf16[64,3072]{1,0:T(8,128)(2,1)S(1)}, u32[]{:S(2)}, u32[]{:S(2)}) collective-permute-start(bf16[64,3072]{1,0:T(8,128)(2,1)} %collective-permute-done.refs_6_), channel_id=1, source_target_pairs={{0,1},{1,0},{2,3},{3,2},{4,5},{5,4},{6,7},{7,6},{8,9},{9,8},{10,11... | collective-permute-start | bytes 1179656 | tf_op jit(solution)/shard_map/ppermute | solution.py:971
  50.2 4.3 %collective-permute-start.16 = (bf16[64,3072]{1,0:T(8,128)(2,1)}, bf16[64,3072]{1,0:T(8,128)(2,1)S(1)}, u32[]{:S(2)}, u32[]{:S(2)}) collective-permute-start(bf16[64,3072]{1,0:T(8,128)(2,1)} %collective-permute-done.13.refs_7_), channel_id=1, source_target_pairs={{0,1},{1,0},{2,3},{3,2},{4,5},{5,4},{6,7},{7,6},{8,9},{9,8},{10,11... | collective-permute-start | bytes 1179656 | tf_op jit(solution)/shard_map/ppermute | solution.py:971
  50.7 3.8 %collective-permute-start.17 = (bf16[64,3072]{1,0:T(8,128)(2,1)}, bf16[64,3072]{1,0:T(8,128)(2,1)S(1)}, u32[]{:S(2)}, u32[]{:S(2)}) collective-permute-start(bf16[64,3072]{1,0:T(8,128)(2,1)} %collective-permute-done.14.refs_8_), channel_id=1, source_target_pairs={{0,1},{1,0},{2,3},{3,2},{4,5},{5,4},{6,7},{7,6},{8,9},{9,8},{10,11... | collective-permute-start | bytes 1179656 | tf_op jit(solution)/shard_map/ppermute | solution.py:971
  50.7 3.7 %collective-permute-start.12 = (bf16[192,768]{1,0:T(8,128)(2,1)}, bf16[192,768]{1,0:T(8,128)(2,1)S(1)}, u32[]{:S(2)}, u32[]{:S(2)}) collective-permute-start(bf16[192,768]{1,0:T(8,128)(2,1)} %collective-permute-done.11.refs_2_), channel_id=1, source_target_pairs={{0,1},{1,0},{2,3},{3,2},{4,5},{5,4},{6,7},{7,6},{8,9},{9,8},{10,11... | collective-permute-start | bytes 884744 | tf_op jit(solution)/shard_map/ppermute | solution.py:971
  52.9 29.8 %collective-permute-start.21 = (bf16[768,768]{1,0:T(8,128)(2,1)}, bf16[768,768]{1,0:T(8,128)(2,1)}, u32[]{:S(2)}, u32[]{:S(2)}) collective-permute-start(bf16[768,768]{1,0:T(8,128)(2,1)} %refs_0_.9), channel_id=1, source_target_pairs={{0,2},{1,3},{2,0},{3,1},{4,6},{5,7},{6,4},{7,5},{8,10},{9,11},{10,... | collective-permute-start | bytes 3538952 | tf_op jit(solution)/shard_map/ppermute | solution.py:971
  78.7 4.9 %collective-permute-start.18 = (bf16[2,768,768]{2,1,0:T(8,128)(2,1)}, bf16[2,768,768]{2,1,0:T(8,128)(2,1)}, u32[]{:S(2)}, u32[]{:S(2)}) collective-permute-start(bf16[2,768,768]{2,1,0:T(8,128)(2,1)} %grad_down.2), channel_id=1, source_target_pairs={{0,1},{1,0},{2,3},{3,2},{4,5},{5,4},{6,7},{7,6},{8,9},{9,8},{10,11... | collective-permute-start | bytes 7077896 | tf_op jit(solution)/shard_map/ppermute | solution.py:971
  82.1 5.8 %collective-permute-start.20 = (bf16[768,768]{1,0:T(8,128)(2,1)S(1)}, bf16[768,768]{1,0:T(8,128)(2,1)S(1)}, u32[]{:S(2)}, u32[]{:S(2)}) collective-permute-start(bf16[768,768]{1,0:T(8,128)(2,1)S(1)} %copy-done.10), channel_id=1, source_target_pairs={{0,1},{1,0},{2,3},{3,2},{4,5},{5,4},{6,7},{7,6},{8,9},{9,8},{10,11... | collective-permute-start | bytes 3538952 | tf_op jit(solution)/shard_map/ppermute | solution.py:971
  82.7 5.3 %collective-permute-start.22 = (bf16[768,768]{1,0:T(8,128)(2,1)}, bf16[768,768]{1,0:T(8,128)(2,1)S(1)}, u32[]{:S(2)}, u32[]{:S(2)}) collective-permute-start(bf16[768,768]{1,0:T(8,128)(2,1)} %collective-permute-done.21.refs_2_), channel_id=1, source_target_pairs={{0,1},{1,0},{2,3},{3,2},{4,5},{5,4},{6,7},{7,6},{8,9},{9,8},{10,11... | collective-permute-start | bytes 3538952 | tf_op jit(solution)/shard_map/ppermute | solution.py:971
  86.5 22.1 %collective-permute-start.19 = (bf16[768,384]{1,0:T(8,128)(2,1)}, bf16[768,384]{1,0:T(8,128)(2,1)}, u32[]{:S(2)}, u32[]{:S(2)}) collective-permute-start(bf16[768,384]{1,0:T(8,128)(2,1)} %get-tuple-element.172), channel_id=1, source_target_pairs={{0,2},{1,3},{2,0},{3,1},{4,6},{5,7},{6,4},{7,5},{8,10},{9,11},{10,... | collective-permute-start | bytes 1769480 | tf_op jit(solution)/shard_map/ppermute | solution.py:971
  87.2 21.4 %collective-permute-start.23 = (bf16[2,384,384]{2,1,0:T(8,128)(2,1)}, bf16[2,384,384]{2,1,0:T(8,128)(2,1)}, u32[]{:S(2)}, u32[]{:S(2)}) collective-permute-start(bf16[2,384,384]{2,1,0:T(8,128)(2,1)} %get-tuple-element.173), channel_id=1, source_target_pairs={{0,4},{4,0},{8,12},{12,8},{16,20},{20,16},{24,28},{28,24},{1,5},{5... | collective-permute-start | bytes 1769480 | tf_op jit(solution)/shard_map/ppermute | solution.py:971
  110.9 10.6 %collective-permute-start.25 = (bf16[384,384]{1,0:T(8,128)(2,1)}, bf16[384,384]{1,0:T(8,128)(2,1)}, u32[]{:S(2)}, u32[]{:S(2)}) collective-permute-start(bf16[384,384]{1,0:T(8,128)(2,1)} %get-tuple-element.185), channel_id=1, source_target_pairs={{0,4},{4,0},{8,12},{12,8},{16,20},{20,16},{24,28},{28,24},{1,5},{5... | collective-permute-start | bytes 884744 | tf_op jit(solution)/shard_map/ppermute | solution.py:971
  112.2 9.3 %collective-permute-start.26 = (bf16[384,384]{1,0:T(8,128)(2,1)}, bf16[384,384]{1,0:T(8,128)(2,1)}, u32[]{:S(2)}, u32[]{:S(2)}) collective-permute-start(bf16[384,384]{1,0:T(8,128)(2,1)} %get-tuple-element.186), channel_id=1, source_target_pairs={{0,2},{1,3},{2,0},{3,1},{4,6},{5,7},{6,4},{7,5},{8,10},{9,11},{10,... | collective-permute-start | bytes 884744 | tf_op jit(solution)/shard_map/ppermute | solution.py:971
  121.5 5.6 %collective-permute-start.24 = (bf16[2,192,3968]{2,1,0:T(8,128)(2,1)S(1)}, bf16[2,192,3968]{2,1,0:T(8,128)(2,1)S(1)}, u32[]{:S(2)}, u32[]{:S(2)}) collective-permute-start(bf16[2,192,3968]{2,1,0:T(8,128)(2,1)S(1)} %get-tuple-element.192), channel_id=1, source_target_pairs={{0,1},{1,0},{2,3},{3,2},{4,5},{5,4},{6,7},{7,6},{8,9},{9,8},{10,11... | collective-permute-start | bytes 9142280 | tf_op jit(solution)/shard_map/ppermute | solution.py:971
  123.4 21.9 %collective-permute-start.28 = (bf16[192,768]{1,0:T(8,128)(2,1)}, bf16[192,768]{1,0:T(8,128)(2,1)}, u32[]{:S(2)}, u32[]{:S(2)}) collective-permute-start(bf16[192,768]{1,0:T(8,128)(2,1)} %get-tuple-element.198), channel_id=1, source_target_pairs={{0,8},{4,12},{8,0},{12,4},{16,24},{20,28},{24,16},{28,20},{1,9},{5... | collective-permute-start | bytes 884744 | tf_op jit(solution)/shard_map/ppermute | solution.py:971
  128.5 21.4 %collective-permute-start.29 = (bf16[2,96,1920]{2,1,0:T(8,128)(2,1)}, bf16[2,96,1920]{2,1,0:T(8,128)(2,1)}, u32[]{:S(2)}, u32[]{:S(2)}) collective-permute-start(bf16[2,96,1920]{2,1,0:T(8,128)(2,1)} %get-tuple-element.203), channel_id=1, source_target_pairs={{0,4},{4,0},{8,12},{12,8},{16,20},{20,16},{24,28},{28,24},{1,5},{5... | collective-permute-start | bytes 2211848 | tf_op jit(solution)/shard_map/ppermute | solution.py:971
  129.3 20.6 %collective-permute-start.27 = (bf16[192,2048]{1,0:T(8,128)(2,1)}, bf16[192,2048]{1,0:T(8,128)(2,1)}, u32[]{:S(2)}, u32[]{:S(2)}) collective-permute-start(bf16[192,2048]{1,0:T(8,128)(2,1)} %get-tuple-element.202), channel_id=1, source_target_pairs={{0,2},{1,3},{2,0},{3,1},{4,6},{5,7},{6,4},{7,5},{8,10},{9,11},{10,... | collective-permute-start | bytes 2359304 | tf_op jit(solution)/shard_map/ppermute | solution.py:971
  147.2 24.9 %collective-permute-start.33 = (bf16[192,768]{1,0:T(8,128)(2,1)}, bf16[192,768]{1,0:T(8,128)(2,1)}, u32[]{:S(2)}, u32[]{:S(2)}) collective-permute-start(bf16[192,768]{1,0:T(8,128)(2,1)} %gradient_sums.19.refs_0_), channel_id=1, source_target_pairs={{0,16},{4,20},{8,24},{12,28},{16,0},{20,4},{24,8},{28,12},{1,17},{... | collective-permute-start | bytes 884744 | tf_op jit(solution)/shard_map/ppermute | solution.py:971
  152.2 11.7 %collective-permute-start.31 = (bf16[96,1920]{1,0:T(8,128)(2,1)}, bf16[96,1920]{1,0:T(8,128)(2,1)}, u32[]{:S(2)}, u32[]{:S(2)}) collective-permute-start(bf16[96,1920]{1,0:T(8,128)(2,1)} %get-tuple-element.213), channel_id=1, source_target_pairs={{0,2},{1,3},{2,0},{3,1},{4,6},{5,7},{6,4},{7,5},{8,10},{9,11},{10,... | collective-permute-start | bytes 1105928 | tf_op jit(solution)/shard_map/ppermute | solution.py:971
  153.5 10.4 %collective-permute-start.30 = (bf16[96,2048]{1,0:T(8,128)(2,1)}, bf16[96,2048]{1,0:T(8,128)(2,1)}, u32[]{:S(2)}, u32[]{:S(2)}) collective-permute-start(bf16[96,2048]{1,0:T(8,128)(2,1)} %get-tuple-element.212), channel_id=1, source_target_pairs={{0,4},{4,0},{8,12},{12,8},{16,20},{20,16},{24,28},{28,24},{1,5},{5... | collective-permute-start | bytes 1179656 | tf_op jit(solution)/shard_map/ppermute | solution.py:971
  166.1 9.8 %collective-permute-start.32 = (bf16[48,3968]{1,0:T(8,128)(2,1)}, bf16[48,3968]{1,0:T(8,128)(2,1)}, u32[]{:S(2)}, u32[]{:S(2)}) collective-permute-start(bf16[48,3968]{1,0:T(8,128)(2,1)} %get-tuple-element.219), channel_id=1, source_target_pairs={{0,8},{4,12},{8,0},{12,4},{16,24},{20,28},{24,16},{28,20},{1,9},{5... | collective-permute-start | bytes 1142792 | tf_op jit(solution)/shard_map/ppermute | solution.py:971
  172.1 3.9 %collective-permute-start.34 = (bf16[2,192,2304]{2,1,0:T(8,128)(2,1)S(1)}, bf16[2,192,2304]{2,1,0:T(8,128)(2,1)S(1)}, u32[]{:S(2)}, u32[]{:S(2)}) collective-permute-start(bf16[2,192,2304]{2,1,0:T(8,128)(2,1)S(1)} %get-tuple-element.228), channel_id=1, source_target_pairs={{0,1},{1,0},{2,3},{3,2},{4,5},{5,4},{6,7},{7,6},{8,9},{9,8},{10,11... | collective-permute-start | bytes 5308424 | tf_op jit(solution)/shard_map/ppermute | solution.py:971
  174.0 16.4 %collective-permute-start.35 = (bf16[192,768]{1,0:T(8,128)(2,1)}, bf16[192,768]{1,0:T(8,128)(2,1)}, u32[]{:S(2)}, u32[]{:S(2)}) collective-permute-start(bf16[192,768]{1,0:T(8,128)(2,1)} %gradient_sums.22.refs_0_), channel_id=1, source_target_pairs={{0,8},{4,12},{8,0},{12,4},{16,24},{20,28},{24,16},{28,20},{1,9},{5... | collective-permute-start | bytes 884744 | tf_op jit(solution)/shard_map/ppermute | solution.py:971
  178.1 27.1 %collective-permute-start.38 = (bf16[48,3968]{1,0:T(8,128)(2,1)}, bf16[48,3968]{1,0:T(8,128)(2,1)}, u32[]{:S(2)}, u32[]{:S(2)}) collective-permute-start(bf16[48,3968]{1,0:T(8,128)(2,1)} %get-tuple-element.233.refs_0_), channel_id=1, source_target_pairs={{0,16},{4,20},{8,24},{12,28},{16,0},{20,4},{24,8},{28,12},{1,17},{... | collective-permute-start | bytes 1142792 | tf_op jit(solution)/shard_map/ppermute | solution.py:971
  179.0 12.7 %collective-permute-start.36 = (bf16[192,1152]{1,0:T(8,128)(2,1)}, bf16[192,1152]{1,0:T(8,128)(2,1)}, u32[]{:S(2)}, u32[]{:S(2)}) collective-permute-start(bf16[192,1152]{1,0:T(8,128)(2,1)} %get-tuple-element.234), channel_id=1, source_target_pairs={{0,2},{1,3},{2,0},{3,1},{4,6},{5,7},{6,4},{7,5},{8,10},{9,11},{10,... | collective-permute-start | bytes 1327112 | tf_op jit(solution)/shard_map/ppermute | solution.py:971
  180.3 12.0 %collective-permute-start.37 = (bf16[2,96,1152]{2,1,0:T(8,128)(2,1)}, bf16[2,96,1152]{2,1,0:T(8,128)(2,1)}, u32[]{:S(2)}, u32[]{:S(2)}) collective-permute-start(bf16[2,96,1152]{2,1,0:T(8,128)(2,1)} %get-tuple-element.235), channel_id=1, source_target_pairs={{0,4},{4,0},{8,12},{12,8},{16,20},{20,16},{24,28},{28,24},{1,5},{5... | collective-permute-start | bytes 1327112 | tf_op jit(solution)/shard_map/ppermute | solution.py:971
  194.3 11.0 %collective-permute-start.39 = (bf16[96,1152]{1,0:T(8,128)(2,1)}, bf16[96,1152]{1,0:T(8,128)(2,1)}, u32[]{:S(2)}, u32[]{:S(2)}) collective-permute-start(bf16[96,1152]{1,0:T(8,128)(2,1)} %get-tuple-element.243), channel_id=1, source_target_pairs={{0,4},{4,0},{8,12},{12,8},{16,20},{20,16},{24,28},{28,24},{1,5},{5... | collective-permute-start | bytes 663560 | tf_op jit(solution)/shard_map/ppermute | solution.py:971
  195.3 10.0 %collective-permute-start.40 = (bf16[96,1152]{1,0:T(8,128)(2,1)}, bf16[96,1152]{1,0:T(8,128)(2,1)}, u32[]{:S(2)}, u32[]{:S(2)}) collective-permute-start(bf16[96,1152]{1,0:T(8,128)(2,1)} %get-tuple-element.244), channel_id=1, source_target_pairs={{0,2},{1,3},{2,0},{3,1},{4,6},{5,7},{6,4},{7,5},{8,10},{9,11},{10,... | collective-permute-start | bytes 663560 | tf_op jit(solution)/shard_map/ppermute | solution.py:971
  206.7 13.8 %collective-permute-start.41 = (bf16[48,3968]{1,0:T(8,128)(2,1)S(1)}, bf16[48,3968]{1,0:T(8,128)(2,1)S(1)}, u32[]{:S(2)}, u32[]{:S(2)}) collective-permute-start(bf16[48,3968]{1,0:T(8,128)(2,1)S(1)} %get-tuple-element.253.refs_0_), channel_id=1, source_target_pairs={{0,8},{4,12},{8,0},{12,4},{16,24},{20,28},{24,16},{28,20},{1,9},{5... | collective-permute-start | bytes 1142792 | tf_op jit(solution)/shard_map/ppermute | solution.py:971
  207.6 12.9 %collective-permute-start.42 = (bf16[48,2304]{1,0:T(8,128)(2,1)S(1)}, bf16[48,2304]{1,0:T(8,128)(2,1)S(1)}, u32[]{:S(2)}, u32[]{:S(2)}) collective-permute-start(bf16[48,2304]{1,0:T(8,128)(2,1)S(1)} %get-tuple-element.254), channel_id=1, source_target_pairs={{0,8},{4,12},{8,0},{12,4},{16,24},{20,28},{24,16},{28,20},{1,9},{5... | collective-permute-start | bytes 663560 | tf_op jit(solution)/shard_map/ppermute | solution.py:971
  208.8 15.4 %collective-permute-start.44 = (bf16[384,768]{1,0:T(8,128)(2,1)S(1)}, bf16[384,768]{1,0:T(8,128)(2,1)S(1)}, u32[]{:S(2)}, u32[]{:S(2)}) collective-permute-start(bf16[384,768]{1,0:T(8,128)(2,1)S(1)} %gradient_sums.24.refs_0_), channel_id=1, source_target_pairs={{0,4},{4,0},{8,12},{12,8},{16,20},{20,16},{24,28},{28,24},{1,5},{5... | collective-permute-start | bytes 1769480 | tf_op jit(solution)/shard_map/ppermute | solution.py:971
  220.6 18.1 %collective-permute-start.47 = (bf16[96,3968]{1,0:T(8,128)(2,1)S(1)}, bf16[96,3968]{1,0:T(8,128)(2,1)S(1)}, u32[]{:S(2)}, u32[]{:S(2)}) collective-permute-start(bf16[96,3968]{1,0:T(8,128)(2,1)S(1)} %get-tuple-element.259.refs_2_), channel_id=1, source_target_pairs={{0,4},{4,0},{8,12},{12,8},{16,20},{20,16},{24,28},{28,24},{1,5},{5... | collective-permute-start | bytes 2285576 | tf_op jit(solution)/shard_map/ppermute | solution.py:971
  221.6 9.9 %collective-permute-start.43 = (bf16[48,2304]{1,0:T(8,128)(2,1)S(1)}, bf16[48,2304]{1,0:T(8,128)(2,1)S(1)}, u32[]{:S(2)}, u32[]{:S(2)}) collective-permute-start(bf16[48,2304]{1,0:T(8,128)(2,1)S(1)} %get-tuple-element.258.refs_0_), channel_id=1, source_target_pairs={{0,16},{4,20},{8,24},{12,28},{16,0},{20,4},{24,8},{28,12},{1,17},{... | collective-permute-start | bytes 663560 | tf_op jit(solution)/shard_map/ppermute | solution.py:971
  231.6 6.0 %collective-permute-start.45 = (bf16[48,2304]{1,0:T(8,128)(2,1)S(1)}, bf16[48,2304]{1,0:T(8,128)(2,1)S(1)}, u32[]{:S(2)}, u32[]{:S(2)}) collective-permute-start(bf16[48,2304]{1,0:T(8,128)(2,1)S(1)} %gradient_sums.28.refs_0_), channel_id=1, source_target_pairs={{0,8},{4,12},{8,0},{12,4},{16,24},{20,28},{24,16},{28,20},{1,9},{5... | collective-permute-start | bytes 663560 | tf_op jit(solution)/shard_map/ppermute | solution.py:971
  237.6 9.9 %collective-permute-start.46 = (bf16[96,2304]{1,0:T(8,128)(2,1)S(1)}, bf16[96,2304]{1,0:T(8,128)(2,1)S(1)}, u32[]{:S(2)}, u32[]{:S(2)}) collective-permute-start(bf16[96,2304]{1,0:T(8,128)(2,1)S(1)} %gradient_sums.29.refs_2_), channel_id=1, source_target_pairs={{0,4},{4,0},{8,12},{12,8},{16,20},{20,16},{24,28},{28,24},{1,5},{5... | collective-permute-start | bytes 1327112 | tf_op jit(solution)/shard_map/ppermute | solution.py:971
  (11 other events, 105.5 us)
